TPU v7x, 32 devices: a whole 2x2x4 slice. The times are simulated.
32 devices in a mesh: rows: 8 (over z, y), cent: 4 (over x, core).
Axes of the slice: x: 2, y: 2, z: 4, core: 2. Of those that a mesh axis runs over, the one named last changes fastest.
Arguments:
- samples: bfloat16 [8192, 512], P('rows'), may hold values from -6 to 6
- weights: float32 [8192], P('rows'), may hold values from 0.2 to 18, as said below
- targets: float32 [16, 8192], P(None, 'rows'), may hold values from -6 to 6
- predictions: float32 [16, 8192], P(None, 'rows'), may hold values from -3 to 3
- centres: bfloat16 [32768, 512], P('rows'), may hold values from -6 to 6
- coefs: float32 [16, 32768], P(None, 'rows'), may hold values from -7 to 7
- block_index: int32 [2, 12288], P(None, 'cent'), may hold values from 0 to 32767, as said below
Outputs:
- new_coefs: float32 [16, 32768], P(None, 'rows')
- new_predictions: float32 [16, 8192], P(None, 'rows')
Inputs may be any that keep to these rules, and one draw needn't show every extreme that they name: Positive sample weights. `block_index`: no pool index appears twice in the whole array. In every step each aligned block of 3072 entries starting at a multiple of 3072 takes exactly 384 indices from each pool shard (index // 4096).
All inputs are finite; a program needn't handle non-finite values.
Results may differ from a plain program's by a relative error of at most 0.008.
Values may be sent and summed in bfloat16 or wider, within the bound.
No kernel may reach another device: no remote copies, remote signals or barrier semaphores. Data moves between devices by JAX's collectives and lax.ppermute only.
A program may use at most 64 MiB of HBM per device.

v0:
```python
import math

import jax
import jax.numpy as jnp
from jax import lax
from jax.sharding import PartitionSpec as P

RIDGE = 1.0


def kernel_tile(rows_x, rows_norm, centre_rows, centre_norm, sharpness, offset):
    products = lax.dot_general(
        rows_x, centre_rows, (((1,), (1,)), ((), ())), preferred_element_type=jnp.float32
    )
    exponent = offset + sharpness * (2.0 * products - rows_norm[:, None] - centre_norm[None, :])
    return jnp.exp(exponent).astype(jnp.bfloat16)


def local(samples, weights, targets, predictions, centres, coefs, block_index):
    feature_count = samples.shape[1]
    rows_dev = samples.shape[0]
    pool_dev = centres.shape[0]
    slice_len = block_index.shape[1]
    target_count = targets.shape[0]
    row_devices = lax.axis_size("rows")
    my_row = lax.axis_index("rows")
    per_owner = slice_len // row_devices
    sharpness = 1.3 / math.sqrt(8.0 * feature_count)
    offset = 2.0 * feature_count * sharpness - 1.5 - 0.5 * math.log(rows_dev * row_devices)
    block_rows = math.gcd(rows_dev, 512)
    row_norm = jnp.sum(jnp.square(samples.astype(jnp.float32)), axis=1)
    positions = jnp.arange(slice_len, dtype=jnp.int32)
    coef_now = coefs
    pred_now = predictions
    for step_idx in range(block_index.shape[0]):
        chosen_idx = block_index[step_idx]
        owners = chosen_idx // pool_dev
        local_pos = chosen_idx - owners * pool_dev
        is_mine = owners == my_row
        slot_pos = jnp.cumsum(is_mine.astype(jnp.int32)) - 1
        slot_pos = jnp.where(is_mine, slot_pos, per_owner)
        own_local = jnp.zeros((per_owner,), jnp.int32).at[slot_pos].set(local_pos, mode="drop")
        centre_rows = lax.all_gather(centres[own_local], "rows", axis=0, tiled=True)
        places = jnp.tile(own_local, row_devices)
        is_valid = positions // per_owner == my_row
        centre_norm = jnp.sum(jnp.square(centre_rows.astype(jnp.float32)), axis=1)
        own_coefs = jnp.where(is_valid[None, :], coef_now[:, places], 0.0)
        weighted = (weights[None, :] * (targets - pred_now)).astype(jnp.bfloat16)
        gradient = -RIDGE * own_coefs
        col_square = jnp.zeros((1, slice_len), jnp.float32)
        for first_row in range(0, rows_dev, block_rows):
            kernel = kernel_tile(
                samples[first_row : first_row + block_rows],
                row_norm[first_row : first_row + block_rows],
                centre_rows,
                centre_norm,
                sharpness,
                offset,
            )
            gradient = gradient + jnp.dot(
                weighted[:, first_row : first_row + block_rows],
                kernel,
                preferred_element_type=jnp.float32,
            )
            kernel_wide = kernel.astype(jnp.float32)
            row_weight = weights[first_row : first_row + block_rows]
            col_square = col_square + jnp.sum(
                row_weight[:, None] * kernel_wide * kernel_wide, axis=0, keepdims=True
            )
        gradient, col_square = lax.psum((gradient, col_square), "rows")
        change_coef = gradient / (col_square + RIDGE)
        coef_low = change_coef.astype(jnp.bfloat16)
        pieces = []
        for first_row in range(0, rows_dev, block_rows):
            kernel = kernel_tile(
                samples[first_row : first_row + block_rows],
                row_norm[first_row : first_row + block_rows],
                centre_rows,
                centre_norm,
                sharpness,
                offset,
            )
            pieces.append(
                lax.dot_general(
                    coef_low, kernel, (((1,), (1,)), ((), ())), preferred_element_type=jnp.float32
                )
            )
        change = jnp.concatenate(pieces, axis=1)
        write_pos = jnp.where(is_valid, places, pool_dev)
        update = (
            jnp.zeros((target_count, pool_dev), jnp.float32)
            .at[:, write_pos]
            .add(change_coef, mode="drop")
        )
        change, update = lax.psum((change, update), "cent")
        coef_now = coef_now + update
        pred_now = pred_now + change
    return (coef_now, pred_now)


def solution(mesh):
    in_specs = (
        P("rows", None),
        P("rows"),
        P(None, "rows"),
        P(None, "rows"),
        P("rows", None),
        P(None, "rows"),
        P(None, "cent"),
    )
    out_specs = (P(None, "rows"), P(None, "rows"))
    return jax.shard_map(local, mesh=mesh, in_specs=in_specs, out_specs=out_specs, check_vma=False)
```

profile of v0, /device:TPU:0, one launch (start us, length us, event | category | flops | bytes accessed | tf_op | source)
XLA Modules:
  0.0 482.6 jit_solution(3256530171506873865)
XLA Ops:
  10.3 11.8 %scatter_custom_fusion = s32[384]{0:T(512)S(1)} fusion(s32[3072]{0:T(1024)S(1)} %bitcast.95, s32[3072]{0:T(1024)S(1)} %fusion.24, s32[]{:T(128)} %constant.51.clone.1), kind=kCustom, calls=%fused_computation.133 | custom fusion | bytes 1540 | tf_op jit(solution)/shard_map/scatter | solution.py:42
  22.1 5.4 %gather_fusion.1 = bf16[384,512]{1,0:T(8,128)(2,1)} fusion(bf16[4096,512]{1,0:T(8,128)(2,1)} %param.11, s32[1024]{0:T(1024)S(1)} %pad_clamp_fusion.1), kind=kCustom, calls=%fused_computation.1 | custom fusion | bytes 787968 | tf_op jit(solution)/shard_map/gather | solution.py:43
  27.6 11.8 %scatter_custom_fusion.2 = s32[384]{0:T(512)S(1)} fusion(s32[3072]{0:T(1024)S(1)} %bitcast.94, s32[3072]{0:T(1024)S(1)} %fusion.30, s32[]{:T(128)} %constant.51.clone.1), kind=kCustom, calls=%fused_computation.131 | custom fusion | bytes 1540 | tf_op jit(solution)/shard_map/scatter | solution.py:42
  39.4 5.3 %gather_fusion.3 = bf16[384,512]{1,0:T(8,128)(2,1)} fusion(bf16[4096,512]{1,0:T(8,128)(2,1)} %param.11, s32[1024]{0:T(1024)S(1)} %pad_clamp_fusion), kind=kCustom, calls=%fused_computation.3 | custom fusion | bytes 787968 | tf_op jit(solution)/shard_map/gather | solution.py:43
  47.7 10.9 %gather_fusion = f32[3072,16]{1,0:T(8,128)} fusion(f32[16,4096]{0,1:T(8,128)S(1)} %copy.19, s32[3072]{0:T(1024)S(1)} %broadcast_clamp_fusion.1), kind=kCustom, calls=%fused_computation | custom fusion | bytes 405504 | tf_op jit(solution)/shard_map/gather | solution.py:47
  60.8 29.6 %all-gather.5.cloned.1.call-done = bf16[3072,512]{1,0:T(8,128)(2,1)} async-done(((bf16[384,512]{1,0:T(8,128)(2,1)}), bf16[3072,512]{1,0:T(8,128)(2,1)}) %all-gather.5.cloned.1.call-update) | async-done | bytes 3145744 | tf_op jit(solution)/shard_map/all_gather | solution.py:43
  90.4 2.7 multiply_reduce_fusion.1
  93.2 3.5 exponential_convert_fusion.3
  103.7 47.6 %all-gather.7.cloned.1.call-done = bf16[3072,512]{1,0:T(8,128)(2,1)} async-done(((bf16[384,512]{1,0:T(8,128)(2,1)}), bf16[3072,512]{1,0:T(8,128)(2,1)}) %all-gather.7.cloned.1.call-update) | async-done | bytes 3145744 | tf_op jit(solution)/shard_map/all_gather | solution.py:43
  151.3 2.7 multiply_reduce_fusion
  154.1 7.7 %fusion.3 = (f32[3072]{0:T(1024)S(1)}, f32[3072]{0:T(1024)S(1)}, bf16[3072,512]{0,1:T(8,128)(2,1)}) fusion(f32[512]{0:T(512)S(1)} %get-tuple-element.26, bf16[3072,512]{0,1:T(8,128)(2,1)S(1)} %copy-done.4, f32[3072]{0:T(1024)S(1)} %multiply_reduce_fusion, f32[512]{0:T(512)S(1)} %get-tuple-element.28, bf16[3072,512]{1,0:T(8,128)(2,1)} %all-gather.7.cloned.1.call-done, ...), kind=kOutput, calls=%fused_computation.15 | convolution fusion | flops 1632626688 | bytes 10002432 | tf_op jit(solution)/shard_map/dot_general | solution.py:12
  161.8 5.1 %fusion.2 = (f32[3072]{0:T(1024)S(1)}, f32[3072]{0:T(1024)S(1)}, bf16[3072,512]{0,1:T(8,128)(2,1)}) fusion(f32[512]{0:T(512)S(1)} %get-tuple-element.27, bf16[3072,512]{0,1:T(8,128)(2,1)S(1)} %exponential_convert_fusion.3, f32[3072]{0:T(1024)S(1)} %multiply_reduce_fusion, f32[512]{0:T(512)S(1)} %get-tuple-element.29, bf16[3072,512]{1,0:T(8,128)(2,1)S(1)} %copy-done.6, ...), kind=kOutput, calls=%fused_computation.14 | convolution fusion | flops 1632626688 | bytes 10002432 | tf_op jit(solution)/shard_map/dot_general | solution.py:12
  166.9 35.4 %all-reduce = (f32[1,3072]{1,0:T(1,128)S(1)}, f32[1,3072]{1,0:T(1,128)}) all-reduce(f32[1,3072]{1,0:T(1,128)S(1)} %bitcast.91, f32[1,3072]{1,0:T(1,128)S(1)} %bitcast.90), channel_id=1, replica_groups=mesh['rows'=8,'cent'=4] {'rows'}, use_global_device_ids=true, to_apply=%region_8.9 | all-reduce | flops 6144 | bytes 49152 | tf_op jit(solution)/shard_map/psum | solution.py:70
  202.4 22.2 %all-reduce.8.cloned.1.call-done = f32[16,3072]{1,0:T(8,128)} async-done(((f32[16,3072]{1,0:T(8,128)}), f32[16,3072]{1,0:T(8,128)}) %all-reduce.8.cloned.1.call-update) | async-done | bytes 196624 | tf_op jit(solution)/shard_map/psum | solution.py:70
  230.9 18.7 %scatter_custom_fusion.1 = f32[16,4096]{0,1:T(8,128)} fusion(s32[3072]{0:T(1024)} %bitcast.93, f32[3072,16]{1,0:T(8,128)} %copy.18, f32[]{:T(128)} %constant.48.clone.1), kind=kCustom, calls=%fused_computation.29 | custom fusion | flops 49152 | bytes 262656 | tf_op jit(solution)/shard_map/scatter-add | solution.py:93
  249.9 51.3 %all-reduce.14.cloned.1.call-done = (f32[16,4096]{0,1:T(8,128)}, f32[16,1024]{1,0:T(8,128)}) async-done(((f32[16,4096]{0,1:T(8,128)}, f32[16,1024]{1,0:T(8,128)}), (f32[16,4096]{0,1:T(8,128)}, f32[16,1024]{1,0:T(8,128)})) %all-reduce.14.cloned.1.call-update) | async-done | bytes 327696 | tf_op jit(solution)/shard_map/psum | solution.py:95
  303.7 10.9 %gather_fusion.2 = f32[3072,16]{1,0:T(8,128)} fusion(f32[16,4096]{0,1:T(8,128)S(1)} %add.223, s32[3072]{0:T(1024)S(1)} %broadcast_clamp_fusion), kind=kCustom, calls=%fused_computation.2 | custom fusion | bytes 405504 | tf_op jit(solution)/shard_map/gather | solution.py:47
  316.5 2.6 convolution_add_fusion.1
  320.6 70.8 %all-reduce.10.cloned.1.call-done = f32[16,3072]{1,0:T(8,128)} async-done(((f32[16,3072]{1,0:T(8,128)}), f32[16,3072]{1,0:T(8,128)}) %all-reduce.10.cloned.1.call-update) | async-done | bytes 196624 | tf_op jit(solution)/shard_map/psum | solution.py:70
  394.1 3.0 fusion.46
  398.7 18.6 %scatter_custom_fusion.3 = f32[16,4096]{0,1:T(8,128)} fusion(s32[3072]{0:T(1024)} %bitcast.92, f32[3072,16]{1,0:T(8,128)} %copy.21, f32[]{:T(128)} %constant.48.clone.1), kind=kCustom, calls=%fused_computation.27 | custom fusion | flops 49152 | bytes 262656 | tf_op jit(solution)/shard_map/scatter-add | solution.py:93
  417.4 51.7 %all-reduce.12.cloned.1.call-done = (f32[16,4096]{0,1:T(8,128)}, f32[16,1024]{1,0:T(8,128)}) async-done(((f32[16,4096]{0,1:T(8,128)}, f32[16,1024]{1,0:T(8,128)}), (f32[16,4096]{0,1:T(8,128)}, f32[16,1024]{1,0:T(8,128)})) %all-reduce.12.cloned.1.call-update) | async-done | bytes 327696 | tf_op jit(solution)/shard_map/psum | solution.py:95
  469.1 3.2 add.236
  472.2 2.9 copy.22
  (117 shorter events, 32.7 us)
Async XLA Ops:
  7.2 83.2 %all-gather.5.cloned.1.call-start = ((), (), s32[]{:S(2)}) async-start(), calls=%async_computation.2 | async-start | bytes 3538944 | tf_op jit(solution)/shard_map/all_gather | solution.py:43
  22.1 23.5 %copy-start.13 = (f32[16,4096]{1,0:T(8,128)S(1)}, f32[16,4096]{1,0:T(8,128)}, u32[]{:S(2)}) copy-start(f32[16,4096]{1,0:T(8,128)} %param.12) | copy-start | bytes 786436
  27.5 123.8 %all-gather.7.cloned.1.call-start = ((), (), s32[]{:S(2)}) async-start(), calls=%async_computation.3 | async-start | bytes 3538944 | tf_op jit(solution)/shard_map/all_gather | solution.py:43
  44.7 15.7 %copy-start.10 = (bf16[1024,512]{1,0:T(8,128)(2,1)S(1)}, bf16[1024,512]{1,0:T(8,128)(2,1)}, u32[]{:S(2)}) copy-start(bf16[1024,512]{1,0:T(8,128)(2,1)} %param.7) | copy-start | bytes 3145732
  44.7 179.8 %all-reduce.8.cloned.1.call-start = ((), (), s32[]{:S(2)}) async-start(), calls=%async_computation | async-start | bytes 393216 | tf_op jit(solution)/shard_map/psum | solution.py:70
  45.6 15.2 %copy-start.21 = (f32[1024]{0:T(1024)S(1)}, f32[1024]{0:T(1024)}, u32[]{:S(2)}) copy-start(f32[1024]{0:T(1024)} %param.8) | copy-start | bytes 12292
  45.6 15.2 %copy-start.14 = (f32[16,1024]{1,0:T(8,128)S(1)}, f32[16,1024]{1,0:T(8,128)}, u32[]{:S(2)}) copy-start(f32[16,1024]{1,0:T(8,128)} %param.9) | copy-start | bytes 196612
  45.6 15.2 %copy-start.16 = (f32[16,1024]{1,0:T(8,128)S(1)}, f32[16,1024]{1,0:T(8,128)}, u32[]{:S(2)}) copy-start(f32[16,1024]{1,0:T(8,128)} %param.10) | copy-start | bytes 196612
  46.2 46.9 %copy-start = (f32[16,4096]{0,1:T(8,128)}, f32[16,4096]{0,1:T(8,128)S(1)}, u32[]{:S(2)}) copy-start(f32[16,4096]{0,1:T(8,128)S(1)} %copy.19) | copy-start | bytes 786436
  60.5 36.3 %copy-start.22 = (pred[3072]{0:T(1024)(128)(4,1)}, pred[3072]{0:T(1024)(128)(4,1)S(1)}, u32[]{:S(2)}) copy-start(pred[3072]{0:T(1024)(128)(4,1)S(1)} %fusion.25) | copy-start | bytes 9220
  103.4 197.8 %all-reduce.14.cloned.1.call-start = ((), (), s32[]{:S(2)}) async-start(), calls=%async_computation.5 | async-start | bytes 4325376 | tf_op jit(solution)/shard_map/psum | solution.py:95
  154.1 7.7 %copy-start.6 = (bf16[3072,512]{1,0:T(8,128)(2,1)S(1)}, bf16[3072,512]{1,0:T(8,128)(2,1)}, u32[]{:S(2)}) copy-start(bf16[3072,512]{1,0:T(8,128)(2,1)} %all-gather.7.cloned.1.call-done) | copy-start | bytes 9437188
  154.1 7.7 %copy-start.12 = (bf16[1024,512]{1,0:T(8,128)(2,1)S(1)}, bf16[1024,512]{1,0:T(8,128)(2,1)}, u32[]{:S(2)}) copy-start(bf16[1024,512]{1,0:T(8,128)(2,1)} %param.7) | copy-start | bytes 3145732
  224.5 4.7 copy-start.8
  229.3 20.6 %copy-start.20 = (s32[3072,1]{0,1:T(1,128)S(1)}, s32[3072,1]{0,1:T(1,128)}, u32[]{:S(2)}) copy-start(s32[3072,1]{0,1:T(1,128)} %get-tuple-element.22) | copy-start | bytes 36868
  249.6 141.9 %all-reduce.10.cloned.1.call-start = ((), (), s32[]{:S(2)}) async-start(), calls=%async_computation.1 | async-start | bytes 393216 | tf_op jit(solution)/shard_map/psum | solution.py:70
  303.7 12.8 %copy-start.15 = (f32[16,1024]{1,0:T(8,128)S(1)}, f32[16,1024]{1,0:T(8,128)}, u32[]{:S(2)}) copy-start(f32[16,1024]{1,0:T(8,128)} %param.9) | copy-start | bytes 196612
  303.7 12.8 %copy-start.17 = (f32[16,1024]{1,0:T(8,128)S(1)}, f32[16,1024]{1,0:T(8,128)}, u32[]{:S(2)}) copy-start(f32[16,1024]{1,0:T(8,128)} %param.10) | copy-start | bytes 196612
  303.7 12.8 %copy-start.19 = (f32[16,1024]{1,0:T(8,128)S(1)}, f32[16,1024]{1,0:T(8,128)}, u32[]{:S(2)}) copy-start(f32[16,1024]{1,0:T(8,128)} %get-tuple-element.15) | copy-start | bytes 196612
  303.7 12.8 %copy-start.23 = (pred[3072]{0:T(1024)(128)(4,1)S(1)}, pred[3072]{0:T(1024)(128)(4,1)}, u32[]{:S(2)}) copy-start(pred[3072]{0:T(1024)(128)(4,1)} %copy-done.22) | copy-start | bytes 9220
  316.5 4.1 copy-start.24
  320.5 148.5 %all-reduce.12.cloned.1.call-start = ((), (), s32[]{:S(2)}) async-start(), calls=%async_computation.4 | async-start | bytes 4325376 | tf_op jit(solution)/shard_map/psum | solution.py:95
  391.5 5.7 %copy-start.9 = (f32[16,3072]{1,0:T(8,128)S(1)}, f32[16,3072]{1,0:T(8,128)}, u32[]{:S(2)}) copy-start(f32[16,3072]{1,0:T(8,128)} %all-reduce.10.cloned.1.call-done) | copy-start | bytes 589828
  469.1 6.0 %copy-start.18 = (f32[16,1024]{1,0:T(8,128)S(1)}, f32[16,1024]{1,0:T(8,128)}, u32[]{:S(2)}) copy-start(f32[16,1024]{1,0:T(8,128)} %get-tuple-element.13) | copy-start | bytes 196612
  (7 other events, 16.5 us)
Sparse Core Ops, SparseCore 0:
  27.6 62.7 all-gather.4
  92.6 58.6 all-gather.6
  155.2 69.3 all-reduce.7
  249.7 51.5 all-reduce.13
  320.7 70.7 all-reduce.9
  417.5 51.5 all-reduce.11
where the time goes:
time: 483 us
  waiting for transfers between devices  273 us (57%)
  local copies, waits for them, and re-layouts  71.3 us (15%)
  other arithmetic  56 us (12%)
  blocking collectives  35.4 us (7%)
  matrix products  31.1 us (6%)
  between operations  14.5 us (3%)
    psum x2, waiting for transfers between devices, local(): change, update = lax.psum((change, update), 'cent')  103 us
    psum x2, waiting for transfers between devices, local(): gradient, col_square = lax.psum((gradient, col_square), 'rows')  93 us
    all_gather x2, waiting for transfers between devices, local(): centre_rows = lax.all_gather(centres[own_local], 'rows', axis=0, tiled=True)  77.2 us
    scatter-add x2, other arithmetic, local(): update = jnp.zeros((target_count, pool_dev), jnp.float32).at[:, write_pos...  37.3 us
    psum x1, blocking collectives, local(): gradient, col_square = lax.psum((gradient, col_square), 'rows')  35.4 us
    gather x4, local copies, waits for them, and re-layouts, local(): own_coefs = jnp.where(is_valid[None, :], coef_now[:, places], 0.0)  25.5 us
    scatter x2, local copies, waits for them, and re-layouts, local(): jnp.zeros((per_owner,), jnp.int32).at[slot_pos].set(local_pos, mode='drop')  23.5 us
    dot_general x4, matrix products, kernel_tile(): lax.dot_general(rows_x, centre_rows, (((1,), (1,)), ((), ())), preferred_...  18.8 us
  transfers between devices with their start and end apart: 6, of which 6 were waited for; matrix products, arithmetic and copies ran while one was open for 12% of the time, Pallas kernels for 0%

commit v1 on v0

v1 whole, which is shorter than its diff:
```python
import functools
import math

import jax
import jax.numpy as jnp
from jax import lax
from jax.experimental import pallas as pl
from jax.experimental.pallas import tpu as pltpu
from jax.sharding import PartitionSpec as P

RIDGE = 1.0
LANES = 128
POOL_BLOCK = 256
LOG2E = math.log2(math.e)
NT = (((1,), (1,)), ((), ()))
F32 = jnp.float32
BF16 = jnp.bfloat16


def split3(x):
    first = x.astype(BF16)
    rest = x - first.astype(F32)
    second = rest.astype(BF16)
    third = (rest - second.astype(F32)).astype(BF16)
    return first, second, third


def split3_outside(x):
    first = lax.reduce_precision(x, 8, 7)
    rest = x - first
    second = lax.reduce_precision(rest, 8, 7)
    third = rest - second
    return first.astype(BF16), second.astype(BF16), third.astype(BF16)


def round_up(value, multiple):
    return -(-value // multiple) * multiple


def compact_kernel(steps, per_step, targets, tile, off_ref, dest_ref, pool_ref, side_ref, out_ref, side_out, norm_ref, coef_ref):
    group = pl.program_id(0)
    blocks = pool_ref.shape[0] // POOL_BLOCK

    @pl.when(group == 0)
    def _():
        out_ref[...] = jnp.zeros_like(out_ref)
        side_out[...] = jnp.zeros_like(side_out)

    for i in range(blocks):
        pool_rows = pool_ref[i * POOL_BLOCK : (i + 1) * POOL_BLOCK, :]
        side_rows = side_ref[i * POOL_BLOCK : (i + 1) * POOL_BLOCK, :]
        for step in range(steps):
            start = off_ref[step, group * blocks + i]
            end = off_ref[step, group * blocks + i + 1]
            base = pl.multiple_of((start // 16) * 16, 16)
            need = end - base
            dest = jnp.concatenate(
                [dest_ref[step, 2 * i : 2 * i + 1, :], dest_ref[step, 2 * i + 1 : 2 * i + 2, :]], axis=1
            ) - base
            for first, size in ((0, 128), (128, 144)):

                @pl.when((need > first) & (end > start))
                def _(first=first, size=size):
                    slots = lax.broadcasted_iota(jnp.int32, (size, POOL_BLOCK), 0) + first
                    pick = jnp.where(slots == dest, 1.0, 0.0).astype(BF16)
                    rows = jnp.dot(pick, pool_rows, preferred_element_type=F32)
                    side = jnp.dot(pick, side_rows, preferred_element_type=F32)
                    at = pl.ds(pl.multiple_of(base + first, 16), size)
                    out_ref[step, at, :] += rows.astype(BF16)
                    side_out[step, at, :] += side.astype(BF16)

    @pl.when(group == pl.num_programs(0) - 1)
    def _():
        features = out_ref.shape[2]
        ones = jnp.ones((8, features), BF16)
        eye = (
            lax.broadcasted_iota(jnp.int32, (3 * targets, LANES), 0)
            == lax.broadcasted_iota(jnp.int32, (3 * targets, LANES), 1)
        )
        eye = jnp.where(eye, 1.0, 0.0).astype(BF16)
        for step in range(steps):
            for first in range(0, per_step, tile):
                rows = out_ref[step, first : first + tile, :].astype(F32)
                square = rows * rows
                high = square.astype(BF16)
                low = (square - high.astype(F32)).astype(BF16)
                norm = lax.dot_general(ones, high, NT, preferred_element_type=F32)
                norm = norm + lax.dot_general(ones, low, NT, preferred_element_type=F32)
                norm_ref[step, :, first : first + tile] = norm
                side = side_out[step, first : first + tile, :]
                parts = lax.dot_general(eye, side, NT, preferred_element_type=F32)
                coef_ref[step, :, first : first + tile] = (
                    parts[:targets] + parts[targets : 2 * targets] + parts[2 * targets :]
                )


def compact(off, dest, pool, side, per_step, targets):
    steps = dest.shape[0]
    pool_dev, features = pool.shape
    groups = pool_dev // (8 * LANES)
    length = round_up(per_step, 16) + POOL_BLOCK + 16
    tile = math.gcd(per_step, 512)
    whole = lambda *shape: pl.BlockSpec(shape, lambda g, off: (0,) * len(shape))
    return pl.pallas_call(
        functools.partial(compact_kernel, steps, per_step, targets, tile),
        name="compact",
        out_shape=(
            jax.ShapeDtypeStruct((steps, length, features), BF16),
            jax.ShapeDtypeStruct((steps, length, LANES), BF16),
            jax.ShapeDtypeStruct((steps, 8, per_step), F32),
            jax.ShapeDtypeStruct((steps, targets, per_step), F32),
        ),
        grid_spec=pltpu.PrefetchScalarGridSpec(
            num_scalar_prefetch=1,
            grid=(groups,),
            in_specs=[
                pl.BlockSpec((steps, 8, LANES), lambda g, off: (0, g, 0)),
                pl.BlockSpec((8 * LANES, features), lambda g, off: (g, 0)),
                pl.BlockSpec((8 * LANES, LANES), lambda g, off: (g, 0)),
            ],
            out_specs=[
                whole(steps, length, features),
                whole(steps, length, LANES),
                whole(steps, 8, per_step),
                whole(steps, targets, per_step),
            ],
        ),
        cost_estimate=pl.CostEstimate(flops=10**10, bytes_accessed=8 * 10**6, transcendentals=0),
    )(off, dest, pool, side)


def block_kernel(steps, targets, quarter, scale, offset, slot_ref, rows_ref, chosen_ref, norm_ref, *refs):
    sums_in, (k_ref, sums_ref, side_ref, row_ref, weight_ref) = refs[-6 - 0], refs[-5:]
    tile, step = pl.program_id(0), pl.program_id(1)

    @pl.when((tile == 0) & (step == 0))
    def _():
        rows = rows_ref[:quarter, :].astype(F32)
        row_ref[...] = jnp.sum(rows * rows, axis=1, keepdims=True) * (scale * LOG2E) - offset * LOG2E
        parts = rows_ref[quarter : quarter + 3, quarter : 2 * quarter].astype(F32)
        weight = jnp.sum(parts, axis=0, keepdims=True)
        weight_ref[...] = jnp.transpose(jnp.broadcast_to(weight, (8, quarter)))[:, :1]
        side_ref[:targets, :] = rows_ref[quarter : quarter + targets, :quarter].astype(F32)
        side_ref[targets:, :] = jnp.broadcast_to(weight, (side_ref.shape[0] - targets, quarter))

    dots = lax.dot_general(rows_ref[:quarter, :], chosen_ref[0], NT, preferred_element_type=F32)
    centre = norm_ref[0, :1, :] * (scale * LOG2E)
    k_low = jnp.exp2(dots * (2.0 * scale * LOG2E) - row_ref[...] - centre).astype(BF16)
    k_ref[0] = k_low
    wide = k_low.astype(F32)
    square = jnp.sum(weight_ref[...] * (wide * wide), axis=0, keepdims=True)

    @pl.when(step == 0)
    def _():
        weighted = rows_ref[quarter : quarter + targets, :quarter]
        share = jnp.dot(weighted, k_low, preferred_element_type=F32)
        if sums_in is None:
            sums_ref[...] = jnp.zeros_like(sums_ref)
            sums_ref[:targets, :] = share
        else:
            sums_ref[...] = sums_in[...]
            sums_ref[:targets, :] += share

    for s in range(steps):

        @pl.when(step == s)
        def _(s=s):
            sums_ref[targets + s : targets + s + 1, :] += square


def block_call(slot, rows, chosen, norm, state, per_step, targets, row_devices, scale, offset):
    steps = chosen.shape[0]
    features = chosen.shape[2]
    quarter = rows.shape[0] - round_up(targets, 16)
    tile = math.gcd(per_step, 512)
    tiles = per_step // tile
    sum_rows = round_up(targets + steps, 8)
    side_rows = round_up(targets + 1, 8)
    in_specs = [
        pl.BlockSpec(rows.shape, lambda j, s, slot: (0, 0)),
        pl.BlockSpec((1, tile, features), lambda j, s, slot: (s, j, 0)),
        pl.BlockSpec((1, 8, tile), lambda j, s, slot: (s, 0, j)),
    ]
    sums_spec = pl.BlockSpec((sum_rows, tile), lambda j, s, slot: (0, j))
    operands = [slot, rows, chosen, norm]
    aliases = {}
    if state is not None:
        in_specs += [pl.BlockSpec(memory_space=pl.ANY), pl.BlockSpec(memory_space=pl.ANY), sums_spec]
        k_all, sums, side = state
        operands += [k_all, side, sums]
        aliases = {4: 0, 5: 2, 6: 1}

    def body(slot_ref, rows_ref, chosen_ref, norm_ref, *refs):
        if state is None:
            refs = (None,) + refs
        else:
            refs = refs[2:]
        block_kernel(
            steps, targets, quarter, scale, offset, slot_ref, rows_ref, chosen_ref, norm_ref, *refs
        )

    entries = quarter * per_step * steps
    return pl.pallas_call(
        body,
        name="kernel_block",
        out_shape=(
            jax.ShapeDtypeStruct((row_devices, quarter, steps * per_step), BF16),
            jax.ShapeDtypeStruct((sum_rows, per_step), F32),
            jax.ShapeDtypeStruct((side_rows, row_devices * quarter), F32),
        ),
        grid_spec=pltpu.PrefetchScalarGridSpec(
            num_scalar_prefetch=1,
            grid=(tiles, steps),
            in_specs=in_specs,
            out_specs=[
                pl.BlockSpec((1, quarter, tile), lambda j, s, slot: (slot[0], 0, s * tiles + j)),
                sums_spec,
                pl.BlockSpec((side_rows, quarter), lambda j, s, slot: (0, slot[0])),
            ],
            scratch_shapes=[pltpu.VMEM((quarter, 1), F32), pltpu.VMEM((quarter, 1), F32)],
        ),
        input_output_aliases=aliases,
        cost_estimate=pl.CostEstimate(
            flops=2 * entries * features, bytes_accessed=2 * entries, transcendentals=entries
        ),
    )(*operands)


def change_kernel(targets, step, sums_ref, square_ref, coef_ref, k_ref, *refs):
    delta_ref, change_ref, low_ref = refs[-3:]
    part = pl.program_id(0)

    @pl.when(part == 0)
    def _():
        total = jnp.sum(sums_ref[:, :targets, :], axis=0)
        square = jnp.sum(square_ref[:, targets + step : targets + step + 1, :], axis=0)
        delta = (total - RIDGE * coef_ref[0]) / (square + RIDGE)
        delta_ref[...] = delta
        low_ref[...] = delta.astype(BF16)

    change = lax.dot_general(low_ref[...], k_ref[0], NT, preferred_element_type=F32)
    if len(refs) > 3:
        change = change + refs[0][0]
    change_ref[0] = change


def change_call(sums, squares, coef, k_all, step, targets, before=None):
    row_devices, quarter, width = k_all.shape
    per_step = sums.shape[2]
    whole = lambda shape: pl.BlockSpec(shape, lambda i: (0,) * len(shape))
    change_spec = pl.BlockSpec((1, targets, quarter), lambda i: (i, 0, 0))
    more = [] if before is None else [before]
    return pl.pallas_call(
        functools.partial(change_kernel, targets, step),
        name="change",
        grid=(row_devices,),
        in_specs=[
            whole(sums.shape),
            whole(squares.shape),
            pl.BlockSpec((1, targets, per_step), lambda i: (step, 0, 0)),
            pl.BlockSpec((1, quarter, per_step), lambda i: (i, 0, step)),
        ]
        + [change_spec] * len(more),
        out_specs=[whole((targets, per_step)), change_spec],
        out_shape=(
            jax.ShapeDtypeStruct((targets, per_step), F32),
            jax.ShapeDtypeStruct((row_devices, targets, quarter), F32),
        ),
        scratch_shapes=[pltpu.VMEM((targets, per_step), BF16)],
        cost_estimate=pl.CostEstimate(
            flops=2 * targets * row_devices * quarter * per_step,
            bytes_accessed=2 * row_devices * quarter * per_step,
            transcendentals=0,
        ),
    )(sums, squares, coef, k_all, *more)


def gradient_kernel(targets, moved_ref, side_ref, k_ref, out_ref):
    part = pl.program_id(0)
    weighted = (side_ref[:targets, :] - moved_ref[0]).astype(BF16)
    share = jnp.dot(weighted, k_ref[0], preferred_element_type=F32)

    @pl.when(part == 0)
    def _():
        out_ref[...] = share

    @pl.when(part > 0)
    def _():
        out_ref[...] += share


def gradient_call(moved, side, k_all, step, targets, per_step):
    row_devices, quarter, width = k_all.shape
    return pl.pallas_call(
        functools.partial(gradient_kernel, targets),
        name="gradient",
        grid=(row_devices,),
        in_specs=[
            pl.BlockSpec((1, targets, quarter), lambda i: (i, 0, 0)),
            pl.BlockSpec((side.shape[0], quarter), lambda i: (0, i)),
            pl.BlockSpec((1, quarter, per_step), lambda i: (i, 0, step)),
        ],
        out_specs=pl.BlockSpec((targets, per_step), lambda i: (0, 0)),
        out_shape=jax.ShapeDtypeStruct((targets, per_step), F32),
        cost_estimate=pl.CostEstimate(
            flops=2 * targets * row_devices * quarter * per_step,
            bytes_accessed=2 * row_devices * quarter * per_step,
            transcendentals=0,
        ),
    )(moved, side, k_all)


def scatter_kernel(targets, per_step, off_ref, dest_ref, delta_ref, coef_ref, out_ref, parts_ref):
    group = pl.program_id(0)
    blocks = out_ref.shape[1] // POOL_BLOCK
    length = parts_ref.shape[1]

    @pl.when(group == 0)
    def _():
        for part, value in enumerate(split3(delta_ref[...])):
            parts_ref[part * targets : (part + 1) * targets, :per_step] = value
        parts_ref[:, per_step:] = jnp.zeros((3 * targets, length - per_step), BF16)

    for i in range(blocks):
        columns = slice(i * POOL_BLOCK, (i + 1) * POOL_BLOCK)
        start = off_ref[0, group * blocks + i]
        end = off_ref[0, group * blocks + i + 1]
        base = pl.multiple_of((start // LANES) * LANES, LANES)
        dest = jnp.concatenate(
            [dest_ref[0, 2 * i : 2 * i + 1, :], dest_ref[0, 2 * i + 1 : 2 * i + 2, :]], axis=1
        ) - base
        out_ref[:, columns] = coef_ref[:, columns]
        for first in range(0, POOL_BLOCK + LANES, LANES):

            @pl.when((end - base > first) & (end > start))
            def _(first=first):
                slots = lax.broadcasted_iota(jnp.int32, (LANES, POOL_BLOCK), 0) + first
                pick = jnp.where(slots == dest, 1.0, 0.0).astype(BF16)
                at = pl.ds(pl.multiple_of(base + first, LANES), LANES)
                moved = jnp.dot(parts_ref[:, at], pick, preferred_element_type=F32)
                out_ref[:, columns] += (
                    moved[:targets] + moved[targets : 2 * targets] + moved[2 * targets :]
                )


def scatter_call(off, dest, delta, coefs, step):
    targets, per_step = delta.shape
    pool_dev = coefs.shape[1]
    groups = pool_dev // (8 * LANES)
    length = round_up(per_step, LANES) + POOL_BLOCK + LANES
    return pl.pallas_call(
        functools.partial(scatter_kernel, targets, per_step),
        name="scatter",
        grid_spec=pltpu.PrefetchScalarGridSpec(
            num_scalar_prefetch=1,
            grid=(groups,),
            in_specs=[
                pl.BlockSpec((1, 8, LANES), lambda g, off: (step, g, 0)),
                pl.BlockSpec((targets, per_step), lambda g, off: (0, 0)),
                pl.BlockSpec((targets, 8 * LANES), lambda g, off: (0, g)),
            ],
            out_specs=pl.BlockSpec((targets, 8 * LANES), lambda g, off: (0, g)),
            scratch_shapes=[pltpu.VMEM((3 * targets, length), BF16)],
        ),
        out_shape=jax.ShapeDtypeStruct((targets, pool_dev), F32),
        cost_estimate=pl.CostEstimate(flops=10**9, bytes_accessed=10**6, transcendentals=0),
    )(off[step : step + 1], dest, delta, coefs)


def swap(value, axis, bit):
    count = lax.axis_size(axis)
    return lax.ppermute(value, axis, [(i, i ^ bit) for i in range(count)])


def bits_of(count):
    return [1 << k for k in range(count.bit_length() - 1)]


def local(samples, weights, targets, predictions, centres, coefs, block_index):
    rows_dev, features = samples.shape
    pool_dev = centres.shape[0]
    steps, slice_len = block_index.shape
    target_count = targets.shape[0]
    row_devices, cent_devices = lax.axis_size("rows"), lax.axis_size("cent")
    my_row, my_cent = lax.axis_index("rows"), lax.axis_index("cent")
    quarter = rows_dev // cent_devices
    per_step = slice_len * cent_devices // row_devices
    sharpness = 1.3 / math.sqrt(8.0 * features)
    offset = 2.0 * features * sharpness - 1.5 - 0.5 * math.log(rows_dev * row_devices)

    at = my_cent * quarter
    own_rows = lax.dynamic_slice_in_dim(samples, at, quarter, 0)
    own_weight = lax.dynamic_slice_in_dim(weights, at, quarter, 0)[None, :]
    own_target = lax.dynamic_slice_in_dim(targets, at, quarter, 1)
    own_pred = lax.dynamic_slice_in_dim(predictions, at, quarter, 1)
    weighted = (own_weight * (own_target - own_pred)).astype(BF16)
    side_count = round_up(target_count, 16)
    weight_parts = jnp.concatenate(split3_outside(own_weight), axis=0)
    side_block = jnp.concatenate(
        [
            jnp.pad(weighted, ((0, side_count - target_count), (0, 0))),
            jnp.pad(weight_parts, ((0, side_count - 3), (0, features - 2 * quarter))),
        ],
        axis=1,
    )
    chunks = {0: jnp.concatenate([own_rows, side_block], axis=0)}

    high_count = pool_dev // LANES
    place = block_index - my_row * pool_dev
    inside = (place >= 0) & (place < pool_dev)
    high = jnp.where(inside, place // LANES, -1)
    low = jnp.where(inside, place % LANES, 0)
    high_hot = (high[:, None, :] == jnp.arange(high_count)[None, :, None]).astype(BF16)
    low_hot = (low[:, None, :] == jnp.arange(LANES)[None, :, None]).astype(BF16)
    member = jnp.einsum("shl,sgl->shg", high_hot, low_hot, preferred_element_type=F32).astype(BF16)
    for bit in bits_of(cent_devices):
        member = member + swap(member, "cent", bit)

    for bit in reversed(bits_of(row_devices)):
        for have in sorted(chunks):
            chunks[have | bit] = swap(chunks[have], "rows", bit)

    upper = (jnp.arange(LANES)[:, None] <= jnp.arange(LANES)[None, :]).astype(BF16)
    before = (jnp.arange(high_count)[:, None] > jnp.arange(high_count)[None, :]).astype(BF16)
    running = jnp.einsum("shg,gk->shk", member, upper, preferred_element_type=F32)
    row_count = running[:, :, -1:]
    row_start = jnp.einsum("hi,sik->shk", before, row_count.astype(BF16), preferred_element_type=F32)
    rank = row_start + running - 1.0
    dest = jnp.where(member > 0, rank, -65536.0).astype(jnp.int32)
    group_rows = POOL_BLOCK // LANES
    off = row_start[:, ::group_rows, 0].astype(jnp.int32)
    off = jnp.concatenate([off, jnp.full((steps, 1), per_step, jnp.int32)], axis=1)

    coef_parts = jnp.concatenate(split3_outside(coefs), axis=0)
    side = jnp.pad(coef_parts, ((0, LANES - 3 * target_count), (0, 0))).T
    chosen, _, norm, own_coef = compact(off, dest, centres, side, per_step, target_count)

    state = None
    for have in sorted(chunks, key=lambda c: (bin(c).count("1"), c)):
        slot = (my_row ^ have).astype(jnp.int32)[None]
        k_all, sums, info = block_call(
            slot, chunks[have], chosen, norm, state, per_step, target_count, row_devices, sharpness, offset
        )
        state = (k_all, sums, info)

    squares = lax.all_gather(sums, "cent")
    gathered = squares
    total_change = None
    coef_now = coefs
    weight_row = info[target_count].reshape(row_devices, 1, quarter)
    moved = None
    for step in range(steps):
        if step > 0:
            share = change * weight_row
            if step > 1:
                share = share - last_change * weight_row
            for bit in bits_of(row_devices):
                share = share + swap(share.astype(BF16), "rows", bit).astype(F32)
            moved = share if moved is None else moved + share
            gradient = gradient_call(moved, info, k_all, step, target_count, per_step)
            gathered = lax.all_gather(gradient, "cent")
        last_change = total_change
        delta, change = change_call(
            gathered, squares, own_coef, k_all, step, target_count, total_change
        )
        total_change = change
        coef_now = scatter_call(off, dest, delta, coef_now, step)

    arrived = lax.all_to_all(total_change, "rows", 0, 0)
    own_change = jnp.sum(arrived, axis=0)
    full = lax.all_gather(own_change, "cent")
    full = full.transpose(1, 0, 2).reshape(target_count, rows_dev)
    return (coef_now, predictions + full)


def solution(mesh):
    in_specs = (
        P("rows", None),
        P("rows"),
        P(None, "rows"),
        P(None, "rows"),
        P("rows", None),
        P(None, "rows"),
        P(None, "cent"),
    )
    out_specs = (P(None, "rows"), P(None, "rows"))
    return jax.shard_map(local, mesh=mesh, in_specs=in_specs, out_specs=out_specs, check_vma=False)
```

time: 483 us -> 178 us (0.37)
  waiting for transfers between devices: 273 us -> 12.5 us
  Pallas kernels: 0 us -> 103 us
  local copies, waits for them, and re-layouts: 71.3 us -> 6.41 us
  other arithmetic: 56 us -> 9.26 us
  matrix products: 31.1 us -> 0.95 us
  starting transfers between devices: 0.91 us -> 22.8 us
  blocking collectives: 35.4 us -> 20.7 us
  between operations: 14.5 us -> 0.84 us
    psum x4 -> x0, waiting for transfers between devices: 196 us -> none  [the longest x2 103 us: local(): change, update = lax.psum((change, update), 'cent')]
    pallas_call x0 -> x14, Pallas kernels: none -> 103 us  [the longest x8 53.6 us: block_call(): pl.pallas_call(body, name='kernel_block', out_shape=(jax.ShapeDtypeStruct...]
    all_gather x2 -> x0, waiting for transfers between devices: 77.2 us -> none  [local(): centre_rows = lax.all_gather(centres[own_local], 'rows', axis=0, tiled=True)]
    scatter-add x2 -> x0, other arithmetic: 37.3 us -> none  [local(): update = jnp.zeros((target_count, pool_dev), jnp.float32).at[:, write_pos...]
    gather x6 -> x0, local copies, waits for them, and re-layouts: 36.2 us -> none  [the longest x4 25.5 us: local(): own_coefs = jnp.where(is_valid[None, :], coef_now[:, places], 0.0)]
    psum x1 -> x0, blocking collectives: 35.4 us -> none  [local(): gradient, col_square = lax.psum((gradient, col_square), 'rows')]
    dot_general x12 -> x3, matrix products: 31.1 us -> 0.95 us  [the longest x1 0.68 us: local(): jnp.einsum('shl,sgl->shg', high_hot, low_hot, preferred_element_type=F32)]
    scatter x2 -> x0, local copies, waits for them, and re-layouts: 23.5 us -> none  [local(): jnp.zeros((per_owner,), jnp.int32).at[slot_pos].set(local_pos, mode='drop')]
  transfers between devices with their start and end apart: 6 -> 13, of which waited for: 6 -> 5; matrix products, arithmetic and copies ran while one was open for 12% -> 4% of each run, Pallas kernels for 0% -> 42%
where the time goes in v1:
time: 178 us; the launch traced here: 176 us
  Pallas kernels  103 us (58%)
  starting transfers between devices  22.8 us (13%)
  blocking collectives  20.7 us (12%)
  waiting for transfers between devices  12.5 us (7%)
  other arithmetic  9.26 us (5%)
  local copies, waits for them, and re-layouts  6.41 us (4%)
    pallas_call x8, Pallas kernels, block_call(): pl.pallas_call(body, name='kernel_block', out_shape=(jax.ShapeDtypeStruct...  53.6 us
    ppermute x12, starting transfers between devices, swap(): return lax.ppermute(value, axis, [(i, i ^ bit) for i in range(count)])  17.9 us
    pallas_call x2, Pallas kernels, change_call(): pl.pallas_call(functools.partial(change_kernel, targets, step), name='cha...  15.4 us
    pallas_call x1, Pallas kernels, compact(): pl.pallas_call(functools.partial(compact_kernel, steps, per_step, targets...  14.4 us
    pallas_call x2, Pallas kernels, scatter_call(): pl.pallas_call(functools.partial(scatter_kernel, targets, per_step), name...  12.7 us
    ppermute x12, waiting for transfers between devices, swap(): return lax.ppermute(value, axis, [(i, i ^ bit) for i in range(count)])  12.5 us
    all_gather x1, blocking collectives, local(): squares = lax.all_gather(sums, 'cent')  8.51 us
    all_gather x1, blocking collectives, local(): gathered = lax.all_gather(gradient, 'cent')  6.99 us
  transfers between devices with their start and end apart: 13, of which 5 were waited for; matrix products, arithmetic and copies ran while one was open for 4% of the time, Pallas kernels for 42%

profile of v1, /device:TPU:0, one launch (start us, length us, event | category | flops | bytes accessed | tf_op | source)
XLA Modules:
  0.0 176.4 jit_solution(5662360236775092812)
XLA Ops:
  2.7 3.1 %collective-permute-start.8 = (bf16[272,512]{1,0:T(8,128)(2,1)S(1)}, bf16[272,512]{1,0:T(8,128)(2,1)}, u32[]{:S(2)}, u32[]{:S(2)}) collective-permute-start(bf16[272,512]{1,0:T(8,128)(2,1)S(1)} %maximum_maximum_fusion.rows_ref), channel_id=1, source_target_pairs={{0,4},{4,0},{8,12},{12,8},{16,20},{20,16},{24,28},{28,24},{1,5},{5... | collective-permute-start | bytes 835592 | tf_op jit(solution)/shard_map/ppermute | solution.py:372
  7.4 2.6 %collective-permute-start.2 = (bf16[272,512]{1,0:T(8,128)(2,1)S(1)}, bf16[272,512]{1,0:T(8,128)(2,1)S(1)}, u32[]{:S(2)}, u32[]{:S(2)}) collective-permute-start(bf16[272,512]{1,0:T(8,128)(2,1)S(1)} %maximum_maximum_fusion.rows_ref), channel_id=1, source_target_pairs={{0,16},{4,20},{8,24},{12,28},{16,0},{20,4},{24,8},{28,12},{1,17},{... | collective-permute-start | bytes 835592 | tf_op jit(solution)/shard_map/ppermute | solution.py:372
  18.7 3.4 %collective-permute-done.2.rows_ref = bf16[272,512]{1,0:T(8,128)(2,1)S(1)} collective-permute-done((bf16[272,512]{1,0:T(8,128)(2,1)S(1)}, bf16[272,512]{1,0:T(8,128)(2,1)S(1)}, u32[]{:S(2)}, u32[]{:S(2)}) %collective-permute-start.2) | collective-permute-done | bytes 278560 | tf_op jit(solution)/shard_map/ppermute | solution.py:372
  22.6 14.4 %compact.1 = (bf16[2,1808,512]{2,1,0:T(8,128)(2,1)}, bf16[2,1808,128]{2,1,0:T(8,128)(2,1)}, f32[2,8,1536]{2,1,0:T(8,128)}, f32[2,16,1536]{2,1,0:T(8,128)}) custom-call(s32[2,17]{1,0:T(2,128)} %concatenate.15.off_ref, s32[2,32,128]{2,1,0:T(8,128)} %select_convert_fusion.dest_ref, bf16[4096,512]{1,0:T(8,128)(2,1)} %pool_ref.1, ...), custom_call_target="tpu_custom_call" | custom-call | flops 10000000000 | bytes 8000000 | tf_op jit(solution)/shard_map/compact/pallas_call | solution.py:104
  37.5 6.7 %kernel_block.8 = (bf16[8,256,3072]{2,1,0:T(8,128)(2,1)}, f32[24,1536]{1,0:T(8,128)}, f32[24,2048]{1,0:T(8,128)}) custom-call(s32[1]{0:T(128)} %bitcast.11.slot_ref, bf16[272,512]{1,0:T(8,128)(2,1)} %copy-done.1, bf16[2,1808,512]{2,1,0:T(8,128)(2,1)} %get-tuple-element.33.chosen_ref, f32[2,8,1536]{2,1,0:T(8,128)} %get-tuple-element.34.norm_ref), custom_call_target="tpu_custom_call" | custom-call | flops 805306368 | bytes 1572864 | tf_op jit(solution)/shard_map/kernel_block/pallas_call | solution.py:203
  45.8 6.7 %kernel_block.9 = (bf16[8,256,3072]{2,1,0:T(8,128)(2,1)}, f32[24,1536]{1,0:T(8,128)}, f32[24,2048]{1,0:T(8,128)}) custom-call(s32[1]{0:T(128)} %bitcast.10.slot_ref, bf16[272,512]{1,0:T(8,128)(2,1)} %collective-permute-done.8.rows_ref, ...), custom_call_target="tpu_custom_call", output_to_operand_aliasing={{0}: (4, {}), {2}: (5, {}), {1}: (6, {})} | custom-call | flops 805306368 | bytes 1572864 | tf_op jit(solution)/shard_map/kernel_block/pallas_call | solution.py:203
  52.5 6.8 %kernel_block.10 = (bf16[8,256,3072]{2,1,0:T(8,128)(2,1)}, f32[24,1536]{1,0:T(8,128)}, f32[24,2048]{1,0:T(8,128)}) custom-call(s32[1]{0:T(128)} %bitcast.9.slot_ref, bf16[272,512]{1,0:T(8,128)(2,1)} %copy-done.3, bf16[2,1808,512]{2,1,0:T(8,128)(2,1)} %get-tuple-element.33.chosen_ref, ...), custom_call_target="tpu_custom_call", output_to_operand_aliasing={{0}: (4, {}), {2}: (5, {}), {1}: (6, {})} | custom-call | flops 805306368 | bytes 1572864 | tf_op jit(solution)/shard_map/kernel_block/pallas_call | solution.py:203
  59.8 6.7 %kernel_block.11 = (bf16[8,256,3072]{2,1,0:T(8,128)(2,1)}, f32[24,1536]{1,0:T(8,128)}, f32[24,2048]{1,0:T(8,128)}) custom-call(s32[1]{0:T(128)} %bitcast.8.slot_ref, bf16[272,512]{1,0:T(8,128)(2,1)} %copy-done.2, bf16[2,1808,512]{2,1,0:T(8,128)(2,1)} %get-tuple-element.33.chosen_ref, ...), custom_call_target="tpu_custom_call", output_to_operand_aliasing={{0}: (4, {}), {2}: (5, {}), {1}: (6, {})} | custom-call | flops 805306368 | bytes 1572864 | tf_op jit(solution)/shard_map/kernel_block/pallas_call | solution.py:203
  67.3 6.7 %kernel_block.12 = (bf16[8,256,3072]{2,1,0:T(8,128)(2,1)}, f32[24,1536]{1,0:T(8,128)}, f32[24,2048]{1,0:T(8,128)}) custom-call(s32[1]{0:T(128)} %bitcast.7.slot_ref, bf16[272,512]{1,0:T(8,128)(2,1)} %copy-done.6, bf16[2,1808,512]{2,1,0:T(8,128)(2,1)} %get-tuple-element.33.chosen_ref, ...), custom_call_target="tpu_custom_call", output_to_operand_aliasing={{0}: (4, {}), {2}: (5, {}), {1}: (6, {})} | custom-call | flops 805306368 | bytes 1572864 | tf_op jit(solution)/shard_map/kernel_block/pallas_call | solution.py:203
  74.7 6.6 %kernel_block.13 = (bf16[8,256,3072]{2,1,0:T(8,128)(2,1)}, f32[24,1536]{1,0:T(8,128)}, f32[24,2048]{1,0:T(8,128)}) custom-call(s32[1]{0:T(128)} %bitcast.6.slot_ref, bf16[272,512]{1,0:T(8,128)(2,1)} %copy-done.5, bf16[2,1808,512]{2,1,0:T(8,128)(2,1)} %get-tuple-element.33.chosen_ref, ...), custom_call_target="tpu_custom_call", output_to_operand_aliasing={{0}: (4, {}), {2}: (5, {}), {1}: (6, {})} | custom-call | flops 805306368 | bytes 1572864 | tf_op jit(solution)/shard_map/kernel_block/pallas_call | solution.py:203
  81.3 6.8 %kernel_block.14 = (bf16[8,256,3072]{2,1,0:T(8,128)(2,1)}, f32[24,1536]{1,0:T(8,128)}, f32[24,2048]{1,0:T(8,128)}) custom-call(s32[1]{0:T(128)} %bitcast.5.slot_ref, bf16[272,512]{1,0:T(8,128)(2,1)} %copy-done.4, bf16[2,1808,512]{2,1,0:T(8,128)(2,1)} %get-tuple-element.33.chosen_ref, ...), custom_call_target="tpu_custom_call", output_to_operand_aliasing={{0}: (4, {}), {2}: (5, {}), {1}: (6, {})} | custom-call | flops 805306368 | bytes 1572864 | tf_op jit(solution)/shard_map/kernel_block/pallas_call | solution.py:203
  88.8 6.6 %kernel_block.15 = (bf16[8,256,3072]{2,1,0:T(8,128)(2,1)}, f32[24,1536]{1,0:T(8,128)}, f32[24,2048]{1,0:T(8,128)}) custom-call(s32[1]{0:T(128)} %bitcast.3.slot_ref, bf16[272,512]{1,0:T(8,128)(2,1)} %copy-done.7, bf16[2,1808,512]{2,1,0:T(8,128)(2,1)} %get-tuple-element.33.chosen_ref, ...), custom_call_target="tpu_custom_call", output_to_operand_aliasing={{0}: (4, {}), {2}: (5, {}), {1}: (6, {})} | custom-call | flops 805306368 | bytes 1572864 | tf_op jit(solution)/shard_map/kernel_block/pallas_call | solution.py:203
  95.5 8.5 %all-gather = f32[96,1536]{1,0:T(8,128)} all-gather(f32[24,1536]{1,0:T(8,128)} %get-tuple-element.56), channel_id=2, replica_groups=mesh['rows'=8,'cent'=4] {'cent'}, dimensions={0}, use_global_device_ids=true | all-gather | bytes 737280 | tf_op jit(solution)/shard_map/all_gather | solution.py:446
  104.9 7.9 %change.2 = (f32[16,1536]{1,0:T(8,128)}, f32[8,16,256]{2,1,0:T(8,128)}) custom-call(f32[4,24,1536]{2,1,0:T(8,128)} %bitcast.24, f32[4,24,1536]{2,1,0:T(8,128)} %bitcast.25, f32[2,16,1536]{2,1,0:T(8,128)} %get-tuple-element.57.coef_ref, bf16[8,256,3072]{2,1,0:T(8,128)(2,1)} %get-tuple-element.58.k_ref), custom_call_target="tpu_custom_call" | custom-call | flops 100663296 | bytes 6291456 | tf_op jit(solution)/shard_map/change/pallas_call | solution.py:253
  115.2 2.8 %collective-permute-done.9 = bf16[8,16,256]{2,1,0:T(8,128)(2,1)S(1)} collective-permute-done((bf16[8,16,256]{2,1,0:T(8,128)(2,1)S(1)}, bf16[8,16,256]{2,1,0:T(8,128)(2,1)S(1)}, u32[]{:S(2)}, u32[]{:S(2)}) %collective-permute-start.9) | collective-permute-done | bytes 65568 | tf_op jit(solution)/shard_map/ppermute | solution.py:372
  120.7 2.7 %collective-permute-done.10 = bf16[8,16,256]{2,1,0:T(8,128)(2,1)S(1)} collective-permute-done((bf16[8,16,256]{2,1,0:T(8,128)(2,1)S(1)}, bf16[8,16,256]{2,1,0:T(8,128)(2,1)S(1)}, u32[]{:S(2)}, u32[]{:S(2)}) %collective-permute-start.10) | collective-permute-done | bytes 65568 | tf_op jit(solution)/shard_map/ppermute | solution.py:372
  124.3 2.7 %collective-permute-start.11 = (bf16[8,16,256]{2,1,0:T(8,128)(2,1)S(1)}, bf16[8,16,256]{2,1,0:T(8,128)(2,1)S(1)}, u32[]{:S(2)}, u32[]{:S(2)}) collective-permute-start(bf16[8,16,256]{2,1,0:T(8,128)(2,1)S(1)} %fusion.5), channel_id=1, source_target_pairs={{0,16},{4,20},{8,24},{12,28},{16,0},{20,4},{24,8},{28,12},{1,17},{... | collective-permute-start | bytes 196616 | tf_op jit(solution)/shard_map/ppermute | solution.py:372
  131.1 6.7 %gradient.1 = f32[16,1536]{1,0:T(8,128)} custom-call(f32[8,16,256]{2,1,0:T(8,128)} %convert_add_fusion.moved_ref, f32[24,2048]{1,0:T(8,128)} %get-tuple-element.60.side_ref, bf16[8,256,3072]{2,1,0:T(8,128)(2,1)} %get-tuple-element.58.k_ref), custom_call_target="tpu_custom_call" | custom-call | flops 100663296 | bytes 6291456 | tf_op jit(solution)/shard_map/gradient/pallas_call | solution.py:294
  137.8 7.0 %all-gather.1 = f32[64,1536]{1,0:T(8,128)} all-gather(f32[16,1536]{1,0:T(8,128)} %gradient.1), channel_id=3, replica_groups=mesh['rows'=8,'cent'=4] {'cent'}, dimensions={0}, use_global_device_ids=true | all-gather | bytes 491520 | tf_op jit(solution)/shard_map/all_gather | solution.py:461
  144.8 7.6 %change.3 = (f32[16,1536]{1,0:T(8,128)}, f32[8,16,256]{2,1,0:T(8,128)}) custom-call(f32[4,16,1536]{2,1,0:T(8,128)} %bitcast.27, f32[4,24,1536]{2,1,0:T(8,128)} %bitcast.26, f32[2,16,1536]{2,1,0:T(8,128)} %get-tuple-element.57.coef_ref, bf16[8,256,3072]{2,1,0:T(8,128)(2,1)} %get-tuple-element.58.k_ref, f32[8,16,256]{2,1,0:T(8,128)} %get-tuple-element.59.refs_0_), custom_call_target="tpu_custom_call" | custom-call | flops 100663296 | bytes 6291456 | tf_op jit(solution)/shard_map/change/pallas_call | solution.py:253
  152.3 4.9 %all-to-all-start = ((f32[8,16,256]{2,1,0:T(8,128)}), f32[8,16,256]{2,1,0:T(8,128)S(1)}, u32[]{:S(2)}, u32[]{:S(2)}) async-start(f32[8,16,256]{2,1,0:T(8,128)} %get-tuple-element.63), calls=%async_computation | async-start | bytes 262144 | tf_op jit(solution)/shard_map/all_to_all | solution.py:469
  157.8 6.4 %scatter.2.coef_ref = f32[16,4096]{1,0:T(8,128)} custom-call(s32[1,17]{1,0:T(1,128)} %get-tuple-element.71.off_ref, s32[2,32,128]{2,1,0:T(8,128)} %select_convert_fusion.dest_ref, f32[16,1536]{1,0:T(8,128)} %get-tuple-element.62.delta_ref, f32[16,4096]{1,0:T(8,128)} %coef_ref.1), custom_call_target="tpu_custom_call" | custom-call | flops 1000000000 | bytes 1000000 | tf_op jit(solution)/shard_map/scatter/pallas_call | solution.py:351
  164.2 6.3 %scatter.3 = f32[16,4096]{1,0:T(8,128)} custom-call(s32[1,17]{1,0:T(1,128)} %get-tuple-element.72.off_ref, s32[2,32,128]{2,1,0:T(8,128)} %select_convert_fusion.dest_ref, f32[16,1536]{1,0:T(8,128)} %get-tuple-element.61.delta_ref, f32[16,4096]{1,0:T(8,128)} %scatter.2.coef_ref), custom_call_target="tpu_custom_call" | custom-call | flops 1000000000 | bytes 1000000 | tf_op jit(solution)/shard_map/scatter/pallas_call | solution.py:351
  170.5 5.2 %all-gather.2 = f32[64,256]{1,0:T(8,128)S(1)} all-gather(f32[16,256]{1,0:T(8,128)S(1)} %reduce_sum.9), channel_id=4, replica_groups=mesh['rows'=8,'cent'=4] {'cent'}, dimensions={0}, use_global_device_ids=true | all-gather | bytes 81920 | tf_op jit(solution)/shard_map/all_gather | solution.py:471
  (70 shorter events, 29.8 us)
Async XLA Ops:
  0.6 1.2 copy-start
  2.7 34.2 %copy-start.1 = (bf16[272,512]{1,0:T(8,128)(2,1)}, bf16[272,512]{1,0:T(8,128)(2,1)S(1)}, u32[]{:S(2)}) copy-start(bf16[272,512]{1,0:T(8,128)(2,1)S(1)} %maximum_maximum_fusion.rows_ref) | copy-start | bytes 835588
  2.7 43.1 %collective-permute-start.8 = (bf16[272,512]{1,0:T(8,128)(2,1)S(1)}, bf16[272,512]{1,0:T(8,128)(2,1)}, u32[]{:S(2)}, u32[]{:S(2)}) collective-permute-start(bf16[272,512]{1,0:T(8,128)(2,1)S(1)} %maximum_maximum_fusion.rows_ref), channel_id=1, source_target_pairs={{0,4},{4,0},{8,12},{12,8},{16,20},{20,16},{24,28},{28,24},{1,5},{5... | collective-permute-start | bytes 835592 | tf_op jit(solution)/shard_map/ppermute | solution.py:372
  5.8 31.2 %collective-permute-start.6 = (bf16[272,512]{1,0:T(8,128)(2,1)S(1)}, bf16[272,512]{1,0:T(8,128)(2,1)S(1)}, u32[]{:S(2)}, u32[]{:S(2)}) collective-permute-start(bf16[272,512]{1,0:T(8,128)(2,1)S(1)} %maximum_maximum_fusion.rows_ref), channel_id=1, source_target_pairs={{0,8},{4,12},{8,0},{12,4},{16,24},{20,28},{24,16},{28,20},{1,9},{5... | collective-permute-start | bytes 835592 | tf_op jit(solution)/shard_map/ppermute | solution.py:372
  7.4 14.8 %collective-permute-start.2 = (bf16[272,512]{1,0:T(8,128)(2,1)S(1)}, bf16[272,512]{1,0:T(8,128)(2,1)S(1)}, u32[]{:S(2)}, u32[]{:S(2)}) collective-permute-start(bf16[272,512]{1,0:T(8,128)(2,1)S(1)} %maximum_maximum_fusion.rows_ref), channel_id=1, source_target_pairs={{0,16},{4,20},{8,24},{12,28},{16,0},{20,4},{24,8},{28,12},{1,17},{... | collective-permute-start | bytes 835592 | tf_op jit(solution)/shard_map/ppermute | solution.py:372
  11.5 1.6 collective-permute-start
  13.1 3.8 %collective-permute-start.1 = (bf16[2,32,128]{2,1,0:T(8,128)(2,1)S(1)}, bf16[2,32,128]{2,1,0:T(8,128)(2,1)S(1)}, u32[]{:S(2)}, u32[]{:S(2)}) collective-permute-start(bf16[2,32,128]{2,1,0:T(8,128)(2,1)S(1)} %add.47), channel_id=1, source_target_pairs={{0,2},{1,3},{2,0},{3,1},{4,6},{5,7},{6,4},{7,5},{8,10},{9,11},{10,... | collective-permute-start | bytes 49160 | tf_op jit(solution)/shard_map/ppermute | solution.py:372
  22.1 22.1 %copy-start.2 = (bf16[272,512]{1,0:T(8,128)(2,1)}, bf16[272,512]{1,0:T(8,128)(2,1)S(1)}, u32[]{:S(2)}) copy-start(bf16[272,512]{1,0:T(8,128)(2,1)S(1)} %collective-permute-done.2.rows_ref) | copy-start | bytes 835588
  22.1 37.1 %collective-permute-start.3 = (bf16[272,512]{1,0:T(8,128)(2,1)S(1)}, bf16[272,512]{1,0:T(8,128)(2,1)S(1)}, u32[]{:S(2)}, u32[]{:S(2)}) collective-permute-start(bf16[272,512]{1,0:T(8,128)(2,1)S(1)} %collective-permute-done.2.rows_ref), channel_id=1, source_target_pairs={{0,8},{4,12},{8,0},{12,4},{16,24},{20,28},{24,16},{28,20},{1,9},{5... | collective-permute-start | bytes 835592 | tf_op jit(solution)/shard_map/ppermute | solution.py:372
  36.9 15.6 %copy-start.3 = (bf16[272,512]{1,0:T(8,128)(2,1)}, bf16[272,512]{1,0:T(8,128)(2,1)S(1)}, u32[]{:S(2)}) copy-start(bf16[272,512]{1,0:T(8,128)(2,1)S(1)} %collective-permute-done.6.rows_ref) | copy-start | bytes 835588
  37.0 29.6 %collective-permute-start.7 = (bf16[272,512]{1,0:T(8,128)(2,1)S(1)}, bf16[272,512]{1,0:T(8,128)(2,1)S(1)}, u32[]{:S(2)}, u32[]{:S(2)}) collective-permute-start(bf16[272,512]{1,0:T(8,128)(2,1)S(1)} %collective-permute-done.6.rows_ref), channel_id=1, source_target_pairs={{0,4},{4,0},{8,12},{12,8},{16,20},{20,16},{24,28},{28,24},{1,5},{5... | collective-permute-start | bytes 835592 | tf_op jit(solution)/shard_map/ppermute | solution.py:372
  44.2 29.8 %collective-permute-start.5 = (bf16[272,512]{1,0:T(8,128)(2,1)S(1)}, bf16[272,512]{1,0:T(8,128)(2,1)S(1)}, u32[]{:S(2)}, u32[]{:S(2)}) collective-permute-start(bf16[272,512]{1,0:T(8,128)(2,1)S(1)} %collective-permute-done.2.rows_ref), channel_id=1, source_target_pairs={{0,4},{4,0},{8,12},{12,8},{16,20},{20,16},{24,28},{28,24},{1,5},{5... | collective-permute-start | bytes 835592 | tf_op jit(solution)/shard_map/ppermute | solution.py:372
  59.3 14.7 %copy-start.4 = (bf16[272,512]{1,0:T(8,128)(2,1)}, bf16[272,512]{1,0:T(8,128)(2,1)S(1)}, u32[]{:S(2)}) copy-start(bf16[272,512]{1,0:T(8,128)(2,1)S(1)} %collective-permute-done.3.rows_ref) | copy-start | bytes 835588
  59.3 28.8 %collective-permute-start.4 = (bf16[272,512]{1,0:T(8,128)(2,1)S(1)}, bf16[272,512]{1,0:T(8,128)(2,1)S(1)}, u32[]{:S(2)}, u32[]{:S(2)}) collective-permute-start(bf16[272,512]{1,0:T(8,128)(2,1)S(1)} %collective-permute-done.3.rows_ref), channel_id=1, source_target_pairs={{0,4},{4,0},{8,12},{12,8},{16,20},{20,16},{24,28},{28,24},{1,5},{5... | collective-permute-start | bytes 835592 | tf_op jit(solution)/shard_map/ppermute | solution.py:372
  66.6 0.7 copy-start.6
  74.0 0.7 copy-start.5
  88.1 0.7 copy-start.7
  113.7 4.4 %collective-permute-start.9 = (bf16[8,16,256]{2,1,0:T(8,128)(2,1)S(1)}, bf16[8,16,256]{2,1,0:T(8,128)(2,1)S(1)}, u32[]{:S(2)}, u32[]{:S(2)}) collective-permute-start(bf16[8,16,256]{2,1,0:T(8,128)(2,1)S(1)} %multiply_convert_fusion), channel_id=1, source_target_pairs={{0,4},{4,0},{8,12},{12,8},{16,20},{20,16},{24,28},{28,24},{1,5},{5... | collective-permute-start | bytes 196616 | tf_op jit(solution)/shard_map/ppermute | solution.py:372
  119.0 4.3 %collective-permute-start.10 = (bf16[8,16,256]{2,1,0:T(8,128)(2,1)S(1)}, bf16[8,16,256]{2,1,0:T(8,128)(2,1)S(1)}, u32[]{:S(2)}, u32[]{:S(2)}) collective-permute-start(bf16[8,16,256]{2,1,0:T(8,128)(2,1)S(1)} %fusion.9), channel_id=1, source_target_pairs={{0,8},{4,12},{8,0},{12,4},{16,24},{20,28},{24,16},{28,20},{1,9},{5... | collective-permute-start | bytes 196616 | tf_op jit(solution)/shard_map/ppermute | solution.py:372
  124.3 5.2 %collective-permute-start.11 = (bf16[8,16,256]{2,1,0:T(8,128)(2,1)S(1)}, bf16[8,16,256]{2,1,0:T(8,128)(2,1)S(1)}, u32[]{:S(2)}, u32[]{:S(2)}) collective-permute-start(bf16[8,16,256]{2,1,0:T(8,128)(2,1)S(1)} %fusion.5), channel_id=1, source_target_pairs={{0,16},{4,20},{8,24},{12,28},{16,0},{20,4},{24,8},{28,12},{1,17},{... | collective-permute-start | bytes 196616 | tf_op jit(solution)/shard_map/ppermute | solution.py:372
  137.8 38.0 %copy-start.8 = (f32[16,1024]{1,0:T(8,128)S(1)}, f32[16,1024]{1,0:T(8,128)}, u32[]{:S(2)}) copy-start(f32[16,1024]{1,0:T(8,128)} %param.10) | copy-start | bytes 196612
  152.3 18.2 %all-to-all-start = ((f32[8,16,256]{2,1,0:T(8,128)}), f32[8,16,256]{2,1,0:T(8,128)S(1)}, u32[]{:S(2)}, u32[]{:S(2)}) async-start(f32[8,16,256]{2,1,0:T(8,128)} %get-tuple-element.63), calls=%async_computation | async-start | bytes 262144 | tf_op jit(solution)/shard_map/all_to_all | solution.py:469

commit v2 on v0

v2 whole, which is shorter than its diff:
```python
import functools
import math

import jax
import jax.numpy as jnp
from jax import lax
from jax.experimental import pallas as pl
from jax.experimental.pallas import tpu as pltpu
from jax.sharding import PartitionSpec as P

RIDGE = 1.0
LANES = 128
POOL_BLOCK = 256
WINDOW = 144
KERNEL_VMEM = 16 * 2**20
LOG2E = math.log2(math.e)
NT = (((1,), (1,)), ((), ()))
F32 = jnp.float32
BF16 = jnp.bfloat16


def split3(x):
    first = x.astype(BF16)
    rest = x - first.astype(F32)
    second = rest.astype(BF16)
    third = (rest - second.astype(F32)).astype(BF16)
    return first, second, third


def split3_outside(x):
    first = lax.reduce_precision(x, 8, 7)
    rest = x - first
    second = lax.reduce_precision(rest, 8, 7)
    third = rest - second
    return first.astype(BF16), second.astype(BF16), third.astype(BF16)


def round_up(value, multiple):
    return -(-value // multiple) * multiple


def in_vmem(count):
    return [pl.BlockSpec(memory_space=pltpu.VMEM)] * count


def params():
    return pltpu.CompilerParams(vmem_limit_bytes=KERNEL_VMEM)


def two_rows(ref, step, block):
    row = 2 * block
    return jnp.concatenate([ref[step, pl.ds(row, 1), :], ref[step, pl.ds(row + 1, 1), :]], axis=1)


def compact_kernel(per_step, targets, off_ref, dest_ref, pool_ref, side_ref, out_ref, norm_ref, coef_ref, side_out):
    steps, features = out_ref.shape[0], out_ref.shape[2]
    blocks = pool_ref.shape[0] // POOL_BLOCK
    tile = math.gcd(per_step, 512)

    def place(block, step, window):
        base = pl.multiple_of((off_ref[step, block] // 16) * 16, 16)
        dest = two_rows(dest_ref, step, block) - base
        slots = lax.broadcasted_iota(jnp.int32, (window, POOL_BLOCK), 0)
        pick = jnp.where(slots == dest, 1.0, 0.0).astype(BF16)
        at = pl.ds(pl.multiple_of(block * POOL_BLOCK, POOL_BLOCK), POOL_BLOCK)
        for source, target in ((pool_ref, out_ref), (side_ref, side_out)):
            rows = jnp.dot(pick, source[at, :], preferred_element_type=F32).astype(BF16)
            target[step, pl.ds(base, 16), :] += rows[:16]
            target[step, pl.ds(pl.multiple_of(base + 16, 16), window - 16), :] = rows[16:]

    for step in range(steps):
        out_ref[step, :16, :] = jnp.zeros((16, features), BF16)
        side_out[step, :16, :] = jnp.zeros((16, LANES), BF16)

    narrow = off_ref[0, blocks + 1] <= WINDOW

    @pl.when(narrow)
    def _():
        @pl.loop(0, blocks // 2)
        def _(pair):
            for i in range(2):
                for step in range(steps):
                    place(2 * pair + i, step, WINDOW)

    @pl.when(jnp.logical_not(narrow))
    def _():
        @pl.loop(0, blocks)
        def _(block):
            for step in range(steps):
                place(block, step, POOL_BLOCK + 16)

    ones = jnp.ones((8, features), BF16)
    eye = lax.broadcasted_iota(jnp.int32, (3 * targets, LANES), 0) == lax.broadcasted_iota(
        jnp.int32, (3 * targets, LANES), 1
    )
    eye = jnp.where(eye, 1.0, 0.0).astype(BF16)
    for step in range(steps):
        for first in range(0, per_step, tile):
            rows = out_ref[step, first : first + tile, :].astype(F32)
            square = rows * rows
            high = square.astype(BF16)
            low = (square - high.astype(F32)).astype(BF16)
            norm = lax.dot_general(ones, high, NT, preferred_element_type=F32)
            norm = norm + lax.dot_general(ones, low, NT, preferred_element_type=F32)
            norm_ref[step, :, first : first + tile] = norm
            side = side_out[step, first : first + tile, :]
            parts = lax.dot_general(eye, side, NT, preferred_element_type=F32)
            coef_ref[step, :, first : first + tile] = (
                parts[:targets] + parts[targets : 2 * targets] + parts[2 * targets :]
            )


def compact(off, dest, pool, side, per_step, targets):
    steps = dest.shape[0]
    features = pool.shape[1]
    length = round_up(per_step, 16) + POOL_BLOCK + 16
    return pl.pallas_call(
        functools.partial(compact_kernel, per_step, targets),
        name="compact",
        in_specs=[pl.BlockSpec(memory_space=pltpu.SMEM)] + in_vmem(3),
        out_specs=in_vmem(3),
        out_shape=(
            pltpu.VMEM((steps, length, features), BF16),
            pltpu.VMEM((steps, 8, per_step), F32),
            pltpu.VMEM((steps, targets, per_step), F32),
        ),
        scratch_shapes=[pltpu.VMEM((steps, length, LANES), BF16)],
        compiler_params=params(),
        cost_estimate=pl.CostEstimate(flops=4 * 10**9, bytes_accessed=8 * 10**6, transcendentals=0),
    )(off, dest, pool, side)


def block_kernel(per_step, targets, quarter, scale, offset, slot_ref, rows_ref, chosen_ref, norm_ref, *refs):
    k_ref, sums_ref, side_ref = refs[-3:]
    sums_in = refs[1] if len(refs) > 3 else None
    steps = chosen_ref.shape[0]
    tile = math.gcd(per_step, 512)
    slot = slot_ref[0]

    rows = rows_ref[:quarter, :]
    wide_rows = rows.astype(F32)
    row_norm = jnp.sum(wide_rows * wide_rows, axis=1, keepdims=True) * (scale * LOG2E) - offset * LOG2E
    parts = rows_ref[quarter : quarter + 3, quarter : 2 * quarter].astype(F32)
    weight = jnp.sum(parts, axis=0, keepdims=True)
    weight_column = jnp.transpose(jnp.broadcast_to(weight, (8, quarter)))[:, :1]
    weighted = rows_ref[quarter : quarter + targets, :quarter]
    side_ref[slot, :targets, :] = weighted.astype(F32)
    side_ref[slot, targets:, :] = jnp.broadcast_to(weight, (side_ref.shape[1] - targets, quarter))

    for first in range(0, per_step, tile):
        for step in range(steps):
            dots = lax.dot_general(
                rows, chosen_ref[step, first : first + tile, :], NT, preferred_element_type=F32
            )
            centre = norm_ref[step, :1, first : first + tile] * (scale * LOG2E)
            k_low = jnp.exp2(dots * (2.0 * scale * LOG2E) - row_norm - centre).astype(BF16)
            k_ref[slot, :, step * per_step + first : step * per_step + first + tile] = k_low
            wide = k_low.astype(F32)
            updates = [(targets + step, 1, jnp.sum(weight_column * (wide * wide), axis=0, keepdims=True))]
            if step == 0:
                updates.append((0, targets, jnp.dot(weighted, k_low, preferred_element_type=F32)))
            for row, count, value in updates:
                if sums_in is not None:
                    value = value + sums_in[row : row + count, first : first + tile]
                sums_ref[row : row + count, first : first + tile] = value


def block_call(slot, rows, chosen, norm, state, per_step, targets, row_devices, scale, offset):
    steps, _, features = chosen.shape
    quarter = rows.shape[0] - round_up(targets, 16)
    operands = [slot, rows, chosen, norm]
    aliases = {}
    if state is not None:
        operands += [pltpu.with_memory_space_constraint(x, pltpu.VMEM) for x in state]
        aliases = {4: 0, 5: 1, 6: 2}
    entries = quarter * per_step * steps
    return pl.pallas_call(
        functools.partial(block_kernel, per_step, targets, quarter, scale, offset),
        name="kernel_block",
        in_specs=[pl.BlockSpec(memory_space=pltpu.SMEM)] + in_vmem(len(operands) - 1),
        out_specs=in_vmem(3),
        out_shape=(
            pltpu.VMEM((row_devices, quarter, steps * per_step), BF16),
            pltpu.VMEM((round_up(targets + steps, 8), per_step), F32),
            pltpu.VMEM((row_devices, round_up(targets + 1, 8), quarter), F32),
        ),
        input_output_aliases=aliases,
        compiler_params=params(),
        cost_estimate=pl.CostEstimate(
            flops=2 * entries * features, bytes_accessed=2 * entries, transcendentals=entries
        ),
    )(*operands)


def pass_cost(k_all, per_step, targets):
    entries = k_all.shape[0] * k_all.shape[1] * per_step
    return pl.CostEstimate(flops=2 * targets * entries, bytes_accessed=2 * entries, transcendentals=0)


def change_kernel(targets, step, sums_ref, square_ref, coef_ref, k_ref, side_ref, *refs):
    before_ref = refs[0] if len(refs) == 4 else None
    delta_ref, change_ref, moved_ref = refs[-3:]
    per_step = delta_ref.shape[1]
    total, square = sums_ref[0, :targets, :], square_ref[0, targets + step : targets + step + 1, :]
    for i in range(1, sums_ref.shape[0]):
        total = total + sums_ref[i, :targets, :]
        square = square + square_ref[i, targets + step : targets + step + 1, :]
    delta = (total - RIDGE * coef_ref[step]) / (square + RIDGE)
    delta_ref[...] = delta
    low = delta.astype(BF16)

    def body(i, _):
        k_low = k_ref[i, :, step * per_step : (step + 1) * per_step]
        change = lax.dot_general(low, k_low, NT, preferred_element_type=F32)
        moved_ref[i] = change * side_ref[i, targets : targets + 1, :]
        change_ref[i] = change if before_ref is None else change + before_ref[i]
        return 0

    lax.fori_loop(0, k_ref.shape[0], body, 0, unroll=2)


def change_call(sums, squares, coef, k_all, side, step, targets, before=None):
    row_devices, quarter, _ = k_all.shape
    per_step = sums.shape[2]
    operands = [sums, squares, coef, pltpu.with_memory_space_constraint(k_all, pltpu.VMEM), side]
    if before is not None:
        operands.append(before)
    change = jax.ShapeDtypeStruct((row_devices, targets, quarter), F32)
    return pl.pallas_call(
        functools.partial(change_kernel, targets, step),
        name="change",
        in_specs=in_vmem(len(operands)),
        out_specs=in_vmem(3),
        out_shape=(jax.ShapeDtypeStruct((targets, per_step), F32), change, change),
        compiler_params=params(),
        cost_estimate=pass_cost(k_all, per_step, targets),
    )(*operands)


def gradient_kernel(targets, step, moved_ref, side_ref, k_ref, out_ref):
    per_step = out_ref.shape[1]
    out_ref[...] = jnp.zeros_like(out_ref)

    def body(i, _):
        weighted = (side_ref[i, :targets, :] - moved_ref[i]).astype(BF16)
        k_low = k_ref[i, :, step * per_step : (step + 1) * per_step]
        out_ref[...] += jnp.dot(weighted, k_low, preferred_element_type=F32)
        return 0

    lax.fori_loop(0, k_ref.shape[0], body, 0, unroll=2)


def gradient_call(moved, side, k_all, step, targets, per_step):
    return pl.pallas_call(
        functools.partial(gradient_kernel, targets, step),
        name="gradient",
        in_specs=in_vmem(3),
        out_specs=in_vmem(1)[0],
        out_shape=jax.ShapeDtypeStruct((targets, per_step), F32),
        compiler_params=params(),
        cost_estimate=pass_cost(k_all, per_step, targets),
    )(moved, side, pltpu.with_memory_space_constraint(k_all, pltpu.VMEM))


def scatter_kernel(targets, off_ref, dest_ref, coef_ref, *refs):
    delta_refs, (out_ref, parts_ref) = refs[:-2], refs[-2:]
    steps = len(delta_refs)
    per_step = delta_refs[0].shape[1]
    blocks = out_ref.shape[1] // POOL_BLOCK
    window = POOL_BLOCK + LANES
    for step in range(steps):
        for part, value in enumerate(split3(delta_refs[step][...])):
            parts_ref[step, part * targets : (part + 1) * targets, :per_step] = value
        parts_ref[step, :, per_step:] = jnp.zeros((3 * targets, parts_ref.shape[2] - per_step), BF16)

    @pl.loop(0, blocks // 2)
    def _(pair):
        for i in range(2):
            block = 2 * pair + i
            columns = pl.ds(pl.multiple_of(block * POOL_BLOCK, POOL_BLOCK), POOL_BLOCK)
            value = coef_ref[:, columns]
            for step in range(steps):
                base = pl.multiple_of((off_ref[step, block] // LANES) * LANES, LANES)
                dest = two_rows(dest_ref, step, block) - base
                slots = lax.broadcasted_iota(jnp.int32, (window, POOL_BLOCK), 0)
                pick = jnp.where(slots == dest, 1.0, 0.0).astype(BF16)
                moved = jnp.dot(parts_ref[step, :, pl.ds(base, window)], pick, preferred_element_type=F32)
                value = value + (moved[:targets] + moved[targets : 2 * targets] + moved[2 * targets :])
            out_ref[:, columns] = value


def scatter_call(off, dest, coefs, deltas):
    targets, per_step = deltas[0].shape
    length = round_up(per_step, LANES) + POOL_BLOCK + LANES
    return pl.pallas_call(
        functools.partial(scatter_kernel, targets),
        name="scatter",
        in_specs=[pl.BlockSpec(memory_space=pltpu.SMEM)] + in_vmem(2 + len(deltas)),
        out_specs=in_vmem(1)[0],
        out_shape=jax.ShapeDtypeStruct(coefs.shape, F32),
        scratch_shapes=[pltpu.VMEM((len(deltas), 3 * targets, length), BF16)],
        compiler_params=params(),
        cost_estimate=pl.CostEstimate(flops=10**9, bytes_accessed=10**6, transcendentals=0),
    )(off, dest, coefs, *deltas)


def swap(value, axis, bit):
    count = lax.axis_size(axis)
    return lax.ppermute(value, axis, [(i, i ^ bit) for i in range(count)])


def bits_of(count):
    return [1 << k for k in range(count.bit_length() - 1)]


def local(samples, weights, targets, predictions, centres, coefs, block_index):
    rows_dev, features = samples.shape
    pool_dev = centres.shape[0]
    steps, slice_len = block_index.shape
    target_count = targets.shape[0]
    row_devices, cent_devices = lax.axis_size("rows"), lax.axis_size("cent")
    my_row, my_cent = lax.axis_index("rows"), lax.axis_index("cent")
    quarter = rows_dev // cent_devices
    per_step = slice_len * cent_devices // row_devices
    sharpness = 1.3 / math.sqrt(8.0 * features)
    offset = 2.0 * features * sharpness - 1.5 - 0.5 * math.log(rows_dev * row_devices)

    at = my_cent * quarter
    own_rows = lax.dynamic_slice_in_dim(samples, at, quarter, 0)
    own_weight = lax.dynamic_slice_in_dim(weights, at, quarter, 0)[None, :]
    own_target = lax.dynamic_slice_in_dim(targets, at, quarter, 1)
    own_pred = lax.dynamic_slice_in_dim(predictions, at, quarter, 1)
    weighted = (own_weight * (own_target - own_pred)).astype(BF16)
    side_count = round_up(target_count, 16)
    weight_parts = jnp.concatenate(split3_outside(own_weight), axis=0)
    side_block = jnp.concatenate(
        [
            jnp.pad(weighted, ((0, side_count - target_count), (0, 0))),
            jnp.pad(weight_parts, ((0, side_count - 3), (0, features - 2 * quarter))),
        ],
        axis=1,
    )
    chunks = {0: jnp.concatenate([own_rows, side_block], axis=0)}

    high_count = pool_dev // LANES
    place = block_index - my_row * pool_dev
    inside = (place >= 0) & (place < pool_dev)
    high = jnp.where(inside, place // LANES, -1)
    low = jnp.where(inside, place % LANES, 0)
    high_hot = (high[:, None, :] == jnp.arange(high_count)[None, :, None]).astype(BF16)
    low_hot = (low[:, None, :] == jnp.arange(LANES)[None, :, None]).astype(BF16)
    member = jnp.einsum("shl,sgl->shg", high_hot, low_hot, preferred_element_type=F32).astype(BF16)
    for bit in bits_of(cent_devices):
        member = member + swap(member, "cent", bit)

    for bit in reversed(bits_of(row_devices)):
        for have in sorted(chunks):
            chunks[have | bit] = swap(chunks[have], "rows", bit)

    upper = (jnp.arange(LANES)[:, None] <= jnp.arange(LANES)[None, :]).astype(BF16)
    before = (jnp.arange(high_count)[:, None] > jnp.arange(high_count)[None, :]).astype(BF16)
    running = jnp.einsum("shg,gk->shk", member, upper, preferred_element_type=F32)
    row_count = running[:, :, -1:]
    row_start = jnp.einsum("hi,sik->shk", before, row_count.astype(BF16), preferred_element_type=F32)
    rank = row_start + running - 1.0
    dest = jnp.where(member > 0, rank, -65536.0).astype(jnp.int32)
    group_rows = POOL_BLOCK // LANES
    off = row_start[:, ::group_rows, 0].astype(jnp.int32)
    end = jnp.concatenate([off[:, 1:], jnp.full((steps, 1), per_step, jnp.int32)], axis=1)
    widest = jnp.broadcast_to(jnp.max(end - off // 16 * 16), (steps, 1))
    off = jnp.concatenate([off, end[:, -1:], widest], axis=1)

    coef_parts = jnp.concatenate(split3_outside(coefs), axis=0)
    side = jnp.pad(coef_parts, ((0, LANES - 3 * target_count), (0, 0))).T
    chosen, norm, own_coef = compact(off, dest, centres, side, per_step, target_count)

    state = None
    for have in sorted(chunks, key=lambda c: (bin(c).count("1"), c)):
        slot = (my_row ^ have).astype(jnp.int32)[None]
        k_all, sums, info = block_call(
            slot, chunks[have], chosen, norm, state, per_step, target_count, row_devices, sharpness, offset
        )
        state = (k_all, sums, info)

    squares = lax.all_gather(sums, "cent")
    gathered = squares
    total_change = None
    deltas = []
    for step in range(steps):
        if step > 0:
            for bit in bits_of(row_devices):
                share = share + swap(share.astype(BF16), "rows", bit).astype(F32)
            moved = share if step == 1 else moved + share
            gradient = gradient_call(moved, info, k_all, step, target_count, per_step)
            gathered = lax.all_gather(gradient, "cent")
        delta, total_change, share = change_call(
            gathered, squares, own_coef, k_all, info, step, target_count, total_change
        )
        deltas.append(delta)
    coef_now = scatter_call(off, dest, coefs, deltas)

    arrived = lax.all_to_all(total_change, "rows", 0, 0)
    own_change = jnp.sum(arrived, axis=0)
    full = lax.all_gather(own_change, "cent")
    full = full.transpose(1, 0, 2).reshape(target_count, rows_dev)
    return (coef_now, predictions + full)


def solution(mesh):
    in_specs = (
        P("rows", None),
        P("rows"),
        P(None, "rows"),
        P(None, "rows"),
        P("rows", None),
        P(None, "rows"),
        P(None, "cent"),
    )
    out_specs = (P(None, "rows"), P(None, "rows"))
    return jax.shard_map(local, mesh=mesh, in_specs=in_specs, out_specs=out_specs, check_vma=False)
```

time: 483 us -> 105 us (0.22)
  waiting for transfers between devices: 273 us -> 21.6 us
  local copies, waits for them, and re-layouts: 71.3 us -> 6.49 us
  other arithmetic: 56 us -> 5.02 us
  Pallas kernels: 0 us -> 33.3 us
  matrix products: 31.1 us -> 0.95 us
  starting transfers between devices: 0.91 us -> 17.4 us
  blocking collectives: 35.4 us -> 19 us
  between operations: 14.5 us -> 0.84 us
    psum x4 -> x0, waiting for transfers between devices: 196 us -> none  [the longest x2 103 us: local(): change, update = lax.psum((change, update), 'cent')]
    all_gather x2 -> x0, waiting for transfers between devices: 77.2 us -> none  [local(): centre_rows = lax.all_gather(centres[own_local], 'rows', axis=0, tiled=True)]
    scatter-add x2 -> x0, other arithmetic: 37.3 us -> none  [local(): update = jnp.zeros((target_count, pool_dev), jnp.float32).at[:, write_pos...]
    gather x6 -> x0, local copies, waits for them, and re-layouts: 36.2 us -> none  [the longest x4 25.5 us: local(): own_coefs = jnp.where(is_valid[None, :], coef_now[:, places], 0.0)]
    psum x1 -> x0, blocking collectives: 35.4 us -> none  [local(): gradient, col_square = lax.psum((gradient, col_square), 'rows')]
    pallas_call x0 -> x13, Pallas kernels: none -> 33.3 us  [the longest x8 16.8 us: block_call(): pl.pallas_call(functools.partial(block_kernel, per_step, targets, quarter...]
    dot_general x12 -> x3, matrix products: 31.1 us -> 0.95 us  [the longest x1 0.68 us: local(): jnp.einsum('shl,sgl->shg', high_hot, low_hot, preferred_element_type=F32)]
    scatter x2 -> x0, local copies, waits for them, and re-layouts: 23.5 us -> none  [local(): jnp.zeros((per_owner,), jnp.int32).at[slot_pos].set(local_pos, mode='drop')]
  transfers between devices with their start and end apart: 6 -> 13, of which waited for: 6 -> 7; matrix products, arithmetic and copies ran while one was open for 12% -> 7% of each run, Pallas kernels for 0% -> 24%
where the time goes in v2:
time: 105 us
  Pallas kernels  33.3 us (32%)
  waiting for transfers between devices  21.6 us (21%)
  blocking collectives  19 us (18%)
  starting transfers between devices  17.4 us (17%)
  local copies, waits for them, and re-layouts  6.49 us (6%)
  other arithmetic  5.02 us (5%)
    ppermute x12, waiting for transfers between devices, swap(): return lax.ppermute(value, axis, [(i, i ^ bit) for i in range(count)])  18.1 us
    pallas_call x8, Pallas kernels, block_call(): pl.pallas_call(functools.partial(block_kernel, per_step, targets, quarter...  16.8 us
    ppermute x12, starting transfers between devices, swap(): return lax.ppermute(value, axis, [(i, i ^ bit) for i in range(count)])  14 us
    all_gather x1, blocking collectives, local(): squares = lax.all_gather(sums, 'cent')  7.53 us
    all_gather x1, blocking collectives, local(): gathered = lax.all_gather(gradient, 'cent')  6.27 us
    pallas_call x1, Pallas kernels, compact(): pl.pallas_call(functools.partial(compact_kernel, per_step, targets), name...  6.02 us
    all_gather x1, blocking collectives, local(): full = lax.all_gather(own_change, 'cent')  5.24 us
    pallas_call x2, Pallas kernels, change_call(): pl.pallas_call(functools.partial(change_kernel, targets, step), name='cha...  4.95 us
  transfers between devices with their start and end apart: 13, of which 7 were waited for; matrix products, arithmetic and copies ran while one was open for 7% of the time, Pallas kernels for 24%

profile of v2, /device:TPU:0, one launch (start us, length us, event | category | flops | bytes accessed | tf_op | source)
XLA Modules:
  0.0 104.6 jit_solution(6174807165839860776)
XLA Ops:
  2.7 3.1 %collective-permute-start.8 = (bf16[272,512]{1,0:T(8,128)(2,1)S(1)}, bf16[272,512]{1,0:T(8,128)(2,1)S(1)}, u32[]{:S(2)}, u32[]{:S(2)}) collective-permute-start(bf16[272,512]{1,0:T(8,128)(2,1)S(1)} %maximum_maximum_fusion.rows_ref), channel_id=1, source_target_pairs={{0,4},{4,0},{8,12},{12,8},{16,20},{20,16},{24,28},{28,24},{1,5},{5... | collective-permute-start | bytes 835592 | tf_op jit(solution)/shard_map/ppermute | solution.py:309
  7.3 2.6 %collective-permute-start.2 = (bf16[272,512]{1,0:T(8,128)(2,1)S(1)}, bf16[272,512]{1,0:T(8,128)(2,1)S(1)}, u32[]{:S(2)}, u32[]{:S(2)}) collective-permute-start(bf16[272,512]{1,0:T(8,128)(2,1)S(1)} %maximum_maximum_fusion.rows_ref), channel_id=1, source_target_pairs={{0,16},{4,20},{8,24},{12,28},{16,0},{20,4},{24,8},{28,12},{1,17},{... | collective-permute-start | bytes 835592 | tf_op jit(solution)/shard_map/ppermute | solution.py:309
  19.8 2.3 %collective-permute-done.2.rows_ref = bf16[272,512]{1,0:T(8,128)(2,1)S(1)} collective-permute-done((bf16[272,512]{1,0:T(8,128)(2,1)S(1)}, bf16[272,512]{1,0:T(8,128)(2,1)S(1)}, u32[]{:S(2)}, u32[]{:S(2)}) %collective-permute-start.2) | collective-permute-done | bytes 278560 | tf_op jit(solution)/shard_map/ppermute | solution.py:309
  22.5 2.2 %copy-done.2 = bf16[4096,512]{1,0:T(8,128)(2,1)S(1)} copy-done((bf16[4096,512]{1,0:T(8,128)(2,1)S(1)}, bf16[4096,512]{1,0:T(8,128)(2,1)}, u32[]{:S(2)}) %copy-start.2) | copy-done | bytes 4194328
  24.7 6.0 %compact.1 = (bf16[2,1808,512]{2,1,0:T(8,128)(2,1)S(1)}, f32[2,8,1536]{2,1,0:T(8,128)S(1)}, f32[2,16,1536]{2,1,0:T(8,128)S(1)}) custom-call(s32[2,18]{1,0:T(2,128)S(1)} %add_add_fusion.off_ref, s32[2,32,128]{2,1,0:T(8,128)S(1)} %select_convert_fusion.dest_ref, bf16[4096,512]{1,0:T(8,128)(2,1)S(1)} %copy-done.2, bf16[4096,128]{1,0:T(8,128)(2,1)S(1)} %pad_bitcast_fusion.side_ref), custom_call_target="tpu_custom_call" | custom-call | flops 4000000000 | bytes 8000000 | tf_op jit(solution)/shard_map/compact/pallas_call | solution.py:117
  31.3 2.1 %kernel_block.8 = (bf16[8,256,3072]{2,1,0:T(8,128)(2,1)S(1)}, f32[24,1536]{1,0:T(8,128)S(1)}, f32[8,24,256]{2,1,0:T(8,128)S(1)}) custom-call(s32[1]{0:T(128)} %bitcast.11.slot_ref, bf16[272,512]{1,0:T(8,128)(2,1)S(1)} %maximum_maximum_fusion.rows_ref, bf16[2,1808,512]{2,1,0:T(8,128)(2,1)S(1)} %get-tuple-element.34.chosen_ref, ...), custom_call_target="tpu_custom_call" | custom-call | flops 805306368 | bytes 1572864 | tf_op jit(solution)/shard_map/kernel_block/pallas_call | solution.py:177
  35.0 2.1 %kernel_block.9 = (bf16[8,256,3072]{2,1,0:T(8,128)(2,1)S(1)}, f32[24,1536]{1,0:T(8,128)S(1)}, f32[8,24,256]{2,1,0:T(8,128)S(1)}) custom-call(s32[1]{0:T(128)} %bitcast.10.slot_ref, bf16[272,512]{1,0:T(8,128)(2,1)S(1)} %collective-permute-done.8.rows_ref, ...), custom_call_target="tpu_custom_call", output_to_operand_aliasing={{0}: (4, {}), {1}: (5, {}), {2}: (6, {})} | custom-call | flops 805306368 | bytes 1572864 | tf_op jit(solution)/shard_map/kernel_block/pallas_call | solution.py:177
  37.1 2.1 %kernel_block.10 = (bf16[8,256,3072]{2,1,0:T(8,128)(2,1)S(1)}, f32[24,1536]{1,0:T(8,128)S(1)}, f32[8,24,256]{2,1,0:T(8,128)S(1)}) custom-call(s32[1]{0:T(128)} %bitcast.9.slot_ref, bf16[272,512]{1,0:T(8,128)(2,1)S(1)} %collective-permute-done.6.rows_ref, ...), custom_call_target="tpu_custom_call", output_to_operand_aliasing={{0}: (4, {}), {1}: (5, {}), {2}: (6, {})} | custom-call | flops 805306368 | bytes 1572864 | tf_op jit(solution)/shard_map/kernel_block/pallas_call | solution.py:177
  39.7 2.1 %kernel_block.11 = (bf16[8,256,3072]{2,1,0:T(8,128)(2,1)S(1)}, f32[24,1536]{1,0:T(8,128)S(1)}, f32[8,24,256]{2,1,0:T(8,128)S(1)}) custom-call(s32[1]{0:T(128)} %bitcast.8.slot_ref, bf16[272,512]{1,0:T(8,128)(2,1)S(1)} %collective-permute-done.2.rows_ref, ...), custom_call_target="tpu_custom_call", output_to_operand_aliasing={{0}: (4, {}), {1}: (5, {}), {2}: (6, {})} | custom-call | flops 805306368 | bytes 1572864 | tf_op jit(solution)/shard_map/kernel_block/pallas_call | solution.py:177
  41.8 2.1 %kernel_block.12 = (bf16[8,256,3072]{2,1,0:T(8,128)(2,1)S(1)}, f32[24,1536]{1,0:T(8,128)S(1)}, f32[8,24,256]{2,1,0:T(8,128)S(1)}) custom-call(s32[1]{0:T(128)} %bitcast.7.slot_ref, bf16[272,512]{1,0:T(8,128)(2,1)S(1)} %collective-permute-done.7.rows_ref, ...), custom_call_target="tpu_custom_call", output_to_operand_aliasing={{0}: (4, {}), {1}: (5, {}), {2}: (6, {})} | custom-call | flops 805306368 | bytes 1572864 | tf_op jit(solution)/shard_map/kernel_block/pallas_call | solution.py:177
  43.9 2.4 %collective-permute-done.5.rows_ref = bf16[272,512]{1,0:T(8,128)(2,1)S(1)} collective-permute-done((bf16[272,512]{1,0:T(8,128)(2,1)S(1)}, bf16[272,512]{1,0:T(8,128)(2,1)S(1)}, u32[]{:S(2)}, u32[]{:S(2)}) %collective-permute-start.5) | collective-permute-done | bytes 278560 | tf_op jit(solution)/shard_map/ppermute | solution.py:309
  48.4 2.3 %kernel_block.14 = (bf16[8,256,3072]{2,1,0:T(8,128)(2,1)S(1)}, f32[24,1536]{1,0:T(8,128)S(1)}, f32[8,24,256]{2,1,0:T(8,128)S(1)}) custom-call(s32[1]{0:T(128)} %bitcast.5.slot_ref, bf16[272,512]{1,0:T(8,128)(2,1)S(1)} %collective-permute-done.3.rows_ref, ...), custom_call_target="tpu_custom_call", output_to_operand_aliasing={{0}: (4, {}), {1}: (5, {}), {2}: (6, {})} | custom-call | flops 805306368 | bytes 1572864 | tf_op jit(solution)/shard_map/kernel_block/pallas_call | solution.py:177
  50.7 2.1 %kernel_block.15 = (bf16[8,256,3072]{2,1,0:T(8,128)(2,1)S(1)}, f32[24,1536]{1,0:T(8,128)S(1)}, f32[8,24,256]{2,1,0:T(8,128)S(1)}) custom-call(s32[1]{0:T(128)} %bitcast.3.slot_ref, bf16[272,512]{1,0:T(8,128)(2,1)S(1)} %collective-permute-done.4.rows_ref, ...), custom_call_target="tpu_custom_call", output_to_operand_aliasing={{0}: (4, {}), {1}: (5, {}), {2}: (6, {})} | custom-call | flops 805306368 | bytes 1572864 | tf_op jit(solution)/shard_map/kernel_block/pallas_call | solution.py:177
  52.8 7.5 %all-gather = f32[96,1536]{1,0:T(8,128)S(1)} all-gather(f32[24,1536]{1,0:T(8,128)S(1)} %get-tuple-element.57), channel_id=2, replica_groups=mesh['rows'=8,'cent'=4] {'cent'}, dimensions={0}, use_global_device_ids=true | all-gather | bytes 737280 | tf_op jit(solution)/shard_map/all_gather | solution.py:385
  60.3 2.1 %change.2 = (f32[16,1536]{1,0:T(8,128)S(1)}, f32[8,16,256]{2,1,0:T(8,128)S(1)}, f32[8,16,256]{2,1,0:T(8,128)S(1)}) custom-call(f32[4,24,1536]{2,1,0:T(8,128)S(1)} %bitcast.28, f32[4,24,1536]{2,1,0:T(8,128)S(1)} %bitcast.29, f32[2,16,1536]{2,1,0:T(8,128)S(1)} %get-tuple-element.58.coef_ref, bf16[8,256,3072]{2,1,0:T(8,128)(2,1)S(1)} %get-tuple-element.59.k_ref, ...), custom_call_target="tpu_custom_call" | custom-call | flops 100663296 | bytes 6291456 | tf_op jit(solution)/shard_map/change/pallas_call | solution.py:229
  63.0 3.9 %collective-permute-done.9 = bf16[8,16,256]{2,1,0:T(8,128)(2,1)S(1)} collective-permute-done((bf16[8,16,256]{2,1,0:T(8,128)(2,1)S(1)}, bf16[8,16,256]{2,1,0:T(8,128)(2,1)S(1)}, u32[]{:S(2)}, u32[]{:S(2)}) %collective-permute-start.9) | collective-permute-done | bytes 65568 | tf_op jit(solution)/shard_map/ppermute | solution.py:309
  67.7 3.5 %collective-permute-done.10 = bf16[8,16,256]{2,1,0:T(8,128)(2,1)S(1)} collective-permute-done((bf16[8,16,256]{2,1,0:T(8,128)(2,1)S(1)}, bf16[8,16,256]{2,1,0:T(8,128)(2,1)S(1)}, u32[]{:S(2)}, u32[]{:S(2)}) %collective-permute-start.10) | collective-permute-done | bytes 65568 | tf_op jit(solution)/shard_map/ppermute | solution.py:309
  71.9 5.3 %collective-permute-done.11 = bf16[8,16,256]{2,1,0:T(8,128)(2,1)S(1)} collective-permute-done((bf16[8,16,256]{2,1,0:T(8,128)(2,1)S(1)}, bf16[8,16,256]{2,1,0:T(8,128)(2,1)S(1)}, u32[]{:S(2)}, u32[]{:S(2)}) %collective-permute-start.11) | collective-permute-done | bytes 65568 | tf_op jit(solution)/shard_map/ppermute | solution.py:309
  78.5 6.3 %all-gather.1 = f32[64,1536]{1,0:T(8,128)S(1)} all-gather(f32[16,1536]{1,0:T(8,128)S(1)} %gradient.1), channel_id=3, replica_groups=mesh['rows'=8,'cent'=4] {'cent'}, dimensions={0}, use_global_device_ids=true | all-gather | bytes 491520 | tf_op jit(solution)/shard_map/all_gather | solution.py:395
  84.8 2.8 %change.3 = (f32[16,1536]{1,0:T(8,128)S(1)}, f32[8,16,256]{2,1,0:T(8,128)}, f32[8,16,256]{2,1,0:T(8,128)}) custom-call(f32[4,16,1536]{2,1,0:T(8,128)S(1)} %bitcast.31, f32[4,24,1536]{2,1,0:T(8,128)S(1)} %bitcast.30, f32[2,16,1536]{2,1,0:T(8,128)S(1)} %get-tuple-element.58.coef_ref, bf16[8,256,3072]{2,1,0:T(8,128)(2,1)S(1)} %get-tuple-element.59.k_ref, ...), custom_call_target="tpu_custom_call" | custom-call | flops 100663296 | bytes 6291456 | tf_op jit(solution)/shard_map/change/pallas_call | solution.py:229
  87.6 3.4 %all-to-all-start = ((f32[8,16,256]{2,1,0:T(8,128)}), f32[8,16,256]{2,1,0:T(8,128)S(1)}, u32[]{:S(2)}, u32[]{:S(2)}) async-start(f32[8,16,256]{2,1,0:T(8,128)} %get-tuple-element.65), calls=%async_computation | async-start | bytes 262144 | tf_op jit(solution)/shard_map/all_to_all | solution.py:402
  91.0 4.2 %scatter.1 = f32[16,4096]{1,0:T(8,128)} custom-call(s32[2,18]{1,0:T(2,128)S(1)} %add_add_fusion.off_ref, s32[2,32,128]{2,1,0:T(8,128)S(1)} %select_convert_fusion.dest_ref, f32[16,4096]{1,0:T(8,128)S(1)} %copy-done.1, f32[16,1536]{1,0:T(8,128)S(1)} %get-tuple-element.61.refs_0_, f32[16,1536]{1,0:T(8,128)S(1)} %get-tuple-element.64.refs_1_), custom_call_target="tpu_custom_call" | custom-call | flops 1000000000 | bytes 1000000 | tf_op jit(solution)/shard_map/scatter/pallas_call | solution.py:295
  95.2 3.5 %all-to-all-done = f32[8,16,256]{2,1,0:T(8,128)S(1)} async-done(((f32[8,16,256]{2,1,0:T(8,128)}), f32[8,16,256]{2,1,0:T(8,128)S(1)}, u32[]{:S(2)}, u32[]{:S(2)}) %all-to-all-start) | async-done | bytes 131104 | tf_op jit(solution)/shard_map/all_to_all | solution.py:402
  98.7 5.2 %all-gather.2 = f32[64,256]{1,0:T(8,128)S(1)} all-gather(f32[16,256]{1,0:T(8,128)S(1)} %reduce_sum.9), channel_id=4, replica_groups=mesh['rows'=8,'cent'=4] {'cent'}, dimensions={0}, use_global_device_ids=true | all-gather | bytes 81920 | tf_op jit(solution)/shard_map/all_gather | solution.py:404
  (60 shorter events, 22.7 us)
Async XLA Ops:
  0.6 1.2 %copy-start = (bf16[1024,512]{1,0:T(8,128)(2,1)S(1)}, bf16[1024,512]{1,0:T(8,128)(2,1)}, u32[]{:S(2)}) copy-start(bf16[1024,512]{1,0:T(8,128)(2,1)} %param.7) | copy-start | bytes 3145732
  2.7 32.3 %collective-permute-start.8 = (bf16[272,512]{1,0:T(8,128)(2,1)S(1)}, bf16[272,512]{1,0:T(8,128)(2,1)S(1)}, u32[]{:S(2)}, u32[]{:S(2)}) collective-permute-start(bf16[272,512]{1,0:T(8,128)(2,1)S(1)} %maximum_maximum_fusion.rows_ref), channel_id=1, source_target_pairs={{0,4},{4,0},{8,12},{12,8},{16,20},{20,16},{24,28},{28,24},{1,5},{5... | collective-permute-start | bytes 835592 | tf_op jit(solution)/shard_map/ppermute | solution.py:309
  5.7 25.0 %collective-permute-start.6 = (bf16[272,512]{1,0:T(8,128)(2,1)S(1)}, bf16[272,512]{1,0:T(8,128)(2,1)S(1)}, u32[]{:S(2)}, u32[]{:S(2)}) collective-permute-start(bf16[272,512]{1,0:T(8,128)(2,1)S(1)} %maximum_maximum_fusion.rows_ref), channel_id=1, source_target_pairs={{0,8},{4,12},{8,0},{12,4},{16,24},{20,28},{24,16},{28,20},{1,9},{5... | collective-permute-start | bytes 835592 | tf_op jit(solution)/shard_map/ppermute | solution.py:309
  7.3 14.8 %collective-permute-start.2 = (bf16[272,512]{1,0:T(8,128)(2,1)S(1)}, bf16[272,512]{1,0:T(8,128)(2,1)S(1)}, u32[]{:S(2)}, u32[]{:S(2)}) collective-permute-start(bf16[272,512]{1,0:T(8,128)(2,1)S(1)} %maximum_maximum_fusion.rows_ref), channel_id=1, source_target_pairs={{0,16},{4,20},{8,24},{12,28},{16,0},{20,4},{24,8},{28,12},{1,17},{... | collective-permute-start | bytes 835592 | tf_op jit(solution)/shard_map/ppermute | solution.py:309
  11.4 2.4 %collective-permute-start = (bf16[2,32,128]{2,1,0:T(8,128)(2,1)S(1)}, bf16[2,32,128]{2,1,0:T(8,128)(2,1)S(1)}, u32[]{:S(2)}, u32[]{:S(2)}) collective-permute-start(bf16[2,32,128]{2,1,0:T(8,128)(2,1)S(1)} %fusion.2), channel_id=1, source_target_pairs={{0,1},{1,0},{2,3},{3,2},{4,5},{5,4},{6,7},{7,6},{8,9},{9,8},{10,11... | collective-permute-start | bytes 49160 | tf_op jit(solution)/shard_map/ppermute | solution.py:309
  13.9 3.8 %collective-permute-start.1 = (bf16[2,32,128]{2,1,0:T(8,128)(2,1)S(1)}, bf16[2,32,128]{2,1,0:T(8,128)(2,1)S(1)}, u32[]{:S(2)}, u32[]{:S(2)}) collective-permute-start(bf16[2,32,128]{2,1,0:T(8,128)(2,1)S(1)} %add.48), channel_id=1, source_target_pairs={{0,2},{1,3},{2,0},{3,1},{4,6},{5,7},{6,4},{7,5},{8,10},{9,11},{10,... | collective-permute-start | bytes 49160 | tf_op jit(solution)/shard_map/ppermute | solution.py:309
  22.1 17.1 %collective-permute-start.3 = (bf16[272,512]{1,0:T(8,128)(2,1)S(1)}, bf16[272,512]{1,0:T(8,128)(2,1)S(1)}, u32[]{:S(2)}, u32[]{:S(2)}) collective-permute-start(bf16[272,512]{1,0:T(8,128)(2,1)S(1)} %collective-permute-done.2.rows_ref), channel_id=1, source_target_pairs={{0,8},{4,12},{8,0},{12,4},{16,24},{20,28},{24,16},{28,20},{1,9},{5... | collective-permute-start | bytes 835592 | tf_op jit(solution)/shard_map/ppermute | solution.py:309
  22.5 2.2 %copy-start.2 = (bf16[4096,512]{1,0:T(8,128)(2,1)S(1)}, bf16[4096,512]{1,0:T(8,128)(2,1)}, u32[]{:S(2)}) copy-start(bf16[4096,512]{1,0:T(8,128)(2,1)} %pool_ref.1) | copy-start | bytes 12582916
  30.7 11.1 %collective-permute-start.7 = (bf16[272,512]{1,0:T(8,128)(2,1)S(1)}, bf16[272,512]{1,0:T(8,128)(2,1)S(1)}, u32[]{:S(2)}, u32[]{:S(2)}) collective-permute-start(bf16[272,512]{1,0:T(8,128)(2,1)S(1)} %collective-permute-done.6.rows_ref), channel_id=1, source_target_pairs={{0,4},{4,0},{8,12},{12,8},{16,20},{20,16},{24,28},{28,24},{1,5},{5... | collective-permute-start | bytes 835592 | tf_op jit(solution)/shard_map/ppermute | solution.py:309
  33.4 12.9 %collective-permute-start.5 = (bf16[272,512]{1,0:T(8,128)(2,1)S(1)}, bf16[272,512]{1,0:T(8,128)(2,1)S(1)}, u32[]{:S(2)}, u32[]{:S(2)}) collective-permute-start(bf16[272,512]{1,0:T(8,128)(2,1)S(1)} %collective-permute-done.2.rows_ref), channel_id=1, source_target_pairs={{0,4},{4,0},{8,12},{12,8},{16,20},{20,16},{24,28},{28,24},{1,5},{5... | collective-permute-start | bytes 835592 | tf_op jit(solution)/shard_map/ppermute | solution.py:309
  39.2 11.5 %collective-permute-start.4 = (bf16[272,512]{1,0:T(8,128)(2,1)S(1)}, bf16[272,512]{1,0:T(8,128)(2,1)S(1)}, u32[]{:S(2)}, u32[]{:S(2)}) collective-permute-start(bf16[272,512]{1,0:T(8,128)(2,1)S(1)} %collective-permute-done.3.rows_ref), channel_id=1, source_target_pairs={{0,4},{4,0},{8,12},{12,8},{16,20},{20,16},{24,28},{28,24},{1,5},{5... | collective-permute-start | bytes 835592 | tf_op jit(solution)/shard_map/ppermute | solution.py:309
  62.5 4.4 %collective-permute-start.9 = (bf16[8,16,256]{2,1,0:T(8,128)(2,1)S(1)}, bf16[8,16,256]{2,1,0:T(8,128)(2,1)S(1)}, u32[]{:S(2)}, u32[]{:S(2)}) collective-permute-start(bf16[8,16,256]{2,1,0:T(8,128)(2,1)S(1)} %convert_element_type.83), channel_id=1, source_target_pairs={{0,4},{4,0},{8,12},{12,8},{16,20},{20,16},{24,28},{28,24},{1,5},{5... | collective-permute-start | bytes 196616 | tf_op jit(solution)/shard_map/ppermute | solution.py:309
  66.9 4.3 %collective-permute-start.10 = (bf16[8,16,256]{2,1,0:T(8,128)(2,1)S(1)}, bf16[8,16,256]{2,1,0:T(8,128)(2,1)S(1)}, u32[]{:S(2)}, u32[]{:S(2)}) collective-permute-start(bf16[8,16,256]{2,1,0:T(8,128)(2,1)S(1)} %fusion.5), channel_id=1, source_target_pairs={{0,8},{4,12},{8,0},{12,4},{16,24},{20,28},{24,16},{28,20},{1,9},{5... | collective-permute-start | bytes 196616 | tf_op jit(solution)/shard_map/ppermute | solution.py:309
  71.2 5.9 %collective-permute-start.11 = (bf16[8,16,256]{2,1,0:T(8,128)(2,1)S(1)}, bf16[8,16,256]{2,1,0:T(8,128)(2,1)S(1)}, u32[]{:S(2)}, u32[]{:S(2)}) collective-permute-start(bf16[8,16,256]{2,1,0:T(8,128)(2,1)S(1)} %fusion.9), channel_id=1, source_target_pairs={{0,16},{4,20},{8,24},{12,28},{16,0},{20,4},{24,8},{28,12},{1,17},{... | collective-permute-start | bytes 196616 | tf_op jit(solution)/shard_map/ppermute | solution.py:309
  77.2 13.8 %copy-start.1 = (f32[16,4096]{1,0:T(8,128)S(1)}, f32[16,4096]{1,0:T(8,128)}, u32[]{:S(2)}) copy-start(f32[16,4096]{1,0:T(8,128)} %coef_ref.1) | copy-start | bytes 786436
  78.5 25.5 %copy-start.3 = (f32[16,1024]{1,0:T(8,128)S(1)}, f32[16,1024]{1,0:T(8,128)}, u32[]{:S(2)}) copy-start(f32[16,1024]{1,0:T(8,128)} %param.10) | copy-start | bytes 196612
  87.6 11.1 %all-to-all-start = ((f32[8,16,256]{2,1,0:T(8,128)}), f32[8,16,256]{2,1,0:T(8,128)S(1)}, u32[]{:S(2)}, u32[]{:S(2)}) async-start(f32[8,16,256]{2,1,0:T(8,128)} %get-tuple-element.65), calls=%async_computation | async-start | bytes 262144 | tf_op jit(solution)/shard_map/all_to_all | solution.py:402

commit v3 on v2

--- a/solution.py
+++ b/solution.py
@@ -52,10 +52,20 @@
     return jnp.concatenate([ref[step, pl.ds(row, 1), :], ref[step, pl.ds(row + 1, 1), :]], axis=1)
 
 
-def compact_kernel(per_step, targets, off_ref, dest_ref, pool_ref, side_ref, out_ref, norm_ref, coef_ref, side_out):
+def compact_kernel(per_step, targets, off_ref, dest_ref, pool_hbm, coefs_ref, out_ref, norm_ref, coef_ref, side_out, pool_ref, parts_ref, arrived):
     steps, features = out_ref.shape[0], out_ref.shape[2]
     blocks = pool_ref.shape[0] // POOL_BLOCK
     tile = math.gcd(per_step, 512)
+
+    def fetch(block):
+        at = pl.ds(pl.multiple_of(block * POOL_BLOCK, POOL_BLOCK), POOL_BLOCK)
+        return pltpu.make_async_copy(pool_hbm.at[at, :], pool_ref.at[at, :], arrived.at[block])
+
+    for block in range(blocks):
+        fetch(block).start()
+    parts_ref[3 * targets :, :] = jnp.zeros((LANES - 3 * targets, parts_ref.shape[1]), BF16)
+    for part, value in enumerate(split3(coefs_ref[...])):
+        parts_ref[part * targets : (part + 1) * targets, :] = value
 
     def place(block, step, window):
         base = pl.multiple_of((off_ref[step, block] // 16) * 16, 16)
@@ -63,8 +73,9 @@
         slots = lax.broadcasted_iota(jnp.int32, (window, POOL_BLOCK), 0)
         pick = jnp.where(slots == dest, 1.0, 0.0).astype(BF16)
         at = pl.ds(pl.multiple_of(block * POOL_BLOCK, POOL_BLOCK), POOL_BLOCK)
-        for source, target in ((pool_ref, out_ref), (side_ref, side_out)):
-            rows = jnp.dot(pick, source[at, :], preferred_element_type=F32).astype(BF16)
+        packed = jnp.dot(pick, pool_ref[at, :], preferred_element_type=F32)
+        side = lax.dot_general(pick, parts_ref[:, at], NT, preferred_element_type=F32)
+        for rows, target in ((packed.astype(BF16), out_ref), (side.astype(BF16), side_out)):
             target[step, pl.ds(base, 16), :] += rows[:16]
             target[step, pl.ds(pl.multiple_of(base + 16, 16), window - 16), :] = rows[16:]
 
@@ -72,13 +83,19 @@
         out_ref[step, :16, :] = jnp.zeros((16, features), BF16)
         side_out[step, :16, :] = jnp.zeros((16, LANES), BF16)
 
-    narrow = off_ref[0, blocks + 1] <= WINDOW
+    widest = 0
+    for step in range(steps):
+        for block in range(blocks):
+            widest = jnp.maximum(widest, off_ref[step, block + 1] - (off_ref[step, block] // 16) * 16)
+    narrow = widest <= WINDOW
 
     @pl.when(narrow)
     def _():
         @pl.loop(0, blocks // 2)
         def _(pair):
             for i in range(2):
+                fetch(2 * pair + i).wait()
+            for i in range(2):
                 for step in range(steps):
                     place(2 * pair + i, step, WINDOW)
 
@@ -86,6 +103,7 @@
     def _():
         @pl.loop(0, blocks)
         def _(block):
+            fetch(block).wait()
             for step in range(steps):
                 place(block, step, POOL_BLOCK + 16)
 
@@ -110,24 +128,34 @@
             )
 
 
-def compact(off, dest, pool, side, per_step, targets):
+def compact(off, dest, pool, coefs, per_step, targets):
     steps = dest.shape[0]
     features = pool.shape[1]
     length = round_up(per_step, 16) + POOL_BLOCK + 16
     return pl.pallas_call(
         functools.partial(compact_kernel, per_step, targets),
         name="compact",
-        in_specs=[pl.BlockSpec(memory_space=pltpu.SMEM)] + in_vmem(3),
+        in_specs=[
+            pl.BlockSpec(memory_space=pltpu.SMEM),
+            *in_vmem(1),
+            pl.BlockSpec(memory_space=pl.ANY),
+            *in_vmem(1),
+        ],
         out_specs=in_vmem(3),
         out_shape=(
             pltpu.VMEM((steps, length, features), BF16),
             pltpu.VMEM((steps, 8, per_step), F32),
             pltpu.VMEM((steps, targets, per_step), F32),
         ),
-        scratch_shapes=[pltpu.VMEM((steps, length, LANES), BF16)],
+        scratch_shapes=[
+            pltpu.VMEM((steps, length, LANES), BF16),
+            pltpu.VMEM(pool.shape, BF16),
+            pltpu.VMEM((LANES, pool.shape[0]), BF16),
+            pltpu.SemaphoreType.DMA((pool.shape[0] // POOL_BLOCK,)),
+        ],
         compiler_params=params(),
         cost_estimate=pl.CostEstimate(flops=4 * 10**9, bytes_accessed=8 * 10**6, transcendentals=0),
-    )(off, dest, pool, side)
+    )(off, dest, pool, coefs)
 
 
 def block_kernel(per_step, targets, quarter, scale, offset, slot_ref, rows_ref, chosen_ref, norm_ref, *refs):
@@ -262,46 +290,41 @@
     )(moved, side, pltpu.with_memory_space_constraint(k_all, pltpu.VMEM))
 
 
-def scatter_kernel(targets, off_ref, dest_ref, coef_ref, *refs):
-    delta_refs, (out_ref, parts_ref) = refs[:-2], refs[-2:]
-    steps = len(delta_refs)
-    per_step = delta_refs[0].shape[1]
+def scatter_kernel(targets, step, off_ref, dest_ref, coef_ref, delta_ref, out_ref, parts_ref):
+    per_step = delta_ref.shape[1]
     blocks = out_ref.shape[1] // POOL_BLOCK
     window = POOL_BLOCK + LANES
-    for step in range(steps):
-        for part, value in enumerate(split3(delta_refs[step][...])):
-            parts_ref[step, part * targets : (part + 1) * targets, :per_step] = value
-        parts_ref[step, :, per_step:] = jnp.zeros((3 * targets, parts_ref.shape[2] - per_step), BF16)
-
-    @pl.loop(0, blocks // 2)
-    def _(pair):
-        for i in range(2):
-            block = 2 * pair + i
+    for part, value in enumerate(split3(delta_ref[...])):
+        parts_ref[part * targets : (part + 1) * targets, :per_step] = value
+    parts_ref[:, per_step:] = jnp.zeros((3 * targets, parts_ref.shape[1] - per_step), BF16)
+
+    @pl.loop(0, blocks // 4)
+    def _(four):
+        for i in range(4):
+            block = 4 * four + i
             columns = pl.ds(pl.multiple_of(block * POOL_BLOCK, POOL_BLOCK), POOL_BLOCK)
-            value = coef_ref[:, columns]
-            for step in range(steps):
-                base = pl.multiple_of((off_ref[step, block] // LANES) * LANES, LANES)
-                dest = two_rows(dest_ref, step, block) - base
-                slots = lax.broadcasted_iota(jnp.int32, (window, POOL_BLOCK), 0)
-                pick = jnp.where(slots == dest, 1.0, 0.0).astype(BF16)
-                moved = jnp.dot(parts_ref[step, :, pl.ds(base, window)], pick, preferred_element_type=F32)
-                value = value + (moved[:targets] + moved[targets : 2 * targets] + moved[2 * targets :])
-            out_ref[:, columns] = value
-
-
-def scatter_call(off, dest, coefs, deltas):
-    targets, per_step = deltas[0].shape
+            base = pl.multiple_of((off_ref[step, block] // LANES) * LANES, LANES)
+            dest = two_rows(dest_ref, step, block) - base
+            slots = lax.broadcasted_iota(jnp.int32, (window, POOL_BLOCK), 0)
+            pick = jnp.where(slots == dest, 1.0, 0.0).astype(BF16)
+            moved = jnp.dot(parts_ref[:, pl.ds(base, window)], pick, preferred_element_type=F32)
+            moved = moved[:targets] + moved[targets : 2 * targets] + moved[2 * targets :]
+            out_ref[:, columns] = coef_ref[:, columns] + moved
+
+
+def scatter_call(off, dest, coefs, delta, step):
+    targets, per_step = delta.shape
     length = round_up(per_step, LANES) + POOL_BLOCK + LANES
     return pl.pallas_call(
-        functools.partial(scatter_kernel, targets),
+        functools.partial(scatter_kernel, targets, step),
         name="scatter",
-        in_specs=[pl.BlockSpec(memory_space=pltpu.SMEM)] + in_vmem(2 + len(deltas)),
+        in_specs=[pl.BlockSpec(memory_space=pltpu.SMEM)] + in_vmem(3),
         out_specs=in_vmem(1)[0],
         out_shape=jax.ShapeDtypeStruct(coefs.shape, F32),
-        scratch_shapes=[pltpu.VMEM((len(deltas), 3 * targets, length), BF16)],
+        scratch_shapes=[pltpu.VMEM((3 * targets, length), BF16)],
         compiler_params=params(),
         cost_estimate=pl.CostEstimate(flops=10**9, bytes_accessed=10**6, transcendentals=0),
-    )(off, dest, coefs, *deltas)
+    )(off, dest, coefs, delta)
 
 
 def swap(value, axis, bit):
@@ -366,16 +389,12 @@
     dest = jnp.where(member > 0, rank, -65536.0).astype(jnp.int32)
     group_rows = POOL_BLOCK // LANES
     off = row_start[:, ::group_rows, 0].astype(jnp.int32)
-    end = jnp.concatenate([off[:, 1:], jnp.full((steps, 1), per_step, jnp.int32)], axis=1)
-    widest = jnp.broadcast_to(jnp.max(end - off // 16 * 16), (steps, 1))
-    off = jnp.concatenate([off, end[:, -1:], widest], axis=1)
-
-    coef_parts = jnp.concatenate(split3_outside(coefs), axis=0)
-    side = jnp.pad(coef_parts, ((0, LANES - 3 * target_count), (0, 0))).T
-    chosen, norm, own_coef = compact(off, dest, centres, side, per_step, target_count)
+    off = jnp.pad(off, ((0, 0), (0, 1)), constant_values=per_step)
+
+    chosen, norm, own_coef = compact(off, dest, centres, coefs, per_step, target_count)
 
     state = None
-    for have in sorted(chunks, key=lambda c: (bin(c).count("1"), c)):
+    for have in range(row_devices):
         slot = (my_row ^ have).astype(jnp.int32)[None]
         k_all, sums, info = block_call(
             slot, chunks[have], chosen, norm, state, per_step, target_count, row_devices, sharpness, offset
@@ -385,19 +404,22 @@
     squares = lax.all_gather(sums, "cent")
     gathered = squares
     total_change = None
-    deltas = []
+    coef_now = coefs
     for step in range(steps):
         if step > 0:
-            for bit in bits_of(row_devices):
-                share = share + swap(share.astype(BF16), "rows", bit).astype(F32)
+            bits = bits_of(row_devices)
+            for first in range(0, len(bits), 2):
+                low = share.astype(BF16)
+                pair = bits[first : first + 2]
+                for bit in pair + ([sum(pair)] if len(pair) > 1 else []):
+                    share = share + swap(low, "rows", bit).astype(F32)
             moved = share if step == 1 else moved + share
             gradient = gradient_call(moved, info, k_all, step, target_count, per_step)
             gathered = lax.all_gather(gradient, "cent")
         delta, total_change, share = change_call(
             gathered, squares, own_coef, k_all, info, step, target_count, total_change
         )
-        deltas.append(delta)
-    coef_now = scatter_call(off, dest, coefs, deltas)
+        coef_now = scatter_call(off, dest, coef_now, delta, step)
 
     arrived = lax.all_to_all(total_change, "rows", 0, 0)
     own_change = jnp.sum(arrived, axis=0)

time: 105 us -> 106 us (level)
  starting transfers between devices: 17.4 us -> 22.3 us
  local copies, waits for them, and re-layouts: 6.49 us -> 3.49 us
  other arithmetic: 5.02 us -> 3.32 us
  Pallas kernels: 33.3 us -> 34.6 us
    ppermute x12 -> x13, starting transfers between devices: 14 us -> 17.9 us  [swap(): return lax.ppermute(value, axis, [(i, i ^ bit) for i in range(count)])]
    concatenate x3 -> x0, local copies, waits for them, and re-layouts: 2.13 us -> none  [the longest x1 1.34 us: local(): coef_parts = jnp.concatenate(split3_outside(coefs), axis=0)]
    transpose x1 -> x0, local copies, waits for them, and re-layouts: 1.43 us -> none  [local(): side = jnp.pad(coef_parts, ((0, LANES - 3 * target_count), (0, 0))).T]
    convert_element_type x3 -> x2, other arithmetic: 1.87 us -> 0.77 us  [split3_outside(): return (first.astype(BF16), second.astype(BF16), third.astype(BF16))]
    ppermute x12 -> x13, waiting for transfers between devices: 18.1 us -> 19.1 us  [swap(): return lax.ppermute(value, axis, [(i, i ^ bit) for i in range(count)])]
    unnamed x8 -> x10, local copies, waits for them, and re-layouts: 2.54 us -> 3.16 us
    pallas_call x1 -> x2, Pallas kernels: 4.18 us -> 4.71 us  [scatter_call(): pl.pallas_call(functools.partial(scatter_kernel, targets, step), name='sc...]
  transfers between devices with their start and end apart: 13 -> 14, of which waited for: 7 -> 7; matrix products, arithmetic and copies ran while one was open for 7% -> 2% of each run, Pallas kernels for 24% -> 25%
where the time goes in v3:
time: 106 us
  Pallas kernels  34.6 us (33%)
  starting transfers between devices  22.3 us (21%)
  waiting for transfers between devices  21.9 us (21%)
  blocking collectives  18.4 us (17%)
  local copies, waits for them, and re-layouts  3.49 us (3%)
  other arithmetic  3.32 us (3%)
    ppermute x13, waiting for transfers between devices, swap(): return lax.ppermute(value, axis, [(i, i ^ bit) for i in range(count)])  19.1 us
    ppermute x13, starting transfers between devices, swap(): return lax.ppermute(value, axis, [(i, i ^ bit) for i in range(count)])  17.9 us
    pallas_call x8, Pallas kernels, block_call(): pl.pallas_call(functools.partial(block_kernel, per_step, targets, quarter...  17 us
    all_gather x1, blocking collectives, local(): squares = lax.all_gather(sums, 'cent')  6.68 us
    pallas_call x1, Pallas kernels, compact(): pl.pallas_call(functools.partial(compact_kernel, per_step, targets), name...  6.61 us
    all_gather x1, blocking collectives, local(): gathered = lax.all_gather(gradient, 'cent')  6.48 us
    all_gather x1, blocking collectives, local(): full = lax.all_gather(own_change, 'cent')  5.24 us
    pallas_call x2, Pallas kernels, change_call(): pl.pallas_call(functools.partial(change_kernel, targets, step), name='cha...  4.95 us
  transfers between devices with their start and end apart: 14, of which 7 were waited for; matrix products, arithmetic and copies ran while one was open for 2% of the time, Pallas kernels for 25%

profile of v3, /device:TPU:0, one launch (start us, length us, event | category | flops | bytes accessed | tf_op | source)
XLA Modules:
  0.0 105.8 jit_solution(3860844590453577427)
XLA Ops:
  4.4 2.6 %collective-permute-start.1 = (bf16[2,32,128]{2,1,0:T(8,128)(2,1)S(1)}, bf16[2,32,128]{2,1,0:T(8,128)(2,1)S(1)}, u32[]{:S(2)}, u32[]{:S(2)}) collective-permute-start(bf16[2,32,128]{2,1,0:T(8,128)(2,1)S(1)} %add.48), channel_id=1, source_target_pairs={{0,2},{1,3},{2,0},{3,1},{4,6},{5,7},{6,4},{7,5},{8,10},{9,11},{10,... | collective-permute-start | bytes 49160 | tf_op jit(solution)/shard_map/ppermute | solution.py:332
  10.2 2.6 %collective-permute-start.2 = (bf16[272,512]{1,0:T(8,128)(2,1)S(1)}, bf16[272,512]{1,0:T(8,128)(2,1)S(1)}, u32[]{:S(2)}, u32[]{:S(2)}) collective-permute-start(bf16[272,512]{1,0:T(8,128)(2,1)S(1)} %maximum_maximum_fusion.rows_ref), channel_id=1, source_target_pairs={{0,16},{4,20},{8,24},{12,28},{16,0},{20,4},{24,8},{28,12},{1,17},{... | collective-permute-start | bytes 835592 | tf_op jit(solution)/shard_map/ppermute | solution.py:332
  13.4 9.5 %collective-permute-done.6.rows_ref = bf16[272,512]{1,0:T(8,128)(2,1)S(1)} collective-permute-done((bf16[272,512]{1,0:T(8,128)(2,1)S(1)}, bf16[272,512]{1,0:T(8,128)(2,1)S(1)}, u32[]{:S(2)}, u32[]{:S(2)}) %collective-permute-start.6) | collective-permute-done | bytes 278560 | tf_op jit(solution)/shard_map/ppermute | solution.py:332
  25.8 2.2 %copy-done.1 = bf16[4096,512]{1,0:T(8,128)(2,1)S(1)} copy-done((bf16[4096,512]{1,0:T(8,128)(2,1)S(1)}, bf16[4096,512]{1,0:T(8,128)(2,1)}, u32[]{:S(2)}) %copy-start.1) | copy-done | bytes 4194328
  28.9 6.6 %compact.1 = (bf16[2,1808,512]{2,1,0:T(8,128)(2,1)S(1)}, f32[2,8,1536]{2,1,0:T(8,128)S(1)}, f32[2,16,1536]{2,1,0:T(8,128)S(1)}) custom-call(s32[2,17]{1,0:T(2,128)S(1)} %pad.8.off_ref, s32[2,32,128]{2,1,0:T(8,128)S(1)} %select_convert_fusion.dest_ref, bf16[4096,512]{1,0:T(8,128)(2,1)S(1)} %copy-done.1, f32[16,4096]{1,0:T(8,128)S(1)} %copy-done.2), custom_call_target="tpu_custom_call" | custom-call | flops 4000000000 | bytes 8000000 | tf_op jit(solution)/shard_map/compact/pallas_call | solution.py:135
  35.5 2.1 %kernel_block.8 = (bf16[8,256,3072]{2,1,0:T(8,128)(2,1)S(1)}, f32[24,1536]{1,0:T(8,128)S(1)}, f32[8,24,256]{2,1,0:T(8,128)S(1)}) custom-call(s32[1]{0:T(128)} %bitcast.10.slot_ref, bf16[272,512]{1,0:T(8,128)(2,1)S(1)} %maximum_maximum_fusion.rows_ref, bf16[2,1808,512]{2,1,0:T(8,128)(2,1)S(1)} %get-tuple-element.34.chosen_ref, ...), custom_call_target="tpu_custom_call" | custom-call | flops 805306368 | bytes 1572864 | tf_op jit(solution)/shard_map/kernel_block/pallas_call | solution.py:205
  38.2 2.1 %kernel_block.9 = (bf16[8,256,3072]{2,1,0:T(8,128)(2,1)S(1)}, f32[24,1536]{1,0:T(8,128)S(1)}, f32[8,24,256]{2,1,0:T(8,128)S(1)}) custom-call(s32[1]{0:T(128)} %bitcast.9.slot_ref, bf16[272,512]{1,0:T(8,128)(2,1)S(1)} %collective-permute-done.8.rows_ref, ...), custom_call_target="tpu_custom_call", output_to_operand_aliasing={{0}: (4, {}), {1}: (5, {}), {2}: (6, {})} | custom-call | flops 805306368 | bytes 1572864 | tf_op jit(solution)/shard_map/kernel_block/pallas_call | solution.py:205
  40.3 2.1 %kernel_block.10 = (bf16[8,256,3072]{2,1,0:T(8,128)(2,1)S(1)}, f32[24,1536]{1,0:T(8,128)S(1)}, f32[8,24,256]{2,1,0:T(8,128)S(1)}) custom-call(s32[1]{0:T(128)} %bitcast.8.slot_ref, bf16[272,512]{1,0:T(8,128)(2,1)S(1)} %collective-permute-done.6.rows_ref, ...), custom_call_target="tpu_custom_call", output_to_operand_aliasing={{0}: (4, {}), {1}: (5, {}), {2}: (6, {})} | custom-call | flops 805306368 | bytes 1572864 | tf_op jit(solution)/shard_map/kernel_block/pallas_call | solution.py:205
  44.0 2.1 %kernel_block.11 = (bf16[8,256,3072]{2,1,0:T(8,128)(2,1)S(1)}, f32[24,1536]{1,0:T(8,128)S(1)}, f32[8,24,256]{2,1,0:T(8,128)S(1)}) custom-call(s32[1]{0:T(128)} %bitcast.7.slot_ref, bf16[272,512]{1,0:T(8,128)(2,1)S(1)} %collective-permute-done.7.rows_ref, ...), custom_call_target="tpu_custom_call", output_to_operand_aliasing={{0}: (4, {}), {1}: (5, {}), {2}: (6, {})} | custom-call | flops 805306368 | bytes 1572864 | tf_op jit(solution)/shard_map/kernel_block/pallas_call | solution.py:205
  46.1 2.1 %kernel_block.12 = (bf16[8,256,3072]{2,1,0:T(8,128)(2,1)S(1)}, f32[24,1536]{1,0:T(8,128)S(1)}, f32[8,24,256]{2,1,0:T(8,128)S(1)}) custom-call(s32[1]{0:T(128)} %bitcast.6.slot_ref, bf16[272,512]{1,0:T(8,128)(2,1)S(1)} %collective-permute-done.2.rows_ref, ...), custom_call_target="tpu_custom_call", output_to_operand_aliasing={{0}: (4, {}), {1}: (5, {}), {2}: (6, {})} | custom-call | flops 805306368 | bytes 1572864 | tf_op jit(solution)/shard_map/kernel_block/pallas_call | solution.py:205
  48.2 2.1 %kernel_block.13 = (bf16[8,256,3072]{2,1,0:T(8,128)(2,1)S(1)}, f32[24,1536]{1,0:T(8,128)S(1)}, f32[8,24,256]{2,1,0:T(8,128)S(1)}) custom-call(s32[1]{0:T(128)} %bitcast.5.slot_ref, bf16[272,512]{1,0:T(8,128)(2,1)S(1)} %collective-permute-done.5.rows_ref, ...), custom_call_target="tpu_custom_call", output_to_operand_aliasing={{0}: (4, {}), {1}: (5, {}), {2}: (6, {})} | custom-call | flops 805306368 | bytes 1572864 | tf_op jit(solution)/shard_map/kernel_block/pallas_call | solution.py:205
  50.3 2.3 %kernel_block.14 = (bf16[8,256,3072]{2,1,0:T(8,128)(2,1)S(1)}, f32[24,1536]{1,0:T(8,128)S(1)}, f32[8,24,256]{2,1,0:T(8,128)S(1)}) custom-call(s32[1]{0:T(128)} %bitcast.4.slot_ref, bf16[272,512]{1,0:T(8,128)(2,1)S(1)} %collective-permute-done.3.rows_ref, ...), custom_call_target="tpu_custom_call", output_to_operand_aliasing={{0}: (4, {}), {1}: (5, {}), {2}: (6, {})} | custom-call | flops 805306368 | bytes 1572864 | tf_op jit(solution)/shard_map/kernel_block/pallas_call | solution.py:205
  52.7 2.1 %kernel_block.15 = (bf16[8,256,3072]{2,1,0:T(8,128)(2,1)S(1)}, f32[24,1536]{1,0:T(8,128)S(1)}, f32[8,24,256]{2,1,0:T(8,128)S(1)}) custom-call(s32[1]{0:T(128)} %bitcast.3.slot_ref, bf16[272,512]{1,0:T(8,128)(2,1)S(1)} %collective-permute-done.4.rows_ref, ...), custom_call_target="tpu_custom_call", output_to_operand_aliasing={{0}: (4, {}), {1}: (5, {}), {2}: (6, {})} | custom-call | flops 805306368 | bytes 1572864 | tf_op jit(solution)/shard_map/kernel_block/pallas_call | solution.py:205
  54.8 6.7 %all-gather = f32[96,1536]{1,0:T(8,128)S(1)} all-gather(f32[24,1536]{1,0:T(8,128)S(1)} %get-tuple-element.57), channel_id=2, replica_groups=mesh['rows'=8,'cent'=4] {'cent'}, dimensions={0}, use_global_device_ids=true | all-gather | bytes 737280 | tf_op jit(solution)/shard_map/all_gather | solution.py:404
  61.5 2.1 %change.2 = (f32[16,1536]{1,0:T(8,128)S(1)}, f32[8,16,256]{2,1,0:T(8,128)S(1)}, f32[8,16,256]{2,1,0:T(8,128)S(1)}) custom-call(f32[4,24,1536]{2,1,0:T(8,128)S(1)} %bitcast.22, f32[4,24,1536]{2,1,0:T(8,128)S(1)} %bitcast.23, f32[2,16,1536]{2,1,0:T(8,128)S(1)} %get-tuple-element.58.coef_ref, bf16[8,256,3072]{2,1,0:T(8,128)(2,1)S(1)} %get-tuple-element.59.k_ref, ...), custom_call_target="tpu_custom_call" | custom-call | flops 100663296 | bytes 6291456 | tf_op jit(solution)/shard_map/change/pallas_call | solution.py:257
  68.2 2.2 %collective-permute-done.11 = bf16[8,16,256]{2,1,0:T(8,128)(2,1)S(1)} collective-permute-done((bf16[8,16,256]{2,1,0:T(8,128)(2,1)S(1)}, bf16[8,16,256]{2,1,0:T(8,128)(2,1)S(1)}, u32[]{:S(2)}, u32[]{:S(2)}) %collective-permute-start.11) | collective-permute-done | bytes 65568 | tf_op jit(solution)/shard_map/ppermute | solution.py:332
  71.0 2.4 %collective-permute-start.12 = (bf16[8,16,256]{2,1,0:T(8,128)(2,1)S(1)}, bf16[8,16,256]{2,1,0:T(8,128)(2,1)S(1)}, u32[]{:S(2)}, u32[]{:S(2)}) collective-permute-start(bf16[8,16,256]{2,1,0:T(8,128)(2,1)S(1)} %fusion.14), channel_id=1, source_target_pairs={{0,16},{4,20},{8,24},{12,28},{16,0},{20,4},{24,8},{28,12},{1,17},{... | collective-permute-start | bytes 196616 | tf_op jit(solution)/shard_map/ppermute | solution.py:332
  73.3 4.0 %collective-permute-done.12 = bf16[8,16,256]{2,1,0:T(8,128)(2,1)S(1)} collective-permute-done((bf16[8,16,256]{2,1,0:T(8,128)(2,1)S(1)}, bf16[8,16,256]{2,1,0:T(8,128)(2,1)S(1)}, u32[]{:S(2)}, u32[]{:S(2)}) %collective-permute-start.12) | collective-permute-done | bytes 65568 | tf_op jit(solution)/shard_map/ppermute | solution.py:332
  78.6 6.5 %all-gather.1 = f32[64,1536]{1,0:T(8,128)S(1)} all-gather(f32[16,1536]{1,0:T(8,128)S(1)} %gradient.1), channel_id=3, replica_groups=mesh['rows'=8,'cent'=4] {'cent'}, dimensions={0}, use_global_device_ids=true | all-gather | bytes 491520 | tf_op jit(solution)/shard_map/all_gather | solution.py:418
  85.1 2.8 %change.3 = (f32[16,1536]{1,0:T(8,128)S(1)}, f32[8,16,256]{2,1,0:T(8,128)}, f32[8,16,256]{2,1,0:T(8,128)}) custom-call(f32[4,16,1536]{2,1,0:T(8,128)S(1)} %bitcast.25, f32[4,24,1536]{2,1,0:T(8,128)S(1)} %bitcast.24, f32[2,16,1536]{2,1,0:T(8,128)S(1)} %get-tuple-element.58.coef_ref, bf16[8,256,3072]{2,1,0:T(8,128)(2,1)S(1)} %get-tuple-element.59.k_ref, ...), custom_call_target="tpu_custom_call" | custom-call | flops 100663296 | bytes 6291456 | tf_op jit(solution)/shard_map/change/pallas_call | solution.py:257
  88.0 4.4 %all-to-all-start = ((f32[8,16,256]{2,1,0:T(8,128)}), f32[8,16,256]{2,1,0:T(8,128)S(1)}, u32[]{:S(2)}, u32[]{:S(2)}) async-start(f32[8,16,256]{2,1,0:T(8,128)} %get-tuple-element.65), calls=%async_computation | async-start | bytes 262144 | tf_op jit(solution)/shard_map/all_to_all | solution.py:424
  94.4 2.7 %scatter.3 = f32[16,4096]{1,0:T(8,128)} custom-call(s32[2,17]{1,0:T(2,128)S(1)} %pad.8.off_ref, s32[2,32,128]{2,1,0:T(8,128)S(1)} %select_convert_fusion.dest_ref, f32[16,4096]{1,0:T(8,128)S(1)} %scatter.2.coef_ref, f32[16,1536]{1,0:T(8,128)S(1)} %get-tuple-element.64.delta_ref), custom_call_target="tpu_custom_call" | custom-call | flops 1000000000 | bytes 1000000 | tf_op jit(solution)/shard_map/scatter/pallas_call | solution.py:318
  97.1 2.8 %all-to-all-done = f32[8,16,256]{2,1,0:T(8,128)S(1)} async-done(((f32[8,16,256]{2,1,0:T(8,128)}), f32[8,16,256]{2,1,0:T(8,128)S(1)}, u32[]{:S(2)}, u32[]{:S(2)}) %all-to-all-start) | async-done | bytes 131104 | tf_op jit(solution)/shard_map/all_to_all | solution.py:424
  99.9 5.2 %all-gather.2 = f32[64,256]{1,0:T(8,128)S(1)} all-gather(f32[16,256]{1,0:T(8,128)S(1)} %reduce_sum.9), channel_id=4, replica_groups=mesh['rows'=8,'cent'=4] {'cent'}, dimensions={0}, use_global_device_ids=true | all-gather | bytes 81920 | tf_op jit(solution)/shard_map/all_gather | solution.py:426
  (56 shorter events, 22.6 us)
Async XLA Ops:
  0.6 3.0 %copy-start = (bf16[1024,512]{1,0:T(8,128)(2,1)S(1)}, bf16[1024,512]{1,0:T(8,128)(2,1)}, u32[]{:S(2)}) copy-start(bf16[1024,512]{1,0:T(8,128)(2,1)} %param.7) | copy-start | bytes 3145732
  2.3 2.1 %collective-permute-start = (bf16[2,32,128]{2,1,0:T(8,128)(2,1)S(1)}, bf16[2,32,128]{2,1,0:T(8,128)(2,1)S(1)}, u32[]{:S(2)}, u32[]{:S(2)}) collective-permute-start(bf16[2,32,128]{2,1,0:T(8,128)(2,1)S(1)} %fusion.2), channel_id=1, source_target_pairs={{0,1},{1,0},{2,3},{3,2},{4,5},{5,4},{6,7},{7,6},{8,9},{9,8},{10,11... | collective-permute-start | bytes 49160 | tf_op jit(solution)/shard_map/ppermute | solution.py:332
  4.4 8.3 %collective-permute-start.1 = (bf16[2,32,128]{2,1,0:T(8,128)(2,1)S(1)}, bf16[2,32,128]{2,1,0:T(8,128)(2,1)S(1)}, u32[]{:S(2)}, u32[]{:S(2)}) collective-permute-start(bf16[2,32,128]{2,1,0:T(8,128)(2,1)S(1)} %add.48), channel_id=1, source_target_pairs={{0,2},{1,3},{2,0},{3,1},{4,6},{5,7},{6,4},{7,5},{8,10},{9,11},{10,... | collective-permute-start | bytes 49160 | tf_op jit(solution)/shard_map/ppermute | solution.py:332
  7.0 31.2 %collective-permute-start.8 = (bf16[272,512]{1,0:T(8,128)(2,1)S(1)}, bf16[272,512]{1,0:T(8,128)(2,1)S(1)}, u32[]{:S(2)}, u32[]{:S(2)}) collective-permute-start(bf16[272,512]{1,0:T(8,128)(2,1)S(1)} %maximum_maximum_fusion.rows_ref), channel_id=1, source_target_pairs={{0,4},{4,0},{8,12},{12,8},{16,20},{20,16},{24,28},{28,24},{1,5},{5... | collective-permute-start | bytes 835592 | tf_op jit(solution)/shard_map/ppermute | solution.py:332
  8.6 14.3 %collective-permute-start.6 = (bf16[272,512]{1,0:T(8,128)(2,1)S(1)}, bf16[272,512]{1,0:T(8,128)(2,1)S(1)}, u32[]{:S(2)}, u32[]{:S(2)}) collective-permute-start(bf16[272,512]{1,0:T(8,128)(2,1)S(1)} %maximum_maximum_fusion.rows_ref), channel_id=1, source_target_pairs={{0,8},{4,12},{8,0},{12,4},{16,24},{20,28},{24,16},{28,20},{1,9},{5... | collective-permute-start | bytes 835592 | tf_op jit(solution)/shard_map/ppermute | solution.py:332
  10.2 15.1 %collective-permute-start.2 = (bf16[272,512]{1,0:T(8,128)(2,1)S(1)}, bf16[272,512]{1,0:T(8,128)(2,1)S(1)}, u32[]{:S(2)}, u32[]{:S(2)}) collective-permute-start(bf16[272,512]{1,0:T(8,128)(2,1)S(1)} %maximum_maximum_fusion.rows_ref), channel_id=1, source_target_pairs={{0,16},{4,20},{8,24},{12,28},{16,0},{20,4},{24,8},{28,12},{1,17},{... | collective-permute-start | bytes 835592 | tf_op jit(solution)/shard_map/ppermute | solution.py:332
  22.9 21.1 %collective-permute-start.7 = (bf16[272,512]{1,0:T(8,128)(2,1)S(1)}, bf16[272,512]{1,0:T(8,128)(2,1)S(1)}, u32[]{:S(2)}, u32[]{:S(2)}) collective-permute-start(bf16[272,512]{1,0:T(8,128)(2,1)S(1)} %collective-permute-done.6.rows_ref), channel_id=1, source_target_pairs={{0,4},{4,0},{8,12},{12,8},{16,20},{20,16},{24,28},{28,24},{1,5},{5... | collective-permute-start | bytes 835592 | tf_op jit(solution)/shard_map/ppermute | solution.py:332
  25.3 17.1 %collective-permute-start.3 = (bf16[272,512]{1,0:T(8,128)(2,1)S(1)}, bf16[272,512]{1,0:T(8,128)(2,1)S(1)}, u32[]{:S(2)}, u32[]{:S(2)}) collective-permute-start(bf16[272,512]{1,0:T(8,128)(2,1)S(1)} %collective-permute-done.2.rows_ref), channel_id=1, source_target_pairs={{0,8},{4,12},{8,0},{12,4},{16,24},{20,28},{24,16},{28,20},{1,9},{5... | collective-permute-start | bytes 835592 | tf_op jit(solution)/shard_map/ppermute | solution.py:332
  25.8 2.2 %copy-start.1 = (bf16[4096,512]{1,0:T(8,128)(2,1)S(1)}, bf16[4096,512]{1,0:T(8,128)(2,1)}, u32[]{:S(2)}) copy-start(bf16[4096,512]{1,0:T(8,128)(2,1)} %pool_hbm.1) | copy-start | bytes 12582916
  27.9 0.9 copy-start.2
  37.6 10.6 %collective-permute-start.5 = (bf16[272,512]{1,0:T(8,128)(2,1)S(1)}, bf16[272,512]{1,0:T(8,128)(2,1)S(1)}, u32[]{:S(2)}, u32[]{:S(2)}) collective-permute-start(bf16[272,512]{1,0:T(8,128)(2,1)S(1)} %collective-permute-done.2.rows_ref), channel_id=1, source_target_pairs={{0,4},{4,0},{8,12},{12,8},{16,20},{20,16},{24,28},{28,24},{1,5},{5... | collective-permute-start | bytes 835592 | tf_op jit(solution)/shard_map/ppermute | solution.py:332
  42.4 10.3 %collective-permute-start.4 = (bf16[272,512]{1,0:T(8,128)(2,1)S(1)}, bf16[272,512]{1,0:T(8,128)(2,1)S(1)}, u32[]{:S(2)}, u32[]{:S(2)}) collective-permute-start(bf16[272,512]{1,0:T(8,128)(2,1)S(1)} %collective-permute-done.3.rows_ref), channel_id=1, source_target_pairs={{0,4},{4,0},{8,12},{12,8},{16,20},{20,16},{24,28},{28,24},{1,5},{5... | collective-permute-start | bytes 835592 | tf_op jit(solution)/shard_map/ppermute | solution.py:332
  63.6 4.6 %collective-permute-start.10 = (bf16[8,16,256]{2,1,0:T(8,128)(2,1)S(1)}, bf16[8,16,256]{2,1,0:T(8,128)(2,1)S(1)}, u32[]{:S(2)}, u32[]{:S(2)}) collective-permute-start(bf16[8,16,256]{2,1,0:T(8,128)(2,1)S(1)} %convert_element_type.69), channel_id=1, source_target_pairs={{0,8},{4,12},{8,0},{12,4},{16,24},{20,28},{24,16},{28,20},{1,9},{5... | collective-permute-start | bytes 196616 | tf_op jit(solution)/shard_map/ppermute | solution.py:332
  65.3 5.2 %collective-permute-start.11 = (bf16[8,16,256]{2,1,0:T(8,128)(2,1)S(1)}, bf16[8,16,256]{2,1,0:T(8,128)(2,1)S(1)}, u32[]{:S(2)}, u32[]{:S(2)}) collective-permute-start(bf16[8,16,256]{2,1,0:T(8,128)(2,1)S(1)} %convert_element_type.69), channel_id=1, source_target_pairs={{0,12},{4,8},{8,4},{12,0},{16,28},{20,24},{24,20},{28,16},{1,13},{... | collective-permute-start | bytes 196616 | tf_op jit(solution)/shard_map/ppermute | solution.py:332
  65.6 5.3 %collective-permute-start.9 = (bf16[8,16,256]{2,1,0:T(8,128)(2,1)S(1)}, bf16[8,16,256]{2,1,0:T(8,128)(2,1)S(1)}, u32[]{:S(2)}, u32[]{:S(2)}) collective-permute-start(bf16[8,16,256]{2,1,0:T(8,128)(2,1)S(1)} %convert_element_type.69), channel_id=1, source_target_pairs={{0,4},{4,0},{8,12},{12,8},{16,20},{20,16},{24,28},{28,24},{1,5},{5... | collective-permute-start | bytes 196616 | tf_op jit(solution)/shard_map/ppermute | solution.py:332
  71.0 6.3 %collective-permute-start.12 = (bf16[8,16,256]{2,1,0:T(8,128)(2,1)S(1)}, bf16[8,16,256]{2,1,0:T(8,128)(2,1)S(1)}, u32[]{:S(2)}, u32[]{:S(2)}) collective-permute-start(bf16[8,16,256]{2,1,0:T(8,128)(2,1)S(1)} %fusion.14), channel_id=1, source_target_pairs={{0,16},{4,20},{8,24},{12,28},{16,0},{20,4},{24,8},{28,12},{1,17},{... | collective-permute-start | bytes 196616 | tf_op jit(solution)/shard_map/ppermute | solution.py:332
  77.3 15.0 %copy-start.3 = (f32[16,4096]{1,0:T(8,128)S(1)}, f32[16,4096]{1,0:T(8,128)}, u32[]{:S(2)}) copy-start(f32[16,4096]{1,0:T(8,128)} %coef_ref.1) | copy-start | bytes 786436
  78.6 26.5 %copy-start.4 = (f32[16,1024]{1,0:T(8,128)S(1)}, f32[16,1024]{1,0:T(8,128)}, u32[]{:S(2)}) copy-start(f32[16,1024]{1,0:T(8,128)} %param.10) | copy-start | bytes 196612
  88.0 11.9 %all-to-all-start = ((f32[8,16,256]{2,1,0:T(8,128)}), f32[8,16,256]{2,1,0:T(8,128)S(1)}, u32[]{:S(2)}, u32[]{:S(2)}) async-start(f32[8,16,256]{2,1,0:T(8,128)} %get-tuple-element.65), calls=%async_computation | async-start | bytes 262144 | tf_op jit(solution)/shard_map/all_to_all | solution.py:424

commit v4 on v3

--- a/solution.py
+++ b/solution.py
@@ -43,6 +43,14 @@
     return [pl.BlockSpec(memory_space=pltpu.VMEM)] * count
 
 
+def in_hbm(x):
+    return pltpu.with_memory_space_constraint(x, pltpu.HBM)
+
+
+def held(x):
+    return pltpu.with_memory_space_constraint(x, pltpu.VMEM)
+
+
 def params():
     return pltpu.CompilerParams(vmem_limit_bytes=KERNEL_VMEM)
 
@@ -52,7 +60,7 @@
     return jnp.concatenate([ref[step, pl.ds(row, 1), :], ref[step, pl.ds(row + 1, 1), :]], axis=1)
 
 
-def compact_kernel(per_step, targets, off_ref, dest_ref, pool_hbm, coefs_ref, out_ref, norm_ref, coef_ref, side_out, pool_ref, parts_ref, arrived):
+def compact_kernel(per_step, targets, off_ref, dest_ref, pool_hbm, coefs_hbm, out_ref, norm_ref, coef_ref, side_out, pool_ref, coefs_ref, parts_ref, arrived, coefs_arrived):
     steps, features = out_ref.shape[0], out_ref.shape[2]
     blocks = pool_ref.shape[0] // POOL_BLOCK
     tile = math.gcd(per_step, 512)
@@ -61,8 +69,11 @@
         at = pl.ds(pl.multiple_of(block * POOL_BLOCK, POOL_BLOCK), POOL_BLOCK)
         return pltpu.make_async_copy(pool_hbm.at[at, :], pool_ref.at[at, :], arrived.at[block])
 
+    coefs_copy = pltpu.make_async_copy(coefs_hbm, coefs_ref, coefs_arrived)
+    coefs_copy.start()
     for block in range(blocks):
         fetch(block).start()
+    coefs_copy.wait()
     parts_ref[3 * targets :, :] = jnp.zeros((LANES - 3 * targets, parts_ref.shape[1]), BF16)
     for part, value in enumerate(split3(coefs_ref[...])):
         parts_ref[part * targets : (part + 1) * targets, :] = value
@@ -138,8 +149,8 @@
         in_specs=[
             pl.BlockSpec(memory_space=pltpu.SMEM),
             *in_vmem(1),
-            pl.BlockSpec(memory_space=pl.ANY),
-            *in_vmem(1),
+            pl.BlockSpec(memory_space=pltpu.HBM),
+            pl.BlockSpec(memory_space=pltpu.HBM),
         ],
         out_specs=in_vmem(3),
         out_shape=(
@@ -150,12 +161,14 @@
         scratch_shapes=[
             pltpu.VMEM((steps, length, LANES), BF16),
             pltpu.VMEM(pool.shape, BF16),
+            pltpu.VMEM(coefs.shape, F32),
             pltpu.VMEM((LANES, pool.shape[0]), BF16),
             pltpu.SemaphoreType.DMA((pool.shape[0] // POOL_BLOCK,)),
+            pltpu.SemaphoreType.DMA,
         ],
         compiler_params=params(),
         cost_estimate=pl.CostEstimate(flops=4 * 10**9, bytes_accessed=8 * 10**6, transcendentals=0),
-    )(off, dest, pool, coefs)
+    )(off, dest, in_hbm(pool), in_hbm(coefs))
 
 
 def block_kernel(per_step, targets, quarter, scale, offset, slot_ref, rows_ref, chosen_ref, norm_ref, *refs):
@@ -196,10 +209,10 @@
 def block_call(slot, rows, chosen, norm, state, per_step, targets, row_devices, scale, offset):
     steps, _, features = chosen.shape
     quarter = rows.shape[0] - round_up(targets, 16)
-    operands = [slot, rows, chosen, norm]
+    operands = [slot, rows, held(chosen), held(norm)]
     aliases = {}
     if state is not None:
-        operands += [pltpu.with_memory_space_constraint(x, pltpu.VMEM) for x in state]
+        operands += [held(x) for x in state]
         aliases = {4: 0, 5: 1, 6: 2}
     entries = quarter * per_step * steps
     return pl.pallas_call(
@@ -225,9 +238,10 @@
     return pl.CostEstimate(flops=2 * targets * entries, bytes_accessed=2 * entries, transcendentals=0)
 
 
-def change_kernel(targets, step, sums_ref, square_ref, coef_ref, k_ref, side_ref, *refs):
-    before_ref = refs[0] if len(refs) == 4 else None
-    delta_ref, change_ref, moved_ref = refs[-3:]
+def change_kernel(targets, step, first, last, me_ref, sums_ref, square_ref, coef_ref, k_ref, side_ref, *refs):
+    before_ref = None if first else refs[0]
+    outs = list(refs if first else refs[1:])
+    delta_ref, change_ref = outs[:2]
     per_step = delta_ref.shape[1]
     total, square = sums_ref[0, :targets, :], square_ref[0, targets + step : targets + step + 1, :]
     for i in range(1, sums_ref.shape[0]):
@@ -240,26 +254,30 @@
     def body(i, _):
         k_low = k_ref[i, :, step * per_step : (step + 1) * per_step]
         change = lax.dot_general(low, k_low, NT, preferred_element_type=F32)
-        moved_ref[i] = change * side_ref[i, targets : targets + 1, :]
-        change_ref[i] = change if before_ref is None else change + before_ref[i]
+        relative = i ^ me_ref[0]
+        if not last:
+            outs[2][i] = change * side_ref[i, targets : targets + 1, :]
+        change_ref[relative] = change if first else change + before_ref[relative]
         return 0
 
     lax.fori_loop(0, k_ref.shape[0], body, 0, unroll=2)
 
 
-def change_call(sums, squares, coef, k_all, side, step, targets, before=None):
+def change_call(me, sums, squares, coef, k_all, side, step, steps, targets, before=None):
     row_devices, quarter, _ = k_all.shape
     per_step = sums.shape[2]
-    operands = [sums, squares, coef, pltpu.with_memory_space_constraint(k_all, pltpu.VMEM), side]
+    last = step == steps - 1
+    operands = [me, sums, squares, coef, held(k_all), side]
     if before is not None:
         operands.append(before)
     change = jax.ShapeDtypeStruct((row_devices, targets, quarter), F32)
+    outs = (jax.ShapeDtypeStruct((targets, per_step), F32), change) + (() if last else (change,))
     return pl.pallas_call(
-        functools.partial(change_kernel, targets, step),
+        functools.partial(change_kernel, targets, step, before is None, last),
         name="change",
-        in_specs=in_vmem(len(operands)),
-        out_specs=in_vmem(3),
-        out_shape=(jax.ShapeDtypeStruct((targets, per_step), F32), change, change),
+        in_specs=[pl.BlockSpec(memory_space=pltpu.SMEM)] + in_vmem(len(operands) - 1),
+        out_specs=in_vmem(len(outs)),
+        out_shape=outs,
         compiler_params=params(),
         cost_estimate=pass_cost(k_all, per_step, targets),
     )(*operands)
@@ -287,7 +305,7 @@
         out_shape=jax.ShapeDtypeStruct((targets, per_step), F32),
         compiler_params=params(),
         cost_estimate=pass_cost(k_all, per_step, targets),
-    )(moved, side, pltpu.with_memory_space_constraint(k_all, pltpu.VMEM))
+    )(moved, side, held(k_all))
 
 
 def scatter_kernel(targets, step, off_ref, dest_ref, coef_ref, delta_ref, out_ref, parts_ref):
@@ -401,6 +419,7 @@
         )
         state = (k_all, sums, info)
 
+    me = my_row.astype(jnp.int32)[None]
     squares = lax.all_gather(sums, "cent")
     gathered = squares
     total_change = None
@@ -416,13 +435,23 @@
             moved = share if step == 1 else moved + share
             gradient = gradient_call(moved, info, k_all, step, target_count, per_step)
             gathered = lax.all_gather(gradient, "cent")
-        delta, total_change, share = change_call(
-            gathered, squares, own_coef, k_all, info, step, target_count, total_change
+        delta, total_change, *more = change_call(
+            me, gathered, squares, own_coef, k_all, info, step, steps, target_count, total_change
         )
+        share = more[0] if more else None
         coef_now = scatter_call(off, dest, coef_now, delta, step)
 
-    arrived = lax.all_to_all(total_change, "rows", 0, 0)
-    own_change = jnp.sum(arrived, axis=0)
+    pieces = total_change
+    bits = bits_of(row_devices)
+    for first in range(0, len(bits), 2):
+        pair = bits[first : first + 2]
+        count = 2 ** len(pair)
+        pieces = pieces.reshape(pieces.shape[0] // count, count, target_count, quarter)
+        kept = pieces[:, 0]
+        for k in range(1, count):
+            kept = kept + swap(pieces[:, k], "rows", k * pair[0])
+        pieces = kept
+    own_change = pieces[0]
     full = lax.all_gather(own_change, "cent")
     full = full.transpose(1, 0, 2).reshape(target_count, rows_dev)
     return (coef_now, predictions + full)

time: 106 us -> 104 us (0.981)
  local copies, waits for them, and re-layouts: 3.49 us -> 0.38 us
  starting transfers between devices: 22.3 us -> 24.3 us
  waiting for transfers between devices: 21.9 us -> 20 us
    ppermute x13 -> x17, starting transfers between devices: 17.9 us -> 24.3 us  [swap(): return lax.ppermute(value, axis, [(i, i ^ bit) for i in range(count)])]
    all_to_all x1 -> x0, starting transfers between devices: 4.42 us -> none  [local(): arrived = lax.all_to_all(total_change, 'rows', 0, 0)]
    unnamed x10 -> x6, local copies, waits for them, and re-layouts: 3.16 us -> 0.02 us
    all_to_all x1 -> x0, waiting for transfers between devices: 2.77 us -> none  [local(): arrived = lax.all_to_all(total_change, 'rows', 0, 0)]
    pallas_call x1, Pallas kernels: 6.61 us -> 8.44 us  [compact(): pl.pallas_call(functools.partial(compact_kernel, per_step, targets), name...]
    ppermute x13 -> x17, waiting for transfers between devices: 19.1 us -> 20 us  [swap(): return lax.ppermute(value, axis, [(i, i ^ bit) for i in range(count)])]
  transfers between devices with their start and end apart: 14 -> 17, of which waited for: 7 -> 7; matrix products, arithmetic and copies ran while one was open for 2% -> 2% of each run, Pallas kernels for 25% -> 27%
where the time goes in v4:
time: 104 us
  Pallas kernels  35.6 us (34%)
  starting transfers between devices  24.3 us (23%)
  waiting for transfers between devices  20 us (19%)
  blocking collectives  18.4 us (18%)
  other arithmetic  3.33 us (3%)
    ppermute x17, starting transfers between devices, swap(): return lax.ppermute(value, axis, [(i, i ^ bit) for i in range(count)])  24.3 us
    ppermute x17, waiting for transfers between devices, swap(): return lax.ppermute(value, axis, [(i, i ^ bit) for i in range(count)])  20 us
    pallas_call x8, Pallas kernels, block_call(): pl.pallas_call(functools.partial(block_kernel, per_step, targets, quarter...  17 us
    pallas_call x1, Pallas kernels, compact(): pl.pallas_call(functools.partial(compact_kernel, per_step, targets), name...  8.44 us
    all_gather x1, blocking collectives, local(): squares = lax.all_gather(sums, 'cent')  6.68 us
    all_gather x1, blocking collectives, local(): gathered = lax.all_gather(gradient, 'cent')  6.48 us
    all_gather x1, blocking collectives, local(): full = lax.all_gather(own_change, 'cent')  5.24 us
    pallas_call x2, Pallas kernels, scatter_call(): pl.pallas_call(functools.partial(scatter_kernel, targets, step), name='sc...  4.69 us
  transfers between devices with their start and end apart: 17, of which 7 were waited for; matrix products, arithmetic and copies ran while one was open for 2% of the time, Pallas kernels for 27%

profile of v4, /device:TPU:0, one launch (start us, length us, event | category | flops | bytes accessed | tf_op | source)
XLA Modules:
  0.0 103.8 jit_solution(14682441391055063672)
XLA Ops:
  4.4 2.6 %collective-permute-start.1 = (bf16[2,32,128]{2,1,0:T(8,128)(2,1)S(1)}, bf16[2,32,128]{2,1,0:T(8,128)(2,1)S(1)}, u32[]{:S(2)}, u32[]{:S(2)}) collective-permute-start(bf16[2,32,128]{2,1,0:T(8,128)(2,1)S(1)} %add.60), channel_id=1, source_target_pairs={{0,2},{1,3},{2,0},{3,1},{4,6},{5,7},{6,4},{7,5},{8,10},{9,11},{10,... | collective-permute-start | bytes 49160 | tf_op jit(solution)/shard_map/ppermute | solution.py:350
  10.2 2.6 %collective-permute-start.2 = (bf16[272,512]{1,0:T(8,128)(2,1)S(1)}, bf16[272,512]{1,0:T(8,128)(2,1)S(1)}, u32[]{:S(2)}, u32[]{:S(2)}) collective-permute-start(bf16[272,512]{1,0:T(8,128)(2,1)S(1)} %maximum_maximum_fusion.rows_ref), channel_id=1, source_target_pairs={{0,16},{4,20},{8,24},{12,28},{16,0},{20,4},{24,8},{28,12},{1,17},{... | collective-permute-start | bytes 835592 | tf_op jit(solution)/shard_map/ppermute | solution.py:350
  13.4 9.5 %collective-permute-done.6.rows_ref = bf16[272,512]{1,0:T(8,128)(2,1)S(1)} collective-permute-done((bf16[272,512]{1,0:T(8,128)(2,1)S(1)}, bf16[272,512]{1,0:T(8,128)(2,1)S(1)}, u32[]{:S(2)}, u32[]{:S(2)}) %collective-permute-start.6) | collective-permute-done | bytes 278560 | tf_op jit(solution)/shard_map/ppermute | solution.py:350
  25.8 8.4 %compact.1 = (bf16[2,1808,512]{2,1,0:T(8,128)(2,1)S(1)}, f32[2,8,1536]{2,1,0:T(8,128)S(1)}, f32[2,16,1536]{2,1,0:T(8,128)S(1)}) custom-call(s32[2,17]{1,0:T(2,128)S(1)} %pad.8.off_ref, s32[2,32,128]{2,1,0:T(8,128)S(1)} %select_convert_fusion.dest_ref, bf16[4096,512]{1,0:T(8,128)(2,1)} %pool_hbm.1, f32[16,4096]{1,0:T(8,128)} %coef_ref.1), custom_call_target="tpu_custom_call" | custom-call | flops 4000000000 | bytes 8000000 | tf_op jit(solution)/shard_map/compact/pallas_call | solution.py:146
  34.2 2.1 %kernel_block.8 = (bf16[8,256,3072]{2,1,0:T(8,128)(2,1)S(1)}, f32[24,1536]{1,0:T(8,128)S(1)}, f32[8,24,256]{2,1,0:T(8,128)S(1)}) custom-call(s32[1]{0:T(128)} %bitcast.3.slot_ref.me_ref, bf16[272,512]{1,0:T(8,128)(2,1)S(1)} %maximum_maximum_fusion.rows_ref, bf16[2,1808,512]{2,1,0:T(8,128)(2,1)S(1)} %get-tuple-element.34.chosen_ref, ...), custom_call_target="tpu_custom_call" | custom-call | flops 805306368 | bytes 1572864 | tf_op jit(solution)/shard_map/kernel_block/pallas_call | solution.py:218
  36.9 2.1 %kernel_block.9 = (bf16[8,256,3072]{2,1,0:T(8,128)(2,1)S(1)}, f32[24,1536]{1,0:T(8,128)S(1)}, f32[8,24,256]{2,1,0:T(8,128)S(1)}) custom-call(s32[1]{0:T(128)} %bitcast.10.slot_ref, bf16[272,512]{1,0:T(8,128)(2,1)S(1)} %collective-permute-done.8.rows_ref, ...), custom_call_target="tpu_custom_call", output_to_operand_aliasing={{0}: (4, {}), {1}: (5, {}), {2}: (6, {})} | custom-call | flops 805306368 | bytes 1572864 | tf_op jit(solution)/shard_map/kernel_block/pallas_call | solution.py:218
  39.0 2.1 %kernel_block.10 = (bf16[8,256,3072]{2,1,0:T(8,128)(2,1)S(1)}, f32[24,1536]{1,0:T(8,128)S(1)}, f32[8,24,256]{2,1,0:T(8,128)S(1)}) custom-call(s32[1]{0:T(128)} %bitcast.9.slot_ref, bf16[272,512]{1,0:T(8,128)(2,1)S(1)} %collective-permute-done.6.rows_ref, ...), custom_call_target="tpu_custom_call", output_to_operand_aliasing={{0}: (4, {}), {1}: (5, {}), {2}: (6, {})} | custom-call | flops 805306368 | bytes 1572864 | tf_op jit(solution)/shard_map/kernel_block/pallas_call | solution.py:218
  42.7 2.1 %kernel_block.11 = (bf16[8,256,3072]{2,1,0:T(8,128)(2,1)S(1)}, f32[24,1536]{1,0:T(8,128)S(1)}, f32[8,24,256]{2,1,0:T(8,128)S(1)}) custom-call(s32[1]{0:T(128)} %bitcast.8.slot_ref, bf16[272,512]{1,0:T(8,128)(2,1)S(1)} %collective-permute-done.7.rows_ref, ...), custom_call_target="tpu_custom_call", output_to_operand_aliasing={{0}: (4, {}), {1}: (5, {}), {2}: (6, {})} | custom-call | flops 805306368 | bytes 1572864 | tf_op jit(solution)/shard_map/kernel_block/pallas_call | solution.py:218
  44.8 2.1 %kernel_block.12 = (bf16[8,256,3072]{2,1,0:T(8,128)(2,1)S(1)}, f32[24,1536]{1,0:T(8,128)S(1)}, f32[8,24,256]{2,1,0:T(8,128)S(1)}) custom-call(s32[1]{0:T(128)} %bitcast.7.slot_ref, bf16[272,512]{1,0:T(8,128)(2,1)S(1)} %collective-permute-done.2.rows_ref, ...), custom_call_target="tpu_custom_call", output_to_operand_aliasing={{0}: (4, {}), {1}: (5, {}), {2}: (6, {})} | custom-call | flops 805306368 | bytes 1572864 | tf_op jit(solution)/shard_map/kernel_block/pallas_call | solution.py:218
  46.9 2.1 %kernel_block.13 = (bf16[8,256,3072]{2,1,0:T(8,128)(2,1)S(1)}, f32[24,1536]{1,0:T(8,128)S(1)}, f32[8,24,256]{2,1,0:T(8,128)S(1)}) custom-call(s32[1]{0:T(128)} %bitcast.6.slot_ref, bf16[272,512]{1,0:T(8,128)(2,1)S(1)} %collective-permute-done.5.rows_ref, ...), custom_call_target="tpu_custom_call", output_to_operand_aliasing={{0}: (4, {}), {1}: (5, {}), {2}: (6, {})} | custom-call | flops 805306368 | bytes 1572864 | tf_op jit(solution)/shard_map/kernel_block/pallas_call | solution.py:218
  49.0 2.3 %kernel_block.14 = (bf16[8,256,3072]{2,1,0:T(8,128)(2,1)S(1)}, f32[24,1536]{1,0:T(8,128)S(1)}, f32[8,24,256]{2,1,0:T(8,128)S(1)}) custom-call(s32[1]{0:T(128)} %bitcast.5.slot_ref, bf16[272,512]{1,0:T(8,128)(2,1)S(1)} %collective-permute-done.3.rows_ref, ...), custom_call_target="tpu_custom_call", output_to_operand_aliasing={{0}: (4, {}), {1}: (5, {}), {2}: (6, {})} | custom-call | flops 805306368 | bytes 1572864 | tf_op jit(solution)/shard_map/kernel_block/pallas_call | solution.py:218
  51.3 2.1 %kernel_block.15 = (bf16[8,256,3072]{2,1,0:T(8,128)(2,1)S(1)}, f32[24,1536]{1,0:T(8,128)S(1)}, f32[8,24,256]{2,1,0:T(8,128)S(1)}) custom-call(s32[1]{0:T(128)} %bitcast.4.slot_ref, bf16[272,512]{1,0:T(8,128)(2,1)S(1)} %collective-permute-done.4.rows_ref, ...), custom_call_target="tpu_custom_call", output_to_operand_aliasing={{0}: (4, {}), {1}: (5, {}), {2}: (6, {})} | custom-call | flops 805306368 | bytes 1572864 | tf_op jit(solution)/shard_map/kernel_block/pallas_call | solution.py:218
  53.4 6.7 %all-gather = f32[96,1536]{1,0:T(8,128)S(1)} all-gather(f32[24,1536]{1,0:T(8,128)S(1)} %get-tuple-element.57), channel_id=2, replica_groups=mesh['rows'=8,'cent'=4] {'cent'}, dimensions={0}, use_global_device_ids=true | all-gather | bytes 737280 | tf_op jit(solution)/shard_map/all_gather | solution.py:423
  60.1 2.1 %change.2 = (f32[16,1536]{1,0:T(8,128)S(1)}, f32[8,16,256]{2,1,0:T(8,128)S(1)}, f32[8,16,256]{2,1,0:T(8,128)S(1)}) custom-call(s32[1]{0:T(128)} %bitcast.3.slot_ref.me_ref, f32[4,24,1536]{2,1,0:T(8,128)S(1)} %bitcast.53, f32[4,24,1536]{2,1,0:T(8,128)S(1)} %bitcast.54, f32[2,16,1536]{2,1,0:T(8,128)S(1)} %get-tuple-element.58.coef_ref, ...), custom_call_target="tpu_custom_call" | custom-call | flops 100663296 | bytes 6291456 | tf_op jit(solution)/shard_map/change/pallas_call | solution.py:275
  66.8 2.2 %collective-permute-done.11 = bf16[8,16,256]{2,1,0:T(8,128)(2,1)S(1)} collective-permute-done((bf16[8,16,256]{2,1,0:T(8,128)(2,1)S(1)}, bf16[8,16,256]{2,1,0:T(8,128)(2,1)S(1)}, u32[]{:S(2)}, u32[]{:S(2)}) %collective-permute-start.11) | collective-permute-done | bytes 65568 | tf_op jit(solution)/shard_map/ppermute | solution.py:350
  69.6 2.4 %collective-permute-start.12 = (bf16[8,16,256]{2,1,0:T(8,128)(2,1)S(1)}, bf16[8,16,256]{2,1,0:T(8,128)(2,1)S(1)}, u32[]{:S(2)}, u32[]{:S(2)}) collective-permute-start(bf16[8,16,256]{2,1,0:T(8,128)(2,1)S(1)} %fusion.19), channel_id=1, source_target_pairs={{0,16},{4,20},{8,24},{12,28},{16,0},{20,4},{24,8},{28,12},{1,17},{... | collective-permute-start | bytes 196616 | tf_op jit(solution)/shard_map/ppermute | solution.py:350
  72.0 3.9 %collective-permute-done.12 = bf16[8,16,256]{2,1,0:T(8,128)(2,1)S(1)} collective-permute-done((bf16[8,16,256]{2,1,0:T(8,128)(2,1)S(1)}, bf16[8,16,256]{2,1,0:T(8,128)(2,1)S(1)}, u32[]{:S(2)}, u32[]{:S(2)}) %collective-permute-start.12) | collective-permute-done | bytes 65568 | tf_op jit(solution)/shard_map/ppermute | solution.py:350
  77.3 6.5 %all-gather.1 = f32[64,1536]{1,0:T(8,128)S(1)} all-gather(f32[16,1536]{1,0:T(8,128)S(1)} %gradient.1), channel_id=3, replica_groups=mesh['rows'=8,'cent'=4] {'cent'}, dimensions={0}, use_global_device_ids=true | all-gather | bytes 491520 | tf_op jit(solution)/shard_map/all_gather | solution.py:437
  83.8 2.1 %change.3 = (f32[16,1536]{1,0:T(8,128)S(1)}, f32[8,16,256]{2,1,0:T(8,128)S(1)}) custom-call(s32[1]{0:T(128)} %bitcast.3.slot_ref.me_ref, f32[4,16,1536]{2,1,0:T(8,128)S(1)} %bitcast.56, f32[4,24,1536]{2,1,0:T(8,128)S(1)} %bitcast.55, f32[2,16,1536]{2,1,0:T(8,128)S(1)} %get-tuple-element.58.coef_ref, bf16[8,256,3072]{2,1,0:T(8,128)(2,1)S(1)} %get-tuple-element.59.k_ref, ...), custom_call_target="tpu_custom_call" | custom-call | flops 100663296 | bytes 6291456 | tf_op jit(solution)/shard_map/change/pallas_call | solution.py:275
  87.6 1.9 %collective-permute-start.15 = (f32[2,16,256]{2,1,0:T(8,128)S(1)}, f32[2,16,256]{2,1,0:T(8,128)S(1)}, u32[]{:S(2)}, u32[]{:S(2)}) collective-permute-start(f32[2,16,256]{2,1,0:T(8,128)S(1)} %get-tuple-element.70), channel_id=1, source_target_pairs={{0,12},{4,8},{8,4},{12,0},{16,28},{20,24},{24,20},{28,16},{1,13},{... | collective-permute-start | bytes 98312 | tf_op jit(solution)/shard_map/ppermute | solution.py:350
  89.5 2.0 %scatter.2.coef_ref = f32[16,4096]{1,0:T(8,128)S(1)} custom-call(s32[2,17]{1,0:T(2,128)S(1)} %pad.8.off_ref, s32[2,32,128]{2,1,0:T(8,128)S(1)} %select_convert_fusion.dest_ref, f32[16,4096]{1,0:T(8,128)S(1)} %copy-done.1, f32[16,1536]{1,0:T(8,128)S(1)} %get-tuple-element.61.delta_ref), custom_call_target="tpu_custom_call" | custom-call | flops 1000000000 | bytes 1000000 | tf_op jit(solution)/shard_map/scatter/pallas_call | solution.py:336
  92.4 2.8 %collective-permute-start.16 = (f32[1,16,256]{2,1,0:T(8,128)S(1)}, f32[1,16,256]{2,1,0:T(8,128)S(1)}, u32[]{:S(2)}, u32[]{:S(2)}) collective-permute-start(f32[1,16,256]{2,1,0:T(8,128)S(1)} %slice_bitcast_fusion.4), channel_id=1, source_target_pairs={{0,16},{4,20},{8,24},{12,28},{16,0},{20,4},{24,8},{28,12},{1,17},{... | collective-permute-start | bytes 49160 | tf_op jit(solution)/shard_map/ppermute | solution.py:350
  95.2 2.7 %scatter.3 = f32[16,4096]{1,0:T(8,128)} custom-call(s32[2,17]{1,0:T(2,128)S(1)} %pad.8.off_ref, s32[2,32,128]{2,1,0:T(8,128)S(1)} %select_convert_fusion.dest_ref, f32[16,4096]{1,0:T(8,128)S(1)} %scatter.2.coef_ref, f32[16,1536]{1,0:T(8,128)S(1)} %get-tuple-element.64.delta_ref), custom_call_target="tpu_custom_call" | custom-call | flops 1000000000 | bytes 1000000 | tf_op jit(solution)/shard_map/scatter/pallas_call | solution.py:336
  97.9 5.2 %all_gather.19 = f32[4,16,256]{2,1,0:T(8,128)S(1)} all-gather(f32[1,16,256]{2,1,0:T(8,128)S(1)} %fusion.14), channel_id=1, replica_groups=mesh['rows'=8,'cent'=4] {'cent'}, dimensions={0}, use_global_device_ids=true | all-gather | bytes 81920 | tf_op jit(solution)/shard_map/all_gather | solution.py:455
  (61 shorter events, 22.2 us)
Async XLA Ops:
  0.6 3.0 %copy-start = (bf16[1024,512]{1,0:T(8,128)(2,1)S(1)}, bf16[1024,512]{1,0:T(8,128)(2,1)}, u32[]{:S(2)}) copy-start(bf16[1024,512]{1,0:T(8,128)(2,1)} %param.7) | copy-start | bytes 3145732
  2.3 2.1 %collective-permute-start = (bf16[2,32,128]{2,1,0:T(8,128)(2,1)S(1)}, bf16[2,32,128]{2,1,0:T(8,128)(2,1)S(1)}, u32[]{:S(2)}, u32[]{:S(2)}) collective-permute-start(bf16[2,32,128]{2,1,0:T(8,128)(2,1)S(1)} %fusion.2), channel_id=1, source_target_pairs={{0,1},{1,0},{2,3},{3,2},{4,5},{5,4},{6,7},{7,6},{8,9},{9,8},{10,11... | collective-permute-start | bytes 49160 | tf_op jit(solution)/shard_map/ppermute | solution.py:350
  4.4 8.3 %collective-permute-start.1 = (bf16[2,32,128]{2,1,0:T(8,128)(2,1)S(1)}, bf16[2,32,128]{2,1,0:T(8,128)(2,1)S(1)}, u32[]{:S(2)}, u32[]{:S(2)}) collective-permute-start(bf16[2,32,128]{2,1,0:T(8,128)(2,1)S(1)} %add.60), channel_id=1, source_target_pairs={{0,2},{1,3},{2,0},{3,1},{4,6},{5,7},{6,4},{7,5},{8,10},{9,11},{10,... | collective-permute-start | bytes 49160 | tf_op jit(solution)/shard_map/ppermute | solution.py:350
  7.0 29.9 %collective-permute-start.8 = (bf16[272,512]{1,0:T(8,128)(2,1)S(1)}, bf16[272,512]{1,0:T(8,128)(2,1)S(1)}, u32[]{:S(2)}, u32[]{:S(2)}) collective-permute-start(bf16[272,512]{1,0:T(8,128)(2,1)S(1)} %maximum_maximum_fusion.rows_ref), channel_id=1, source_target_pairs={{0,4},{4,0},{8,12},{12,8},{16,20},{20,16},{24,28},{28,24},{1,5},{5... | collective-permute-start | bytes 835592 | tf_op jit(solution)/shard_map/ppermute | solution.py:350
  8.6 14.3 %collective-permute-start.6 = (bf16[272,512]{1,0:T(8,128)(2,1)S(1)}, bf16[272,512]{1,0:T(8,128)(2,1)S(1)}, u32[]{:S(2)}, u32[]{:S(2)}) collective-permute-start(bf16[272,512]{1,0:T(8,128)(2,1)S(1)} %maximum_maximum_fusion.rows_ref), channel_id=1, source_target_pairs={{0,8},{4,12},{8,0},{12,4},{16,24},{20,28},{24,16},{28,20},{1,9},{5... | collective-permute-start | bytes 835592 | tf_op jit(solution)/shard_map/ppermute | solution.py:350
  10.2 15.1 %collective-permute-start.2 = (bf16[272,512]{1,0:T(8,128)(2,1)S(1)}, bf16[272,512]{1,0:T(8,128)(2,1)S(1)}, u32[]{:S(2)}, u32[]{:S(2)}) collective-permute-start(bf16[272,512]{1,0:T(8,128)(2,1)S(1)} %maximum_maximum_fusion.rows_ref), channel_id=1, source_target_pairs={{0,16},{4,20},{8,24},{12,28},{16,0},{20,4},{24,8},{28,12},{1,17},{... | collective-permute-start | bytes 835592 | tf_op jit(solution)/shard_map/ppermute | solution.py:350
  22.9 19.7 %collective-permute-start.7 = (bf16[272,512]{1,0:T(8,128)(2,1)S(1)}, bf16[272,512]{1,0:T(8,128)(2,1)S(1)}, u32[]{:S(2)}, u32[]{:S(2)}) collective-permute-start(bf16[272,512]{1,0:T(8,128)(2,1)S(1)} %collective-permute-done.6.rows_ref), channel_id=1, source_target_pairs={{0,4},{4,0},{8,12},{12,8},{16,20},{20,16},{24,28},{28,24},{1,5},{5... | collective-permute-start | bytes 835592 | tf_op jit(solution)/shard_map/ppermute | solution.py:350
  25.3 15.8 %collective-permute-start.3 = (bf16[272,512]{1,0:T(8,128)(2,1)S(1)}, bf16[272,512]{1,0:T(8,128)(2,1)S(1)}, u32[]{:S(2)}, u32[]{:S(2)}) collective-permute-start(bf16[272,512]{1,0:T(8,128)(2,1)S(1)} %collective-permute-done.2.rows_ref), channel_id=1, source_target_pairs={{0,8},{4,12},{8,0},{12,4},{16,24},{20,28},{24,16},{28,20},{1,9},{5... | collective-permute-start | bytes 835592 | tf_op jit(solution)/shard_map/ppermute | solution.py:350
  36.3 10.6 %collective-permute-start.5 = (bf16[272,512]{1,0:T(8,128)(2,1)S(1)}, bf16[272,512]{1,0:T(8,128)(2,1)S(1)}, u32[]{:S(2)}, u32[]{:S(2)}) collective-permute-start(bf16[272,512]{1,0:T(8,128)(2,1)S(1)} %collective-permute-done.2.rows_ref), channel_id=1, source_target_pairs={{0,4},{4,0},{8,12},{12,8},{16,20},{20,16},{24,28},{28,24},{1,5},{5... | collective-permute-start | bytes 835592 | tf_op jit(solution)/shard_map/ppermute | solution.py:350
  41.1 10.2 %collective-permute-start.4 = (bf16[272,512]{1,0:T(8,128)(2,1)S(1)}, bf16[272,512]{1,0:T(8,128)(2,1)S(1)}, u32[]{:S(2)}, u32[]{:S(2)}) collective-permute-start(bf16[272,512]{1,0:T(8,128)(2,1)S(1)} %collective-permute-done.3.rows_ref), channel_id=1, source_target_pairs={{0,4},{4,0},{8,12},{12,8},{16,20},{20,16},{24,28},{28,24},{1,5},{5... | collective-permute-start | bytes 835592 | tf_op jit(solution)/shard_map/ppermute | solution.py:350
  62.3 4.6 %collective-permute-start.10 = (bf16[8,16,256]{2,1,0:T(8,128)(2,1)S(1)}, bf16[8,16,256]{2,1,0:T(8,128)(2,1)S(1)}, u32[]{:S(2)}, u32[]{:S(2)}) collective-permute-start(bf16[8,16,256]{2,1,0:T(8,128)(2,1)S(1)} %convert_element_type.69), channel_id=1, source_target_pairs={{0,8},{4,12},{8,0},{12,4},{16,24},{20,28},{24,16},{28,20},{1,9},{5... | collective-permute-start | bytes 196616 | tf_op jit(solution)/shard_map/ppermute | solution.py:350
  63.9 5.2 %collective-permute-start.11 = (bf16[8,16,256]{2,1,0:T(8,128)(2,1)S(1)}, bf16[8,16,256]{2,1,0:T(8,128)(2,1)S(1)}, u32[]{:S(2)}, u32[]{:S(2)}) collective-permute-start(bf16[8,16,256]{2,1,0:T(8,128)(2,1)S(1)} %convert_element_type.69), channel_id=1, source_target_pairs={{0,12},{4,8},{8,4},{12,0},{16,28},{20,24},{24,20},{28,16},{1,13},{... | collective-permute-start | bytes 196616 | tf_op jit(solution)/shard_map/ppermute | solution.py:350
  64.3 5.3 %collective-permute-start.9 = (bf16[8,16,256]{2,1,0:T(8,128)(2,1)S(1)}, bf16[8,16,256]{2,1,0:T(8,128)(2,1)S(1)}, u32[]{:S(2)}, u32[]{:S(2)}) collective-permute-start(bf16[8,16,256]{2,1,0:T(8,128)(2,1)S(1)} %convert_element_type.69), channel_id=1, source_target_pairs={{0,4},{4,0},{8,12},{12,8},{16,20},{20,16},{24,28},{28,24},{1,5},{5... | collective-permute-start | bytes 196616 | tf_op jit(solution)/shard_map/ppermute | solution.py:350
  69.6 6.3 %collective-permute-start.12 = (bf16[8,16,256]{2,1,0:T(8,128)(2,1)S(1)}, bf16[8,16,256]{2,1,0:T(8,128)(2,1)S(1)}, u32[]{:S(2)}, u32[]{:S(2)}) collective-permute-start(bf16[8,16,256]{2,1,0:T(8,128)(2,1)S(1)} %fusion.19), channel_id=1, source_target_pairs={{0,16},{4,20},{8,24},{12,28},{16,0},{20,4},{24,8},{28,12},{1,17},{... | collective-permute-start | bytes 196616 | tf_op jit(solution)/shard_map/ppermute | solution.py:350
  76.0 13.5 %copy-start.1 = (f32[16,4096]{1,0:T(8,128)S(1)}, f32[16,4096]{1,0:T(8,128)}, u32[]{:S(2)}) copy-start(f32[16,4096]{1,0:T(8,128)} %coef_ref.1) | copy-start | bytes 786436
  77.3 25.9 %copy-start.2 = (f32[16,1024]{1,0:T(8,128)S(1)}, f32[16,1024]{1,0:T(8,128)}, u32[]{:S(2)}) copy-start(f32[16,1024]{1,0:T(8,128)} %param.10) | copy-start | bytes 196612
  85.9 5.6 %collective-permute-start.13 = (f32[2,16,256]{2,1,0:T(8,128)S(1)}, f32[2,16,256]{2,1,0:T(8,128)S(1)}, u32[]{:S(2)}, u32[]{:S(2)}) collective-permute-start(f32[2,16,256]{2,1,0:T(8,128)S(1)} %get-tuple-element.68), channel_id=1, source_target_pairs={{0,4},{4,0},{8,12},{12,8},{16,20},{20,16},{24,28},{28,24},{1,5},{5... | collective-permute-start | bytes 98312 | tf_op jit(solution)/shard_map/ppermute | solution.py:350
  87.3 4.2 %collective-permute-start.14 = (f32[2,16,256]{2,1,0:T(8,128)S(1)}, f32[2,16,256]{2,1,0:T(8,128)S(1)}, u32[]{:S(2)}, u32[]{:S(2)}) collective-permute-start(f32[2,16,256]{2,1,0:T(8,128)S(1)} %get-tuple-element.69), channel_id=1, source_target_pairs={{0,8},{4,12},{8,0},{12,4},{16,24},{20,28},{24,16},{28,20},{1,9},{5... | collective-permute-start | bytes 98312 | tf_op jit(solution)/shard_map/ppermute | solution.py:350
  87.6 4.8 %collective-permute-start.15 = (f32[2,16,256]{2,1,0:T(8,128)S(1)}, f32[2,16,256]{2,1,0:T(8,128)S(1)}, u32[]{:S(2)}, u32[]{:S(2)}) collective-permute-start(f32[2,16,256]{2,1,0:T(8,128)S(1)} %get-tuple-element.70), channel_id=1, source_target_pairs={{0,12},{4,8},{8,4},{12,0},{16,28},{20,24},{24,20},{28,16},{1,13},{... | collective-permute-start | bytes 98312 | tf_op jit(solution)/shard_map/ppermute | solution.py:350
  92.4 5.5 %collective-permute-start.16 = (f32[1,16,256]{2,1,0:T(8,128)S(1)}, f32[1,16,256]{2,1,0:T(8,128)S(1)}, u32[]{:S(2)}, u32[]{:S(2)}) collective-permute-start(f32[1,16,256]{2,1,0:T(8,128)S(1)} %slice_bitcast_fusion.4), channel_id=1, source_target_pairs={{0,16},{4,20},{8,24},{12,28},{16,0},{20,4},{24,8},{28,12},{1,17},{... | collective-permute-start | bytes 49160 | tf_op jit(solution)/shard_map/ppermute | solution.py:350

commit v5 on v4

--- a/solution.py
+++ b/solution.py
@@ -12,6 +12,8 @@
 LANES = 128
 POOL_BLOCK = 256
 WINDOW = 144
+TILE = 512
+GROUPS = [(0, 1), (2, 3), (4, 6), (5,), (7,)]
 KERNEL_VMEM = 16 * 2**20
 LOG2E = math.log2(math.e)
 NT = (((1,), (1,)), ((), ()))
@@ -78,17 +80,23 @@
     for part, value in enumerate(split3(coefs_ref[...])):
         parts_ref[part * targets : (part + 1) * targets, :] = value
 
-    def place(block, step, window):
-        base = pl.multiple_of((off_ref[step, block] // 16) * 16, 16)
-        dest = two_rows(dest_ref, step, block) - base
-        slots = lax.broadcasted_iota(jnp.int32, (window, POOL_BLOCK), 0)
-        pick = jnp.where(slots == dest, 1.0, 0.0).astype(BF16)
+    def place(block, window):
+        bases, picks = [], []
+        for step in range(steps):
+            bases.append(pl.multiple_of((off_ref[step, block] // 16) * 16, 16))
+            dest = two_rows(dest_ref, step, block) - bases[step]
+            slots = lax.broadcasted_iota(jnp.int32, (window, POOL_BLOCK), 0)
+            picks.append(jnp.where(slots == dest, 1.0, 0.0).astype(BF16))
+        pick = jnp.concatenate(picks, axis=0)
         at = pl.ds(pl.multiple_of(block * POOL_BLOCK, POOL_BLOCK), POOL_BLOCK)
-        packed = jnp.dot(pick, pool_ref[at, :], preferred_element_type=F32)
-        side = lax.dot_general(pick, parts_ref[:, at], NT, preferred_element_type=F32)
-        for rows, target in ((packed.astype(BF16), out_ref), (side.astype(BF16), side_out)):
-            target[step, pl.ds(base, 16), :] += rows[:16]
-            target[step, pl.ds(pl.multiple_of(base + 16, 16), window - 16), :] = rows[16:]
+        packed = jnp.dot(pick, pool_ref[at, :], preferred_element_type=F32).astype(BF16)
+        side = lax.dot_general(pick, parts_ref[:, at], NT, preferred_element_type=F32).astype(BF16)
+        for step in range(steps):
+            first = step * window
+            after = pl.ds(pl.multiple_of(bases[step] + 16, 16), window - 16)
+            for rows, target in ((packed, out_ref), (side, side_out)):
+                target[step, pl.ds(bases[step], 16), :] += rows[first : first + 16]
+                target[step, after, :] = rows[first + 16 : first + window]
 
     for step in range(steps):
         out_ref[step, :16, :] = jnp.zeros((16, features), BF16)
@@ -107,16 +115,14 @@
             for i in range(2):
                 fetch(2 * pair + i).wait()
             for i in range(2):
-                for step in range(steps):
-                    place(2 * pair + i, step, WINDOW)
+                place(2 * pair + i, WINDOW)
 
     @pl.when(jnp.logical_not(narrow))
     def _():
         @pl.loop(0, blocks)
         def _(block):
             fetch(block).wait()
-            for step in range(steps):
-                place(block, step, POOL_BLOCK + 16)
+            place(block, POOL_BLOCK + 16)
 
     ones = jnp.ones((8, features), BF16)
     eye = lax.broadcasted_iota(jnp.int32, (3 * targets, LANES), 0) == lax.broadcasted_iota(
@@ -171,22 +177,24 @@
     )(off, dest, in_hbm(pool), in_hbm(coefs))
 
 
-def block_kernel(per_step, targets, quarter, scale, offset, slot_ref, rows_ref, chosen_ref, norm_ref, *refs):
-    k_ref, sums_ref, side_ref = refs[-3:]
-    sums_in = refs[1] if len(refs) > 3 else None
+def block_kernel(per_step, targets, quarter, count, scale, offset, slot_ref, chosen_ref, norm_ref, *refs):
+    chunk_refs, (k_ref, sums_ref, side_ref) = refs[:count], refs[-3:]
+    sums_in = refs[count + 1] if len(refs) > count + 3 else None
     steps = chosen_ref.shape[0]
-    tile = math.gcd(per_step, 512)
-    slot = slot_ref[0]
-
-    rows = rows_ref[:quarter, :]
+    tile = math.gcd(per_step, TILE)
+
+    rows = jnp.concatenate([ref[:quarter, :] for ref in chunk_refs], axis=0)
     wide_rows = rows.astype(F32)
     row_norm = jnp.sum(wide_rows * wide_rows, axis=1, keepdims=True) * (scale * LOG2E) - offset * LOG2E
-    parts = rows_ref[quarter : quarter + 3, quarter : 2 * quarter].astype(F32)
-    weight = jnp.sum(parts, axis=0, keepdims=True)
-    weight_column = jnp.transpose(jnp.broadcast_to(weight, (8, quarter)))[:, :1]
-    weighted = rows_ref[quarter : quarter + targets, :quarter]
-    side_ref[slot, :targets, :] = weighted.astype(F32)
-    side_ref[slot, targets:, :] = jnp.broadcast_to(weight, (side_ref.shape[1] - targets, quarter))
+    columns = []
+    for i, ref in enumerate(chunk_refs):
+        parts = ref[quarter : quarter + 3, quarter : 2 * quarter].astype(F32)
+        weight = jnp.sum(parts, axis=0, keepdims=True)
+        columns.append(jnp.transpose(jnp.broadcast_to(weight, (8, quarter)))[:, :1])
+        side_ref[slot_ref[i], :targets, :] = ref[quarter : quarter + targets, :quarter].astype(F32)
+        side_ref[slot_ref[i], targets:, :] = jnp.broadcast_to(weight, (side_ref.shape[1] - targets, quarter))
+    weight_column = jnp.concatenate(columns, axis=0)
+    weighted = jnp.concatenate([ref[quarter : quarter + targets, :quarter] for ref in chunk_refs], axis=1)
 
     for first in range(0, per_step, tile):
         for step in range(steps):
@@ -195,28 +203,31 @@
             )
             centre = norm_ref[step, :1, first : first + tile] * (scale * LOG2E)
             k_low = jnp.exp2(dots * (2.0 * scale * LOG2E) - row_norm - centre).astype(BF16)
-            k_ref[slot, :, step * per_step + first : step * per_step + first + tile] = k_low
+            at = step * per_step + first
+            for i in range(count):
+                k_ref[slot_ref[i], :, at : at + tile] = k_low[i * quarter : (i + 1) * quarter]
             wide = k_low.astype(F32)
             updates = [(targets + step, 1, jnp.sum(weight_column * (wide * wide), axis=0, keepdims=True))]
             if step == 0:
                 updates.append((0, targets, jnp.dot(weighted, k_low, preferred_element_type=F32)))
-            for row, count, value in updates:
+            for row, size, value in updates:
                 if sums_in is not None:
-                    value = value + sums_in[row : row + count, first : first + tile]
-                sums_ref[row : row + count, first : first + tile] = value
-
-
-def block_call(slot, rows, chosen, norm, state, per_step, targets, row_devices, scale, offset):
+                    value = value + sums_in[row : row + size, first : first + tile]
+                sums_ref[row : row + size, first : first + tile] = value
+
+
+def block_call(slots, chunks, chosen, norm, state, per_step, targets, row_devices, scale, offset):
     steps, _, features = chosen.shape
-    quarter = rows.shape[0] - round_up(targets, 16)
-    operands = [slot, rows, held(chosen), held(norm)]
+    count = len(chunks)
+    quarter = chunks[0].shape[0] - round_up(targets, 16)
+    operands = [slots, held(chosen), held(norm), *chunks]
     aliases = {}
     if state is not None:
+        aliases = {len(operands) + i: i for i in range(3)}
         operands += [held(x) for x in state]
-        aliases = {4: 0, 5: 1, 6: 2}
-    entries = quarter * per_step * steps
+    entries = count * quarter * per_step * steps
     return pl.pallas_call(
-        functools.partial(block_kernel, per_step, targets, quarter, scale, offset),
+        functools.partial(block_kernel, per_step, targets, quarter, count, scale, offset),
         name="kernel_block",
         in_specs=[pl.BlockSpec(memory_space=pltpu.SMEM)] + in_vmem(len(operands) - 1),
         out_specs=in_vmem(3),
@@ -354,6 +365,12 @@
     return [1 << k for k in range(count.bit_length() - 1)]
 
 
+def groups_of(row_devices):
+    if row_devices == 8:
+        return GROUPS
+    return [(have,) for have in range(row_devices)]
+
+
 def local(samples, weights, targets, predictions, centres, coefs, block_index):
     rows_dev, features = samples.shape
     pool_dev = centres.shape[0]
@@ -396,7 +413,10 @@
 
     for bit in reversed(bits_of(row_devices)):
         for have in sorted(chunks):
-            chunks[have | bit] = swap(chunks[have], "rows", bit)
+            source = chunks[have]
+            if bit == 1 and have == row_devices // 2:
+                source = lax.optimization_barrier(source + lax.optimization_barrier(jnp.zeros((), BF16)))
+            chunks[have | bit] = swap(source, "rows", bit)
 
     upper = (jnp.arange(LANES)[:, None] <= jnp.arange(LANES)[None, :]).astype(BF16)
     before = (jnp.arange(high_count)[:, None] > jnp.arange(high_count)[None, :]).astype(BF16)
@@ -412,10 +432,11 @@
     chosen, norm, own_coef = compact(off, dest, centres, coefs, per_step, target_count)
 
     state = None
-    for have in range(row_devices):
-        slot = (my_row ^ have).astype(jnp.int32)[None]
+    for group in groups_of(row_devices):
+        slots = my_row.astype(jnp.int32) ^ jnp.array(group, jnp.int32)
         k_all, sums, info = block_call(
-            slot, chunks[have], chosen, norm, state, per_step, target_count, row_devices, sharpness, offset
+            slots, [chunks[have] for have in group], chosen, norm, state,
+            per_step, target_count, row_devices, sharpness, offset,
         )
         state = (k_all, sums, info)
 

time: 104 us -> 98 us (0.942)
  waiting for transfers between devices: 20 us -> 14.7 us
  starting transfers between devices: 24.3 us -> 21.8 us
  other arithmetic: 3.33 us -> 4.67 us
    ppermute x17, waiting for transfers between devices: 20 us -> 14.7 us  [swap(): return lax.ppermute(value, axis, [(i, i ^ bit) for i in range(count)])]
    ppermute x17, starting transfers between devices: 24.3 us -> 21.8 us  [swap(): return lax.ppermute(value, axis, [(i, i ^ bit) for i in range(count)])]
    xor x0 -> x3, other arithmetic: none -> 1.32 us  [local(): slots = my_row.astype(jnp.int32) ^ jnp.array(group, jnp.int32)]
    pallas_call x8 -> x5, Pallas kernels: 17 us -> 16.4 us  [block_call(): pl.pallas_call(functools.partial(block_kernel, per_step, targets, quarter...]
  transfers between devices with their start and end apart: 17 -> 17, of which waited for: 7 -> 8; matrix products, arithmetic and copies ran while one was open for 2% -> 4% of each run, Pallas kernels for 27% -> 28%
where the time goes in v5:
time: 98 us; the launch traced here: 97.7 us
  Pallas kernels  35 us (36%)
  starting transfers between devices  21.8 us (22%)
  blocking collectives  19 us (19%)
  waiting for transfers between devices  14.7 us (15%)
  other arithmetic  4.67 us (5%)
    ppermute x17, starting transfers between devices, swap(): return lax.ppermute(value, axis, [(i, i ^ bit) for i in range(count)])  21.8 us
    pallas_call x5, Pallas kernels, block_call(): pl.pallas_call(functools.partial(block_kernel, per_step, targets, quarter...  16.4 us
    ppermute x17, waiting for transfers between devices, swap(): return lax.ppermute(value, axis, [(i, i ^ bit) for i in range(count)])  14.7 us
    pallas_call x1, Pallas kernels, compact(): pl.pallas_call(functools.partial(compact_kernel, per_step, targets), name...  8.45 us
    all_gather x1, blocking collectives, local(): squares = lax.all_gather(sums, 'cent')  7.52 us
    all_gather x1, blocking collectives, local(): gathered = lax.all_gather(gradient, 'cent')  6.27 us
    all_gather x1, blocking collectives, local(): full = lax.all_gather(own_change, 'cent')  5.22 us
    pallas_call x2, Pallas kernels, scatter_call(): pl.pallas_call(functools.partial(scatter_kernel, targets, step), name='sc...  4.69 us
  transfers between devices with their start and end apart: 17, of which 8 were waited for; matrix products, arithmetic and copies ran while one was open for 4% of the time, Pallas kernels for 28%

profile of v5, /device:TPU:0, one launch (start us, length us, event | category | flops | bytes accessed | tf_op | source)
XLA Modules:
  0.0 97.7 jit_solution(5780377917498459550)
XLA Ops:
  2.7 3.1 %collective-permute-start.8 = (bf16[272,512]{1,0:T(8,128)(2,1)S(1)}, bf16[272,512]{1,0:T(8,128)(2,1)S(1)}, u32[]{:S(2)}, u32[]{:S(2)}) collective-permute-start(bf16[272,512]{1,0:T(8,128)(2,1)S(1)} %maximum_maximum_fusion.refs_0_), channel_id=1, source_target_pairs={{0,4},{4,0},{8,12},{12,8},{16,20},{20,16},{24,28},{28,24},{1,5},{5... | collective-permute-start | bytes 835592 | tf_op jit(solution)/shard_map/ppermute | solution.py:361
  5.7 1.6 %collective-permute-start.6 = (bf16[272,512]{1,0:T(8,128)(2,1)S(1)}, bf16[272,512]{1,0:T(8,128)(2,1)S(1)}, u32[]{:S(2)}, u32[]{:S(2)}) collective-permute-start(bf16[272,512]{1,0:T(8,128)(2,1)S(1)} %maximum_maximum_fusion.refs_0_), channel_id=1, source_target_pairs={{0,8},{4,12},{8,0},{12,4},{16,24},{20,28},{24,16},{28,20},{1,9},{5... | collective-permute-start | bytes 835592 | tf_op jit(solution)/shard_map/ppermute | solution.py:361
  7.3 2.6 %collective-permute-start.2 = (bf16[272,512]{1,0:T(8,128)(2,1)S(1)}, bf16[272,512]{1,0:T(8,128)(2,1)S(1)}, u32[]{:S(2)}, u32[]{:S(2)}) collective-permute-start(bf16[272,512]{1,0:T(8,128)(2,1)S(1)} %maximum_maximum_fusion.refs_0_), channel_id=1, source_target_pairs={{0,16},{4,20},{8,24},{12,28},{16,0},{20,4},{24,8},{28,12},{1,17},{... | collective-permute-start | bytes 835592 | tf_op jit(solution)/shard_map/ppermute | solution.py:361
  12.8 1.6 %collective-permute-start.1 = (bf16[2,32,128]{2,1,0:T(8,128)(2,1)S(1)}, bf16[2,32,128]{2,1,0:T(8,128)(2,1)S(1)}, u32[]{:S(2)}, u32[]{:S(2)}) collective-permute-start(bf16[2,32,128]{2,1,0:T(8,128)(2,1)S(1)} %add.66), channel_id=1, source_target_pairs={{0,2},{1,3},{2,0},{3,1},{4,6},{5,7},{6,4},{7,5},{8,10},{9,11},{10,... | collective-permute-start | bytes 49160 | tf_op jit(solution)/shard_map/ppermute | solution.py:361
  14.4 2.2 %collective-permute-done.1 = bf16[2,32,128]{2,1,0:T(8,128)(2,1)S(1)} collective-permute-done((bf16[2,32,128]{2,1,0:T(8,128)(2,1)S(1)}, bf16[2,32,128]{2,1,0:T(8,128)(2,1)S(1)}, u32[]{:S(2)}, u32[]{:S(2)}) %collective-permute-start.1) | collective-permute-done | bytes 16416 | tf_op jit(solution)/shard_map/ppermute | solution.py:361
  17.3 8.4 %compact.1 = (bf16[2,1808,512]{2,1,0:T(8,128)(2,1)S(1)}, f32[2,8,1536]{2,1,0:T(8,128)S(1)}, f32[2,16,1536]{2,1,0:T(8,128)S(1)}) custom-call(s32[2,17]{1,0:T(2,128)S(1)} %pad.8.off_ref, s32[2,32,128]{2,1,0:T(8,128)S(1)} %select_convert_fusion.dest_ref, bf16[4096,512]{1,0:T(8,128)(2,1)} %pool_hbm.1, f32[16,4096]{1,0:T(8,128)} %coef_ref.1), custom_call_target="tpu_custom_call" | custom-call | flops 4000000000 | bytes 8000000 | tf_op jit(solution)/shard_map/compact/pallas_call | solution.py:152
  26.8 1.6 %collective-permute-start.5 = (bf16[272,512]{1,0:T(8,128)(2,1)S(1)}, bf16[272,512]{1,0:T(8,128)(2,1)S(1)}, u32[]{:S(2)}, u32[]{:S(2)}) collective-permute-start(bf16[272,512]{1,0:T(8,128)(2,1)S(1)} %broadcast_add_fusion), channel_id=1, source_target_pairs={{0,4},{4,0},{8,12},{12,8},{16,20},{20,16},{24,28},{28,24},{1,5},{5... | collective-permute-start | bytes 835592 | tf_op jit(solution)/shard_map/ppermute | solution.py:361
  28.4 4.0 %kernel_block.5 = (bf16[8,256,3072]{2,1,0:T(8,128)(2,1)S(1)}, f32[24,1536]{1,0:T(8,128)S(1)}, f32[8,24,256]{2,1,0:T(8,128)S(1)}) custom-call(s32[2]{0:T(128)S(1)} %iota_xor_fusion.slot_ref, bf16[2,1808,512]{2,1,0:T(8,128)(2,1)S(1)} %get-tuple-element.25.chosen_ref, f32[2,8,1536]{2,1,0:T(8,128)S(1)} %get-tuple-element.26.norm_ref, ...), custom_call_target="tpu_custom_call" | custom-call | flops 1610612736 | bytes 3145728 | tf_op jit(solution)/shard_map/kernel_block/pallas_call | solution.py:229
  32.4 1.9 %collective-permute-done.3.refs_1_ = bf16[272,512]{1,0:T(8,128)(2,1)S(1)} collective-permute-done((bf16[272,512]{1,0:T(8,128)(2,1)S(1)}, bf16[272,512]{1,0:T(8,128)(2,1)S(1)}, u32[]{:S(2)}, u32[]{:S(2)}) %collective-permute-start.3) | collective-permute-done | bytes 278560 | tf_op jit(solution)/shard_map/ppermute | solution.py:361
  35.8 4.0 %kernel_block.6 = (bf16[8,256,3072]{2,1,0:T(8,128)(2,1)S(1)}, f32[24,1536]{1,0:T(8,128)S(1)}, f32[8,24,256]{2,1,0:T(8,128)S(1)}) custom-call(s32[2]{0:T(128)S(1)} %broadcast_xor_fusion.slot_ref, bf16[2,1808,512]{2,1,0:T(8,128)(2,1)S(1)} %get-tuple-element.25.chosen_ref, ...), custom_call_target="tpu_custom_call", output_to_operand_aliasing={{0}: (5, {}), {1}: (6, {}), {2}: (7, {})} | custom-call | flops 1610612736 | bytes 3145728 | tf_op jit(solution)/shard_map/kernel_block/pallas_call | solution.py:229
  39.8 4.0 %kernel_block.7 = (bf16[8,256,3072]{2,1,0:T(8,128)(2,1)S(1)}, f32[24,1536]{1,0:T(8,128)S(1)}, f32[8,24,256]{2,1,0:T(8,128)S(1)}) custom-call(s32[2]{0:T(128)S(1)} %broadcast_xor_fusion.1.slot_ref, bf16[2,1808,512]{2,1,0:T(8,128)(2,1)S(1)} %get-tuple-element.25.chosen_ref, ...), custom_call_target="tpu_custom_call", output_to_operand_aliasing={{0}: (5, {}), {1}: (6, {}), {2}: (7, {})} | custom-call | flops 1610612736 | bytes 3145728 | tf_op jit(solution)/shard_map/kernel_block/pallas_call | solution.py:229
  43.8 2.3 %kernel_block.8 = (bf16[8,256,3072]{2,1,0:T(8,128)(2,1)S(1)}, f32[24,1536]{1,0:T(8,128)S(1)}, f32[8,24,256]{2,1,0:T(8,128)S(1)}) custom-call(s32[1]{0:T(128)S(6)} %xor.23.slot_ref, bf16[2,1808,512]{2,1,0:T(8,128)(2,1)S(1)} %get-tuple-element.25.chosen_ref, ...), custom_call_target="tpu_custom_call", output_to_operand_aliasing={{0}: (4, {}), {1}: (5, {}), {2}: (6, {})} | custom-call | flops 805306368 | bytes 1572864 | tf_op jit(solution)/shard_map/kernel_block/pallas_call | solution.py:229
  46.1 2.1 %kernel_block.9 = (bf16[8,256,3072]{2,1,0:T(8,128)(2,1)S(1)}, f32[24,1536]{1,0:T(8,128)S(1)}, f32[8,24,256]{2,1,0:T(8,128)S(1)}) custom-call(s32[1]{0:T(128)S(6)} %xor.22.slot_ref, bf16[2,1808,512]{2,1,0:T(8,128)(2,1)S(1)} %get-tuple-element.25.chosen_ref, ...), custom_call_target="tpu_custom_call", output_to_operand_aliasing={{0}: (4, {}), {1}: (5, {}), {2}: (6, {})} | custom-call | flops 805306368 | bytes 1572864 | tf_op jit(solution)/shard_map/kernel_block/pallas_call | solution.py:229
  48.2 7.5 %all-gather = f32[96,1536]{1,0:T(8,128)S(1)} all-gather(f32[24,1536]{1,0:T(8,128)S(1)} %get-tuple-element.39), channel_id=2, replica_groups=mesh['rows'=8,'cent'=4] {'cent'}, dimensions={0}, use_global_device_ids=true | all-gather | bytes 737280 | tf_op jit(solution)/shard_map/all_gather | solution.py:444
  55.7 2.1 %change.2 = (f32[16,1536]{1,0:T(8,128)S(1)}, f32[8,16,256]{2,1,0:T(8,128)S(1)}, f32[8,16,256]{2,1,0:T(8,128)S(1)}) custom-call(s32[1]{0:T(128)} %bitcast.3.me_ref, f32[4,24,1536]{2,1,0:T(8,128)S(1)} %bitcast.46, f32[4,24,1536]{2,1,0:T(8,128)S(1)} %bitcast.47, f32[2,16,1536]{2,1,0:T(8,128)S(1)} %get-tuple-element.40.coef_ref, ...), custom_call_target="tpu_custom_call" | custom-call | flops 100663296 | bytes 6291456 | tf_op jit(solution)/shard_map/change/pallas_call | solution.py:286
  58.4 1.5 %collective-permute-start.11 = (bf16[8,16,256]{2,1,0:T(8,128)(2,1)S(1)}, bf16[8,16,256]{2,1,0:T(8,128)(2,1)S(1)}, u32[]{:S(2)}, u32[]{:S(2)}) collective-permute-start(bf16[8,16,256]{2,1,0:T(8,128)(2,1)S(1)} %convert_element_type.69), channel_id=1, source_target_pairs={{0,12},{4,8},{8,4},{12,0},{16,28},{20,24},{24,20},{28,16},{1,13},{... | collective-permute-start | bytes 196616 | tf_op jit(solution)/shard_map/ppermute | solution.py:361
  65.4 5.5 %collective-permute-done.12 = bf16[8,16,256]{2,1,0:T(8,128)(2,1)S(1)} collective-permute-done((bf16[8,16,256]{2,1,0:T(8,128)(2,1)S(1)}, bf16[8,16,256]{2,1,0:T(8,128)(2,1)S(1)}, u32[]{:S(2)}, u32[]{:S(2)}) %collective-permute-start.12) | collective-permute-done | bytes 65568 | tf_op jit(solution)/shard_map/ppermute | solution.py:361
  72.3 6.3 %all-gather.1 = f32[64,1536]{1,0:T(8,128)S(1)} all-gather(f32[16,1536]{1,0:T(8,128)S(1)} %gradient.1), channel_id=3, replica_groups=mesh['rows'=8,'cent'=4] {'cent'}, dimensions={0}, use_global_device_ids=true | all-gather | bytes 491520 | tf_op jit(solution)/shard_map/all_gather | solution.py:458
  78.5 2.1 %change.3 = (f32[16,1536]{1,0:T(8,128)S(1)}, f32[8,16,256]{2,1,0:T(8,128)S(1)}) custom-call(s32[1]{0:T(128)} %bitcast.3.me_ref, f32[4,16,1536]{2,1,0:T(8,128)S(1)} %bitcast.49, f32[4,24,1536]{2,1,0:T(8,128)S(1)} %bitcast.48, f32[2,16,1536]{2,1,0:T(8,128)S(1)} %get-tuple-element.40.coef_ref, bf16[8,256,3072]{2,1,0:T(8,128)(2,1)S(1)} %get-tuple-element.41.k_ref, ...), custom_call_target="tpu_custom_call" | custom-call | flops 100663296 | bytes 6291456 | tf_op jit(solution)/shard_map/change/pallas_call | solution.py:286
  80.7 1.6 %collective-permute-start.13 = (f32[2,16,256]{2,1,0:T(8,128)S(1)}, f32[2,16,256]{2,1,0:T(8,128)S(1)}, u32[]{:S(2)}, u32[]{:S(2)}) collective-permute-start(f32[2,16,256]{2,1,0:T(8,128)S(1)} %get-tuple-element.50), channel_id=1, source_target_pairs={{0,4},{4,0},{8,12},{12,8},{16,20},{20,16},{24,28},{28,24},{1,5},{5... | collective-permute-start | bytes 98312 | tf_op jit(solution)/shard_map/ppermute | solution.py:361
  82.3 2.0 %collective-permute-start.15 = (f32[2,16,256]{2,1,0:T(8,128)S(1)}, f32[2,16,256]{2,1,0:T(8,128)S(1)}, u32[]{:S(2)}, u32[]{:S(2)}) collective-permute-start(f32[2,16,256]{2,1,0:T(8,128)S(1)} %get-tuple-element.52), channel_id=1, source_target_pairs={{0,12},{4,8},{8,4},{12,0},{16,28},{20,24},{24,20},{28,16},{1,13},{... | collective-permute-start | bytes 98312 | tf_op jit(solution)/shard_map/ppermute | solution.py:361
  84.2 2.0 %scatter.2.coef_ref = f32[16,4096]{1,0:T(8,128)S(1)} custom-call(s32[2,17]{1,0:T(2,128)S(1)} %pad.8.off_ref, s32[2,32,128]{2,1,0:T(8,128)S(1)} %select_convert_fusion.dest_ref, f32[16,4096]{1,0:T(8,128)S(1)} %copy-done.1, f32[16,1536]{1,0:T(8,128)S(1)} %get-tuple-element.43.delta_ref), custom_call_target="tpu_custom_call" | custom-call | flops 1000000000 | bytes 1000000 | tf_op jit(solution)/shard_map/scatter/pallas_call | solution.py:347
  88.4 2.7 %scatter.3 = f32[16,4096]{1,0:T(8,128)} custom-call(s32[2,17]{1,0:T(2,128)S(1)} %pad.8.off_ref, s32[2,32,128]{2,1,0:T(8,128)S(1)} %select_convert_fusion.dest_ref, f32[16,4096]{1,0:T(8,128)S(1)} %scatter.2.coef_ref, f32[16,1536]{1,0:T(8,128)S(1)} %get-tuple-element.46.delta_ref), custom_call_target="tpu_custom_call" | custom-call | flops 1000000000 | bytes 1000000 | tf_op jit(solution)/shard_map/scatter/pallas_call | solution.py:347
  91.8 5.2 %all_gather.19 = f32[4,16,256]{2,1,0:T(8,128)S(1)} all-gather(f32[1,16,256]{2,1,0:T(8,128)S(1)} %fusion.14), channel_id=1, replica_groups=mesh['rows'=8,'cent'=4] {'cent'}, dimensions={0}, use_global_device_ids=true | all-gather | bytes 81920 | tf_op jit(solution)/shard_map/all_gather | solution.py:476
  (62 shorter events, 19.0 us)
Async XLA Ops:
  0.6 1.2 %copy-start = (bf16[1024,512]{1,0:T(8,128)(2,1)S(1)}, bf16[1024,512]{1,0:T(8,128)(2,1)}, u32[]{:S(2)}) copy-start(bf16[1024,512]{1,0:T(8,128)(2,1)} %param.12) | copy-start | bytes 3145732
  2.7 25.7 %collective-permute-start.8 = (bf16[272,512]{1,0:T(8,128)(2,1)S(1)}, bf16[272,512]{1,0:T(8,128)(2,1)S(1)}, u32[]{:S(2)}, u32[]{:S(2)}) collective-permute-start(bf16[272,512]{1,0:T(8,128)(2,1)S(1)} %maximum_maximum_fusion.refs_0_), channel_id=1, source_target_pairs={{0,4},{4,0},{8,12},{12,8},{16,20},{20,16},{24,28},{28,24},{1,5},{5... | collective-permute-start | bytes 835592 | tf_op jit(solution)/shard_map/ppermute | solution.py:361
  5.7 20.0 %collective-permute-start.6 = (bf16[272,512]{1,0:T(8,128)(2,1)S(1)}, bf16[272,512]{1,0:T(8,128)(2,1)S(1)}, u32[]{:S(2)}, u32[]{:S(2)}) collective-permute-start(bf16[272,512]{1,0:T(8,128)(2,1)S(1)} %maximum_maximum_fusion.refs_0_), channel_id=1, source_target_pairs={{0,8},{4,12},{8,0},{12,4},{16,24},{20,28},{24,16},{28,20},{1,9},{5... | collective-permute-start | bytes 835592 | tf_op jit(solution)/shard_map/ppermute | solution.py:361
  7.3 19.0 %collective-permute-start.2 = (bf16[272,512]{1,0:T(8,128)(2,1)S(1)}, bf16[272,512]{1,0:T(8,128)(2,1)S(1)}, u32[]{:S(2)}, u32[]{:S(2)}) collective-permute-start(bf16[272,512]{1,0:T(8,128)(2,1)S(1)} %maximum_maximum_fusion.refs_0_), channel_id=1, source_target_pairs={{0,16},{4,20},{8,24},{12,28},{16,0},{20,4},{24,8},{28,12},{1,17},{... | collective-permute-start | bytes 835592 | tf_op jit(solution)/shard_map/ppermute | solution.py:361
  11.4 1.4 %collective-permute-start = (bf16[2,32,128]{2,1,0:T(8,128)(2,1)S(1)}, bf16[2,32,128]{2,1,0:T(8,128)(2,1)S(1)}, u32[]{:S(2)}, u32[]{:S(2)}) collective-permute-start(bf16[2,32,128]{2,1,0:T(8,128)(2,1)S(1)} %fusion.2), channel_id=1, source_target_pairs={{0,1},{1,0},{2,3},{3,2},{4,5},{5,4},{6,7},{7,6},{8,9},{9,8},{10,11... | collective-permute-start | bytes 49160 | tf_op jit(solution)/shard_map/ppermute | solution.py:361
  12.8 3.8 %collective-permute-start.1 = (bf16[2,32,128]{2,1,0:T(8,128)(2,1)S(1)}, bf16[2,32,128]{2,1,0:T(8,128)(2,1)S(1)}, u32[]{:S(2)}, u32[]{:S(2)}) collective-permute-start(bf16[2,32,128]{2,1,0:T(8,128)(2,1)S(1)} %add.66), channel_id=1, source_target_pairs={{0,2},{1,3},{2,0},{3,1},{4,6},{5,7},{6,4},{7,5},{8,10},{9,11},{10,... | collective-permute-start | bytes 49160 | tf_op jit(solution)/shard_map/ppermute | solution.py:361
  25.8 10.0 %collective-permute-start.7 = (bf16[272,512]{1,0:T(8,128)(2,1)S(1)}, bf16[272,512]{1,0:T(8,128)(2,1)S(1)}, u32[]{:S(2)}, u32[]{:S(2)}) collective-permute-start(bf16[272,512]{1,0:T(8,128)(2,1)S(1)} %collective-permute-done.6.refs_0_), channel_id=1, source_target_pairs={{0,4},{4,0},{8,12},{12,8},{16,20},{20,16},{24,28},{28,24},{1,5},{5... | collective-permute-start | bytes 835592 | tf_op jit(solution)/shard_map/ppermute | solution.py:361
  26.3 7.9 %collective-permute-start.3 = (bf16[272,512]{1,0:T(8,128)(2,1)S(1)}, bf16[272,512]{1,0:T(8,128)(2,1)S(1)}, u32[]{:S(2)}, u32[]{:S(2)}) collective-permute-start(bf16[272,512]{1,0:T(8,128)(2,1)S(1)} %collective-permute-done.2.refs_0_), channel_id=1, source_target_pairs={{0,8},{4,12},{8,0},{12,4},{16,24},{20,28},{24,16},{28,20},{1,9},{5... | collective-permute-start | bytes 835592 | tf_op jit(solution)/shard_map/ppermute | solution.py:361
  26.8 16.9 %collective-permute-start.5 = (bf16[272,512]{1,0:T(8,128)(2,1)S(1)}, bf16[272,512]{1,0:T(8,128)(2,1)S(1)}, u32[]{:S(2)}, u32[]{:S(2)}) collective-permute-start(bf16[272,512]{1,0:T(8,128)(2,1)S(1)} %broadcast_add_fusion), channel_id=1, source_target_pairs={{0,4},{4,0},{8,12},{12,8},{16,20},{20,16},{24,28},{28,24},{1,5},{5... | collective-permute-start | bytes 835592 | tf_op jit(solution)/shard_map/ppermute | solution.py:361
  34.3 11.8 %collective-permute-start.4 = (bf16[272,512]{1,0:T(8,128)(2,1)S(1)}, bf16[272,512]{1,0:T(8,128)(2,1)S(1)}, u32[]{:S(2)}, u32[]{:S(2)}) collective-permute-start(bf16[272,512]{1,0:T(8,128)(2,1)S(1)} %collective-permute-done.3.refs_1_), channel_id=1, source_target_pairs={{0,4},{4,0},{8,12},{12,8},{16,20},{20,16},{24,28},{28,24},{1,5},{5... | collective-permute-start | bytes 835592 | tf_op jit(solution)/shard_map/ppermute | solution.py:361
  57.9 5.0 %collective-permute-start.10 = (bf16[8,16,256]{2,1,0:T(8,128)(2,1)S(1)}, bf16[8,16,256]{2,1,0:T(8,128)(2,1)S(1)}, u32[]{:S(2)}, u32[]{:S(2)}) collective-permute-start(bf16[8,16,256]{2,1,0:T(8,128)(2,1)S(1)} %convert_element_type.69), channel_id=1, source_target_pairs={{0,8},{4,12},{8,0},{12,4},{16,24},{20,28},{24,16},{28,20},{1,9},{5... | collective-permute-start | bytes 196616 | tf_op jit(solution)/shard_map/ppermute | solution.py:361
  58.4 5.3 %collective-permute-start.11 = (bf16[8,16,256]{2,1,0:T(8,128)(2,1)S(1)}, bf16[8,16,256]{2,1,0:T(8,128)(2,1)S(1)}, u32[]{:S(2)}, u32[]{:S(2)}) collective-permute-start(bf16[8,16,256]{2,1,0:T(8,128)(2,1)S(1)} %convert_element_type.69), channel_id=1, source_target_pairs={{0,12},{4,8},{8,4},{12,0},{16,28},{20,24},{24,20},{28,16},{1,13},{... | collective-permute-start | bytes 196616 | tf_op jit(solution)/shard_map/ppermute | solution.py:361
  59.9 5.0 %collective-permute-start.9 = (bf16[8,16,256]{2,1,0:T(8,128)(2,1)S(1)}, bf16[8,16,256]{2,1,0:T(8,128)(2,1)S(1)}, u32[]{:S(2)}, u32[]{:S(2)}) collective-permute-start(bf16[8,16,256]{2,1,0:T(8,128)(2,1)S(1)} %convert_element_type.69), channel_id=1, source_target_pairs={{0,4},{4,0},{8,12},{12,8},{16,20},{20,16},{24,28},{28,24},{1,5},{5... | collective-permute-start | bytes 196616 | tf_op jit(solution)/shard_map/ppermute | solution.py:361
  65.0 5.9 %collective-permute-start.12 = (bf16[8,16,256]{2,1,0:T(8,128)(2,1)S(1)}, bf16[8,16,256]{2,1,0:T(8,128)(2,1)S(1)}, u32[]{:S(2)}, u32[]{:S(2)}) collective-permute-start(bf16[8,16,256]{2,1,0:T(8,128)(2,1)S(1)} %fusion.19), channel_id=1, source_target_pairs={{0,16},{4,20},{8,24},{12,28},{16,0},{20,4},{24,8},{28,12},{1,17},{... | collective-permute-start | bytes 196616 | tf_op jit(solution)/shard_map/ppermute | solution.py:361
  71.0 13.3 %copy-start.1 = (f32[16,4096]{1,0:T(8,128)S(1)}, f32[16,4096]{1,0:T(8,128)}, u32[]{:S(2)}) copy-start(f32[16,4096]{1,0:T(8,128)} %coef_ref.1) | copy-start | bytes 786436
  72.2 24.8 %copy-start.2 = (f32[16,1024]{1,0:T(8,128)S(1)}, f32[16,1024]{1,0:T(8,128)}, u32[]{:S(2)}) copy-start(f32[16,1024]{1,0:T(8,128)} %param.15) | copy-start | bytes 196612
  80.7 5.6 %collective-permute-start.13 = (f32[2,16,256]{2,1,0:T(8,128)S(1)}, f32[2,16,256]{2,1,0:T(8,128)S(1)}, u32[]{:S(2)}, u32[]{:S(2)}) collective-permute-start(f32[2,16,256]{2,1,0:T(8,128)S(1)} %get-tuple-element.50), channel_id=1, source_target_pairs={{0,4},{4,0},{8,12},{12,8},{16,20},{20,16},{24,28},{28,24},{1,5},{5... | collective-permute-start | bytes 98312 | tf_op jit(solution)/shard_map/ppermute | solution.py:361
  82.3 4.0 %collective-permute-start.14 = (f32[2,16,256]{2,1,0:T(8,128)S(1)}, f32[2,16,256]{2,1,0:T(8,128)S(1)}, u32[]{:S(2)}, u32[]{:S(2)}) collective-permute-start(f32[2,16,256]{2,1,0:T(8,128)S(1)} %get-tuple-element.51), channel_id=1, source_target_pairs={{0,8},{4,12},{8,0},{12,4},{16,24},{20,28},{24,16},{28,20},{1,9},{5... | collective-permute-start | bytes 98312 | tf_op jit(solution)/shard_map/ppermute | solution.py:361
  82.3 4.8 %collective-permute-start.15 = (f32[2,16,256]{2,1,0:T(8,128)S(1)}, f32[2,16,256]{2,1,0:T(8,128)S(1)}, u32[]{:S(2)}, u32[]{:S(2)}) collective-permute-start(f32[2,16,256]{2,1,0:T(8,128)S(1)} %get-tuple-element.52), channel_id=1, source_target_pairs={{0,12},{4,8},{8,4},{12,0},{16,28},{20,24},{24,20},{28,16},{1,13},{... | collective-permute-start | bytes 98312 | tf_op jit(solution)/shard_map/ppermute | solution.py:361
  87.1 4.7 %collective-permute-start.16 = (f32[1,16,256]{2,1,0:T(8,128)S(1)}, f32[1,16,256]{2,1,0:T(8,128)S(1)}, u32[]{:S(2)}, u32[]{:S(2)}) collective-permute-start(f32[1,16,256]{2,1,0:T(8,128)S(1)} %slice_bitcast_fusion.4), channel_id=1, source_target_pairs={{0,16},{4,20},{8,24},{12,28},{16,0},{20,4},{24,8},{28,12},{1,17},{... | collective-permute-start | bytes 49160 | tf_op jit(solution)/shard_map/ppermute | solution.py:361

commit v6 on v5

v6 whole, which is shorter than its diff:
```python
import functools
import math

import jax
import jax.numpy as jnp
from jax import lax
from jax.experimental import pallas as pl
from jax.experimental.pallas import tpu as pltpu
from jax.sharding import PartitionSpec as P

RIDGE = 1.0
LANES = 128
POOL_BLOCK = 256
WINDOW = 144
TILE = 512
FIRST_GROUPS = [(0, 1), (2, 3), (4,), (6,), (5,), (7,)]
LATER_GROUPS = [(0, 1), (2, 3), (4, 6), (5, 7)]
KERNEL_VMEM = 16 * 2**20
LOG2E = math.log2(math.e)
NT = (((1,), (1,)), ((), ()))
F32 = jnp.float32
BF16 = jnp.bfloat16


def split3(x):
    first = x.astype(BF16)
    rest = x - first.astype(F32)
    second = rest.astype(BF16)
    third = (rest - second.astype(F32)).astype(BF16)
    return first, second, third


def split3_outside(x):
    first = lax.reduce_precision(x, 8, 7)
    rest = x - first
    second = lax.reduce_precision(rest, 8, 7)
    third = rest - second
    return first.astype(BF16), second.astype(BF16), third.astype(BF16)


def round_up(value, multiple):
    return -(-value // multiple) * multiple


def in_vmem(count):
    return [pl.BlockSpec(memory_space=pltpu.VMEM)] * count


def in_hbm(x):
    return pltpu.with_memory_space_constraint(x, pltpu.HBM)


def held(x):
    return pltpu.with_memory_space_constraint(x, pltpu.VMEM)


def params():
    return pltpu.CompilerParams(vmem_limit_bytes=KERNEL_VMEM)


def two_rows(ref, step, block):
    row = 2 * block
    return jnp.concatenate([ref[step, pl.ds(row, 1), :], ref[step, pl.ds(row + 1, 1), :]], axis=1)


def compact_kernel(step, per_step, targets, off_ref, dest_ref, pool_hbm, coefs_hbm, out_ref, norm_ref, coef_ref, side_out, pool_ref, coefs_ref, parts_ref, arrived, coefs_arrived):
    features = out_ref.shape[1]
    blocks = pool_ref.shape[0] // POOL_BLOCK
    tile = math.gcd(per_step, 512)

    def fetch(block):
        at = pl.ds(pl.multiple_of(block * POOL_BLOCK, POOL_BLOCK), POOL_BLOCK)
        return pltpu.make_async_copy(pool_hbm.at[at, :], pool_ref.at[at, :], arrived.at[block])

    coefs_copy = pltpu.make_async_copy(coefs_hbm, coefs_ref, coefs_arrived)
    coefs_copy.start()
    for block in range(blocks):
        fetch(block).start()
    widest = 0
    for block in range(blocks):
        widest = jnp.maximum(widest, off_ref[step, block + 1] - (off_ref[step, block] // 16) * 16)
    narrow = widest <= WINDOW
    out_ref[:16, :] = jnp.zeros((16, features), BF16)
    side_out[:16, :] = jnp.zeros((16, LANES), BF16)
    coefs_copy.wait()
    parts_ref[3 * targets :, :] = jnp.zeros((LANES - 3 * targets, parts_ref.shape[1]), BF16)
    for part, value in enumerate(split3(coefs_ref[...])):
        parts_ref[part * targets : (part + 1) * targets, :] = value

    def place(block, window):
        base = pl.multiple_of((off_ref[step, block] // 16) * 16, 16)
        dest = two_rows(dest_ref, step, block) - base
        slots = lax.broadcasted_iota(jnp.int32, (window, POOL_BLOCK), 0)
        pick = jnp.where(slots == dest, 1.0, 0.0).astype(BF16)
        at = pl.ds(pl.multiple_of(block * POOL_BLOCK, POOL_BLOCK), POOL_BLOCK)
        after = pl.ds(pl.multiple_of(base + 16, 16), window - 16)
        packed = jnp.dot(pick, pool_ref[at, :], preferred_element_type=F32).astype(BF16)
        side = lax.dot_general(pick, parts_ref[:, at], NT, preferred_element_type=F32).astype(BF16)
        for rows, target in ((packed, out_ref), (side, side_out)):
            target[pl.ds(base, 16), :] += rows[:16]
            target[after, :] = rows[16:]

    @pl.when(narrow)
    def _():
        @pl.loop(0, blocks // 4)
        def _(four):
            for i in range(4):
                fetch(4 * four + i).wait()
            for i in range(4):
                place(4 * four + i, WINDOW)

    @pl.when(jnp.logical_not(narrow))
    def _():
        @pl.loop(0, blocks)
        def _(block):
            fetch(block).wait()
            place(block, POOL_BLOCK + 16)

    ones = jnp.ones((8, features), BF16)
    eye = lax.broadcasted_iota(jnp.int32, (3 * targets, LANES), 0) == lax.broadcasted_iota(
        jnp.int32, (3 * targets, LANES), 1
    )
    eye = jnp.where(eye, 1.0, 0.0).astype(BF16)
    for first in range(0, per_step, tile):
        rows = out_ref[first : first + tile, :].astype(F32)
        square = rows * rows
        high = square.astype(BF16)
        low = (square - high.astype(F32)).astype(BF16)
        norm = lax.dot_general(ones, high, NT, preferred_element_type=F32)
        norm_ref[:, first : first + tile] = norm + lax.dot_general(ones, low, NT, preferred_element_type=F32)
        parts = lax.dot_general(eye, side_out[first : first + tile, :], NT, preferred_element_type=F32)
        coef_ref[:, first : first + tile] = (
            parts[:targets] + parts[targets : 2 * targets] + parts[2 * targets :]
        )


def compact(step, off, dest, pool, coefs, per_step, targets):
    features = pool.shape[1]
    length = round_up(per_step, 16) + POOL_BLOCK + 16
    return pl.pallas_call(
        functools.partial(compact_kernel, step, per_step, targets),
        name="compact",
        in_specs=[
            pl.BlockSpec(memory_space=pltpu.SMEM),
            *in_vmem(1),
            pl.BlockSpec(memory_space=pltpu.HBM),
            pl.BlockSpec(memory_space=pltpu.HBM),
        ],
        out_specs=in_vmem(3),
        out_shape=(
            pltpu.VMEM((length, features), BF16),
            pltpu.VMEM((8, per_step), F32),
            pltpu.VMEM((targets, per_step), F32),
        ),
        scratch_shapes=[
            pltpu.VMEM((length, LANES), BF16),
            pltpu.VMEM(pool.shape, BF16),
            pltpu.VMEM(coefs.shape, F32),
            pltpu.VMEM((LANES, pool.shape[0]), BF16),
            pltpu.SemaphoreType.DMA((pool.shape[0] // POOL_BLOCK,)),
            pltpu.SemaphoreType.DMA,
        ],
        compiler_params=params(),
        cost_estimate=pl.CostEstimate(flops=2 * 10**9, bytes_accessed=6 * 10**6, transcendentals=0),
    )(off, dest, in_hbm(pool), in_hbm(coefs))


def block_kernel(first_step, targets, quarter, count, scale, offset, slot_ref, chosen_ref, norm_ref, *refs):
    chunk_refs = refs[:count]
    outs = refs[count:]
    outs_count = 3 if first_step else 2
    sums_in = outs[1] if len(outs) > outs_count else None
    outs = outs[-outs_count:]
    k_ref, sums_ref = outs[:2]
    per_step = sums_ref.shape[1]
    square_row = targets if first_step else 0
    tile = math.gcd(per_step, TILE)

    rows = jnp.concatenate([ref[:quarter, :] for ref in chunk_refs], axis=0)
    wide_rows = rows.astype(F32)
    row_norm = jnp.sum(wide_rows * wide_rows, axis=1, keepdims=True) * (scale * LOG2E) - offset * LOG2E
    columns = []
    for i, ref in enumerate(chunk_refs):
        parts = ref[quarter : quarter + 3, quarter : 2 * quarter].astype(F32)
        weight = jnp.sum(parts, axis=0, keepdims=True)
        columns.append(jnp.transpose(jnp.broadcast_to(weight, (8, quarter)))[:, :1])
        if first_step:
            side_ref = outs[2]
            side_ref[slot_ref[i], :targets, :] = ref[quarter : quarter + targets, :quarter].astype(F32)
            side_ref[slot_ref[i], targets:, :] = jnp.broadcast_to(
                weight, (side_ref.shape[1] - targets, quarter)
            )
    weight_column = jnp.concatenate(columns, axis=0)
    weighted = jnp.concatenate([ref[quarter : quarter + targets, :quarter] for ref in chunk_refs], axis=1)

    for first in range(0, per_step, tile):
        dots = lax.dot_general(rows, chosen_ref[first : first + tile, :], NT, preferred_element_type=F32)
        centre = norm_ref[:1, first : first + tile] * (scale * LOG2E)
        k_low = jnp.exp2(dots * (2.0 * scale * LOG2E) - row_norm - centre).astype(BF16)
        for i in range(count):
            k_ref[slot_ref[i], :, first : first + tile] = k_low[i * quarter : (i + 1) * quarter]
        wide = k_low.astype(F32)
        updates = [(square_row, 1, jnp.sum(weight_column * (wide * wide), axis=0, keepdims=True))]
        if first_step:
            updates.append((0, targets, jnp.dot(weighted, k_low, preferred_element_type=F32)))
        for row, size, value in updates:
            if sums_in is not None:
                value = value + sums_in[row : row + size, first : first + tile]
            sums_ref[row : row + size, first : first + tile] = value


def block_call(first_step, slots, chunks, chosen, norm, state, targets, row_devices, scale, offset):
    features = chosen.shape[1]
    per_step = norm.shape[1]
    count = len(chunks)
    quarter = chunks[0].shape[0] - round_up(targets, 16)
    operands = [slots, held(chosen), held(norm), *chunks]
    outs = [
        pltpu.VMEM((row_devices, quarter, per_step), BF16),
        pltpu.VMEM((round_up(targets + 1, 8) if first_step else 8, per_step), F32),
    ]
    if first_step:
        outs.append(pltpu.VMEM((row_devices, round_up(targets + 1, 8), quarter), F32))
    aliases = {}
    if state is not None:
        aliases = {len(operands) + i: i for i in range(len(outs))}
        operands += [held(x) for x in state]
    entries = count * quarter * per_step
    return pl.pallas_call(
        functools.partial(block_kernel, first_step, targets, quarter, count, scale, offset),
        name="kernel_block",
        in_specs=[pl.BlockSpec(memory_space=pltpu.SMEM)] + in_vmem(len(operands) - 1),
        out_specs=in_vmem(len(outs)),
        out_shape=tuple(outs),
        input_output_aliases=aliases,
        compiler_params=params(),
        cost_estimate=pl.CostEstimate(
            flops=2 * entries * features, bytes_accessed=2 * entries, transcendentals=entries
        ),
    )(*operands)


def pass_cost(k_step, targets):
    entries = math.prod(k_step.shape)
    return pl.CostEstimate(flops=2 * targets * entries, bytes_accessed=2 * entries, transcendentals=0)


def change_kernel(targets, first, last, me_ref, sums_ref, coef_ref, k_ref, side_ref, *refs):
    before_ref = None if first else refs[0]
    outs = list(refs if first else refs[1:])
    delta_ref, change_ref = outs[:2]
    total = sums_ref[0]
    for i in range(1, sums_ref.shape[0]):
        total = total + sums_ref[i]
    delta = (total[:targets] - RIDGE * coef_ref[...]) / (total[targets : targets + 1] + RIDGE)
    delta_ref[...] = delta
    low = delta.astype(BF16)

    def body(i, _):
        change = lax.dot_general(low, k_ref[i], NT, preferred_element_type=F32)
        relative = i ^ me_ref[0]
        if not last:
            outs[2][i] = change * side_ref[i, targets : targets + 1, :]
        change_ref[relative] = change if first else change + before_ref[relative]
        return 0

    lax.fori_loop(0, k_ref.shape[0], body, 0, unroll=2)


def change_call(me, sums, coef, k_step, side, last, targets, before=None):
    row_devices, quarter, per_step = k_step.shape
    operands = [me, sums, coef, held(k_step), side]
    if before is not None:
        operands.append(before)
    change = jax.ShapeDtypeStruct((row_devices, targets, quarter), F32)
    outs = (jax.ShapeDtypeStruct((targets, per_step), F32), change) + (() if last else (change,))
    return pl.pallas_call(
        functools.partial(change_kernel, targets, before is None, last),
        name="change",
        in_specs=[pl.BlockSpec(memory_space=pltpu.SMEM)] + in_vmem(len(operands) - 1),
        out_specs=in_vmem(len(outs)),
        out_shape=outs,
        compiler_params=params(),
        cost_estimate=pass_cost(k_step, targets),
    )(*operands)


def gradient_kernel(targets, moved_ref, side_ref, k_ref, square_ref, out_ref):
    out_ref[:targets, :] = jnp.zeros((targets, out_ref.shape[1]), F32)
    out_ref[targets : targets + 1, :] = square_ref[:1, :]

    def body(i, _):
        weighted = (side_ref[i, :targets, :] - moved_ref[i]).astype(BF16)
        out_ref[:targets, :] += jnp.dot(weighted, k_ref[i], preferred_element_type=F32)
        return 0

    lax.fori_loop(0, k_ref.shape[0], body, 0, unroll=2)


def gradient_call(moved, side, k_step, squares, targets):
    return pl.pallas_call(
        functools.partial(gradient_kernel, targets),
        name="gradient",
        in_specs=in_vmem(4),
        out_specs=in_vmem(1)[0],
        out_shape=jax.ShapeDtypeStruct((round_up(targets + 1, 8), k_step.shape[2]), F32),
        compiler_params=params(),
        cost_estimate=pass_cost(k_step, targets),
    )(moved, side, held(k_step), squares)


def scatter_kernel(targets, step, off_ref, dest_ref, coef_ref, delta_ref, out_ref, parts_ref):
    per_step = delta_ref.shape[1]
    blocks = out_ref.shape[1] // POOL_BLOCK
    window = POOL_BLOCK + LANES
    for part, value in enumerate(split3(delta_ref[...])):
        parts_ref[part * targets : (part + 1) * targets, :per_step] = value
    parts_ref[:, per_step:] = jnp.zeros((3 * targets, parts_ref.shape[1] - per_step), BF16)

    @pl.loop(0, blocks // 4)
    def _(four):
        for i in range(4):
            block = 4 * four + i
            columns = pl.ds(pl.multiple_of(block * POOL_BLOCK, POOL_BLOCK), POOL_BLOCK)
            base = pl.multiple_of((off_ref[step, block] // LANES) * LANES, LANES)
            dest = two_rows(dest_ref, step, block) - base
            slots = lax.broadcasted_iota(jnp.int32, (window, POOL_BLOCK), 0)
            pick = jnp.where(slots == dest, 1.0, 0.0).astype(BF16)
            moved = jnp.dot(parts_ref[:, pl.ds(base, window)], pick, preferred_element_type=F32)
            moved = moved[:targets] + moved[targets : 2 * targets] + moved[2 * targets :]
            out_ref[:, columns] = coef_ref[:, columns] + moved


def scatter_call(off, dest, coefs, delta, step):
    targets, per_step = delta.shape
    length = round_up(per_step, LANES) + POOL_BLOCK + LANES
    return pl.pallas_call(
        functools.partial(scatter_kernel, targets, step),
        name="scatter",
        in_specs=[pl.BlockSpec(memory_space=pltpu.SMEM)] + in_vmem(3),
        out_specs=in_vmem(1)[0],
        out_shape=jax.ShapeDtypeStruct(coefs.shape, F32),
        scratch_shapes=[pltpu.VMEM((3 * targets, length), BF16)],
        compiler_params=params(),
        cost_estimate=pl.CostEstimate(flops=10**9, bytes_accessed=10**6, transcendentals=0),
    )(off, dest, coefs, delta)


def swap(value, axis, bit):
    count = lax.axis_size(axis)
    return lax.ppermute(value, axis, [(i, i ^ bit) for i in range(count)])


def bits_of(count):
    return [1 << k for k in range(count.bit_length() - 1)]


def groups_of(row_devices, step):
    if row_devices == 8:
        return FIRST_GROUPS if step == 0 else LATER_GROUPS
    return [(have,) for have in range(row_devices)]


def local(samples, weights, targets, predictions, centres, coefs, block_index):
    rows_dev, features = samples.shape
    pool_dev = centres.shape[0]
    steps, slice_len = block_index.shape
    target_count = targets.shape[0]
    row_devices, cent_devices = lax.axis_size("rows"), lax.axis_size("cent")
    my_row, my_cent = lax.axis_index("rows"), lax.axis_index("cent")
    quarter = rows_dev // cent_devices
    per_step = slice_len * cent_devices // row_devices
    sharpness = 1.3 / math.sqrt(8.0 * features)
    offset = 2.0 * features * sharpness - 1.5 - 0.5 * math.log(rows_dev * row_devices)

    at = my_cent * quarter
    own_rows = lax.dynamic_slice_in_dim(samples, at, quarter, 0)
    own_weight = lax.dynamic_slice_in_dim(weights, at, quarter, 0)[None, :]
    own_target = lax.dynamic_slice_in_dim(targets, at, quarter, 1)
    own_pred = lax.dynamic_slice_in_dim(predictions, at, quarter, 1)
    weighted = (own_weight * (own_target - own_pred)).astype(BF16)
    side_count = round_up(target_count, 16)
    weight_parts = jnp.concatenate(split3_outside(own_weight), axis=0)
    side_block = jnp.concatenate(
        [
            jnp.pad(weighted, ((0, side_count - target_count), (0, 0))),
            jnp.pad(weight_parts, ((0, side_count - 3), (0, features - 2 * quarter))),
        ],
        axis=1,
    )
    chunks = {0: jnp.concatenate([own_rows, side_block], axis=0)}

    high_count = pool_dev // LANES
    place = block_index - my_row * pool_dev
    inside = (place >= 0) & (place < pool_dev)
    high = jnp.where(inside, place // LANES, -1)
    low = jnp.where(inside, place % LANES, 0)
    high_hot = (high[:, None, :] == jnp.arange(high_count)[None, :, None]).astype(BF16)
    low_hot = (low[:, None, :] == jnp.arange(LANES)[None, :, None]).astype(BF16)
    member = jnp.einsum("shl,sgl->shg", high_hot, low_hot, preferred_element_type=F32).astype(BF16)
    for bit in bits_of(cent_devices):
        member = member + swap(member, "cent", bit)

    for bit in reversed(bits_of(row_devices)):
        for have in sorted(chunks):
            source = chunks[have]
            if bit == 1 and have == row_devices // 2:
                source = lax.optimization_barrier(source + lax.optimization_barrier(jnp.zeros((), BF16)))
            chunks[have | bit] = swap(source, "rows", bit)

    upper = (jnp.arange(LANES)[:, None] <= jnp.arange(LANES)[None, :]).astype(BF16)
    before = (jnp.arange(high_count)[:, None] > jnp.arange(high_count)[None, :]).astype(BF16)
    running = jnp.einsum("shg,gk->shk", member, upper, preferred_element_type=F32)
    row_count = running[:, :, -1:]
    row_start = jnp.einsum("hi,sik->shk", before, row_count.astype(BF16), preferred_element_type=F32)
    rank = row_start + running - 1.0
    dest = jnp.where(member > 0, rank, -65536.0).astype(jnp.int32)
    group_rows = POOL_BLOCK // LANES
    off = row_start[:, ::group_rows, 0].astype(jnp.int32)
    off = jnp.pad(off, ((0, 0), (0, 1)), constant_values=per_step)

    blocks = []
    own_coefs = []
    for step in range(steps):
        chosen, norm, own_coef = compact(step, off, dest, centres, coefs, per_step, target_count)
        own_coefs.append(own_coef)
        state = None
        for group in groups_of(row_devices, step):
            slots = my_row.astype(jnp.int32) ^ jnp.array(group, jnp.int32)
            state = block_call(
                step == 0, slots, [chunks[have] for have in group], chosen, norm, state,
                target_count, row_devices, sharpness, offset,
            )
        blocks.append(state)

    me = my_row.astype(jnp.int32)[None]
    info = blocks[0][2]
    sums = blocks[0][1]
    total_change = None
    deltas = []
    for step in range(steps):
        if step > 0:
            bits = bits_of(row_devices)
            for first in range(0, len(bits), 2):
                low = share.astype(BF16)
                pair = bits[first : first + 2]
                for bit in pair + ([sum(pair)] if len(pair) > 1 else []):
                    share = share + swap(low, "rows", bit).astype(F32)
            moved = share if step == 1 else moved + share
            sums = gradient_call(moved, info, blocks[step][0], blocks[step][1], target_count)
        delta, total_change, *more = change_call(
            me, lax.all_gather(sums, "cent"), own_coefs[step], blocks[step][0], info,
            step == steps - 1, target_count, total_change,
        )
        share = more[0] if more else None
        deltas.append(delta)
    coef_now = coefs
    for step in reversed(range(steps)):
        coef_now = scatter_call(off, dest, coef_now, deltas[step], step)

    pieces = total_change
    bits = bits_of(row_devices)
    for first in range(0, len(bits), 2):
        pair = bits[first : first + 2]
        count = 2 ** len(pair)
        pieces = pieces.reshape(pieces.shape[0] // count, count, target_count, quarter)
        kept = pieces[:, 0]
        for k in range(1, count):
            kept = kept + swap(pieces[:, k], "rows", k * pair[0])
        pieces = kept
    own_change = pieces[0]
    full = lax.all_gather(own_change, "cent")
    full = full.transpose(1, 0, 2).reshape(target_count, rows_dev)
    return (coef_now, predictions + full)


def solution(mesh):
    in_specs = (
        P("rows", None),
        P("rows"),
        P(None, "rows"),
        P(None, "rows"),
        P("rows", None),
        P(None, "rows"),
        P(None, "cent"),
    )
    out_specs = (P(None, "rows"), P(None, "rows"))
    return jax.shard_map(local, mesh=mesh, in_specs=in_specs, out_specs=out_specs, check_vma=False)
```

time: 98 us -> 101 us (1.031)
  Pallas kernels: 35 us -> 41.1 us
  waiting for transfers between devices: 14.7 us -> 12 us
  starting transfers between devices: 21.8 us -> 20 us
    pallas_call x9 -> x15, Pallas kernels: 30.3 us -> 36.4 us  [the longest x10 19.4 us: block_call(): pl.pallas_call(functools.partial(block_kernel, first_step, targets, quart...]
    ppermute x17, waiting for transfers between devices: 14.7 us -> 12 us  [swap(): return lax.ppermute(value, axis, [(i, i ^ bit) for i in range(count)])]
    ppermute x17, starting transfers between devices: 21.8 us -> 20 us  [swap(): return lax.ppermute(value, axis, [(i, i ^ bit) for i in range(count)])]
  transfers between devices with their start and end apart: 17 -> 17, of which waited for: 8 -> 9; matrix products, arithmetic and copies ran while one was open for 4% -> 4% of each run, Pallas kernels for 28% -> 34%
where the time goes in v6:
time: 101 us
  Pallas kernels  41.1 us (41%)
  starting transfers between devices  20 us (20%)
  blocking collectives  19.6 us (19%)
  waiting for transfers between devices  12 us (12%)
  other arithmetic  5.33 us (5%)
    ppermute x17, starting transfers between devices, swap(): return lax.ppermute(value, axis, [(i, i ^ bit) for i in range(count)])  20 us
    pallas_call x10, Pallas kernels, block_call(): pl.pallas_call(functools.partial(block_kernel, first_step, targets, quart...  19.4 us
    all_gather x2, blocking collectives, local(): lax.all_gather(sums, 'cent')  14.4 us
    ppermute x17, waiting for transfers between devices, swap(): return lax.ppermute(value, axis, [(i, i ^ bit) for i in range(count)])  12 us
    pallas_call x2, Pallas kernels, compact(): pl.pallas_call(functools.partial(compact_kernel, step, per_step, targets)...  11.6 us
    all_gather x1, blocking collectives, local(): full = lax.all_gather(own_change, 'cent')  5.22 us
    pallas_call x2, Pallas kernels, scatter_call(): pl.pallas_call(functools.partial(scatter_kernel, targets, step), name='sc...  4.69 us
    pallas_call x2, Pallas kernels, change_call(): pl.pallas_call(functools.partial(change_kernel, targets, before is None,...  4.21 us
  transfers between devices with their start and end apart: 17, of which 9 were waited for; matrix products, arithmetic and copies ran while one was open for 4% of the time, Pallas kernels for 34%

profile of v6, /device:TPU:0, one launch (start us, length us, event | category | flops | bytes accessed | tf_op | source)
XLA Modules:
  0.0 100.6 jit_solution(5284731901069114710)
XLA Ops:
  2.7 4.1 %collective-permute-start.2 = (bf16[272,512]{1,0:T(8,128)(2,1)S(1)}, bf16[272,512]{1,0:T(8,128)(2,1)S(1)}, u32[]{:S(2)}, u32[]{:S(2)}) collective-permute-start(bf16[272,512]{1,0:T(8,128)(2,1)S(1)} %maximum_maximum_fusion.refs_0_), channel_id=1, source_target_pairs={{0,16},{4,20},{8,24},{12,28},{16,0},{20,4},{24,8},{28,12},{1,17},{... | collective-permute-start | bytes 835592 | tf_op jit(solution)/shard_map/ppermute | solution.py:351
  6.8 1.6 %collective-permute-start.6 = (bf16[272,512]{1,0:T(8,128)(2,1)S(1)}, bf16[272,512]{1,0:T(8,128)(2,1)S(1)}, u32[]{:S(2)}, u32[]{:S(2)}) collective-permute-start(bf16[272,512]{1,0:T(8,128)(2,1)S(1)} %maximum_maximum_fusion.refs_0_), channel_id=1, source_target_pairs={{0,8},{4,12},{8,0},{12,4},{16,24},{20,28},{24,16},{28,20},{1,9},{5... | collective-permute-start | bytes 835592 | tf_op jit(solution)/shard_map/ppermute | solution.py:351
  13.5 1.6 %collective-permute-start.1 = (bf16[2,32,128]{2,1,0:T(8,128)(2,1)S(1)}, bf16[2,32,128]{2,1,0:T(8,128)(2,1)S(1)}, u32[]{:S(2)}, u32[]{:S(2)}) collective-permute-start(bf16[2,32,128]{2,1,0:T(8,128)(2,1)S(1)} %add.66), channel_id=1, source_target_pairs={{0,2},{1,3},{2,0},{3,1},{4,6},{5,7},{6,4},{7,5},{8,10},{9,11},{10,... | collective-permute-start | bytes 49160 | tf_op jit(solution)/shard_map/ppermute | solution.py:351
  15.1 2.2 %collective-permute-done.1 = bf16[2,32,128]{2,1,0:T(8,128)(2,1)S(1)} collective-permute-done((bf16[2,32,128]{2,1,0:T(8,128)(2,1)S(1)}, bf16[2,32,128]{2,1,0:T(8,128)(2,1)S(1)}, u32[]{:S(2)}, u32[]{:S(2)}) %collective-permute-start.1) | collective-permute-done | bytes 16416 | tf_op jit(solution)/shard_map/ppermute | solution.py:351
  18.0 5.7 %compact.2 = (bf16[1808,512]{1,0:T(8,128)(2,1)S(1)}, f32[8,1536]{1,0:T(8,128)S(1)}, f32[16,1536]{1,0:T(8,128)S(1)}) custom-call(s32[2,17]{1,0:T(2,128)S(1)} %pad.8.off_ref, s32[2,32,128]{2,1,0:T(8,128)S(1)} %select_convert_fusion.dest_ref, bf16[4096,512]{1,0:T(8,128)(2,1)} %pool_hbm.3, f32[16,4096]{1,0:T(8,128)} %coef_ref.1), custom_call_target="tpu_custom_call" | custom-call | flops 2000000000 | bytes 6000000 | tf_op jit(solution)/shard_map/compact/pallas_call | solution.py:140
  23.7 5.9 %compact.3 = (bf16[1808,512]{1,0:T(8,128)(2,1)S(1)}, f32[8,1536]{1,0:T(8,128)S(1)}, f32[16,1536]{1,0:T(8,128)S(1)}) custom-call(s32[2,17]{1,0:T(2,128)S(1)} %pad.8.off_ref, s32[2,32,128]{2,1,0:T(8,128)S(1)} %select_convert_fusion.dest_ref, bf16[4096,512]{1,0:T(8,128)(2,1)} %pool_hbm.3, f32[16,4096]{1,0:T(8,128)} %coef_ref.1), custom_call_target="tpu_custom_call" | custom-call | flops 2000000000 | bytes 6000000 | tf_op jit(solution)/shard_map/compact/pallas_call | solution.py:140
  30.6 1.6 %collective-permute-start.5 = (bf16[272,512]{1,0:T(8,128)(2,1)S(1)}, bf16[272,512]{1,0:T(8,128)(2,1)S(1)}, u32[]{:S(2)}, u32[]{:S(2)}) collective-permute-start(bf16[272,512]{1,0:T(8,128)(2,1)S(1)} %broadcast_add_fusion), channel_id=1, source_target_pairs={{0,4},{4,0},{8,12},{12,8},{16,20},{20,16},{24,28},{28,24},{1,5},{5... | collective-permute-start | bytes 835592 | tf_op jit(solution)/shard_map/ppermute | solution.py:351
  32.2 2.7 %kernel_block.10 = (bf16[8,256,1536]{2,1,0:T(8,128)(2,1)S(1)}, f32[24,1536]{1,0:T(8,128)S(1)}, f32[8,24,256]{2,1,0:T(8,128)S(1)}) custom-call(s32[2]{0:T(128)S(1)} %iota_xor_fusion.slot_ref, bf16[1808,512]{1,0:T(8,128)(2,1)S(1)} %get-tuple-element.39.chosen_ref, f32[8,1536]{1,0:T(8,128)S(1)} %get-tuple-element.40.norm_ref, ...), custom_call_target="tpu_custom_call" | custom-call | flops 805306368 | bytes 1572864 | tf_op jit(solution)/shard_map/kernel_block/pallas_call | solution.py:229
  34.8 3.0 %collective-permute-done.3.refs_0_.refs_1_ = bf16[272,512]{1,0:T(8,128)(2,1)S(1)} collective-permute-done((bf16[272,512]{1,0:T(8,128)(2,1)S(1)}, bf16[272,512]{1,0:T(8,128)(2,1)S(1)}, u32[]{:S(2)}, u32[]{:S(2)}) %collective-permute-start.3) | collective-permute-done | bytes 278560 | tf_op jit(solution)/shard_map/ppermute | solution.py:351
  38.3 2.1 %kernel_block.16 = (bf16[8,256,1536]{2,1,0:T(8,128)(2,1)S(1)}, f32[8,1536]{1,0:T(8,128)S(1)}) custom-call(s32[2]{0:T(128)S(1)} %iota_xor_fusion.slot_ref, bf16[1808,512]{1,0:T(8,128)(2,1)S(1)} %get-tuple-element.61.chosen_ref, f32[8,1536]{1,0:T(8,128)S(1)} %get-tuple-element.62.norm_ref, bf16[272,512]{1,0:T(8,128)(2,1)S(1)} %maximum_maximum_fusion.refs_0_, ...), custom_call_target="tpu_custom_call" | custom-call | flops 805306368 | bytes 1572864 | tf_op jit(solution)/shard_map/kernel_block/pallas_call | solution.py:229
  40.4 2.7 %kernel_block.11 = (bf16[8,256,1536]{2,1,0:T(8,128)(2,1)S(1)}, f32[24,1536]{1,0:T(8,128)S(1)}, f32[8,24,256]{2,1,0:T(8,128)S(1)}) custom-call(s32[2]{0:T(128)S(1)} %broadcast_xor_fusion.2.slot_ref, bf16[1808,512]{1,0:T(8,128)(2,1)S(1)} %get-tuple-element.39.chosen_ref, ...), custom_call_target="tpu_custom_call", output_to_operand_aliasing={{0}: (5, {}), {1}: (6, {}), {2}: (7, {})} | custom-call | flops 805306368 | bytes 1572864 | tf_op jit(solution)/shard_map/kernel_block/pallas_call | solution.py:229
  47.4 2.1 %kernel_block.17 = (bf16[8,256,1536]{2,1,0:T(8,128)(2,1)S(1)}, f32[8,1536]{1,0:T(8,128)S(1)}) custom-call(s32[2]{0:T(128)S(1)} %broadcast_xor_fusion.2.slot_ref, bf16[1808,512]{1,0:T(8,128)(2,1)S(1)} %get-tuple-element.61.chosen_ref, f32[8,1536]{1,0:T(8,128)S(1)} %get-tuple-element.62.norm_ref, ...), custom_call_target="tpu_custom_call", output_to_operand_aliasing={{0}: (5, {}), {1}: (6, {})} | custom-call | flops 805306368 | bytes 1572864 | tf_op jit(solution)/shard_map/kernel_block/pallas_call | solution.py:229
  51.4 7.7 %all-gather = f32[96,1536]{1,0:T(8,128)S(1)} all-gather(f32[24,1536]{1,0:T(8,128)S(1)} %get-tuple-element.56), channel_id=2, replica_groups=mesh['rows'=8,'cent'=4] {'cent'}, dimensions={0}, use_global_device_ids=true | all-gather | bytes 737280 | tf_op jit(solution)/shard_map/all_gather | solution.py:452
  59.1 2.1 %change.2 = (f32[16,1536]{1,0:T(8,128)S(1)}, f32[8,16,256]{2,1,0:T(8,128)S(1)}, f32[8,16,256]{2,1,0:T(8,128)S(1)}) custom-call(s32[1]{0:T(128)} %bitcast.3.me_ref, f32[4,24,1536]{2,1,0:T(8,128)S(1)} %bitcast.46, f32[16,1536]{1,0:T(8,128)S(1)} %get-tuple-element.57.coef_ref, bf16[8,256,1536]{2,1,0:T(8,128)(2,1)S(1)} %get-tuple-element.58.k_ref, ...), custom_call_target="tpu_custom_call" | custom-call | flops 100663296 | bytes 6291456 | tf_op jit(solution)/shard_map/change/pallas_call | solution.py:277
  61.2 1.6 %collective-permute-start.11 = (bf16[8,16,256]{2,1,0:T(8,128)(2,1)S(1)}, bf16[8,16,256]{2,1,0:T(8,128)(2,1)S(1)}, u32[]{:S(2)}, u32[]{:S(2)}) collective-permute-start(bf16[8,16,256]{2,1,0:T(8,128)(2,1)S(1)} %convert_element_type.69), channel_id=1, source_target_pairs={{0,12},{4,8},{8,4},{12,0},{16,28},{20,24},{24,20},{28,16},{1,13},{... | collective-permute-start | bytes 196616 | tf_op jit(solution)/shard_map/ppermute | solution.py:351
  64.8 2.1 %kernel_block.18 = (bf16[8,256,1536]{2,1,0:T(8,128)(2,1)S(1)}, f32[8,1536]{1,0:T(8,128)S(1)}) custom-call(s32[2]{0:T(128)S(1)} %broadcast_xor_fusion.slot_ref, bf16[1808,512]{1,0:T(8,128)(2,1)S(1)} %get-tuple-element.61.chosen_ref, f32[8,1536]{1,0:T(8,128)S(1)} %get-tuple-element.62.norm_ref, ...), custom_call_target="tpu_custom_call", output_to_operand_aliasing={{0}: (5, {}), {1}: (6, {})} | custom-call | flops 805306368 | bytes 1572864 | tf_op jit(solution)/shard_map/kernel_block/pallas_call | solution.py:229
  68.6 2.1 %kernel_block.19 = (bf16[8,256,1536]{2,1,0:T(8,128)(2,1)S(1)}, f32[8,1536]{1,0:T(8,128)S(1)}) custom-call(s32[2]{0:T(128)S(1)} %broadcast_xor_fusion.1.slot_ref, bf16[1808,512]{1,0:T(8,128)(2,1)S(1)} %get-tuple-element.61.chosen_ref, f32[8,1536]{1,0:T(8,128)S(1)} %get-tuple-element.62.norm_ref, ...), custom_call_target="tpu_custom_call", output_to_operand_aliasing={{0}: (5, {}), {1}: (6, {})} | custom-call | flops 805306368 | bytes 1572864 | tf_op jit(solution)/shard_map/kernel_block/pallas_call | solution.py:229
  70.7 3.0 %collective-permute-done.12 = bf16[8,16,256]{2,1,0:T(8,128)(2,1)S(1)} collective-permute-done((bf16[8,16,256]{2,1,0:T(8,128)(2,1)S(1)}, bf16[8,16,256]{2,1,0:T(8,128)(2,1)S(1)}, u32[]{:S(2)}, u32[]{:S(2)}) %collective-permute-start.12) | collective-permute-done | bytes 65568 | tf_op jit(solution)/shard_map/ppermute | solution.py:351
  75.0 6.7 %all-gather.1 = f32[96,1536]{1,0:T(8,128)S(1)} all-gather(f32[24,1536]{1,0:T(8,128)S(1)} %gradient.1), channel_id=3, replica_groups=mesh['rows'=8,'cent'=4] {'cent'}, dimensions={0}, use_global_device_ids=true | all-gather | bytes 737280 | tf_op jit(solution)/shard_map/all_gather | solution.py:452
  81.7 2.1 %change.3 = (f32[16,1536]{1,0:T(8,128)S(1)}, f32[8,16,256]{2,1,0:T(8,128)S(1)}) custom-call(s32[1]{0:T(128)} %bitcast.3.me_ref, f32[4,24,1536]{2,1,0:T(8,128)S(1)} %bitcast.47, f32[16,1536]{1,0:T(8,128)S(1)} %get-tuple-element.71.coef_ref, bf16[8,256,1536]{2,1,0:T(8,128)(2,1)S(1)} %get-tuple-element.69.k_ref, f32[8,24,256]{2,1,0:T(8,128)S(1)} %get-tuple-element.59.side_ref, ...), custom_call_target="tpu_custom_call" | custom-call | flops 100663296 | bytes 6291456 | tf_op jit(solution)/shard_map/change/pallas_call | solution.py:277
  83.8 1.8 %collective-permute-start.15 = (f32[2,16,256]{2,1,0:T(8,128)S(1)}, f32[2,16,256]{2,1,0:T(8,128)S(1)}, u32[]{:S(2)}, u32[]{:S(2)}) collective-permute-start(f32[2,16,256]{2,1,0:T(8,128)S(1)} %get-tuple-element.80), channel_id=1, source_target_pairs={{0,12},{4,8},{8,4},{12,0},{16,28},{20,24},{24,20},{28,16},{1,13},{... | collective-permute-start | bytes 98312 | tf_op jit(solution)/shard_map/ppermute | solution.py:351
  87.4 2.0 %scatter.2.coef_ref = f32[16,4096]{1,0:T(8,128)S(1)} custom-call(s32[2,17]{1,0:T(2,128)S(1)} %pad.8.off_ref, s32[2,32,128]{2,1,0:T(8,128)S(1)} %select_convert_fusion.dest_ref, f32[16,4096]{1,0:T(8,128)S(1)} %copy-done.1, f32[16,1536]{1,0:T(8,128)S(1)} %get-tuple-element.73.delta_ref), custom_call_target="tpu_custom_call" | custom-call | flops 1000000000 | bytes 1000000 | tf_op jit(solution)/shard_map/scatter/pallas_call | solution.py:337
  90.6 2.7 %scatter.3 = f32[16,4096]{1,0:T(8,128)} custom-call(s32[2,17]{1,0:T(2,128)S(1)} %pad.8.off_ref, s32[2,32,128]{2,1,0:T(8,128)S(1)} %select_convert_fusion.dest_ref, f32[16,4096]{1,0:T(8,128)S(1)} %scatter.2.coef_ref, f32[16,1536]{1,0:T(8,128)S(1)} %get-tuple-element.74.delta_ref), custom_call_target="tpu_custom_call" | custom-call | flops 1000000000 | bytes 1000000 | tf_op jit(solution)/shard_map/scatter/pallas_call | solution.py:337
  94.7 5.2 %all_gather.19 = f32[4,16,256]{2,1,0:T(8,128)S(1)} all-gather(f32[1,16,256]{2,1,0:T(8,128)S(1)} %fusion.14), channel_id=1, replica_groups=mesh['rows'=8,'cent'=4] {'cent'}, dimensions={0}, use_global_device_ids=true | all-gather | bytes 81920 | tf_op jit(solution)/shard_map/all_gather | solution.py:472
  (69 shorter events, 25.7 us)
Async XLA Ops:
  0.6 1.2 %copy-start = (bf16[1024,512]{1,0:T(8,128)(2,1)S(1)}, bf16[1024,512]{1,0:T(8,128)(2,1)}, u32[]{:S(2)}) copy-start(bf16[1024,512]{1,0:T(8,128)(2,1)} %param.17) | copy-start | bytes 3145732
  2.7 26.8 %collective-permute-start.2 = (bf16[272,512]{1,0:T(8,128)(2,1)S(1)}, bf16[272,512]{1,0:T(8,128)(2,1)S(1)}, u32[]{:S(2)}, u32[]{:S(2)}) collective-permute-start(bf16[272,512]{1,0:T(8,128)(2,1)S(1)} %maximum_maximum_fusion.refs_0_), channel_id=1, source_target_pairs={{0,16},{4,20},{8,24},{12,28},{16,0},{20,4},{24,8},{28,12},{1,17},{... | collective-permute-start | bytes 835592 | tf_op jit(solution)/shard_map/ppermute | solution.py:351
  6.8 23.2 %collective-permute-start.6 = (bf16[272,512]{1,0:T(8,128)(2,1)S(1)}, bf16[272,512]{1,0:T(8,128)(2,1)S(1)}, u32[]{:S(2)}, u32[]{:S(2)}) collective-permute-start(bf16[272,512]{1,0:T(8,128)(2,1)S(1)} %maximum_maximum_fusion.refs_0_), channel_id=1, source_target_pairs={{0,8},{4,12},{8,0},{12,4},{16,24},{20,28},{24,16},{28,20},{1,9},{5... | collective-permute-start | bytes 835592 | tf_op jit(solution)/shard_map/ppermute | solution.py:351
  8.4 23.8 %collective-permute-start.8 = (bf16[272,512]{1,0:T(8,128)(2,1)S(1)}, bf16[272,512]{1,0:T(8,128)(2,1)S(1)}, u32[]{:S(2)}, u32[]{:S(2)}) collective-permute-start(bf16[272,512]{1,0:T(8,128)(2,1)S(1)} %maximum_maximum_fusion.refs_0_), channel_id=1, source_target_pairs={{0,4},{4,0},{8,12},{12,8},{16,20},{20,16},{24,28},{28,24},{1,5},{5... | collective-permute-start | bytes 835592 | tf_op jit(solution)/shard_map/ppermute | solution.py:351
  11.4 2.0 %collective-permute-start = (bf16[2,32,128]{2,1,0:T(8,128)(2,1)S(1)}, bf16[2,32,128]{2,1,0:T(8,128)(2,1)S(1)}, u32[]{:S(2)}, u32[]{:S(2)}) collective-permute-start(bf16[2,32,128]{2,1,0:T(8,128)(2,1)S(1)} %fusion.2), channel_id=1, source_target_pairs={{0,1},{1,0},{2,3},{3,2},{4,5},{5,4},{6,7},{7,6},{8,9},{9,8},{10,11... | collective-permute-start | bytes 49160 | tf_op jit(solution)/shard_map/ppermute | solution.py:351
  13.5 3.8 %collective-permute-start.1 = (bf16[2,32,128]{2,1,0:T(8,128)(2,1)S(1)}, bf16[2,32,128]{2,1,0:T(8,128)(2,1)S(1)}, u32[]{:S(2)}, u32[]{:S(2)}) collective-permute-start(bf16[2,32,128]{2,1,0:T(8,128)(2,1)S(1)} %add.66), channel_id=1, source_target_pairs={{0,2},{1,3},{2,0},{3,1},{4,6},{5,7},{6,4},{7,5},{8,10},{9,11},{10,... | collective-permute-start | bytes 49160 | tf_op jit(solution)/shard_map/ppermute | solution.py:351
  29.5 8.3 %collective-permute-start.3 = (bf16[272,512]{1,0:T(8,128)(2,1)S(1)}, bf16[272,512]{1,0:T(8,128)(2,1)S(1)}, u32[]{:S(2)}, u32[]{:S(2)}) collective-permute-start(bf16[272,512]{1,0:T(8,128)(2,1)S(1)} %collective-permute-done.2.refs_0_), channel_id=1, source_target_pairs={{0,8},{4,12},{8,0},{12,4},{16,24},{20,28},{24,16},{28,20},{1,9},{5... | collective-permute-start | bytes 835592 | tf_op jit(solution)/shard_map/ppermute | solution.py:351
  30.1 10.4 %collective-permute-start.7 = (bf16[272,512]{1,0:T(8,128)(2,1)S(1)}, bf16[272,512]{1,0:T(8,128)(2,1)S(1)}, u32[]{:S(2)}, u32[]{:S(2)}) collective-permute-start(bf16[272,512]{1,0:T(8,128)(2,1)S(1)} %collective-permute-done.6.refs_0_), channel_id=1, source_target_pairs={{0,4},{4,0},{8,12},{12,8},{16,20},{20,16},{24,28},{28,24},{1,5},{5... | collective-permute-start | bytes 835592 | tf_op jit(solution)/shard_map/ppermute | solution.py:351
  30.6 15.4 %collective-permute-start.5 = (bf16[272,512]{1,0:T(8,128)(2,1)S(1)}, bf16[272,512]{1,0:T(8,128)(2,1)S(1)}, u32[]{:S(2)}, u32[]{:S(2)}) collective-permute-start(bf16[272,512]{1,0:T(8,128)(2,1)S(1)} %broadcast_add_fusion), channel_id=1, source_target_pairs={{0,4},{4,0},{8,12},{12,8},{16,20},{20,16},{24,28},{28,24},{1,5},{5... | collective-permute-start | bytes 835592 | tf_op jit(solution)/shard_map/ppermute | solution.py:351
  37.8 12.1 %collective-permute-start.4 = (bf16[272,512]{1,0:T(8,128)(2,1)S(1)}, bf16[272,512]{1,0:T(8,128)(2,1)S(1)}, u32[]{:S(2)}, u32[]{:S(2)}) collective-permute-start(bf16[272,512]{1,0:T(8,128)(2,1)S(1)} %collective-permute-done.3.refs_0_.refs_1_), channel_id=1, source_target_pairs={{0,4},{4,0},{8,12},{12,8},{16,20},{20,16},{24,28},{28,24},{1,5},{5... | collective-permute-start | bytes 835592 | tf_op jit(solution)/shard_map/ppermute | solution.py:351
  61.2 5.6 %collective-permute-start.11 = (bf16[8,16,256]{2,1,0:T(8,128)(2,1)S(1)}, bf16[8,16,256]{2,1,0:T(8,128)(2,1)S(1)}, u32[]{:S(2)}, u32[]{:S(2)}) collective-permute-start(bf16[8,16,256]{2,1,0:T(8,128)(2,1)S(1)} %convert_element_type.69), channel_id=1, source_target_pairs={{0,12},{4,8},{8,4},{12,0},{16,28},{20,24},{24,20},{28,16},{1,13},{... | collective-permute-start | bytes 196616 | tf_op jit(solution)/shard_map/ppermute | solution.py:351
  62.8 4.8 %collective-permute-start.10 = (bf16[8,16,256]{2,1,0:T(8,128)(2,1)S(1)}, bf16[8,16,256]{2,1,0:T(8,128)(2,1)S(1)}, u32[]{:S(2)}, u32[]{:S(2)}) collective-permute-start(bf16[8,16,256]{2,1,0:T(8,128)(2,1)S(1)} %convert_element_type.69), channel_id=1, source_target_pairs={{0,8},{4,12},{8,0},{12,4},{16,24},{20,28},{24,16},{28,20},{1,9},{5... | collective-permute-start | bytes 196616 | tf_op jit(solution)/shard_map/ppermute | solution.py:351
  63.9 4.3 %collective-permute-start.9 = (bf16[8,16,256]{2,1,0:T(8,128)(2,1)S(1)}, bf16[8,16,256]{2,1,0:T(8,128)(2,1)S(1)}, u32[]{:S(2)}, u32[]{:S(2)}) collective-permute-start(bf16[8,16,256]{2,1,0:T(8,128)(2,1)S(1)} %convert_element_type.69), channel_id=1, source_target_pairs={{0,4},{4,0},{8,12},{12,8},{16,20},{20,16},{24,28},{28,24},{1,5},{5... | collective-permute-start | bytes 196616 | tf_op jit(solution)/shard_map/ppermute | solution.py:351
  68.2 5.5 %collective-permute-start.12 = (bf16[8,16,256]{2,1,0:T(8,128)(2,1)S(1)}, bf16[8,16,256]{2,1,0:T(8,128)(2,1)S(1)}, u32[]{:S(2)}, u32[]{:S(2)}) collective-permute-start(bf16[8,16,256]{2,1,0:T(8,128)(2,1)S(1)} %fusion.19), channel_id=1, source_target_pairs={{0,16},{4,20},{8,24},{12,28},{16,0},{20,4},{24,8},{28,12},{1,17},{... | collective-permute-start | bytes 196616 | tf_op jit(solution)/shard_map/ppermute | solution.py:351
  73.7 13.7 %copy-start.1 = (f32[16,4096]{1,0:T(8,128)S(1)}, f32[16,4096]{1,0:T(8,128)}, u32[]{:S(2)}) copy-start(f32[16,4096]{1,0:T(8,128)} %coef_ref.1) | copy-start | bytes 786436
  81.7 18.3 %copy-start.2 = (f32[16,1024]{1,0:T(8,128)S(1)}, f32[16,1024]{1,0:T(8,128)}, u32[]{:S(2)}) copy-start(f32[16,1024]{1,0:T(8,128)} %param.20) | copy-start | bytes 196612
  83.8 5.6 %collective-permute-start.15 = (f32[2,16,256]{2,1,0:T(8,128)S(1)}, f32[2,16,256]{2,1,0:T(8,128)S(1)}, u32[]{:S(2)}, u32[]{:S(2)}) collective-permute-start(f32[2,16,256]{2,1,0:T(8,128)S(1)} %get-tuple-element.80), channel_id=1, source_target_pairs={{0,12},{4,8},{8,4},{12,0},{16,28},{20,24},{24,20},{28,16},{1,13},{... | collective-permute-start | bytes 98312 | tf_op jit(solution)/shard_map/ppermute | solution.py:351
  85.6 3.9 %collective-permute-start.14 = (f32[2,16,256]{2,1,0:T(8,128)S(1)}, f32[2,16,256]{2,1,0:T(8,128)S(1)}, u32[]{:S(2)}, u32[]{:S(2)}) collective-permute-start(f32[2,16,256]{2,1,0:T(8,128)S(1)} %get-tuple-element.79), channel_id=1, source_target_pairs={{0,8},{4,12},{8,0},{12,4},{16,24},{20,28},{24,16},{28,20},{1,9},{5... | collective-permute-start | bytes 98312 | tf_op jit(solution)/shard_map/ppermute | solution.py:351
  86.1 3.9 %collective-permute-start.13 = (f32[2,16,256]{2,1,0:T(8,128)S(1)}, f32[2,16,256]{2,1,0:T(8,128)S(1)}, u32[]{:S(2)}, u32[]{:S(2)}) collective-permute-start(f32[2,16,256]{2,1,0:T(8,128)S(1)} %get-tuple-element.78), channel_id=1, source_target_pairs={{0,4},{4,0},{8,12},{12,8},{16,20},{20,16},{24,28},{28,24},{1,5},{5... | collective-permute-start | bytes 98312 | tf_op jit(solution)/shard_map/ppermute | solution.py:351
  90.0 4.7 %collective-permute-start.16 = (f32[1,16,256]{2,1,0:T(8,128)S(1)}, f32[1,16,256]{2,1,0:T(8,128)S(1)}, u32[]{:S(2)}, u32[]{:S(2)}) collective-permute-start(f32[1,16,256]{2,1,0:T(8,128)S(1)} %slice_bitcast_fusion.4), channel_id=1, source_target_pairs={{0,16},{4,20},{8,24},{12,28},{16,0},{20,4},{24,8},{28,12},{1,17},{... | collective-permute-start | bytes 49160 | tf_op jit(solution)/shard_map/ppermute | solution.py:351

commit v7 on v6

--- a/solution.py
+++ b/solution.py
@@ -165,9 +165,11 @@
     )(off, dest, in_hbm(pool), in_hbm(coefs))
 
 
-def block_kernel(first_step, targets, quarter, count, scale, offset, slot_ref, chosen_ref, norm_ref, *refs):
+def block_kernel(first_step, targets, quarter, group, scale, offset, me_ref, chosen_ref, norm_ref, *refs):
+    count = len(group)
     chunk_refs = refs[:count]
     outs = refs[count:]
+    slots = [me_ref[0] ^ have for have in group]
     outs_count = 3 if first_step else 2
     sums_in = outs[1] if len(outs) > outs_count else None
     outs = outs[-outs_count:]
@@ -186,8 +188,8 @@
         columns.append(jnp.transpose(jnp.broadcast_to(weight, (8, quarter)))[:, :1])
         if first_step:
             side_ref = outs[2]
-            side_ref[slot_ref[i], :targets, :] = ref[quarter : quarter + targets, :quarter].astype(F32)
-            side_ref[slot_ref[i], targets:, :] = jnp.broadcast_to(
+            side_ref[slots[i], :targets, :] = ref[quarter : quarter + targets, :quarter].astype(F32)
+            side_ref[slots[i], targets:, :] = jnp.broadcast_to(
                 weight, (side_ref.shape[1] - targets, quarter)
             )
     weight_column = jnp.concatenate(columns, axis=0)
@@ -198,7 +200,7 @@
         centre = norm_ref[:1, first : first + tile] * (scale * LOG2E)
         k_low = jnp.exp2(dots * (2.0 * scale * LOG2E) - row_norm - centre).astype(BF16)
         for i in range(count):
-            k_ref[slot_ref[i], :, first : first + tile] = k_low[i * quarter : (i + 1) * quarter]
+            k_ref[slots[i], :, first : first + tile] = k_low[i * quarter : (i + 1) * quarter]
         wide = k_low.astype(F32)
         updates = [(square_row, 1, jnp.sum(weight_column * (wide * wide), axis=0, keepdims=True))]
         if first_step:
@@ -209,12 +211,12 @@
             sums_ref[row : row + size, first : first + tile] = value
 
 
-def block_call(first_step, slots, chunks, chosen, norm, state, targets, row_devices, scale, offset):
+def block_call(first_step, me, group, chunks, chosen, norm, state, targets, row_devices, scale, offset):
     features = chosen.shape[1]
     per_step = norm.shape[1]
     count = len(chunks)
     quarter = chunks[0].shape[0] - round_up(targets, 16)
-    operands = [slots, held(chosen), held(norm), *chunks]
+    operands = [me, held(chosen), held(norm), *chunks]
     outs = [
         pltpu.VMEM((row_devices, quarter, per_step), BF16),
         pltpu.VMEM((round_up(targets + 1, 8) if first_step else 8, per_step), F32),
@@ -227,7 +229,7 @@
         operands += [held(x) for x in state]
     entries = count * quarter * per_step
     return pl.pallas_call(
-        functools.partial(block_kernel, first_step, targets, quarter, count, scale, offset),
+        functools.partial(block_kernel, first_step, targets, quarter, group, scale, offset),
         name="kernel_block",
         in_specs=[pl.BlockSpec(memory_space=pltpu.SMEM)] + in_vmem(len(operands) - 1),
         out_specs=in_vmem(len(outs)),
@@ -351,6 +353,24 @@
     return lax.ppermute(value, axis, [(i, i ^ bit) for i in range(count)])
 
 
+def own_buffer(value):
+    return lax.optimization_barrier(value + lax.optimization_barrier(jnp.zeros((), value.dtype)))
+
+
+def swap_both(value, row_bit, cent_bit):
+    rows, cents = lax.axis_size("rows"), lax.axis_size("cent")
+    pairs = [
+        (r * cents + c, (r ^ row_bit) * cents + (c ^ cent_bit)) for r in range(rows) for c in range(cents)
+    ]
+    return lax.ppermute(value, ("rows", "cent"), pairs)
+
+
+def in_order(mine, other, my_cent, bit):
+    high = (my_cent & bit) > 0
+    at = mine.ndim - 2
+    return jnp.stack([jnp.where(high, other, mine), jnp.where(high, mine, other)], axis=at)
+
+
 def bits_of(count):
     return [1 << k for k in range(count.bit_length() - 1)]
 
@@ -405,7 +425,7 @@
         for have in sorted(chunks):
             source = chunks[have]
             if bit == 1 and have == row_devices // 2:
-                source = lax.optimization_barrier(source + lax.optimization_barrier(jnp.zeros((), BF16)))
+                source = own_buffer(source)
             chunks[have | bit] = swap(source, "rows", bit)
 
     upper = (jnp.arange(LANES)[:, None] <= jnp.arange(LANES)[None, :]).astype(BF16)
@@ -419,6 +439,7 @@
     off = row_start[:, ::group_rows, 0].astype(jnp.int32)
     off = jnp.pad(off, ((0, 0), (0, 1)), constant_values=per_step)
 
+    me = my_row.astype(jnp.int32)[None]
     blocks = []
     own_coefs = []
     for step in range(steps):
@@ -426,14 +447,12 @@
         own_coefs.append(own_coef)
         state = None
         for group in groups_of(row_devices, step):
-            slots = my_row.astype(jnp.int32) ^ jnp.array(group, jnp.int32)
             state = block_call(
-                step == 0, slots, [chunks[have] for have in group], chosen, norm, state,
+                step == 0, me, group, [chunks[have] for have in group], chosen, norm, state,
                 target_count, row_devices, sharpness, offset,
             )
         blocks.append(state)
 
-    me = my_row.astype(jnp.int32)[None]
     info = blocks[0][2]
     sums = blocks[0][1]
     total_change = None
@@ -460,16 +479,23 @@
 
     pieces = total_change
     bits = bits_of(row_devices)
-    for first in range(0, len(bits), 2):
-        pair = bits[first : first + 2]
+    for first in range(0, len(bits) - 1, 2):
+        pair = bits[: len(bits) - 1][first : first + 2]
         count = 2 ** len(pair)
         pieces = pieces.reshape(pieces.shape[0] // count, count, target_count, quarter)
         kept = pieces[:, 0]
         for k in range(1, count):
             kept = kept + swap(pieces[:, k], "rows", k * pair[0])
         pieces = kept
-    own_change = pieces[0]
-    full = lax.all_gather(own_change, "cent")
+    far, *near = reversed(bits_of(cent_devices))
+    mine = pieces[0] + swap(pieces[1], "rows", bits[-1])
+    other = swap(pieces[0], "cent", far)
+    other = other + swap_both(own_buffer(pieces[1]), bits[-1], far)
+    full = in_order(mine, other, my_cent, far)
+    for bit in near:
+        other = swap(full, "cent", bit)
+        full = in_order(full, other, my_cent, bit)
+    full = full.reshape(cent_devices, target_count, quarter)
     full = full.transpose(1, 0, 2).reshape(target_count, rows_dev)
     return (coef_now, predictions + full)
 

time: 101 us -> 97.5 us (0.965)
  starting transfers between devices: 20 us -> 26.2 us
  blocking collectives: 19.6 us -> 14.3 us
  Pallas kernels: 41.1 us -> 37.9 us
  other arithmetic: 5.33 us -> 3.38 us
  waiting for transfers between devices: 12 us -> 13.3 us
    all_gather x1 -> x0, blocking collectives: 5.22 us -> none  [local(): full = lax.all_gather(own_change, 'cent')]
    ppermute x17 -> x19, starting transfers between devices: 20 us -> 24.8 us  [swap(): return lax.ppermute(value, axis, [(i, i ^ bit) for i in range(count)])]
    pallas_call x10, Pallas kernels: 19.4 us -> 16.1 us  [block_call(): pl.pallas_call(functools.partial(block_kernel, first_step, targets, quart...]
    ppermute x0 -> x1, waiting for transfers between devices: none -> 2.2 us  [swap_both(): return lax.ppermute(value, ('rows', 'cent'), pairs)]
    xor x4 -> x0, other arithmetic: 1.98 us -> none  [local(): slots = my_row.astype(jnp.int32) ^ jnp.array(group, jnp.int32)]
    ppermute x0 -> x1, starting transfers between devices: none -> 1.33 us  [swap_both(): return lax.ppermute(value, ('rows', 'cent'), pairs)]
    ppermute x17 -> x19, waiting for transfers between devices: 12 us -> 11.1 us  [swap(): return lax.ppermute(value, axis, [(i, i ^ bit) for i in range(count)])]
  transfers between devices with their start and end apart: 17 -> 20, of which waited for: 9 -> 11; matrix products, arithmetic and copies ran while one was open for 4% -> 2% of each run, Pallas kernels for 34% -> 32%
where the time goes in v7:
time: 97.5 us; the launch traced here: 97.2 us
  Pallas kernels  37.9 us (39%)
  starting transfers between devices  26.2 us (27%)
  blocking collectives  14.3 us (15%)
  waiting for transfers between devices  13.3 us (14%)
  other arithmetic  3.38 us (3%)
    ppermute x19, starting transfers between devices, swap(): return lax.ppermute(value, axis, [(i, i ^ bit) for i in range(count)])  24.8 us
    pallas_call x10, Pallas kernels, block_call(): pl.pallas_call(functools.partial(block_kernel, first_step, targets, quart...  16.1 us
    all_gather x2, blocking collectives, local(): lax.all_gather(sums, 'cent')  14.3 us
    pallas_call x2, Pallas kernels, compact(): pl.pallas_call(functools.partial(compact_kernel, step, per_step, targets)...  11.6 us
    ppermute x19, waiting for transfers between devices, swap(): return lax.ppermute(value, axis, [(i, i ^ bit) for i in range(count)])  11.1 us
    pallas_call x2, Pallas kernels, scatter_call(): pl.pallas_call(functools.partial(scatter_kernel, targets, step), name='sc...  4.69 us
    pallas_call x2, Pallas kernels, change_call(): pl.pallas_call(functools.partial(change_kernel, targets, before is None,...  4.21 us
    ppermute x1, waiting for transfers between devices, swap_both(): return lax.ppermute(value, ('rows', 'cent'), pairs)  2.2 us
  transfers between devices with their start and end apart: 20, of which 11 were waited for; matrix products, arithmetic and copies ran while one was open for 2% of the time, Pallas kernels for 32%

profile of v7, /device:TPU:0, one launch (start us, length us, event | category | flops | bytes accessed | tf_op | source)
XLA Modules:
  0.0 97.2 jit_solution(6040054461185074810)
XLA Ops:
  4.4 2.6 %collective-permute-start.1 = (bf16[2,32,128]{2,1,0:T(8,128)(2,1)S(1)}, bf16[2,32,128]{2,1,0:T(8,128)(2,1)S(1)}, u32[]{:S(2)}, u32[]{:S(2)}) collective-permute-start(bf16[2,32,128]{2,1,0:T(8,128)(2,1)S(1)} %add.75), channel_id=1, source_target_pairs={{0,2},{1,3},{2,0},{3,1},{4,6},{5,7},{6,4},{7,5},{8,10},{9,11},{10,... | collective-permute-start | bytes 49160 | tf_op jit(solution)/shard_map/ppermute | solution.py:353
  7.0 2.7 %collective-permute-start.2 = (bf16[272,512]{1,0:T(8,128)(2,1)S(1)}, bf16[272,512]{1,0:T(8,128)(2,1)S(1)}, u32[]{:S(2)}, u32[]{:S(2)}) collective-permute-start(bf16[272,512]{1,0:T(8,128)(2,1)S(1)} %maximum_maximum_fusion.refs_0_), channel_id=1, source_target_pairs={{0,16},{4,20},{8,24},{12,28},{16,0},{20,4},{24,8},{28,12},{1,17},{... | collective-permute-start | bytes 835592 | tf_op jit(solution)/shard_map/ppermute | solution.py:353
  9.7 1.6 %collective-permute-start.6 = (bf16[272,512]{1,0:T(8,128)(2,1)S(1)}, bf16[272,512]{1,0:T(8,128)(2,1)S(1)}, u32[]{:S(2)}, u32[]{:S(2)}) collective-permute-start(bf16[272,512]{1,0:T(8,128)(2,1)S(1)} %maximum_maximum_fusion.refs_0_), channel_id=1, source_target_pairs={{0,8},{4,12},{8,0},{12,4},{16,24},{20,28},{24,16},{28,20},{1,9},{5... | collective-permute-start | bytes 835592 | tf_op jit(solution)/shard_map/ppermute | solution.py:353
  13.4 5.7 %compact.2 = (bf16[1808,512]{1,0:T(8,128)(2,1)S(1)}, f32[8,1536]{1,0:T(8,128)S(1)}, f32[16,1536]{1,0:T(8,128)S(1)}) custom-call(s32[2,17]{1,0:T(2,128)S(1)} %pad.8.off_ref, s32[2,32,128]{2,1,0:T(8,128)S(1)} %select_convert_fusion.dest_ref, bf16[4096,512]{1,0:T(8,128)(2,1)} %pool_hbm.3, f32[16,4096]{1,0:T(8,128)} %coef_ref.1), custom_call_target="tpu_custom_call" | custom-call | flops 2000000000 | bytes 6000000 | tf_op jit(solution)/shard_map/compact/pallas_call | solution.py:140
  19.1 5.9 %compact.3 = (bf16[1808,512]{1,0:T(8,128)(2,1)S(1)}, f32[8,1536]{1,0:T(8,128)S(1)}, f32[16,1536]{1,0:T(8,128)S(1)}) custom-call(s32[2,17]{1,0:T(2,128)S(1)} %pad.8.off_ref, s32[2,32,128]{2,1,0:T(8,128)S(1)} %select_convert_fusion.dest_ref, bf16[4096,512]{1,0:T(8,128)(2,1)} %pool_hbm.3, f32[16,4096]{1,0:T(8,128)} %coef_ref.1), custom_call_target="tpu_custom_call" | custom-call | flops 2000000000 | bytes 6000000 | tf_op jit(solution)/shard_map/compact/pallas_call | solution.py:140
  26.1 1.6 %collective-permute-start.5 = (bf16[272,512]{1,0:T(8,128)(2,1)S(1)}, bf16[272,512]{1,0:T(8,128)(2,1)S(1)}, u32[]{:S(2)}, u32[]{:S(2)}) collective-permute-start(bf16[272,512]{1,0:T(8,128)(2,1)S(1)} %broadcast_add_fusion), channel_id=1, source_target_pairs={{0,4},{4,0},{8,12},{12,8},{16,20},{20,16},{24,28},{28,24},{1,5},{5... | collective-permute-start | bytes 835592 | tf_op jit(solution)/shard_map/ppermute | solution.py:353
  27.7 2.1 %kernel_block.10 = (bf16[8,256,1536]{2,1,0:T(8,128)(2,1)S(1)}, f32[24,1536]{1,0:T(8,128)S(1)}, f32[8,24,256]{2,1,0:T(8,128)S(1)}) custom-call(s32[1]{0:T(128)} %bitcast.3.me_ref, bf16[1808,512]{1,0:T(8,128)(2,1)S(1)} %get-tuple-element.39.chosen_ref, f32[8,1536]{1,0:T(8,128)S(1)} %get-tuple-element.40.norm_ref, ...), custom_call_target="tpu_custom_call" | custom-call | flops 805306368 | bytes 1572864 | tf_op jit(solution)/shard_map/kernel_block/pallas_call | solution.py:231
  29.8 3.2 %collective-permute-done.3.refs_0_.refs_1_ = bf16[272,512]{1,0:T(8,128)(2,1)S(1)} collective-permute-done((bf16[272,512]{1,0:T(8,128)(2,1)S(1)}, bf16[272,512]{1,0:T(8,128)(2,1)S(1)}, u32[]{:S(2)}, u32[]{:S(2)}) %collective-permute-start.3) | collective-permute-done | bytes 278560 | tf_op jit(solution)/shard_map/ppermute | solution.py:353
  33.5 1.6 %kernel_block.16 = (bf16[8,256,1536]{2,1,0:T(8,128)(2,1)S(1)}, f32[8,1536]{1,0:T(8,128)S(1)}) custom-call(s32[1]{0:T(128)} %bitcast.3.me_ref, bf16[1808,512]{1,0:T(8,128)(2,1)S(1)} %get-tuple-element.61.chosen_ref, f32[8,1536]{1,0:T(8,128)S(1)} %get-tuple-element.62.norm_ref, bf16[272,512]{1,0:T(8,128)(2,1)S(1)} %maximum_maximum_fusion.refs_0_, ...), custom_call_target="tpu_custom_call" | custom-call | flops 805306368 | bytes 1572864 | tf_op jit(solution)/shard_map/kernel_block/pallas_call | solution.py:231
  35.1 2.1 %kernel_block.11 = (bf16[8,256,1536]{2,1,0:T(8,128)(2,1)S(1)}, f32[24,1536]{1,0:T(8,128)S(1)}, f32[8,24,256]{2,1,0:T(8,128)S(1)}) custom-call(s32[1]{0:T(128)} %bitcast.3.me_ref, bf16[1808,512]{1,0:T(8,128)(2,1)S(1)} %get-tuple-element.39.chosen_ref, ...), custom_call_target="tpu_custom_call", output_to_operand_aliasing={{0}: (5, {}), {1}: (6, {}), {2}: (7, {})} | custom-call | flops 805306368 | bytes 1572864 | tf_op jit(solution)/shard_map/kernel_block/pallas_call | solution.py:231
  42.5 1.5 %kernel_block.17 = (bf16[8,256,1536]{2,1,0:T(8,128)(2,1)S(1)}, f32[8,1536]{1,0:T(8,128)S(1)}) custom-call(s32[1]{0:T(128)} %bitcast.3.me_ref, bf16[1808,512]{1,0:T(8,128)(2,1)S(1)} %get-tuple-element.61.chosen_ref, f32[8,1536]{1,0:T(8,128)S(1)} %get-tuple-element.62.norm_ref, ...), custom_call_target="tpu_custom_call", output_to_operand_aliasing={{0}: (5, {}), {1}: (6, {})} | custom-call | flops 805306368 | bytes 1572864 | tf_op jit(solution)/shard_map/kernel_block/pallas_call | solution.py:231
  46.6 6.9 %all-gather = f32[96,1536]{1,0:T(8,128)S(1)} all-gather(f32[24,1536]{1,0:T(8,128)S(1)} %get-tuple-element.56), channel_id=2, replica_groups=mesh['rows'=8,'cent'=4] {'cent'}, dimensions={0}, use_global_device_ids=true | all-gather | bytes 737280 | tf_op jit(solution)/shard_map/all_gather | solution.py:471
  53.5 2.1 %change.2 = (f32[16,1536]{1,0:T(8,128)S(1)}, f32[8,16,256]{2,1,0:T(8,128)S(1)}, f32[8,16,256]{2,1,0:T(8,128)S(1)}) custom-call(s32[1]{0:T(128)} %bitcast.3.me_ref, f32[4,24,1536]{2,1,0:T(8,128)S(1)} %bitcast.58, f32[16,1536]{1,0:T(8,128)S(1)} %get-tuple-element.57.coef_ref, bf16[8,256,1536]{2,1,0:T(8,128)(2,1)S(1)} %get-tuple-element.58.k_ref, ...), custom_call_target="tpu_custom_call" | custom-call | flops 100663296 | bytes 6291456 | tf_op jit(solution)/shard_map/change/pallas_call | solution.py:279
  55.6 1.6 %collective-permute-start.11 = (bf16[8,16,256]{2,1,0:T(8,128)(2,1)S(1)}, bf16[8,16,256]{2,1,0:T(8,128)(2,1)S(1)}, u32[]{:S(2)}, u32[]{:S(2)}) collective-permute-start(bf16[8,16,256]{2,1,0:T(8,128)(2,1)S(1)} %convert_element_type.69), channel_id=1, source_target_pairs={{0,12},{4,8},{8,4},{12,0},{16,28},{20,24},{24,20},{28,16},{1,13},{... | collective-permute-start | bytes 196616 | tf_op jit(solution)/shard_map/ppermute | solution.py:353
  59.2 1.5 %kernel_block.18 = (bf16[8,256,1536]{2,1,0:T(8,128)(2,1)S(1)}, f32[8,1536]{1,0:T(8,128)S(1)}) custom-call(s32[1]{0:T(128)} %bitcast.3.me_ref, bf16[1808,512]{1,0:T(8,128)(2,1)S(1)} %get-tuple-element.61.chosen_ref, f32[8,1536]{1,0:T(8,128)S(1)} %get-tuple-element.62.norm_ref, ...), custom_call_target="tpu_custom_call", output_to_operand_aliasing={{0}: (5, {}), {1}: (6, {})} | custom-call | flops 805306368 | bytes 1572864 | tf_op jit(solution)/shard_map/kernel_block/pallas_call | solution.py:231
  62.4 2.6 %collective-permute-start.12 = (bf16[8,16,256]{2,1,0:T(8,128)(2,1)S(1)}, bf16[8,16,256]{2,1,0:T(8,128)(2,1)S(1)}, u32[]{:S(2)}, u32[]{:S(2)}) collective-permute-start(bf16[8,16,256]{2,1,0:T(8,128)(2,1)S(1)} %fusion.17), channel_id=1, source_target_pairs={{0,16},{4,20},{8,24},{12,28},{16,0},{20,4},{24,8},{28,12},{1,17},{... | collective-permute-start | bytes 196616 | tf_op jit(solution)/shard_map/ppermute | solution.py:353
  66.5 1.5 %collective-permute-done.12 = bf16[8,16,256]{2,1,0:T(8,128)(2,1)S(1)} collective-permute-done((bf16[8,16,256]{2,1,0:T(8,128)(2,1)S(1)}, bf16[8,16,256]{2,1,0:T(8,128)(2,1)S(1)}, u32[]{:S(2)}, u32[]{:S(2)}) %collective-permute-start.12) | collective-permute-done | bytes 65568 | tf_op jit(solution)/shard_map/ppermute | solution.py:353
  69.3 7.4 %all-gather.1 = f32[96,1536]{1,0:T(8,128)S(1)} all-gather(f32[24,1536]{1,0:T(8,128)S(1)} %gradient.1), channel_id=3, replica_groups=mesh['rows'=8,'cent'=4] {'cent'}, dimensions={0}, use_global_device_ids=true | all-gather | bytes 737280 | tf_op jit(solution)/shard_map/all_gather | solution.py:471
  76.8 2.1 %change.3 = (f32[16,1536]{1,0:T(8,128)S(1)}, f32[8,16,256]{2,1,0:T(8,128)S(1)}) custom-call(s32[1]{0:T(128)} %bitcast.3.me_ref, f32[4,24,1536]{2,1,0:T(8,128)S(1)} %bitcast.59, f32[16,1536]{1,0:T(8,128)S(1)} %get-tuple-element.71.coef_ref, bf16[8,256,1536]{2,1,0:T(8,128)(2,1)S(1)} %get-tuple-element.69.k_ref, f32[8,24,256]{2,1,0:T(8,128)S(1)} %get-tuple-element.59.side_ref, ...), custom_call_target="tpu_custom_call" | custom-call | flops 100663296 | bytes 6291456 | tf_op jit(solution)/shard_map/change/pallas_call | solution.py:279
  78.9 1.8 %collective-permute-start.15 = (f32[2,16,256]{2,1,0:T(8,128)S(1)}, f32[2,16,256]{2,1,0:T(8,128)S(1)}, u32[]{:S(2)}, u32[]{:S(2)}) collective-permute-start(f32[2,16,256]{2,1,0:T(8,128)S(1)} %get-tuple-element.80), channel_id=1, source_target_pairs={{0,12},{4,8},{8,4},{12,0},{16,28},{20,24},{24,20},{28,16},{1,13},{... | collective-permute-start | bytes 98312 | tf_op jit(solution)/shard_map/ppermute | solution.py:353
  85.1 2.5 %collective-permute-start.18 = (f32[16,256]{1,0:T(8,128)S(1)}, f32[16,256]{1,0:T(8,128)S(1)}, u32[]{:S(2)}, u32[]{:S(2)}) collective-permute-start(f32[16,256]{1,0:T(8,128)S(1)} %get-tuple-element.86), channel_id=1, source_target_pairs={{0,16},{4,20},{8,24},{12,28},{16,0},{20,4},{24,8},{28,12},{1,17},{... | collective-permute-start | bytes 49160 | tf_op jit(solution)/shard_map/ppermute | solution.py:353
  89.5 2.0 %scatter.2.coef_ref = f32[16,4096]{1,0:T(8,128)S(1)} custom-call(s32[2,17]{1,0:T(2,128)S(1)} %pad.8.off_ref, s32[2,32,128]{2,1,0:T(8,128)S(1)} %select_convert_fusion.dest_ref, f32[16,4096]{1,0:T(8,128)S(1)} %copy-done.1, f32[16,1536]{1,0:T(8,128)S(1)} %get-tuple-element.73.delta_ref), custom_call_target="tpu_custom_call" | custom-call | flops 1000000000 | bytes 1000000 | tf_op jit(solution)/shard_map/scatter/pallas_call | solution.py:339
  91.5 2.2 %collective-permute-done.17 = f32[16,256]{1,0:T(8,128)S(1)} collective-permute-done((f32[16,256]{1,0:T(8,128)S(1)}, f32[16,256]{1,0:T(8,128)S(1)}, u32[]{:S(2)}, u32[]{:S(2)}) %collective-permute-start.17) | collective-permute-done | bytes 16416 | tf_op jit(solution)/shard_map/ppermute | solution.py:365
  93.8 2.7 %scatter.3 = f32[16,4096]{1,0:T(8,128)} custom-call(s32[2,17]{1,0:T(2,128)S(1)} %pad.8.off_ref, s32[2,32,128]{2,1,0:T(8,128)S(1)} %select_convert_fusion.dest_ref, f32[16,4096]{1,0:T(8,128)S(1)} %scatter.2.coef_ref, f32[16,1536]{1,0:T(8,128)S(1)} %get-tuple-element.74.delta_ref), custom_call_target="tpu_custom_call" | custom-call | flops 1000000000 | bytes 1000000 | tf_op jit(solution)/shard_map/scatter/pallas_call | solution.py:339
  (74 shorter events, 28.9 us)
Async XLA Ops:
  0.6 3.0 %copy-start = (bf16[1024,512]{1,0:T(8,128)(2,1)S(1)}, bf16[1024,512]{1,0:T(8,128)(2,1)}, u32[]{:S(2)}) copy-start(bf16[1024,512]{1,0:T(8,128)(2,1)} %param.7) | copy-start | bytes 3145732
  2.3 2.1 %collective-permute-start = (bf16[2,32,128]{2,1,0:T(8,128)(2,1)S(1)}, bf16[2,32,128]{2,1,0:T(8,128)(2,1)S(1)}, u32[]{:S(2)}, u32[]{:S(2)}) collective-permute-start(bf16[2,32,128]{2,1,0:T(8,128)(2,1)S(1)} %fusion.2), channel_id=1, source_target_pairs={{0,1},{1,0},{2,3},{3,2},{4,5},{5,4},{6,7},{7,6},{8,9},{9,8},{10,11... | collective-permute-start | bytes 49160 | tf_op jit(solution)/shard_map/ppermute | solution.py:353
  4.4 8.3 %collective-permute-start.1 = (bf16[2,32,128]{2,1,0:T(8,128)(2,1)S(1)}, bf16[2,32,128]{2,1,0:T(8,128)(2,1)S(1)}, u32[]{:S(2)}, u32[]{:S(2)}) collective-permute-start(bf16[2,32,128]{2,1,0:T(8,128)(2,1)S(1)} %add.75), channel_id=1, source_target_pairs={{0,2},{1,3},{2,0},{3,1},{4,6},{5,7},{6,4},{7,5},{8,10},{9,11},{10,... | collective-permute-start | bytes 49160 | tf_op jit(solution)/shard_map/ppermute | solution.py:353
  7.0 18.0 %collective-permute-start.2 = (bf16[272,512]{1,0:T(8,128)(2,1)S(1)}, bf16[272,512]{1,0:T(8,128)(2,1)S(1)}, u32[]{:S(2)}, u32[]{:S(2)}) collective-permute-start(bf16[272,512]{1,0:T(8,128)(2,1)S(1)} %maximum_maximum_fusion.refs_0_), channel_id=1, source_target_pairs={{0,16},{4,20},{8,24},{12,28},{16,0},{20,4},{24,8},{28,12},{1,17},{... | collective-permute-start | bytes 835592 | tf_op jit(solution)/shard_map/ppermute | solution.py:353
  9.7 15.9 %collective-permute-start.6 = (bf16[272,512]{1,0:T(8,128)(2,1)S(1)}, bf16[272,512]{1,0:T(8,128)(2,1)S(1)}, u32[]{:S(2)}, u32[]{:S(2)}) collective-permute-start(bf16[272,512]{1,0:T(8,128)(2,1)S(1)} %maximum_maximum_fusion.refs_0_), channel_id=1, source_target_pairs={{0,8},{4,12},{8,0},{12,4},{16,24},{20,28},{24,16},{28,20},{1,9},{5... | collective-permute-start | bytes 835592 | tf_op jit(solution)/shard_map/ppermute | solution.py:353
  11.3 16.4 %collective-permute-start.8 = (bf16[272,512]{1,0:T(8,128)(2,1)S(1)}, bf16[272,512]{1,0:T(8,128)(2,1)S(1)}, u32[]{:S(2)}, u32[]{:S(2)}) collective-permute-start(bf16[272,512]{1,0:T(8,128)(2,1)S(1)} %maximum_maximum_fusion.refs_0_), channel_id=1, source_target_pairs={{0,4},{4,0},{8,12},{12,8},{16,20},{20,16},{24,28},{28,24},{1,5},{5... | collective-permute-start | bytes 835592 | tf_op jit(solution)/shard_map/ppermute | solution.py:353
  25.0 8.0 %collective-permute-start.3 = (bf16[272,512]{1,0:T(8,128)(2,1)S(1)}, bf16[272,512]{1,0:T(8,128)(2,1)S(1)}, u32[]{:S(2)}, u32[]{:S(2)}) collective-permute-start(bf16[272,512]{1,0:T(8,128)(2,1)S(1)} %collective-permute-done.2.refs_0_), channel_id=1, source_target_pairs={{0,8},{4,12},{8,0},{12,4},{16,24},{20,28},{24,16},{28,20},{1,9},{5... | collective-permute-start | bytes 835592 | tf_op jit(solution)/shard_map/ppermute | solution.py:353
  25.5 9.5 %collective-permute-start.7 = (bf16[272,512]{1,0:T(8,128)(2,1)S(1)}, bf16[272,512]{1,0:T(8,128)(2,1)S(1)}, u32[]{:S(2)}, u32[]{:S(2)}) collective-permute-start(bf16[272,512]{1,0:T(8,128)(2,1)S(1)} %collective-permute-done.6.refs_0_), channel_id=1, source_target_pairs={{0,4},{4,0},{8,12},{12,8},{16,20},{20,16},{24,28},{28,24},{1,5},{5... | collective-permute-start | bytes 835592 | tf_op jit(solution)/shard_map/ppermute | solution.py:353
  26.1 15.0 %collective-permute-start.5 = (bf16[272,512]{1,0:T(8,128)(2,1)S(1)}, bf16[272,512]{1,0:T(8,128)(2,1)S(1)}, u32[]{:S(2)}, u32[]{:S(2)}) collective-permute-start(bf16[272,512]{1,0:T(8,128)(2,1)S(1)} %broadcast_add_fusion), channel_id=1, source_target_pairs={{0,4},{4,0},{8,12},{12,8},{16,20},{20,16},{24,28},{28,24},{1,5},{5... | collective-permute-start | bytes 835592 | tf_op jit(solution)/shard_map/ppermute | solution.py:353
  33.0 12.1 %collective-permute-start.4 = (bf16[272,512]{1,0:T(8,128)(2,1)S(1)}, bf16[272,512]{1,0:T(8,128)(2,1)S(1)}, u32[]{:S(2)}, u32[]{:S(2)}) collective-permute-start(bf16[272,512]{1,0:T(8,128)(2,1)S(1)} %collective-permute-done.3.refs_0_.refs_1_), channel_id=1, source_target_pairs={{0,4},{4,0},{8,12},{12,8},{16,20},{20,16},{24,28},{28,24},{1,5},{5... | collective-permute-start | bytes 835592 | tf_op jit(solution)/shard_map/ppermute | solution.py:353
  55.6 5.4 %collective-permute-start.11 = (bf16[8,16,256]{2,1,0:T(8,128)(2,1)S(1)}, bf16[8,16,256]{2,1,0:T(8,128)(2,1)S(1)}, u32[]{:S(2)}, u32[]{:S(2)}) collective-permute-start(bf16[8,16,256]{2,1,0:T(8,128)(2,1)S(1)} %convert_element_type.69), channel_id=1, source_target_pairs={{0,12},{4,8},{8,4},{12,0},{16,28},{20,24},{24,20},{28,16},{1,13},{... | collective-permute-start | bytes 196616 | tf_op jit(solution)/shard_map/ppermute | solution.py:353
  57.2 4.3 %collective-permute-start.10 = (bf16[8,16,256]{2,1,0:T(8,128)(2,1)S(1)}, bf16[8,16,256]{2,1,0:T(8,128)(2,1)S(1)}, u32[]{:S(2)}, u32[]{:S(2)}) collective-permute-start(bf16[8,16,256]{2,1,0:T(8,128)(2,1)S(1)} %convert_element_type.69), channel_id=1, source_target_pairs={{0,8},{4,12},{8,0},{12,4},{16,24},{20,28},{24,16},{28,20},{1,9},{5... | collective-permute-start | bytes 196616 | tf_op jit(solution)/shard_map/ppermute | solution.py:353
  57.6 4.7 %collective-permute-start.9 = (bf16[8,16,256]{2,1,0:T(8,128)(2,1)S(1)}, bf16[8,16,256]{2,1,0:T(8,128)(2,1)S(1)}, u32[]{:S(2)}, u32[]{:S(2)}) collective-permute-start(bf16[8,16,256]{2,1,0:T(8,128)(2,1)S(1)} %convert_element_type.69), channel_id=1, source_target_pairs={{0,4},{4,0},{8,12},{12,8},{16,20},{20,16},{24,28},{28,24},{1,5},{5... | collective-permute-start | bytes 196616 | tf_op jit(solution)/shard_map/ppermute | solution.py:353
  62.4 5.7 %collective-permute-start.12 = (bf16[8,16,256]{2,1,0:T(8,128)(2,1)S(1)}, bf16[8,16,256]{2,1,0:T(8,128)(2,1)S(1)}, u32[]{:S(2)}, u32[]{:S(2)}) collective-permute-start(bf16[8,16,256]{2,1,0:T(8,128)(2,1)S(1)} %fusion.17), channel_id=1, source_target_pairs={{0,16},{4,20},{8,24},{12,28},{16,0},{20,4},{24,8},{28,12},{1,17},{... | collective-permute-start | bytes 196616 | tf_op jit(solution)/shard_map/ppermute | solution.py:353
  68.1 21.5 %copy-start.1 = (f32[16,4096]{1,0:T(8,128)S(1)}, f32[16,4096]{1,0:T(8,128)}, u32[]{:S(2)}) copy-start(f32[16,4096]{1,0:T(8,128)} %coef_ref.1) | copy-start | bytes 786436
  76.8 19.8 %copy-start.2 = (f32[16,1024]{1,0:T(8,128)S(1)}, f32[16,1024]{1,0:T(8,128)}, u32[]{:S(2)}) copy-start(f32[16,1024]{1,0:T(8,128)} %param.10) | copy-start | bytes 196612
  78.9 4.9 %collective-permute-start.15 = (f32[2,16,256]{2,1,0:T(8,128)S(1)}, f32[2,16,256]{2,1,0:T(8,128)S(1)}, u32[]{:S(2)}, u32[]{:S(2)}) collective-permute-start(f32[2,16,256]{2,1,0:T(8,128)S(1)} %get-tuple-element.80), channel_id=1, source_target_pairs={{0,12},{4,8},{8,4},{12,0},{16,28},{20,24},{24,20},{28,16},{1,13},{... | collective-permute-start | bytes 98312 | tf_op jit(solution)/shard_map/ppermute | solution.py:353
  80.7 3.9 %collective-permute-start.14 = (f32[2,16,256]{2,1,0:T(8,128)S(1)}, f32[2,16,256]{2,1,0:T(8,128)S(1)}, u32[]{:S(2)}, u32[]{:S(2)}) collective-permute-start(f32[2,16,256]{2,1,0:T(8,128)S(1)} %get-tuple-element.79), channel_id=1, source_target_pairs={{0,8},{4,12},{8,0},{12,4},{16,24},{20,28},{24,16},{28,20},{1,9},{5... | collective-permute-start | bytes 98312 | tf_op jit(solution)/shard_map/ppermute | solution.py:353
  81.1 3.9 %collective-permute-start.13 = (f32[2,16,256]{2,1,0:T(8,128)S(1)}, f32[2,16,256]{2,1,0:T(8,128)S(1)}, u32[]{:S(2)}, u32[]{:S(2)}) collective-permute-start(f32[2,16,256]{2,1,0:T(8,128)S(1)} %get-tuple-element.78), channel_id=1, source_target_pairs={{0,4},{4,0},{8,12},{12,8},{16,20},{20,16},{24,28},{28,24},{1,5},{5... | collective-permute-start | bytes 98312 | tf_op jit(solution)/shard_map/ppermute | solution.py:353
  85.1 6.5 %collective-permute-start.18 = (f32[16,256]{1,0:T(8,128)S(1)}, f32[16,256]{1,0:T(8,128)S(1)}, u32[]{:S(2)}, u32[]{:S(2)}) collective-permute-start(f32[16,256]{1,0:T(8,128)S(1)} %get-tuple-element.86), channel_id=1, source_target_pairs={{0,16},{4,20},{8,24},{12,28},{16,0},{20,4},{24,8},{28,12},{1,17},{... | collective-permute-start | bytes 49160 | tf_op jit(solution)/shard_map/ppermute | solution.py:353
  87.5 4.0 %collective-permute-start.16 = (f32[16,256]{1,0:T(8,128)S(1)}, f32[16,256]{1,0:T(8,128)S(1)}, u32[]{:S(2)}, u32[]{:S(2)}) collective-permute-start(f32[16,256]{1,0:T(8,128)S(1)} %get-tuple-element.85), channel_id=1, source_target_pairs={{0,2},{1,3},{2,0},{3,1},{4,6},{5,7},{6,4},{7,5},{8,10},{9,11},{10,... | collective-permute-start | bytes 49160 | tf_op jit(solution)/shard_map/ppermute | solution.py:353
  88.2 5.5 %collective-permute-start.17 = (f32[16,256]{1,0:T(8,128)S(1)}, f32[16,256]{1,0:T(8,128)S(1)}, u32[]{:S(2)}, u32[]{:S(2)}) collective-permute-start(f32[16,256]{1,0:T(8,128)S(1)} %broadcast_add_fusion.1), channel_id=1, source_target_pairs={{0,18},{1,19},{2,16},{3,17},{4,22},{5,23},{6,20},{7,21},{8,26},{9,... | collective-permute-start | bytes 49160 | tf_op jit(solution)/shard_map/ppermute | solution.py:365
  93.7 2.8 %collective-permute-start.19 = (f32[2,16,256]{2,1,0:T(8,128)S(1)}, f32[2,16,256]{2,1,0:T(8,128)S(1)}, u32[]{:S(2)}, u32[]{:S(2)}) collective-permute-start(f32[2,16,256]{2,1,0:T(8,128)S(1)} %pad_maximum_fusion.1), channel_id=1, source_target_pairs={{0,1},{1,0},{2,3},{3,2},{4,5},{5,4},{6,7},{7,6},{8,9},{9,8},{10,11... | collective-permute-start | bytes 98312 | tf_op jit(solution)/shard_map/ppermute | solution.py:353

commit v8 on v6

--- a/solution.py
+++ b/solution.py
@@ -13,8 +13,8 @@
 POOL_BLOCK = 256
 WINDOW = 144
 TILE = 512
-FIRST_GROUPS = [(0, 1), (2, 3), (4,), (6,), (5,), (7,)]
-LATER_GROUPS = [(0, 1), (2, 3), (4, 6), (5, 7)]
+FIRST_GROUPS = [(0, 1), (2, 4), (5, 6), (3, 7)]
+LATER_GROUPS = [(0, 1), (2, 4), (5, 6), (3, 7)]
 KERNEL_VMEM = 16 * 2**20
 LOG2E = math.log2(math.e)
 NT = (((1,), (1,)), ((), ()))
@@ -63,7 +63,12 @@
     return jnp.concatenate([ref[step, pl.ds(row, 1), :], ref[step, pl.ds(row + 1, 1), :]], axis=1)
 
 
-def compact_kernel(step, per_step, targets, off_ref, dest_ref, pool_hbm, coefs_hbm, out_ref, norm_ref, coef_ref, side_out, pool_ref, coefs_ref, parts_ref, arrived, coefs_arrived):
+def compact_kernel(step, per_step, targets, off_ref, dest_ref, *refs):
+    loads = step == 0
+    if loads:
+        pool_hbm, coefs_hbm, out_ref, norm_ref, coef_ref, pool_ref, parts_ref, side_out, coefs_ref, arrived, coefs_arrived = refs
+    else:
+        pool_ref, parts_ref, out_ref, norm_ref, coef_ref, side_out = refs
     features = out_ref.shape[1]
     blocks = pool_ref.shape[0] // POOL_BLOCK
     tile = math.gcd(per_step, 512)
@@ -72,20 +77,22 @@
         at = pl.ds(pl.multiple_of(block * POOL_BLOCK, POOL_BLOCK), POOL_BLOCK)
         return pltpu.make_async_copy(pool_hbm.at[at, :], pool_ref.at[at, :], arrived.at[block])
 
-    coefs_copy = pltpu.make_async_copy(coefs_hbm, coefs_ref, coefs_arrived)
-    coefs_copy.start()
-    for block in range(blocks):
-        fetch(block).start()
+    if loads:
+        coefs_copy = pltpu.make_async_copy(coefs_hbm, coefs_ref, coefs_arrived)
+        coefs_copy.start()
+        for block in range(blocks):
+            fetch(block).start()
     widest = 0
     for block in range(blocks):
         widest = jnp.maximum(widest, off_ref[step, block + 1] - (off_ref[step, block] // 16) * 16)
     narrow = widest <= WINDOW
     out_ref[:16, :] = jnp.zeros((16, features), BF16)
     side_out[:16, :] = jnp.zeros((16, LANES), BF16)
-    coefs_copy.wait()
-    parts_ref[3 * targets :, :] = jnp.zeros((LANES - 3 * targets, parts_ref.shape[1]), BF16)
-    for part, value in enumerate(split3(coefs_ref[...])):
-        parts_ref[part * targets : (part + 1) * targets, :] = value
+    if loads:
+        coefs_copy.wait()
+        parts_ref[3 * targets :, :] = jnp.zeros((LANES - 3 * targets, parts_ref.shape[1]), BF16)
+        for part, value in enumerate(split3(coefs_ref[...])):
+            parts_ref[part * targets : (part + 1) * targets, :] = value
 
     def place(block, window):
         base = pl.multiple_of((off_ref[step, block] // 16) * 16, 16)
@@ -104,8 +111,9 @@
     def _():
         @pl.loop(0, blocks // 4)
         def _(four):
-            for i in range(4):
-                fetch(4 * four + i).wait()
+            if loads:
+                for i in range(4):
+                    fetch(4 * four + i).wait()
             for i in range(4):
                 place(4 * four + i, WINDOW)
 
@@ -113,7 +121,8 @@
     def _():
         @pl.loop(0, blocks)
         def _(block):
-            fetch(block).wait()
+            if loads:
+                fetch(block).wait()
             place(block, POOL_BLOCK + 16)
 
     ones = jnp.ones((8, features), BF16)
@@ -137,37 +146,41 @@
 def compact(step, off, dest, pool, coefs, per_step, targets):
     features = pool.shape[1]
     length = round_up(per_step, 16) + POOL_BLOCK + 16
+    loads = step == 0
+    outs = [
+        pltpu.VMEM((length, features), BF16),
+        pltpu.VMEM((8, per_step), F32),
+        pltpu.VMEM((targets, per_step), F32),
+    ]
+    scratch = [pltpu.VMEM((length, LANES), BF16)]
+    sources = in_vmem(2)
+    operands = [held(pool), held(coefs)]
+    if loads:
+        outs += [pltpu.VMEM(pool.shape, BF16), pltpu.VMEM((LANES, pool.shape[0]), BF16)]
+        scratch += [
+            pltpu.VMEM(coefs.shape, F32),
+            pltpu.SemaphoreType.DMA((pool.shape[0] // POOL_BLOCK,)),
+            pltpu.SemaphoreType.DMA,
+        ]
+        sources = [pl.BlockSpec(memory_space=pltpu.HBM)] * 2
+        operands = [in_hbm(pool), in_hbm(coefs)]
     return pl.pallas_call(
         functools.partial(compact_kernel, step, per_step, targets),
         name="compact",
-        in_specs=[
-            pl.BlockSpec(memory_space=pltpu.SMEM),
-            *in_vmem(1),
-            pl.BlockSpec(memory_space=pltpu.HBM),
-            pl.BlockSpec(memory_space=pltpu.HBM),
-        ],
-        out_specs=in_vmem(3),
-        out_shape=(
-            pltpu.VMEM((length, features), BF16),
-            pltpu.VMEM((8, per_step), F32),
-            pltpu.VMEM((targets, per_step), F32),
-        ),
-        scratch_shapes=[
-            pltpu.VMEM((length, LANES), BF16),
-            pltpu.VMEM(pool.shape, BF16),
-            pltpu.VMEM(coefs.shape, F32),
-            pltpu.VMEM((LANES, pool.shape[0]), BF16),
-            pltpu.SemaphoreType.DMA((pool.shape[0] // POOL_BLOCK,)),
-            pltpu.SemaphoreType.DMA,
-        ],
+        in_specs=[pl.BlockSpec(memory_space=pltpu.SMEM), *in_vmem(1), *sources],
+        out_specs=in_vmem(len(outs)),
+        out_shape=tuple(outs),
+        scratch_shapes=scratch,
         compiler_params=params(),
         cost_estimate=pl.CostEstimate(flops=2 * 10**9, bytes_accessed=6 * 10**6, transcendentals=0),
-    )(off, dest, in_hbm(pool), in_hbm(coefs))
-
-
-def block_kernel(first_step, targets, quarter, count, scale, offset, slot_ref, chosen_ref, norm_ref, *refs):
+    )(off, dest, *operands)
+
+
+def block_kernel(first_step, targets, quarter, group, scale, offset, me_ref, chosen_ref, norm_ref, *refs):
+    count = len(group)
     chunk_refs = refs[:count]
     outs = refs[count:]
+    slots = [me_ref[0] ^ have for have in group]
     outs_count = 3 if first_step else 2
     sums_in = outs[1] if len(outs) > outs_count else None
     outs = outs[-outs_count:]
@@ -186,8 +199,8 @@
         columns.append(jnp.transpose(jnp.broadcast_to(weight, (8, quarter)))[:, :1])
         if first_step:
             side_ref = outs[2]
-            side_ref[slot_ref[i], :targets, :] = ref[quarter : quarter + targets, :quarter].astype(F32)
-            side_ref[slot_ref[i], targets:, :] = jnp.broadcast_to(
+            side_ref[slots[i], :targets, :] = ref[quarter : quarter + targets, :quarter].astype(F32)
+            side_ref[slots[i], targets:, :] = jnp.broadcast_to(
                 weight, (side_ref.shape[1] - targets, quarter)
             )
     weight_column = jnp.concatenate(columns, axis=0)
@@ -198,7 +211,7 @@
         centre = norm_ref[:1, first : first + tile] * (scale * LOG2E)
         k_low = jnp.exp2(dots * (2.0 * scale * LOG2E) - row_norm - centre).astype(BF16)
         for i in range(count):
-            k_ref[slot_ref[i], :, first : first + tile] = k_low[i * quarter : (i + 1) * quarter]
+            k_ref[slots[i], :, first : first + tile] = k_low[i * quarter : (i + 1) * quarter]
         wide = k_low.astype(F32)
         updates = [(square_row, 1, jnp.sum(weight_column * (wide * wide), axis=0, keepdims=True))]
         if first_step:
@@ -209,12 +222,12 @@
             sums_ref[row : row + size, first : first + tile] = value
 
 
-def block_call(first_step, slots, chunks, chosen, norm, state, targets, row_devices, scale, offset):
+def block_call(first_step, me, group, chunks, chosen, norm, state, targets, row_devices, scale, offset):
     features = chosen.shape[1]
     per_step = norm.shape[1]
     count = len(chunks)
     quarter = chunks[0].shape[0] - round_up(targets, 16)
-    operands = [slots, held(chosen), held(norm), *chunks]
+    operands = [me, held(chosen), held(norm), *chunks]
     outs = [
         pltpu.VMEM((row_devices, quarter, per_step), BF16),
         pltpu.VMEM((round_up(targets + 1, 8) if first_step else 8, per_step), F32),
@@ -227,7 +240,7 @@
         operands += [held(x) for x in state]
     entries = count * quarter * per_step
     return pl.pallas_call(
-        functools.partial(block_kernel, first_step, targets, quarter, count, scale, offset),
+        functools.partial(block_kernel, first_step, targets, quarter, group, scale, offset),
         name="kernel_block",
         in_specs=[pl.BlockSpec(memory_space=pltpu.SMEM)] + in_vmem(len(operands) - 1),
         out_specs=in_vmem(len(outs)),
@@ -351,8 +364,16 @@
     return lax.ppermute(value, axis, [(i, i ^ bit) for i in range(count)])
 
 
+def own_buffer(value):
+    return lax.optimization_barrier(value + lax.optimization_barrier(jnp.zeros((), value.dtype)))
+
+
 def bits_of(count):
     return [1 << k for k in range(count.bit_length() - 1)]
+
+
+def last_hop(chunk, row_devices):
+    return 2 if (chunk, row_devices) == (3, 8) else chunk & -chunk
 
 
 def groups_of(row_devices, step):
@@ -401,12 +422,12 @@
     for bit in bits_of(cent_devices):
         member = member + swap(member, "cent", bit)
 
-    for bit in reversed(bits_of(row_devices)):
-        for have in sorted(chunks):
-            source = chunks[have]
-            if bit == 1 and have == row_devices // 2:
-                source = lax.optimization_barrier(source + lax.optimization_barrier(jnp.zeros((), BF16)))
-            chunks[have | bit] = swap(source, "rows", bit)
+    for chunk in sorted(range(1, row_devices), key=lambda chunk: (bin(chunk).count("1"), chunk)):
+        bit = last_hop(chunk, row_devices)
+        source = chunks[chunk ^ bit]
+        if bit == 1 and chunk ^ bit == row_devices // 2:
+            source = own_buffer(source)
+        chunks[chunk] = swap(source, "rows", bit)
 
     upper = (jnp.arange(LANES)[:, None] <= jnp.arange(LANES)[None, :]).astype(BF16)
     before = (jnp.arange(high_count)[:, None] > jnp.arange(high_count)[None, :]).astype(BF16)
@@ -419,21 +440,24 @@
     off = row_start[:, ::group_rows, 0].astype(jnp.int32)
     off = jnp.pad(off, ((0, 0), (0, 1)), constant_values=per_step)
 
+    me = my_row.astype(jnp.int32)[None]
     blocks = []
     own_coefs = []
+    shard = []
     for step in range(steps):
-        chosen, norm, own_coef = compact(step, off, dest, centres, coefs, per_step, target_count)
+        chosen, norm, own_coef, *more = compact(
+            step, off, dest, *((centres, coefs) if step == 0 else shard), per_step, target_count
+        )
+        shard = more or shard
         own_coefs.append(own_coef)
         state = None
         for group in groups_of(row_devices, step):
-            slots = my_row.astype(jnp.int32) ^ jnp.array(group, jnp.int32)
             state = block_call(
-                step == 0, slots, [chunks[have] for have in group], chosen, norm, state,
+                step == 0, me, group, [chunks[have] for have in group], chosen, norm, state,
                 target_count, row_devices, sharpness, offset,
             )
         blocks.append(state)
 
-    me = my_row.astype(jnp.int32)[None]
     info = blocks[0][2]
     sums = blocks[0][1]
     total_change = None

time: 101 us -> 94.3 us (0.934)
  Pallas kernels: 41.1 us -> 34.1 us
  starting transfers between devices: 20 us -> 22.5 us
  other arithmetic: 5.33 us -> 3.35 us
    pallas_call x10 -> x8, Pallas kernels: 19.4 us -> 14.6 us  [block_call(): pl.pallas_call(functools.partial(block_kernel, first_step, targets, quart...]
    ppermute x17, starting transfers between devices: 20 us -> 22.5 us  [swap(): return lax.ppermute(value, axis, [(i, i ^ bit) for i in range(count)])]
    pallas_call x2, Pallas kernels: 11.6 us -> 9.29 us  [compact(): pl.pallas_call(functools.partial(compact_kernel, step, per_step, targets)...]
    xor x4 -> x0, other arithmetic: 1.98 us -> none  [local(): slots = my_row.astype(jnp.int32) ^ jnp.array(group, jnp.int32)]
  transfers between devices with their start and end apart: 17 -> 17, of which waited for: 9 -> 8; matrix products, arithmetic and copies ran while one was open for 4% -> 2% of each run, Pallas kernels for 34% -> 28%
where the time goes in v8:
time: 94.3 us; the launch traced here: 94 us
  Pallas kernels  34.1 us (36%)
  starting transfers between devices  22.5 us (24%)
  blocking collectives  19.5 us (21%)
  waiting for transfers between devices  12.3 us (13%)
  other arithmetic  3.35 us (4%)
  matrix products  0.95 us (1%)
    ppermute x17, starting transfers between devices, swap(): return lax.ppermute(value, axis, [(i, i ^ bit) for i in range(count)])  22.5 us
    pallas_call x8, Pallas kernels, block_call(): pl.pallas_call(functools.partial(block_kernel, first_step, targets, quart...  14.6 us
    all_gather x2, blocking collectives, local(): lax.all_gather(sums, 'cent')  14.3 us
    ppermute x17, waiting for transfers between devices, swap(): return lax.ppermute(value, axis, [(i, i ^ bit) for i in range(count)])  12.3 us
    pallas_call x2, Pallas kernels, compact(): pl.pallas_call(functools.partial(compact_kernel, step, per_step, targets)...  9.29 us
    all_gather x1, blocking collectives, local(): full = lax.all_gather(own_change, 'cent')  5.22 us
    pallas_call x2, Pallas kernels, scatter_call(): pl.pallas_call(functools.partial(scatter_kernel, targets, step), name='sc...  4.69 us
    pallas_call x2, Pallas kernels, change_call(): pl.pallas_call(functools.partial(change_kernel, targets, before is None,...  4.21 us
  transfers between devices with their start and end apart: 17, of which 8 were waited for; matrix products, arithmetic and copies ran while one was open for 2% of the time, Pallas kernels for 28%

profile of v8, /device:TPU:0, one launch (start us, length us, event | category | flops | bytes accessed | tf_op | source)
XLA Modules:
  0.0 94.0 jit_solution(13151674949386930710)
XLA Ops:
  4.4 2.6 %collective-permute-start.1 = (bf16[2,32,128]{2,1,0:T(8,128)(2,1)S(1)}, bf16[2,32,128]{2,1,0:T(8,128)(2,1)S(1)}, u32[]{:S(2)}, u32[]{:S(2)}) collective-permute-start(bf16[2,32,128]{2,1,0:T(8,128)(2,1)S(1)} %add.66), channel_id=1, source_target_pairs={{0,2},{1,3},{2,0},{3,1},{4,6},{5,7},{6,4},{7,5},{8,10},{9,11},{10,... | collective-permute-start | bytes 49160 | tf_op jit(solution)/shard_map/ppermute | solution.py:364
  7.0 1.6 %collective-permute-start.2 = (bf16[272,512]{1,0:T(8,128)(2,1)S(1)}, bf16[272,512]{1,0:T(8,128)(2,1)S(1)}, u32[]{:S(2)}, u32[]{:S(2)}) collective-permute-start(bf16[272,512]{1,0:T(8,128)(2,1)S(1)} %maximum_maximum_fusion.refs_0_), channel_id=1, source_target_pairs={{0,4},{4,0},{8,12},{12,8},{16,20},{20,16},{24,28},{28,24},{1,5},{5... | collective-permute-start | bytes 835592 | tf_op jit(solution)/shard_map/ppermute | solution.py:364
  8.6 2.6 %collective-permute-start.4 = (bf16[272,512]{1,0:T(8,128)(2,1)S(1)}, bf16[272,512]{1,0:T(8,128)(2,1)S(1)}, u32[]{:S(2)}, u32[]{:S(2)}) collective-permute-start(bf16[272,512]{1,0:T(8,128)(2,1)S(1)} %maximum_maximum_fusion.refs_0_), channel_id=1, source_target_pairs={{0,16},{4,20},{8,24},{12,28},{16,0},{20,4},{24,8},{28,12},{1,17},{... | collective-permute-start | bytes 835592 | tf_op jit(solution)/shard_map/ppermute | solution.py:364
  11.2 1.6 %collective-permute-start.8 = (bf16[272,512]{1,0:T(8,128)(2,1)S(1)}, bf16[272,512]{1,0:T(8,128)(2,1)S(1)}, u32[]{:S(2)}, u32[]{:S(2)}) collective-permute-start(bf16[272,512]{1,0:T(8,128)(2,1)S(1)} %maximum_maximum_fusion.refs_0_), channel_id=1, source_target_pairs={{0,8},{4,12},{8,0},{12,4},{16,24},{20,28},{24,16},{28,20},{1,9},{5... | collective-permute-start | bytes 835592 | tf_op jit(solution)/shard_map/ppermute | solution.py:364
  13.4 5.7 %compact.2 = (bf16[1808,512]{1,0:T(8,128)(2,1)S(1)}, f32[8,1536]{1,0:T(8,128)S(1)}, f32[16,1536]{1,0:T(8,128)S(1)}, bf16[4096,512]{1,0:T(8,128)(2,1)S(1)}, bf16[128,4096]{1,0:T(8,128)(2,1)S(1)}) custom-call(s32[2,17]{1,0:T(2,128)S(1)} %pad.8.off_ref, s32[2,32,128]{2,1,0:T(8,128)S(1)} %select_convert_fusion.dest_ref, bf16[4096,512]{1,0:T(8,128)(2,1)} %refs_0_.1, ...), custom_call_target="tpu_custom_call" | custom-call | flops 2000000000 | bytes 6000000 | tf_op jit(solution)/shard_map/compact/pallas_call | solution.py:167
  19.2 3.6 %compact.3 = (bf16[1808,512]{1,0:T(8,128)(2,1)S(1)}, f32[8,1536]{1,0:T(8,128)S(1)}, f32[16,1536]{1,0:T(8,128)S(1)}) custom-call(s32[2,17]{1,0:T(2,128)S(1)} %pad.8.off_ref, s32[2,32,128]{2,1,0:T(8,128)S(1)} %select_convert_fusion.dest_ref, bf16[4096,512]{1,0:T(8,128)(2,1)S(1)} %get-tuple-element.51.refs_0_, bf16[128,4096]{1,0:T(8,128)(2,1)S(1)} %get-tuple-element.52.refs_1_), custom_call_target="tpu_custom_call" | custom-call | flops 2000000000 | bytes 6000000 | tf_op jit(solution)/shard_map/compact/pallas_call | solution.py:167
  26.7 2.1 %kernel_block.8 = (bf16[8,256,1536]{2,1,0:T(8,128)(2,1)S(1)}, f32[24,1536]{1,0:T(8,128)S(1)}, f32[8,24,256]{2,1,0:T(8,128)S(1)}) custom-call(s32[1]{0:T(128)} %bitcast.3.me_ref, bf16[1808,512]{1,0:T(8,128)(2,1)S(1)} %get-tuple-element.35.chosen_ref, f32[8,1536]{1,0:T(8,128)S(1)} %get-tuple-element.36.norm_ref, ...), custom_call_target="tpu_custom_call" | custom-call | flops 805306368 | bytes 1572864 | tf_op jit(solution)/shard_map/kernel_block/pallas_call | solution.py:242
  28.8 4.8 %collective-permute-done.5.refs_1_ = bf16[272,512]{1,0:T(8,128)(2,1)S(1)} collective-permute-done((bf16[272,512]{1,0:T(8,128)(2,1)S(1)}, bf16[272,512]{1,0:T(8,128)(2,1)S(1)}, u32[]{:S(2)}, u32[]{:S(2)}) %collective-permute-start.5) | collective-permute-done | bytes 278560 | tf_op jit(solution)/shard_map/ppermute | solution.py:364
  34.1 1.6 %kernel_block.12 = (bf16[8,256,1536]{2,1,0:T(8,128)(2,1)S(1)}, f32[8,1536]{1,0:T(8,128)S(1)}) custom-call(s32[1]{0:T(128)} %bitcast.3.me_ref, bf16[1808,512]{1,0:T(8,128)(2,1)S(1)} %get-tuple-element.53.chosen_ref, f32[8,1536]{1,0:T(8,128)S(1)} %get-tuple-element.54.norm_ref, bf16[272,512]{1,0:T(8,128)(2,1)S(1)} %maximum_maximum_fusion.refs_0_, ...), custom_call_target="tpu_custom_call" | custom-call | flops 805306368 | bytes 1572864 | tf_op jit(solution)/shard_map/kernel_block/pallas_call | solution.py:242
  37.2 2.1 %kernel_block.9 = (bf16[8,256,1536]{2,1,0:T(8,128)(2,1)S(1)}, f32[24,1536]{1,0:T(8,128)S(1)}, f32[8,24,256]{2,1,0:T(8,128)S(1)}) custom-call(s32[1]{0:T(128)} %bitcast.3.me_ref, bf16[1808,512]{1,0:T(8,128)(2,1)S(1)} %get-tuple-element.35.chosen_ref, ...), custom_call_target="tpu_custom_call", output_to_operand_aliasing={{0}: (5, {}), {1}: (6, {}), {2}: (7, {})} | custom-call | flops 805306368 | bytes 1572864 | tf_op jit(solution)/shard_map/kernel_block/pallas_call | solution.py:242
  39.3 2.1 %kernel_block.10 = (bf16[8,256,1536]{2,1,0:T(8,128)(2,1)S(1)}, f32[24,1536]{1,0:T(8,128)S(1)}, f32[8,24,256]{2,1,0:T(8,128)S(1)}) custom-call(s32[1]{0:T(128)} %bitcast.3.me_ref, bf16[1808,512]{1,0:T(8,128)(2,1)S(1)} %get-tuple-element.35.chosen_ref, ...), custom_call_target="tpu_custom_call", output_to_operand_aliasing={{0}: (5, {}), {1}: (6, {}), {2}: (7, {})} | custom-call | flops 805306368 | bytes 1572864 | tf_op jit(solution)/shard_map/kernel_block/pallas_call | solution.py:242
  41.5 2.1 %kernel_block.11 = (bf16[8,256,1536]{2,1,0:T(8,128)(2,1)S(1)}, f32[24,1536]{1,0:T(8,128)S(1)}, f32[8,24,256]{2,1,0:T(8,128)S(1)}) custom-call(s32[1]{0:T(128)} %bitcast.3.me_ref, bf16[1808,512]{1,0:T(8,128)(2,1)S(1)} %get-tuple-element.35.chosen_ref, ...), custom_call_target="tpu_custom_call", output_to_operand_aliasing={{0}: (5, {}), {1}: (6, {}), {2}: (7, {})} | custom-call | flops 805306368 | bytes 1572864 | tf_op jit(solution)/shard_map/kernel_block/pallas_call | solution.py:242
  43.6 6.9 %all-gather = f32[96,1536]{1,0:T(8,128)S(1)} all-gather(f32[24,1536]{1,0:T(8,128)S(1)} %get-tuple-element.46), channel_id=2, replica_groups=mesh['rows'=8,'cent'=4] {'cent'}, dimensions={0}, use_global_device_ids=true | all-gather | bytes 737280 | tf_op jit(solution)/shard_map/all_gather | solution.py:476
  50.5 2.1 %change.2 = (f32[16,1536]{1,0:T(8,128)S(1)}, f32[8,16,256]{2,1,0:T(8,128)S(1)}, f32[8,16,256]{2,1,0:T(8,128)S(1)}) custom-call(s32[1]{0:T(128)} %bitcast.3.me_ref, f32[4,24,1536]{2,1,0:T(8,128)S(1)} %bitcast.46, f32[16,1536]{1,0:T(8,128)S(1)} %get-tuple-element.47.coef_ref, bf16[8,256,1536]{2,1,0:T(8,128)(2,1)S(1)} %get-tuple-element.48.k_ref, ...), custom_call_target="tpu_custom_call" | custom-call | flops 100663296 | bytes 6291456 | tf_op jit(solution)/shard_map/change/pallas_call | solution.py:290
  52.7 1.6 %collective-permute-start.11 = (bf16[8,16,256]{2,1,0:T(8,128)(2,1)S(1)}, bf16[8,16,256]{2,1,0:T(8,128)(2,1)S(1)}, u32[]{:S(2)}, u32[]{:S(2)}) collective-permute-start(bf16[8,16,256]{2,1,0:T(8,128)(2,1)S(1)} %convert_element_type.69), channel_id=1, source_target_pairs={{0,12},{4,8},{8,4},{12,0},{16,28},{20,24},{24,20},{28,16},{1,13},{... | collective-permute-start | bytes 196616 | tf_op jit(solution)/shard_map/ppermute | solution.py:364
  56.2 1.5 %kernel_block.14 = (bf16[8,256,1536]{2,1,0:T(8,128)(2,1)S(1)}, f32[8,1536]{1,0:T(8,128)S(1)}) custom-call(s32[1]{0:T(128)} %bitcast.3.me_ref, bf16[1808,512]{1,0:T(8,128)(2,1)S(1)} %get-tuple-element.53.chosen_ref, f32[8,1536]{1,0:T(8,128)S(1)} %get-tuple-element.54.norm_ref, ...), custom_call_target="tpu_custom_call", output_to_operand_aliasing={{0}: (5, {}), {1}: (6, {})} | custom-call | flops 805306368 | bytes 1572864 | tf_op jit(solution)/shard_map/kernel_block/pallas_call | solution.py:242
  60.0 2.0 %collective-permute-start.12 = (bf16[8,16,256]{2,1,0:T(8,128)(2,1)S(1)}, bf16[8,16,256]{2,1,0:T(8,128)(2,1)S(1)}, u32[]{:S(2)}, u32[]{:S(2)}) collective-permute-start(bf16[8,16,256]{2,1,0:T(8,128)(2,1)S(1)} %fusion.19), channel_id=1, source_target_pairs={{0,16},{4,20},{8,24},{12,28},{16,0},{20,4},{24,8},{28,12},{1,17},{... | collective-permute-start | bytes 196616 | tf_op jit(solution)/shard_map/ppermute | solution.py:364
  63.6 2.4 %collective-permute-done.12 = bf16[8,16,256]{2,1,0:T(8,128)(2,1)S(1)} collective-permute-done((bf16[8,16,256]{2,1,0:T(8,128)(2,1)S(1)}, bf16[8,16,256]{2,1,0:T(8,128)(2,1)S(1)}, u32[]{:S(2)}, u32[]{:S(2)}) %collective-permute-start.12) | collective-permute-done | bytes 65568 | tf_op jit(solution)/shard_map/ppermute | solution.py:364
  67.3 7.4 %all-gather.1 = f32[96,1536]{1,0:T(8,128)S(1)} all-gather(f32[24,1536]{1,0:T(8,128)S(1)} %gradient.1), channel_id=3, replica_groups=mesh['rows'=8,'cent'=4] {'cent'}, dimensions={0}, use_global_device_ids=true | all-gather | bytes 737280 | tf_op jit(solution)/shard_map/all_gather | solution.py:476
  74.7 2.1 %change.3 = (f32[16,1536]{1,0:T(8,128)S(1)}, f32[8,16,256]{2,1,0:T(8,128)S(1)}) custom-call(s32[1]{0:T(128)} %bitcast.3.me_ref, f32[4,24,1536]{2,1,0:T(8,128)S(1)} %bitcast.47, f32[16,1536]{1,0:T(8,128)S(1)} %get-tuple-element.63.coef_ref, bf16[8,256,1536]{2,1,0:T(8,128)(2,1)S(1)} %get-tuple-element.61.k_ref, f32[8,24,256]{2,1,0:T(8,128)S(1)} %get-tuple-element.49.side_ref, ...), custom_call_target="tpu_custom_call" | custom-call | flops 100663296 | bytes 6291456 | tf_op jit(solution)/shard_map/change/pallas_call | solution.py:290
  77.6 1.8 %collective-permute-start.14 = (f32[2,16,256]{2,1,0:T(8,128)S(1)}, f32[2,16,256]{2,1,0:T(8,128)S(1)}, u32[]{:S(2)}, u32[]{:S(2)}) collective-permute-start(f32[2,16,256]{2,1,0:T(8,128)S(1)} %get-tuple-element.71), channel_id=1, source_target_pairs={{0,8},{4,12},{8,0},{12,4},{16,24},{20,28},{24,16},{28,20},{1,9},{5... | collective-permute-start | bytes 98312 | tf_op jit(solution)/shard_map/ppermute | solution.py:364
  80.4 2.0 %scatter.2.coef_ref = f32[16,4096]{1,0:T(8,128)S(1)} custom-call(s32[2,17]{1,0:T(2,128)S(1)} %pad.8.off_ref, s32[2,32,128]{2,1,0:T(8,128)S(1)} %select_convert_fusion.dest_ref, f32[16,4096]{1,0:T(8,128)S(1)} %copy-done.1, f32[16,1536]{1,0:T(8,128)S(1)} %get-tuple-element.65.delta_ref), custom_call_target="tpu_custom_call" | custom-call | flops 1000000000 | bytes 1000000 | tf_op jit(solution)/shard_map/scatter/pallas_call | solution.py:350
  84.8 2.7 %scatter.3 = f32[16,4096]{1,0:T(8,128)} custom-call(s32[2,17]{1,0:T(2,128)S(1)} %pad.8.off_ref, s32[2,32,128]{2,1,0:T(8,128)S(1)} %select_convert_fusion.dest_ref, f32[16,4096]{1,0:T(8,128)S(1)} %scatter.2.coef_ref, f32[16,1536]{1,0:T(8,128)S(1)} %get-tuple-element.66.delta_ref), custom_call_target="tpu_custom_call" | custom-call | flops 1000000000 | bytes 1000000 | tf_op jit(solution)/shard_map/scatter/pallas_call | solution.py:350
  88.2 5.2 %all_gather.19 = f32[4,16,256]{2,1,0:T(8,128)S(1)} all-gather(f32[1,16,256]{2,1,0:T(8,128)S(1)} %fusion.14), channel_id=1, replica_groups=mesh['rows'=8,'cent'=4] {'cent'}, dimensions={0}, use_global_device_ids=true | all-gather | bytes 81920 | tf_op jit(solution)/shard_map/all_gather | solution.py:496
  (63 shorter events, 22.9 us)
Async XLA Ops:
  0.6 3.0 %copy-start = (bf16[1024,512]{1,0:T(8,128)(2,1)S(1)}, bf16[1024,512]{1,0:T(8,128)(2,1)}, u32[]{:S(2)}) copy-start(bf16[1024,512]{1,0:T(8,128)(2,1)} %param.7) | copy-start | bytes 3145732
  2.3 2.1 %collective-permute-start = (bf16[2,32,128]{2,1,0:T(8,128)(2,1)S(1)}, bf16[2,32,128]{2,1,0:T(8,128)(2,1)S(1)}, u32[]{:S(2)}, u32[]{:S(2)}) collective-permute-start(bf16[2,32,128]{2,1,0:T(8,128)(2,1)S(1)} %fusion.2), channel_id=1, source_target_pairs={{0,1},{1,0},{2,3},{3,2},{4,5},{5,4},{6,7},{7,6},{8,9},{9,8},{10,11... | collective-permute-start | bytes 49160 | tf_op jit(solution)/shard_map/ppermute | solution.py:364
  4.4 8.3 %collective-permute-start.1 = (bf16[2,32,128]{2,1,0:T(8,128)(2,1)S(1)}, bf16[2,32,128]{2,1,0:T(8,128)(2,1)S(1)}, u32[]{:S(2)}, u32[]{:S(2)}) collective-permute-start(bf16[2,32,128]{2,1,0:T(8,128)(2,1)S(1)} %add.66), channel_id=1, source_target_pairs={{0,2},{1,3},{2,0},{3,1},{4,6},{5,7},{6,4},{7,5},{8,10},{9,11},{10,... | collective-permute-start | bytes 49160 | tf_op jit(solution)/shard_map/ppermute | solution.py:364
  7.0 18.2 %collective-permute-start.2 = (bf16[272,512]{1,0:T(8,128)(2,1)S(1)}, bf16[272,512]{1,0:T(8,128)(2,1)S(1)}, u32[]{:S(2)}, u32[]{:S(2)}) collective-permute-start(bf16[272,512]{1,0:T(8,128)(2,1)S(1)} %maximum_maximum_fusion.refs_0_), channel_id=1, source_target_pairs={{0,4},{4,0},{8,12},{12,8},{16,20},{20,16},{24,28},{28,24},{1,5},{5... | collective-permute-start | bytes 835592 | tf_op jit(solution)/shard_map/ppermute | solution.py:364
  8.6 15.5 %collective-permute-start.4 = (bf16[272,512]{1,0:T(8,128)(2,1)S(1)}, bf16[272,512]{1,0:T(8,128)(2,1)S(1)}, u32[]{:S(2)}, u32[]{:S(2)}) collective-permute-start(bf16[272,512]{1,0:T(8,128)(2,1)S(1)} %maximum_maximum_fusion.refs_0_), channel_id=1, source_target_pairs={{0,16},{4,20},{8,24},{12,28},{16,0},{20,4},{24,8},{28,12},{1,17},{... | collective-permute-start | bytes 835592 | tf_op jit(solution)/shard_map/ppermute | solution.py:364
  11.2 24.5 %collective-permute-start.8 = (bf16[272,512]{1,0:T(8,128)(2,1)S(1)}, bf16[272,512]{1,0:T(8,128)(2,1)S(1)}, u32[]{:S(2)}, u32[]{:S(2)}) collective-permute-start(bf16[272,512]{1,0:T(8,128)(2,1)S(1)} %maximum_maximum_fusion.refs_0_), channel_id=1, source_target_pairs={{0,8},{4,12},{8,0},{12,4},{16,24},{20,28},{24,16},{28,20},{1,9},{5... | collective-permute-start | bytes 835592 | tf_op jit(solution)/shard_map/ppermute | solution.py:364
  24.1 9.5 %collective-permute-start.5 = (bf16[272,512]{1,0:T(8,128)(2,1)S(1)}, bf16[272,512]{1,0:T(8,128)(2,1)S(1)}, u32[]{:S(2)}, u32[]{:S(2)}) collective-permute-start(bf16[272,512]{1,0:T(8,128)(2,1)S(1)} %collective-permute-done.4.refs_1_), channel_id=1, source_target_pairs={{0,8},{4,12},{8,0},{12,4},{16,24},{20,28},{24,16},{28,20},{1,9},{5... | collective-permute-start | bytes 835592 | tf_op jit(solution)/shard_map/ppermute | solution.py:364
  24.7 14.7 %collective-permute-start.7 = (bf16[272,512]{1,0:T(8,128)(2,1)S(1)}, bf16[272,512]{1,0:T(8,128)(2,1)S(1)}, u32[]{:S(2)}, u32[]{:S(2)}) collective-permute-start(bf16[272,512]{1,0:T(8,128)(2,1)S(1)} %broadcast_add_fusion), channel_id=1, source_target_pairs={{0,4},{4,0},{8,12},{12,8},{16,20},{20,16},{24,28},{28,24},{1,5},{5... | collective-permute-start | bytes 835592 | tf_op jit(solution)/shard_map/ppermute | solution.py:364
  25.2 16.2 %collective-permute-start.3 = (bf16[272,512]{1,0:T(8,128)(2,1)S(1)}, bf16[272,512]{1,0:T(8,128)(2,1)S(1)}, u32[]{:S(2)}, u32[]{:S(2)}) collective-permute-start(bf16[272,512]{1,0:T(8,128)(2,1)S(1)} %collective-permute-done.2.refs_1_), channel_id=1, source_target_pairs={{0,8},{4,12},{8,0},{12,4},{16,24},{20,28},{24,16},{28,20},{1,9},{5... | collective-permute-start | bytes 835592 | tf_op jit(solution)/shard_map/ppermute | solution.py:364
  33.6 7.9 %collective-permute-start.6 = (bf16[272,512]{1,0:T(8,128)(2,1)S(1)}, bf16[272,512]{1,0:T(8,128)(2,1)S(1)}, u32[]{:S(2)}, u32[]{:S(2)}) collective-permute-start(bf16[272,512]{1,0:T(8,128)(2,1)S(1)} %collective-permute-done.5.refs_1_), channel_id=1, source_target_pairs={{0,4},{4,0},{8,12},{12,8},{16,20},{20,16},{24,28},{28,24},{1,5},{5... | collective-permute-start | bytes 835592 | tf_op jit(solution)/shard_map/ppermute | solution.py:364
  52.7 5.9 %collective-permute-start.11 = (bf16[8,16,256]{2,1,0:T(8,128)(2,1)S(1)}, bf16[8,16,256]{2,1,0:T(8,128)(2,1)S(1)}, u32[]{:S(2)}, u32[]{:S(2)}) collective-permute-start(bf16[8,16,256]{2,1,0:T(8,128)(2,1)S(1)} %convert_element_type.69), channel_id=1, source_target_pairs={{0,12},{4,8},{8,4},{12,0},{16,28},{20,24},{24,20},{28,16},{1,13},{... | collective-permute-start | bytes 196616 | tf_op jit(solution)/shard_map/ppermute | solution.py:364
  54.3 5.2 %collective-permute-start.10 = (bf16[8,16,256]{2,1,0:T(8,128)(2,1)S(1)}, bf16[8,16,256]{2,1,0:T(8,128)(2,1)S(1)}, u32[]{:S(2)}, u32[]{:S(2)}) collective-permute-start(bf16[8,16,256]{2,1,0:T(8,128)(2,1)S(1)} %convert_element_type.69), channel_id=1, source_target_pairs={{0,8},{4,12},{8,0},{12,4},{16,24},{20,28},{24,16},{28,20},{1,9},{5... | collective-permute-start | bytes 196616 | tf_op jit(solution)/shard_map/ppermute | solution.py:364
  55.7 4.3 %collective-permute-start.9 = (bf16[8,16,256]{2,1,0:T(8,128)(2,1)S(1)}, bf16[8,16,256]{2,1,0:T(8,128)(2,1)S(1)}, u32[]{:S(2)}, u32[]{:S(2)}) collective-permute-start(bf16[8,16,256]{2,1,0:T(8,128)(2,1)S(1)} %convert_element_type.69), channel_id=1, source_target_pairs={{0,4},{4,0},{8,12},{12,8},{16,20},{20,16},{24,28},{28,24},{1,5},{5... | collective-permute-start | bytes 196616 | tf_op jit(solution)/shard_map/ppermute | solution.py:364
  60.0 5.9 %collective-permute-start.12 = (bf16[8,16,256]{2,1,0:T(8,128)(2,1)S(1)}, bf16[8,16,256]{2,1,0:T(8,128)(2,1)S(1)}, u32[]{:S(2)}, u32[]{:S(2)}) collective-permute-start(bf16[8,16,256]{2,1,0:T(8,128)(2,1)S(1)} %fusion.19), channel_id=1, source_target_pairs={{0,16},{4,20},{8,24},{12,28},{16,0},{20,4},{24,8},{28,12},{1,17},{... | collective-permute-start | bytes 196616 | tf_op jit(solution)/shard_map/ppermute | solution.py:364
  66.0 14.4 %copy-start.1 = (f32[16,4096]{1,0:T(8,128)S(1)}, f32[16,4096]{1,0:T(8,128)}, u32[]{:S(2)}) copy-start(f32[16,4096]{1,0:T(8,128)} %coef_ref.1) | copy-start | bytes 786436
  74.7 18.7 %copy-start.2 = (f32[16,1024]{1,0:T(8,128)S(1)}, f32[16,1024]{1,0:T(8,128)}, u32[]{:S(2)}) copy-start(f32[16,1024]{1,0:T(8,128)} %param.10) | copy-start | bytes 196612
  76.8 5.6 %collective-permute-start.15 = (f32[2,16,256]{2,1,0:T(8,128)S(1)}, f32[2,16,256]{2,1,0:T(8,128)S(1)}, u32[]{:S(2)}, u32[]{:S(2)}) collective-permute-start(f32[2,16,256]{2,1,0:T(8,128)S(1)} %get-tuple-element.72), channel_id=1, source_target_pairs={{0,12},{4,8},{8,4},{12,0},{16,28},{20,24},{24,20},{28,16},{1,13},{... | collective-permute-start | bytes 98312 | tf_op jit(solution)/shard_map/ppermute | solution.py:364
  77.6 4.8 %collective-permute-start.14 = (f32[2,16,256]{2,1,0:T(8,128)S(1)}, f32[2,16,256]{2,1,0:T(8,128)S(1)}, u32[]{:S(2)}, u32[]{:S(2)}) collective-permute-start(f32[2,16,256]{2,1,0:T(8,128)S(1)} %get-tuple-element.71), channel_id=1, source_target_pairs={{0,8},{4,12},{8,0},{12,4},{16,24},{20,28},{24,16},{28,20},{1,9},{5... | collective-permute-start | bytes 98312 | tf_op jit(solution)/shard_map/ppermute | solution.py:364
  79.4 3.9 %collective-permute-start.13 = (f32[2,16,256]{2,1,0:T(8,128)S(1)}, f32[2,16,256]{2,1,0:T(8,128)S(1)}, u32[]{:S(2)}, u32[]{:S(2)}) collective-permute-start(f32[2,16,256]{2,1,0:T(8,128)S(1)} %get-tuple-element.70), channel_id=1, source_target_pairs={{0,4},{4,0},{8,12},{12,8},{16,20},{20,16},{24,28},{28,24},{1,5},{5... | collective-permute-start | bytes 98312 | tf_op jit(solution)/shard_map/ppermute | solution.py:364
  83.4 4.8 %collective-permute-start.16 = (f32[1,16,256]{2,1,0:T(8,128)S(1)}, f32[1,16,256]{2,1,0:T(8,128)S(1)}, u32[]{:S(2)}, u32[]{:S(2)}) collective-permute-start(f32[1,16,256]{2,1,0:T(8,128)S(1)} %slice_bitcast_fusion.4), channel_id=1, source_target_pairs={{0,16},{4,20},{8,24},{12,28},{16,0},{20,4},{24,8},{28,12},{1,17},{... | collective-permute-start | bytes 49160 | tf_op jit(solution)/shard_map/ppermute | solution.py:364

commit v9 on v8

--- a/solution.py
+++ b/solution.py
@@ -80,7 +80,7 @@
     if loads:
         coefs_copy = pltpu.make_async_copy(coefs_hbm, coefs_ref, coefs_arrived)
         coefs_copy.start()
-        for block in range(blocks):
+        for block in range(8):
             fetch(block).start()
     widest = 0
     for block in range(blocks):
@@ -112,6 +112,12 @@
         @pl.loop(0, blocks // 4)
         def _(four):
             if loads:
+
+                @pl.when(four + 2 < blocks // 4)
+                def _():
+                    for i in range(4):
+                        fetch(4 * four + 8 + i).start()
+
                 for i in range(4):
                     fetch(4 * four + i).wait()
             for i in range(4):
@@ -119,6 +125,10 @@
 
     @pl.when(jnp.logical_not(narrow))
     def _():
+        if loads:
+            for block in range(8, blocks):
+                fetch(block).start()
+
         @pl.loop(0, blocks)
         def _(block):
             if loads:

time: 94.3 us -> 94.3 us (level)
  no operation moved by 1% of the time
where the time goes in v9:
time: 94.3 us; the launch traced here: 94 us
  Pallas kernels  33.9 us (36%)
  starting transfers between devices  22.5 us (24%)
  blocking collectives  19.5 us (21%)
  waiting for transfers between devices  12.5 us (13%)
  other arithmetic  3.35 us (4%)
  matrix products  0.95 us (1%)
    ppermute x17, starting transfers between devices, swap(): return lax.ppermute(value, axis, [(i, i ^ bit) for i in range(count)])  22.5 us
    pallas_call x8, Pallas kernels, block_call(): pl.pallas_call(functools.partial(block_kernel, first_step, targets, quart...  14.6 us
    all_gather x2, blocking collectives, local(): lax.all_gather(sums, 'cent')  14.3 us
    ppermute x17, waiting for transfers between devices, swap(): return lax.ppermute(value, axis, [(i, i ^ bit) for i in range(count)])  12.5 us
    pallas_call x2, Pallas kernels, compact(): pl.pallas_call(functools.partial(compact_kernel, step, per_step, targets)...  9.09 us
    all_gather x1, blocking collectives, local(): full = lax.all_gather(own_change, 'cent')  5.22 us
    pallas_call x2, Pallas kernels, scatter_call(): pl.pallas_call(functools.partial(scatter_kernel, targets, step), name='sc...  4.69 us
    pallas_call x2, Pallas kernels, change_call(): pl.pallas_call(functools.partial(change_kernel, targets, before is None,...  4.21 us
  transfers between devices with their start and end apart: 17, of which 8 were waited for; matrix products, arithmetic and copies ran while one was open for 2% of the time, Pallas kernels for 28%

profile of v9, /device:TPU:0, one launch (start us, length us, event | category | flops | bytes accessed | tf_op | source)
XLA Modules:
  0.0 94.0 jit_solution(10961894192652761170)
XLA Ops:
  4.4 2.6 %collective-permute-start.1 = (bf16[2,32,128]{2,1,0:T(8,128)(2,1)S(1)}, bf16[2,32,128]{2,1,0:T(8,128)(2,1)S(1)}, u32[]{:S(2)}, u32[]{:S(2)}) collective-permute-start(bf16[2,32,128]{2,1,0:T(8,128)(2,1)S(1)} %add.66), channel_id=1, source_target_pairs={{0,2},{1,3},{2,0},{3,1},{4,6},{5,7},{6,4},{7,5},{8,10},{9,11},{10,... | collective-permute-start | bytes 49160 | tf_op jit(solution)/shard_map/ppermute | solution.py:374
  7.0 1.6 %collective-permute-start.2 = (bf16[272,512]{1,0:T(8,128)(2,1)S(1)}, bf16[272,512]{1,0:T(8,128)(2,1)S(1)}, u32[]{:S(2)}, u32[]{:S(2)}) collective-permute-start(bf16[272,512]{1,0:T(8,128)(2,1)S(1)} %maximum_maximum_fusion.refs_0_), channel_id=1, source_target_pairs={{0,4},{4,0},{8,12},{12,8},{16,20},{20,16},{24,28},{28,24},{1,5},{5... | collective-permute-start | bytes 835592 | tf_op jit(solution)/shard_map/ppermute | solution.py:374
  8.6 2.6 %collective-permute-start.4 = (bf16[272,512]{1,0:T(8,128)(2,1)S(1)}, bf16[272,512]{1,0:T(8,128)(2,1)S(1)}, u32[]{:S(2)}, u32[]{:S(2)}) collective-permute-start(bf16[272,512]{1,0:T(8,128)(2,1)S(1)} %maximum_maximum_fusion.refs_0_), channel_id=1, source_target_pairs={{0,16},{4,20},{8,24},{12,28},{16,0},{20,4},{24,8},{28,12},{1,17},{... | collective-permute-start | bytes 835592 | tf_op jit(solution)/shard_map/ppermute | solution.py:374
  11.2 1.6 %collective-permute-start.8 = (bf16[272,512]{1,0:T(8,128)(2,1)S(1)}, bf16[272,512]{1,0:T(8,128)(2,1)S(1)}, u32[]{:S(2)}, u32[]{:S(2)}) collective-permute-start(bf16[272,512]{1,0:T(8,128)(2,1)S(1)} %maximum_maximum_fusion.refs_0_), channel_id=1, source_target_pairs={{0,8},{4,12},{8,0},{12,4},{16,24},{20,28},{24,16},{28,20},{1,9},{5... | collective-permute-start | bytes 835592 | tf_op jit(solution)/shard_map/ppermute | solution.py:374
  13.4 5.5 %compact.2 = (bf16[1808,512]{1,0:T(8,128)(2,1)S(1)}, f32[8,1536]{1,0:T(8,128)S(1)}, f32[16,1536]{1,0:T(8,128)S(1)}, bf16[4096,512]{1,0:T(8,128)(2,1)S(1)}, bf16[128,4096]{1,0:T(8,128)(2,1)S(1)}) custom-call(s32[2,17]{1,0:T(2,128)S(1)} %pad.8.off_ref, s32[2,32,128]{2,1,0:T(8,128)S(1)} %select_convert_fusion.dest_ref, bf16[4096,512]{1,0:T(8,128)(2,1)} %refs_0_.1, ...), custom_call_target="tpu_custom_call" | custom-call | flops 2000000000 | bytes 6000000 | tf_op jit(solution)/shard_map/compact/pallas_call | solution.py:177
  19.0 3.6 %compact.3 = (bf16[1808,512]{1,0:T(8,128)(2,1)S(1)}, f32[8,1536]{1,0:T(8,128)S(1)}, f32[16,1536]{1,0:T(8,128)S(1)}) custom-call(s32[2,17]{1,0:T(2,128)S(1)} %pad.8.off_ref, s32[2,32,128]{2,1,0:T(8,128)S(1)} %select_convert_fusion.dest_ref, bf16[4096,512]{1,0:T(8,128)(2,1)S(1)} %get-tuple-element.51.refs_0_, bf16[128,4096]{1,0:T(8,128)(2,1)S(1)} %get-tuple-element.52.refs_1_), custom_call_target="tpu_custom_call" | custom-call | flops 2000000000 | bytes 6000000 | tf_op jit(solution)/shard_map/compact/pallas_call | solution.py:177
  26.7 2.1 %kernel_block.8 = (bf16[8,256,1536]{2,1,0:T(8,128)(2,1)S(1)}, f32[24,1536]{1,0:T(8,128)S(1)}, f32[8,24,256]{2,1,0:T(8,128)S(1)}) custom-call(s32[1]{0:T(128)} %bitcast.3.me_ref, bf16[1808,512]{1,0:T(8,128)(2,1)S(1)} %get-tuple-element.35.chosen_ref, f32[8,1536]{1,0:T(8,128)S(1)} %get-tuple-element.36.norm_ref, ...), custom_call_target="tpu_custom_call" | custom-call | flops 805306368 | bytes 1572864 | tf_op jit(solution)/shard_map/kernel_block/pallas_call | solution.py:252
  28.8 4.8 %collective-permute-done.5.refs_1_ = bf16[272,512]{1,0:T(8,128)(2,1)S(1)} collective-permute-done((bf16[272,512]{1,0:T(8,128)(2,1)S(1)}, bf16[272,512]{1,0:T(8,128)(2,1)S(1)}, u32[]{:S(2)}, u32[]{:S(2)}) %collective-permute-start.5) | collective-permute-done | bytes 278560 | tf_op jit(solution)/shard_map/ppermute | solution.py:374
  34.1 1.6 %kernel_block.12 = (bf16[8,256,1536]{2,1,0:T(8,128)(2,1)S(1)}, f32[8,1536]{1,0:T(8,128)S(1)}) custom-call(s32[1]{0:T(128)} %bitcast.3.me_ref, bf16[1808,512]{1,0:T(8,128)(2,1)S(1)} %get-tuple-element.53.chosen_ref, f32[8,1536]{1,0:T(8,128)S(1)} %get-tuple-element.54.norm_ref, bf16[272,512]{1,0:T(8,128)(2,1)S(1)} %maximum_maximum_fusion.refs_0_, ...), custom_call_target="tpu_custom_call" | custom-call | flops 805306368 | bytes 1572864 | tf_op jit(solution)/shard_map/kernel_block/pallas_call | solution.py:252
  37.2 2.1 %kernel_block.9 = (bf16[8,256,1536]{2,1,0:T(8,128)(2,1)S(1)}, f32[24,1536]{1,0:T(8,128)S(1)}, f32[8,24,256]{2,1,0:T(8,128)S(1)}) custom-call(s32[1]{0:T(128)} %bitcast.3.me_ref, bf16[1808,512]{1,0:T(8,128)(2,1)S(1)} %get-tuple-element.35.chosen_ref, ...), custom_call_target="tpu_custom_call", output_to_operand_aliasing={{0}: (5, {}), {1}: (6, {}), {2}: (7, {})} | custom-call | flops 805306368 | bytes 1572864 | tf_op jit(solution)/shard_map/kernel_block/pallas_call | solution.py:252
  39.3 2.1 %kernel_block.10 = (bf16[8,256,1536]{2,1,0:T(8,128)(2,1)S(1)}, f32[24,1536]{1,0:T(8,128)S(1)}, f32[8,24,256]{2,1,0:T(8,128)S(1)}) custom-call(s32[1]{0:T(128)} %bitcast.3.me_ref, bf16[1808,512]{1,0:T(8,128)(2,1)S(1)} %get-tuple-element.35.chosen_ref, ...), custom_call_target="tpu_custom_call", output_to_operand_aliasing={{0}: (5, {}), {1}: (6, {}), {2}: (7, {})} | custom-call | flops 805306368 | bytes 1572864 | tf_op jit(solution)/shard_map/kernel_block/pallas_call | solution.py:252
  41.5 2.1 %kernel_block.11 = (bf16[8,256,1536]{2,1,0:T(8,128)(2,1)S(1)}, f32[24,1536]{1,0:T(8,128)S(1)}, f32[8,24,256]{2,1,0:T(8,128)S(1)}) custom-call(s32[1]{0:T(128)} %bitcast.3.me_ref, bf16[1808,512]{1,0:T(8,128)(2,1)S(1)} %get-tuple-element.35.chosen_ref, ...), custom_call_target="tpu_custom_call", output_to_operand_aliasing={{0}: (5, {}), {1}: (6, {}), {2}: (7, {})} | custom-call | flops 805306368 | bytes 1572864 | tf_op jit(solution)/shard_map/kernel_block/pallas_call | solution.py:252
  43.6 6.9 %all-gather = f32[96,1536]{1,0:T(8,128)S(1)} all-gather(f32[24,1536]{1,0:T(8,128)S(1)} %get-tuple-element.46), channel_id=2, replica_groups=mesh['rows'=8,'cent'=4] {'cent'}, dimensions={0}, use_global_device_ids=true | all-gather | bytes 737280 | tf_op jit(solution)/shard_map/all_gather | solution.py:486
  50.5 2.1 %change.2 = (f32[16,1536]{1,0:T(8,128)S(1)}, f32[8,16,256]{2,1,0:T(8,128)S(1)}, f32[8,16,256]{2,1,0:T(8,128)S(1)}) custom-call(s32[1]{0:T(128)} %bitcast.3.me_ref, f32[4,24,1536]{2,1,0:T(8,128)S(1)} %bitcast.46, f32[16,1536]{1,0:T(8,128)S(1)} %get-tuple-element.47.coef_ref, bf16[8,256,1536]{2,1,0:T(8,128)(2,1)S(1)} %get-tuple-element.48.k_ref, ...), custom_call_target="tpu_custom_call" | custom-call | flops 100663296 | bytes 6291456 | tf_op jit(solution)/shard_map/change/pallas_call | solution.py:300
  52.7 1.6 %collective-permute-start.11 = (bf16[8,16,256]{2,1,0:T(8,128)(2,1)S(1)}, bf16[8,16,256]{2,1,0:T(8,128)(2,1)S(1)}, u32[]{:S(2)}, u32[]{:S(2)}) collective-permute-start(bf16[8,16,256]{2,1,0:T(8,128)(2,1)S(1)} %convert_element_type.69), channel_id=1, source_target_pairs={{0,12},{4,8},{8,4},{12,0},{16,28},{20,24},{24,20},{28,16},{1,13},{... | collective-permute-start | bytes 196616 | tf_op jit(solution)/shard_map/ppermute | solution.py:374
  56.2 1.5 %kernel_block.14 = (bf16[8,256,1536]{2,1,0:T(8,128)(2,1)S(1)}, f32[8,1536]{1,0:T(8,128)S(1)}) custom-call(s32[1]{0:T(128)} %bitcast.3.me_ref, bf16[1808,512]{1,0:T(8,128)(2,1)S(1)} %get-tuple-element.53.chosen_ref, f32[8,1536]{1,0:T(8,128)S(1)} %get-tuple-element.54.norm_ref, ...), custom_call_target="tpu_custom_call", output_to_operand_aliasing={{0}: (5, {}), {1}: (6, {})} | custom-call | flops 805306368 | bytes 1572864 | tf_op jit(solution)/shard_map/kernel_block/pallas_call | solution.py:252
  60.0 2.0 %collective-permute-start.12 = (bf16[8,16,256]{2,1,0:T(8,128)(2,1)S(1)}, bf16[8,16,256]{2,1,0:T(8,128)(2,1)S(1)}, u32[]{:S(2)}, u32[]{:S(2)}) collective-permute-start(bf16[8,16,256]{2,1,0:T(8,128)(2,1)S(1)} %fusion.19), channel_id=1, source_target_pairs={{0,16},{4,20},{8,24},{12,28},{16,0},{20,4},{24,8},{28,12},{1,17},{... | collective-permute-start | bytes 196616 | tf_op jit(solution)/shard_map/ppermute | solution.py:374
  63.6 2.4 %collective-permute-done.12 = bf16[8,16,256]{2,1,0:T(8,128)(2,1)S(1)} collective-permute-done((bf16[8,16,256]{2,1,0:T(8,128)(2,1)S(1)}, bf16[8,16,256]{2,1,0:T(8,128)(2,1)S(1)}, u32[]{:S(2)}, u32[]{:S(2)}) %collective-permute-start.12) | collective-permute-done | bytes 65568 | tf_op jit(solution)/shard_map/ppermute | solution.py:374
  67.3 7.4 %all-gather.1 = f32[96,1536]{1,0:T(8,128)S(1)} all-gather(f32[24,1536]{1,0:T(8,128)S(1)} %gradient.1), channel_id=3, replica_groups=mesh['rows'=8,'cent'=4] {'cent'}, dimensions={0}, use_global_device_ids=true | all-gather | bytes 737280 | tf_op jit(solution)/shard_map/all_gather | solution.py:486
  74.7 2.1 %change.3 = (f32[16,1536]{1,0:T(8,128)S(1)}, f32[8,16,256]{2,1,0:T(8,128)S(1)}) custom-call(s32[1]{0:T(128)} %bitcast.3.me_ref, f32[4,24,1536]{2,1,0:T(8,128)S(1)} %bitcast.47, f32[16,1536]{1,0:T(8,128)S(1)} %get-tuple-element.63.coef_ref, bf16[8,256,1536]{2,1,0:T(8,128)(2,1)S(1)} %get-tuple-element.61.k_ref, f32[8,24,256]{2,1,0:T(8,128)S(1)} %get-tuple-element.49.side_ref, ...), custom_call_target="tpu_custom_call" | custom-call | flops 100663296 | bytes 6291456 | tf_op jit(solution)/shard_map/change/pallas_call | solution.py:300
  77.6 1.8 %collective-permute-start.14 = (f32[2,16,256]{2,1,0:T(8,128)S(1)}, f32[2,16,256]{2,1,0:T(8,128)S(1)}, u32[]{:S(2)}, u32[]{:S(2)}) collective-permute-start(f32[2,16,256]{2,1,0:T(8,128)S(1)} %get-tuple-element.71), channel_id=1, source_target_pairs={{0,8},{4,12},{8,0},{12,4},{16,24},{20,28},{24,16},{28,20},{1,9},{5... | collective-permute-start | bytes 98312 | tf_op jit(solution)/shard_map/ppermute | solution.py:374
  80.4 2.0 %scatter.2.coef_ref = f32[16,4096]{1,0:T(8,128)S(1)} custom-call(s32[2,17]{1,0:T(2,128)S(1)} %pad.8.off_ref, s32[2,32,128]{2,1,0:T(8,128)S(1)} %select_convert_fusion.dest_ref, f32[16,4096]{1,0:T(8,128)S(1)} %copy-done.1, f32[16,1536]{1,0:T(8,128)S(1)} %get-tuple-element.65.delta_ref), custom_call_target="tpu_custom_call" | custom-call | flops 1000000000 | bytes 1000000 | tf_op jit(solution)/shard_map/scatter/pallas_call | solution.py:360
  84.8 2.7 %scatter.3 = f32[16,4096]{1,0:T(8,128)} custom-call(s32[2,17]{1,0:T(2,128)S(1)} %pad.8.off_ref, s32[2,32,128]{2,1,0:T(8,128)S(1)} %select_convert_fusion.dest_ref, f32[16,4096]{1,0:T(8,128)S(1)} %scatter.2.coef_ref, f32[16,1536]{1,0:T(8,128)S(1)} %get-tuple-element.66.delta_ref), custom_call_target="tpu_custom_call" | custom-call | flops 1000000000 | bytes 1000000 | tf_op jit(solution)/shard_map/scatter/pallas_call | solution.py:360
  88.2 5.2 %all_gather.19 = f32[4,16,256]{2,1,0:T(8,128)S(1)} all-gather(f32[1,16,256]{2,1,0:T(8,128)S(1)} %fusion.14), channel_id=1, replica_groups=mesh['rows'=8,'cent'=4] {'cent'}, dimensions={0}, use_global_device_ids=true | all-gather | bytes 81920 | tf_op jit(solution)/shard_map/all_gather | solution.py:506
  (63 shorter events, 23.1 us)
Async XLA Ops:
  0.6 3.0 %copy-start = (bf16[1024,512]{1,0:T(8,128)(2,1)S(1)}, bf16[1024,512]{1,0:T(8,128)(2,1)}, u32[]{:S(2)}) copy-start(bf16[1024,512]{1,0:T(8,128)(2,1)} %param.7) | copy-start | bytes 3145732
  2.3 2.1 %collective-permute-start = (bf16[2,32,128]{2,1,0:T(8,128)(2,1)S(1)}, bf16[2,32,128]{2,1,0:T(8,128)(2,1)S(1)}, u32[]{:S(2)}, u32[]{:S(2)}) collective-permute-start(bf16[2,32,128]{2,1,0:T(8,128)(2,1)S(1)} %fusion.2), channel_id=1, source_target_pairs={{0,1},{1,0},{2,3},{3,2},{4,5},{5,4},{6,7},{7,6},{8,9},{9,8},{10,11... | collective-permute-start | bytes 49160 | tf_op jit(solution)/shard_map/ppermute | solution.py:374
  4.4 8.3 %collective-permute-start.1 = (bf16[2,32,128]{2,1,0:T(8,128)(2,1)S(1)}, bf16[2,32,128]{2,1,0:T(8,128)(2,1)S(1)}, u32[]{:S(2)}, u32[]{:S(2)}) collective-permute-start(bf16[2,32,128]{2,1,0:T(8,128)(2,1)S(1)} %add.66), channel_id=1, source_target_pairs={{0,2},{1,3},{2,0},{3,1},{4,6},{5,7},{6,4},{7,5},{8,10},{9,11},{10,... | collective-permute-start | bytes 49160 | tf_op jit(solution)/shard_map/ppermute | solution.py:374
  7.0 18.2 %collective-permute-start.2 = (bf16[272,512]{1,0:T(8,128)(2,1)S(1)}, bf16[272,512]{1,0:T(8,128)(2,1)S(1)}, u32[]{:S(2)}, u32[]{:S(2)}) collective-permute-start(bf16[272,512]{1,0:T(8,128)(2,1)S(1)} %maximum_maximum_fusion.refs_0_), channel_id=1, source_target_pairs={{0,4},{4,0},{8,12},{12,8},{16,20},{20,16},{24,28},{28,24},{1,5},{5... | collective-permute-start | bytes 835592 | tf_op jit(solution)/shard_map/ppermute | solution.py:374
  8.6 15.5 %collective-permute-start.4 = (bf16[272,512]{1,0:T(8,128)(2,1)S(1)}, bf16[272,512]{1,0:T(8,128)(2,1)S(1)}, u32[]{:S(2)}, u32[]{:S(2)}) collective-permute-start(bf16[272,512]{1,0:T(8,128)(2,1)S(1)} %maximum_maximum_fusion.refs_0_), channel_id=1, source_target_pairs={{0,16},{4,20},{8,24},{12,28},{16,0},{20,4},{24,8},{28,12},{1,17},{... | collective-permute-start | bytes 835592 | tf_op jit(solution)/shard_map/ppermute | solution.py:374
  11.2 24.5 %collective-permute-start.8 = (bf16[272,512]{1,0:T(8,128)(2,1)S(1)}, bf16[272,512]{1,0:T(8,128)(2,1)S(1)}, u32[]{:S(2)}, u32[]{:S(2)}) collective-permute-start(bf16[272,512]{1,0:T(8,128)(2,1)S(1)} %maximum_maximum_fusion.refs_0_), channel_id=1, source_target_pairs={{0,8},{4,12},{8,0},{12,4},{16,24},{20,28},{24,16},{28,20},{1,9},{5... | collective-permute-start | bytes 835592 | tf_op jit(solution)/shard_map/ppermute | solution.py:374
  24.1 9.5 %collective-permute-start.5 = (bf16[272,512]{1,0:T(8,128)(2,1)S(1)}, bf16[272,512]{1,0:T(8,128)(2,1)S(1)}, u32[]{:S(2)}, u32[]{:S(2)}) collective-permute-start(bf16[272,512]{1,0:T(8,128)(2,1)S(1)} %collective-permute-done.4.refs_1_), channel_id=1, source_target_pairs={{0,8},{4,12},{8,0},{12,4},{16,24},{20,28},{24,16},{28,20},{1,9},{5... | collective-permute-start | bytes 835592 | tf_op jit(solution)/shard_map/ppermute | solution.py:374
  24.7 14.7 %collective-permute-start.7 = (bf16[272,512]{1,0:T(8,128)(2,1)S(1)}, bf16[272,512]{1,0:T(8,128)(2,1)S(1)}, u32[]{:S(2)}, u32[]{:S(2)}) collective-permute-start(bf16[272,512]{1,0:T(8,128)(2,1)S(1)} %broadcast_add_fusion), channel_id=1, source_target_pairs={{0,4},{4,0},{8,12},{12,8},{16,20},{20,16},{24,28},{28,24},{1,5},{5... | collective-permute-start | bytes 835592 | tf_op jit(solution)/shard_map/ppermute | solution.py:374
  25.2 16.2 %collective-permute-start.3 = (bf16[272,512]{1,0:T(8,128)(2,1)S(1)}, bf16[272,512]{1,0:T(8,128)(2,1)S(1)}, u32[]{:S(2)}, u32[]{:S(2)}) collective-permute-start(bf16[272,512]{1,0:T(8,128)(2,1)S(1)} %collective-permute-done.2.refs_1_), channel_id=1, source_target_pairs={{0,8},{4,12},{8,0},{12,4},{16,24},{20,28},{24,16},{28,20},{1,9},{5... | collective-permute-start | bytes 835592 | tf_op jit(solution)/shard_map/ppermute | solution.py:374
  33.6 7.9 %collective-permute-start.6 = (bf16[272,512]{1,0:T(8,128)(2,1)S(1)}, bf16[272,512]{1,0:T(8,128)(2,1)S(1)}, u32[]{:S(2)}, u32[]{:S(2)}) collective-permute-start(bf16[272,512]{1,0:T(8,128)(2,1)S(1)} %collective-permute-done.5.refs_1_), channel_id=1, source_target_pairs={{0,4},{4,0},{8,12},{12,8},{16,20},{20,16},{24,28},{28,24},{1,5},{5... | collective-permute-start | bytes 835592 | tf_op jit(solution)/shard_map/ppermute | solution.py:374
  52.7 5.9 %collective-permute-start.11 = (bf16[8,16,256]{2,1,0:T(8,128)(2,1)S(1)}, bf16[8,16,256]{2,1,0:T(8,128)(2,1)S(1)}, u32[]{:S(2)}, u32[]{:S(2)}) collective-permute-start(bf16[8,16,256]{2,1,0:T(8,128)(2,1)S(1)} %convert_element_type.69), channel_id=1, source_target_pairs={{0,12},{4,8},{8,4},{12,0},{16,28},{20,24},{24,20},{28,16},{1,13},{... | collective-permute-start | bytes 196616 | tf_op jit(solution)/shard_map/ppermute | solution.py:374
  54.3 5.2 %collective-permute-start.10 = (bf16[8,16,256]{2,1,0:T(8,128)(2,1)S(1)}, bf16[8,16,256]{2,1,0:T(8,128)(2,1)S(1)}, u32[]{:S(2)}, u32[]{:S(2)}) collective-permute-start(bf16[8,16,256]{2,1,0:T(8,128)(2,1)S(1)} %convert_element_type.69), channel_id=1, source_target_pairs={{0,8},{4,12},{8,0},{12,4},{16,24},{20,28},{24,16},{28,20},{1,9},{5... | collective-permute-start | bytes 196616 | tf_op jit(solution)/shard_map/ppermute | solution.py:374
  55.7 4.3 %collective-permute-start.9 = (bf16[8,16,256]{2,1,0:T(8,128)(2,1)S(1)}, bf16[8,16,256]{2,1,0:T(8,128)(2,1)S(1)}, u32[]{:S(2)}, u32[]{:S(2)}) collective-permute-start(bf16[8,16,256]{2,1,0:T(8,128)(2,1)S(1)} %convert_element_type.69), channel_id=1, source_target_pairs={{0,4},{4,0},{8,12},{12,8},{16,20},{20,16},{24,28},{28,24},{1,5},{5... | collective-permute-start | bytes 196616 | tf_op jit(solution)/shard_map/ppermute | solution.py:374
  60.0 5.9 %collective-permute-start.12 = (bf16[8,16,256]{2,1,0:T(8,128)(2,1)S(1)}, bf16[8,16,256]{2,1,0:T(8,128)(2,1)S(1)}, u32[]{:S(2)}, u32[]{:S(2)}) collective-permute-start(bf16[8,16,256]{2,1,0:T(8,128)(2,1)S(1)} %fusion.19), channel_id=1, source_target_pairs={{0,16},{4,20},{8,24},{12,28},{16,0},{20,4},{24,8},{28,12},{1,17},{... | collective-permute-start | bytes 196616 | tf_op jit(solution)/shard_map/ppermute | solution.py:374
  66.0 14.4 %copy-start.1 = (f32[16,4096]{1,0:T(8,128)S(1)}, f32[16,4096]{1,0:T(8,128)}, u32[]{:S(2)}) copy-start(f32[16,4096]{1,0:T(8,128)} %coef_ref.1) | copy-start | bytes 786436
  74.7 18.7 %copy-start.2 = (f32[16,1024]{1,0:T(8,128)S(1)}, f32[16,1024]{1,0:T(8,128)}, u32[]{:S(2)}) copy-start(f32[16,1024]{1,0:T(8,128)} %param.10) | copy-start | bytes 196612
  76.8 5.6 %collective-permute-start.15 = (f32[2,16,256]{2,1,0:T(8,128)S(1)}, f32[2,16,256]{2,1,0:T(8,128)S(1)}, u32[]{:S(2)}, u32[]{:S(2)}) collective-permute-start(f32[2,16,256]{2,1,0:T(8,128)S(1)} %get-tuple-element.72), channel_id=1, source_target_pairs={{0,12},{4,8},{8,4},{12,0},{16,28},{20,24},{24,20},{28,16},{1,13},{... | collective-permute-start | bytes 98312 | tf_op jit(solution)/shard_map/ppermute | solution.py:374
  77.6 4.8 %collective-permute-start.14 = (f32[2,16,256]{2,1,0:T(8,128)S(1)}, f32[2,16,256]{2,1,0:T(8,128)S(1)}, u32[]{:S(2)}, u32[]{:S(2)}) collective-permute-start(f32[2,16,256]{2,1,0:T(8,128)S(1)} %get-tuple-element.71), channel_id=1, source_target_pairs={{0,8},{4,12},{8,0},{12,4},{16,24},{20,28},{24,16},{28,20},{1,9},{5... | collective-permute-start | bytes 98312 | tf_op jit(solution)/shard_map/ppermute | solution.py:374
  79.4 3.9 %collective-permute-start.13 = (f32[2,16,256]{2,1,0:T(8,128)S(1)}, f32[2,16,256]{2,1,0:T(8,128)S(1)}, u32[]{:S(2)}, u32[]{:S(2)}) collective-permute-start(f32[2,16,256]{2,1,0:T(8,128)S(1)} %get-tuple-element.70), channel_id=1, source_target_pairs={{0,4},{4,0},{8,12},{12,8},{16,20},{20,16},{24,28},{28,24},{1,5},{5... | collective-permute-start | bytes 98312 | tf_op jit(solution)/shard_map/ppermute | solution.py:374
  83.4 4.8 %collective-permute-start.16 = (f32[1,16,256]{2,1,0:T(8,128)S(1)}, f32[1,16,256]{2,1,0:T(8,128)S(1)}, u32[]{:S(2)}, u32[]{:S(2)}) collective-permute-start(f32[1,16,256]{2,1,0:T(8,128)S(1)} %slice_bitcast_fusion.4), channel_id=1, source_target_pairs={{0,16},{4,20},{8,24},{12,28},{16,0},{20,4},{24,8},{28,12},{1,17},{... | collective-permute-start | bytes 49160 | tf_op jit(solution)/shard_map/ppermute | solution.py:374

commit v10 on v8

--- a/solution.py
+++ b/solution.py
@@ -63,67 +63,101 @@
     return jnp.concatenate([ref[step, pl.ds(row, 1), :], ref[step, pl.ds(row + 1, 1), :]], axis=1)
 
 
+def pool_copy(source, target, half, block, done):
+    at = pl.ds(pl.multiple_of(block * POOL_BLOCK, POOL_BLOCK), POOL_BLOCK)
+    start = half * target.shape[0] + block * POOL_BLOCK
+    start = pl.multiple_of(start, POOL_BLOCK)
+    return pltpu.make_async_copy(source.at[pl.ds(start, POOL_BLOCK), :], target.at[at, :], done.at[block])
+
+
+def load_kernel(targets, pool_hbm, coefs_hbm, pool_ref, parts_ref, coefs_ref, arrived, coefs_arrived):
+    copies = [pool_copy(pool_hbm, pool_ref, 0, block, arrived) for block in range(arrived.shape[0])]
+    coefs_copy = pltpu.make_async_copy(coefs_hbm, coefs_ref, coefs_arrived)
+    coefs_copy.start()
+    for copy in copies:
+        copy.start()
+    coefs_copy.wait()
+    parts_ref[3 * targets :, :] = jnp.zeros((LANES - 3 * targets, parts_ref.shape[1]), BF16)
+    for part, value in enumerate(split3(coefs_ref[...])):
+        parts_ref[part * targets : (part + 1) * targets, :] = value
+    for copy in copies:
+        copy.wait()
+
+
+def load_call(pool, coefs):
+    return pl.pallas_call(
+        functools.partial(load_kernel, coefs.shape[0]),
+        name="load",
+        in_specs=[pl.BlockSpec(memory_space=pltpu.HBM)] * 2,
+        out_specs=in_vmem(2),
+        out_shape=(
+            pltpu.VMEM((pool.shape[0] // 2, pool.shape[1]), BF16),
+            pltpu.VMEM((LANES, pool.shape[0]), BF16),
+        ),
+        scratch_shapes=[
+            pltpu.VMEM(coefs.shape, F32),
+            pltpu.SemaphoreType.DMA((pool.shape[0] // POOL_BLOCK // 2,)),
+            pltpu.SemaphoreType.DMA,
+        ],
+        compiler_params=params(),
+        cost_estimate=pl.CostEstimate(flops=10**6, bytes_accessed=3 * 10**6, transcendentals=0),
+    )(in_hbm(pool), in_hbm(coefs))
+
+
 def compact_kernel(step, per_step, targets, off_ref, dest_ref, *refs):
     loads = step == 0
     if loads:
-        pool_hbm, coefs_hbm, out_ref, norm_ref, coef_ref, pool_ref, parts_ref, side_out, coefs_ref, arrived, coefs_arrived = refs
+        first_ref, parts_ref, pool_hbm, out_ref, norm_ref, coef_ref, second_ref, side_out, arrived = refs
     else:
-        pool_ref, parts_ref, out_ref, norm_ref, coef_ref, side_out = refs
+        first_ref, second_ref, parts_ref, out_ref, norm_ref, coef_ref, side_out = refs
     features = out_ref.shape[1]
-    blocks = pool_ref.shape[0] // POOL_BLOCK
+    half = first_ref.shape[0] // POOL_BLOCK
+    blocks = 2 * half
     tile = math.gcd(per_step, 512)
 
-    def fetch(block):
-        at = pl.ds(pl.multiple_of(block * POOL_BLOCK, POOL_BLOCK), POOL_BLOCK)
-        return pltpu.make_async_copy(pool_hbm.at[at, :], pool_ref.at[at, :], arrived.at[block])
-
     if loads:
-        coefs_copy = pltpu.make_async_copy(coefs_hbm, coefs_ref, coefs_arrived)
-        coefs_copy.start()
-        for block in range(blocks):
-            fetch(block).start()
+        for block in range(half):
+            pool_copy(pool_hbm, second_ref, 1, block, arrived).start()
     widest = 0
     for block in range(blocks):
         widest = jnp.maximum(widest, off_ref[step, block + 1] - (off_ref[step, block] // 16) * 16)
     narrow = widest <= WINDOW
     out_ref[:16, :] = jnp.zeros((16, features), BF16)
     side_out[:16, :] = jnp.zeros((16, LANES), BF16)
-    if loads:
-        coefs_copy.wait()
-        parts_ref[3 * targets :, :] = jnp.zeros((LANES - 3 * targets, parts_ref.shape[1]), BF16)
-        for part, value in enumerate(split3(coefs_ref[...])):
-            parts_ref[part * targets : (part + 1) * targets, :] = value
-
-    def place(block, window):
+
+    def place(pool_ref, part, index, window):
+        block = part * half + index
         base = pl.multiple_of((off_ref[step, block] // 16) * 16, 16)
         dest = two_rows(dest_ref, step, block) - base
         slots = lax.broadcasted_iota(jnp.int32, (window, POOL_BLOCK), 0)
         pick = jnp.where(slots == dest, 1.0, 0.0).astype(BF16)
         at = pl.ds(pl.multiple_of(block * POOL_BLOCK, POOL_BLOCK), POOL_BLOCK)
+        inner = pl.ds(pl.multiple_of(index * POOL_BLOCK, POOL_BLOCK), POOL_BLOCK)
         after = pl.ds(pl.multiple_of(base + 16, 16), window - 16)
-        packed = jnp.dot(pick, pool_ref[at, :], preferred_element_type=F32).astype(BF16)
+        packed = jnp.dot(pick, pool_ref[inner, :], preferred_element_type=F32).astype(BF16)
         side = lax.dot_general(pick, parts_ref[:, at], NT, preferred_element_type=F32).astype(BF16)
         for rows, target in ((packed, out_ref), (side, side_out)):
             target[pl.ds(base, 16), :] += rows[:16]
             target[after, :] = rows[16:]
 
+    def walk(window, width):
+        for part, pool_ref in enumerate((first_ref, second_ref)):
+
+            @pl.loop(0, half // width)
+            def _(group, part=part, pool_ref=pool_ref):
+                if loads and part == 1:
+                    for i in range(width):
+                        pool_copy(pool_hbm, second_ref, 1, width * group + i, arrived).wait()
+                for i in range(width):
+                    place(pool_ref, part, width * group + i, window)
+
     @pl.when(narrow)
     def _():
-        @pl.loop(0, blocks // 4)
-        def _(four):
-            if loads:
-                for i in range(4):
-                    fetch(4 * four + i).wait()
-            for i in range(4):
-                place(4 * four + i, WINDOW)
+        walk(WINDOW, 4)
 
     @pl.when(jnp.logical_not(narrow))
     def _():
-        @pl.loop(0, blocks)
-        def _(block):
-            if loads:
-                fetch(block).wait()
-            place(block, POOL_BLOCK + 16)
+        walk(POOL_BLOCK + 16, 1)
 
     ones = jnp.ones((8, features), BF16)
     eye = lax.broadcasted_iota(jnp.int32, (3 * targets, LANES), 0) == lax.broadcasted_iota(
@@ -143,37 +177,33 @@
         )
 
 
-def compact(step, off, dest, pool, coefs, per_step, targets):
-    features = pool.shape[1]
+def compact(step, off, dest, pool, parts, pool_hbm, per_step, targets):
+    features = pool_hbm.shape[1]
     length = round_up(per_step, 16) + POOL_BLOCK + 16
-    loads = step == 0
     outs = [
         pltpu.VMEM((length, features), BF16),
         pltpu.VMEM((8, per_step), F32),
         pltpu.VMEM((targets, per_step), F32),
     ]
     scratch = [pltpu.VMEM((length, LANES), BF16)]
-    sources = in_vmem(2)
-    operands = [held(pool), held(coefs)]
-    if loads:
-        outs += [pltpu.VMEM(pool.shape, BF16), pltpu.VMEM((LANES, pool.shape[0]), BF16)]
-        scratch += [
-            pltpu.VMEM(coefs.shape, F32),
-            pltpu.SemaphoreType.DMA((pool.shape[0] // POOL_BLOCK,)),
-            pltpu.SemaphoreType.DMA,
-        ]
-        sources = [pl.BlockSpec(memory_space=pltpu.HBM)] * 2
-        operands = [in_hbm(pool), in_hbm(coefs)]
+    operands = [off, dest, *[held(half) for half in pool], held(parts)]
+    specs = [pl.BlockSpec(memory_space=pltpu.SMEM), *in_vmem(len(operands) - 1)]
+    if step == 0:
+        half = pool[0].shape
+        outs.append(pltpu.VMEM(half, BF16))
+        scratch.append(pltpu.SemaphoreType.DMA((half[0] // POOL_BLOCK,)))
+        specs.append(pl.BlockSpec(memory_space=pltpu.HBM))
+        operands.append(in_hbm(pool_hbm))
     return pl.pallas_call(
         functools.partial(compact_kernel, step, per_step, targets),
         name="compact",
-        in_specs=[pl.BlockSpec(memory_space=pltpu.SMEM), *in_vmem(1), *sources],
+        in_specs=specs,
         out_specs=in_vmem(len(outs)),
         out_shape=tuple(outs),
         scratch_shapes=scratch,
         compiler_params=params(),
         cost_estimate=pl.CostEstimate(flops=2 * 10**9, bytes_accessed=6 * 10**6, transcendentals=0),
-    )(off, dest, *operands)
+    )(*operands)
 
 
 def block_kernel(first_step, targets, quarter, group, scale, offset, me_ref, chosen_ref, norm_ref, *refs):
@@ -436,19 +466,21 @@
     row_start = jnp.einsum("hi,sik->shk", before, row_count.astype(BF16), preferred_element_type=F32)
     rank = row_start + running - 1.0
     dest = jnp.where(member > 0, rank, -65536.0).astype(jnp.int32)
-    group_rows = POOL_BLOCK // LANES
-    off = row_start[:, ::group_rows, 0].astype(jnp.int32)
-    off = jnp.pad(off, ((0, 0), (0, 1)), constant_values=per_step)
+    limits = jnp.arange(pool_dev // POOL_BLOCK + 1) * (POOL_BLOCK // LANES)
+    earlier = (limits[:, None] > jnp.arange(high_count)[None, :]).astype(BF16)
+    off = jnp.einsum("bi,sik->sb", earlier, row_count.astype(BF16), preferred_element_type=F32)
+    off = off.astype(jnp.int32)
 
     me = my_row.astype(jnp.int32)[None]
     blocks = []
     own_coefs = []
-    shard = []
+    first_half, parts = load_call(centres, coefs)
+    pool = [first_half]
     for step in range(steps):
         chosen, norm, own_coef, *more = compact(
-            step, off, dest, *((centres, coefs) if step == 0 else shard), per_step, target_count
+            step, off, dest, pool, parts, centres, per_step, target_count
         )
-        shard = more or shard
+        pool += more
         own_coefs.append(own_coef)
         state = None
         for group in groups_of(row_devices, step):

time: 94.3 us -> 93.4 us (level)
    pallas_call x2, Pallas kernels: 9.29 us -> 7.31 us  [compact(): pl.pallas_call(functools.partial(compact_kernel, step, per_step, targets)...]
    pallas_call x0 -> x1, Pallas kernels: none -> 1.7 us  [load_call(): pl.pallas_call(functools.partial(load_kernel, coefs.shape[0]), name='load...]
  transfers between devices with their start and end apart: 17 -> 17, of which waited for: 8 -> 8; matrix products, arithmetic and copies ran while one was open for 2% -> 3% of each run, Pallas kernels for 28% -> 28%
where the time goes in v10:
time: 93.4 us; the launch traced here: 93.1 us
  Pallas kernels  33.8 us (36%)
  starting transfers between devices  21.8 us (23%)
  blocking collectives  19.6 us (21%)
  waiting for transfers between devices  12.2 us (13%)
  other arithmetic  3.36 us (4%)
  matrix products  1.15 us (1%)
    ppermute x17, starting transfers between devices, swap(): return lax.ppermute(value, axis, [(i, i ^ bit) for i in range(count)])  21.8 us
    pallas_call x8, Pallas kernels, block_call(): pl.pallas_call(functools.partial(block_kernel, first_step, targets, quart...  14.6 us
    all_gather x2, blocking collectives, local(): lax.all_gather(sums, 'cent')  14.4 us
    ppermute x17, waiting for transfers between devices, swap(): return lax.ppermute(value, axis, [(i, i ^ bit) for i in range(count)])  12.2 us
    pallas_call x2, Pallas kernels, compact(): pl.pallas_call(functools.partial(compact_kernel, step, per_step, targets)...  7.31 us
    all_gather x1, blocking collectives, local(): full = lax.all_gather(own_change, 'cent')  5.22 us
    pallas_call x2, Pallas kernels, scatter_call(): pl.pallas_call(functools.partial(scatter_kernel, targets, step), name='sc...  4.69 us
    pallas_call x2, Pallas kernels, change_call(): pl.pallas_call(functools.partial(change_kernel, targets, before is None,...  4.21 us
  transfers between devices with their start and end apart: 17, of which 8 were waited for; matrix products, arithmetic and copies ran while one was open for 3% of the time, Pallas kernels for 28%

profile of v10, /device:TPU:0, one launch (start us, length us, event | category | flops | bytes accessed | tf_op | source)
XLA Modules:
  0.0 93.1 jit_solution(16370503057061792205)
XLA Ops:
  4.4 2.6 %collective-permute-start.2 = (bf16[272,512]{1,0:T(8,128)(2,1)S(1)}, bf16[272,512]{1,0:T(8,128)(2,1)S(1)}, u32[]{:S(2)}, u32[]{:S(2)}) collective-permute-start(bf16[272,512]{1,0:T(8,128)(2,1)S(1)} %maximum_maximum_fusion.refs_0_), channel_id=1, source_target_pairs={{0,4},{4,0},{8,12},{12,8},{16,20},{20,16},{24,28},{28,24},{1,5},{5... | collective-permute-start | bytes 835592 | tf_op jit(solution)/shard_map/ppermute | solution.py:394
  7.0 2.6 %collective-permute-start.4 = (bf16[272,512]{1,0:T(8,128)(2,1)S(1)}, bf16[272,512]{1,0:T(8,128)(2,1)S(1)}, u32[]{:S(2)}, u32[]{:S(2)}) collective-permute-start(bf16[272,512]{1,0:T(8,128)(2,1)S(1)} %maximum_maximum_fusion.refs_0_), channel_id=1, source_target_pairs={{0,16},{4,20},{8,24},{12,28},{16,0},{20,4},{24,8},{28,12},{1,17},{... | collective-permute-start | bytes 835592 | tf_op jit(solution)/shard_map/ppermute | solution.py:394
  9.6 1.6 %collective-permute-start.8 = (bf16[272,512]{1,0:T(8,128)(2,1)S(1)}, bf16[272,512]{1,0:T(8,128)(2,1)S(1)}, u32[]{:S(2)}, u32[]{:S(2)}) collective-permute-start(bf16[272,512]{1,0:T(8,128)(2,1)S(1)} %maximum_maximum_fusion.refs_0_), channel_id=1, source_target_pairs={{0,8},{4,12},{8,0},{12,4},{16,24},{20,28},{24,16},{28,20},{1,9},{5... | collective-permute-start | bytes 835592 | tf_op jit(solution)/shard_map/ppermute | solution.py:394
  12.8 1.7 %load.1 = (bf16[2048,512]{1,0:T(8,128)(2,1)S(1)}, bf16[128,4096]{1,0:T(8,128)(2,1)S(1)}) custom-call(bf16[4096,512]{1,0:T(8,128)(2,1)} %refs_2_.1, f32[16,4096]{1,0:T(8,128)} %coef_ref.1), custom_call_target="tpu_custom_call" | custom-call | flops 1000000 | bytes 3000000 | tf_op jit(solution)/shard_map/load/pallas_call | solution.py:88
  15.7 3.7 %compact.2 = (bf16[1808,512]{1,0:T(8,128)(2,1)S(1)}, f32[8,1536]{1,0:T(8,128)S(1)}, f32[16,1536]{1,0:T(8,128)S(1)}, bf16[2048,512]{1,0:T(8,128)(2,1)S(1)}) custom-call(s32[2,17]{1,0:T(2,128)S(1)} %convolution_convert_fusion.off_ref, s32[2,32,128]{2,1,0:T(8,128)S(1)} %select_convert_fusion.dest_ref, bf16[2048,512]{1,0:T(8,128)(2,1)S(1)} %get-tuple-element.36.refs_0_, ...), custom_call_target="tpu_custom_call" | custom-call | flops 2000000000 | bytes 6000000 | tf_op jit(solution)/shard_map/compact/pallas_call | solution.py:197
  19.5 3.6 %compact.3 = (bf16[1808,512]{1,0:T(8,128)(2,1)S(1)}, f32[8,1536]{1,0:T(8,128)S(1)}, f32[16,1536]{1,0:T(8,128)S(1)}) custom-call(s32[2,17]{1,0:T(2,128)S(1)} %convolution_convert_fusion.off_ref, s32[2,32,128]{2,1,0:T(8,128)S(1)} %select_convert_fusion.dest_ref, bf16[2048,512]{1,0:T(8,128)(2,1)S(1)} %get-tuple-element.36.refs_0_, ...), custom_call_target="tpu_custom_call" | custom-call | flops 2000000000 | bytes 6000000 | tf_op jit(solution)/shard_map/compact/pallas_call | solution.py:197
  24.2 1.6 %collective-permute-start.3 = (bf16[272,512]{1,0:T(8,128)(2,1)S(1)}, bf16[272,512]{1,0:T(8,128)(2,1)S(1)}, u32[]{:S(2)}, u32[]{:S(2)}) collective-permute-start(bf16[272,512]{1,0:T(8,128)(2,1)S(1)} %collective-permute-done.2.refs_1_), channel_id=1, source_target_pairs={{0,8},{4,12},{8,0},{12,4},{16,24},{20,28},{24,16},{28,20},{1,9},{5... | collective-permute-start | bytes 835592 | tf_op jit(solution)/shard_map/ppermute | solution.py:394
  25.7 2.1 %kernel_block.8 = (bf16[8,256,1536]{2,1,0:T(8,128)(2,1)S(1)}, f32[24,1536]{1,0:T(8,128)S(1)}, f32[8,24,256]{2,1,0:T(8,128)S(1)}) custom-call(s32[1]{0:T(128)} %bitcast.1.me_ref, bf16[1808,512]{1,0:T(8,128)(2,1)S(1)} %get-tuple-element.38.chosen_ref, f32[8,1536]{1,0:T(8,128)S(1)} %get-tuple-element.39.norm_ref, ...), custom_call_target="tpu_custom_call" | custom-call | flops 805306368 | bytes 1572864 | tf_op jit(solution)/shard_map/kernel_block/pallas_call | solution.py:272
  27.9 4.8 %collective-permute-done.5.refs_1_ = bf16[272,512]{1,0:T(8,128)(2,1)S(1)} collective-permute-done((bf16[272,512]{1,0:T(8,128)(2,1)S(1)}, bf16[272,512]{1,0:T(8,128)(2,1)S(1)}, u32[]{:S(2)}, u32[]{:S(2)}) %collective-permute-start.5) | collective-permute-done | bytes 278560 | tf_op jit(solution)/shard_map/ppermute | solution.py:394
  33.2 1.6 %kernel_block.12 = (bf16[8,256,1536]{2,1,0:T(8,128)(2,1)S(1)}, f32[8,1536]{1,0:T(8,128)S(1)}) custom-call(s32[1]{0:T(128)} %bitcast.1.me_ref, bf16[1808,512]{1,0:T(8,128)(2,1)S(1)} %get-tuple-element.55.chosen_ref, f32[8,1536]{1,0:T(8,128)S(1)} %get-tuple-element.56.norm_ref, bf16[272,512]{1,0:T(8,128)(2,1)S(1)} %maximum_maximum_fusion.refs_0_, ...), custom_call_target="tpu_custom_call" | custom-call | flops 805306368 | bytes 1572864 | tf_op jit(solution)/shard_map/kernel_block/pallas_call | solution.py:272
  36.3 2.1 %kernel_block.9 = (bf16[8,256,1536]{2,1,0:T(8,128)(2,1)S(1)}, f32[24,1536]{1,0:T(8,128)S(1)}, f32[8,24,256]{2,1,0:T(8,128)S(1)}) custom-call(s32[1]{0:T(128)} %bitcast.1.me_ref, bf16[1808,512]{1,0:T(8,128)(2,1)S(1)} %get-tuple-element.38.chosen_ref, ...), custom_call_target="tpu_custom_call", output_to_operand_aliasing={{0}: (5, {}), {1}: (6, {}), {2}: (7, {})} | custom-call | flops 805306368 | bytes 1572864 | tf_op jit(solution)/shard_map/kernel_block/pallas_call | solution.py:272
  38.4 2.1 %kernel_block.10 = (bf16[8,256,1536]{2,1,0:T(8,128)(2,1)S(1)}, f32[24,1536]{1,0:T(8,128)S(1)}, f32[8,24,256]{2,1,0:T(8,128)S(1)}) custom-call(s32[1]{0:T(128)} %bitcast.1.me_ref, bf16[1808,512]{1,0:T(8,128)(2,1)S(1)} %get-tuple-element.38.chosen_ref, ...), custom_call_target="tpu_custom_call", output_to_operand_aliasing={{0}: (5, {}), {1}: (6, {}), {2}: (7, {})} | custom-call | flops 805306368 | bytes 1572864 | tf_op jit(solution)/shard_map/kernel_block/pallas_call | solution.py:272
  40.6 2.1 %kernel_block.11 = (bf16[8,256,1536]{2,1,0:T(8,128)(2,1)S(1)}, f32[24,1536]{1,0:T(8,128)S(1)}, f32[8,24,256]{2,1,0:T(8,128)S(1)}) custom-call(s32[1]{0:T(128)} %bitcast.1.me_ref, bf16[1808,512]{1,0:T(8,128)(2,1)S(1)} %get-tuple-element.38.chosen_ref, ...), custom_call_target="tpu_custom_call", output_to_operand_aliasing={{0}: (5, {}), {1}: (6, {}), {2}: (7, {})} | custom-call | flops 805306368 | bytes 1572864 | tf_op jit(solution)/shard_map/kernel_block/pallas_call | solution.py:272
  42.7 7.7 %all-gather = f32[96,1536]{1,0:T(8,128)S(1)} all-gather(f32[24,1536]{1,0:T(8,128)S(1)} %get-tuple-element.49), channel_id=2, replica_groups=mesh['rows'=8,'cent'=4] {'cent'}, dimensions={0}, use_global_device_ids=true | all-gather | bytes 737280 | tf_op jit(solution)/shard_map/all_gather | solution.py:508
  50.4 2.1 %change.2 = (f32[16,1536]{1,0:T(8,128)S(1)}, f32[8,16,256]{2,1,0:T(8,128)S(1)}, f32[8,16,256]{2,1,0:T(8,128)S(1)}) custom-call(s32[1]{0:T(128)} %bitcast.1.me_ref, f32[4,24,1536]{2,1,0:T(8,128)S(1)} %bitcast.44, f32[16,1536]{1,0:T(8,128)S(1)} %get-tuple-element.50.coef_ref, bf16[8,256,1536]{2,1,0:T(8,128)(2,1)S(1)} %get-tuple-element.51.k_ref, ...), custom_call_target="tpu_custom_call" | custom-call | flops 100663296 | bytes 6291456 | tf_op jit(solution)/shard_map/change/pallas_call | solution.py:320
  54.0 1.6 %collective-permute-start.10 = (bf16[8,16,256]{2,1,0:T(8,128)(2,1)S(1)}, bf16[8,16,256]{2,1,0:T(8,128)(2,1)S(1)}, u32[]{:S(2)}, u32[]{:S(2)}) collective-permute-start(bf16[8,16,256]{2,1,0:T(8,128)(2,1)S(1)} %convert_element_type.68), channel_id=1, source_target_pairs={{0,8},{4,12},{8,0},{12,4},{16,24},{20,28},{24,16},{28,20},{1,9},{5... | collective-permute-start | bytes 196616 | tf_op jit(solution)/shard_map/ppermute | solution.py:394
  59.9 1.6 %collective-permute-start.12 = (bf16[8,16,256]{2,1,0:T(8,128)(2,1)S(1)}, bf16[8,16,256]{2,1,0:T(8,128)(2,1)S(1)}, u32[]{:S(2)}, u32[]{:S(2)}) collective-permute-start(bf16[8,16,256]{2,1,0:T(8,128)(2,1)S(1)} %fusion.19), channel_id=1, source_target_pairs={{0,16},{4,20},{8,24},{12,28},{16,0},{20,4},{24,8},{28,12},{1,17},{... | collective-permute-start | bytes 196616 | tf_op jit(solution)/shard_map/ppermute | solution.py:394
  63.1 2.8 %collective-permute-done.12 = bf16[8,16,256]{2,1,0:T(8,128)(2,1)S(1)} collective-permute-done((bf16[8,16,256]{2,1,0:T(8,128)(2,1)S(1)}, bf16[8,16,256]{2,1,0:T(8,128)(2,1)S(1)}, u32[]{:S(2)}, u32[]{:S(2)}) %collective-permute-start.12) | collective-permute-done | bytes 65568 | tf_op jit(solution)/shard_map/ppermute | solution.py:394
  67.2 6.7 %all-gather.1 = f32[96,1536]{1,0:T(8,128)S(1)} all-gather(f32[24,1536]{1,0:T(8,128)S(1)} %gradient.1), channel_id=3, replica_groups=mesh['rows'=8,'cent'=4] {'cent'}, dimensions={0}, use_global_device_ids=true | all-gather | bytes 737280 | tf_op jit(solution)/shard_map/all_gather | solution.py:508
  73.8 2.1 %change.3 = (f32[16,1536]{1,0:T(8,128)S(1)}, f32[8,16,256]{2,1,0:T(8,128)S(1)}) custom-call(s32[1]{0:T(128)} %bitcast.1.me_ref, f32[4,24,1536]{2,1,0:T(8,128)S(1)} %bitcast.45, f32[16,1536]{1,0:T(8,128)S(1)} %get-tuple-element.65.coef_ref, bf16[8,256,1536]{2,1,0:T(8,128)(2,1)S(1)} %get-tuple-element.63.k_ref, f32[8,24,256]{2,1,0:T(8,128)S(1)} %get-tuple-element.52.side_ref, ...), custom_call_target="tpu_custom_call" | custom-call | flops 100663296 | bytes 6291456 | tf_op jit(solution)/shard_map/change/pallas_call | solution.py:320
  76.4 2.2 %collective-permute-start.14 = (f32[2,16,256]{2,1,0:T(8,128)S(1)}, f32[2,16,256]{2,1,0:T(8,128)S(1)}, u32[]{:S(2)}, u32[]{:S(2)}) collective-permute-start(f32[2,16,256]{2,1,0:T(8,128)S(1)} %get-tuple-element.73), channel_id=1, source_target_pairs={{0,8},{4,12},{8,0},{12,4},{16,24},{20,28},{24,16},{28,20},{1,9},{5... | collective-permute-start | bytes 98312 | tf_op jit(solution)/shard_map/ppermute | solution.py:394
  79.5 2.0 %scatter.2.coef_ref = f32[16,4096]{1,0:T(8,128)S(1)} custom-call(s32[2,17]{1,0:T(2,128)S(1)} %convolution_convert_fusion.off_ref, s32[2,32,128]{2,1,0:T(8,128)S(1)} %select_convert_fusion.dest_ref, f32[16,4096]{1,0:T(8,128)S(1)} %copy-done.1, f32[16,1536]{1,0:T(8,128)S(1)} %get-tuple-element.67.delta_ref), custom_call_target="tpu_custom_call" | custom-call | flops 1000000000 | bytes 1000000 | tf_op jit(solution)/shard_map/scatter/pallas_call | solution.py:380
  83.6 2.7 %scatter.3 = f32[16,4096]{1,0:T(8,128)} custom-call(s32[2,17]{1,0:T(2,128)S(1)} %convolution_convert_fusion.off_ref, s32[2,32,128]{2,1,0:T(8,128)S(1)} %select_convert_fusion.dest_ref, f32[16,4096]{1,0:T(8,128)S(1)} %scatter.2.coef_ref, f32[16,1536]{1,0:T(8,128)S(1)} %get-tuple-element.68.delta_ref), custom_call_target="tpu_custom_call" | custom-call | flops 1000000000 | bytes 1000000 | tf_op jit(solution)/shard_map/scatter/pallas_call | solution.py:380
  87.3 5.2 %all_gather.19 = f32[4,16,256]{2,1,0:T(8,128)S(1)} all-gather(f32[1,16,256]{2,1,0:T(8,128)S(1)} %fusion.14), channel_id=1, replica_groups=mesh['rows'=8,'cent'=4] {'cent'}, dimensions={0}, use_global_device_ids=true | all-gather | bytes 81920 | tf_op jit(solution)/shard_map/all_gather | solution.py:528
  (63 shorter events, 23.4 us)
Async XLA Ops:
  0.6 3.0 %copy-start = (bf16[1024,512]{1,0:T(8,128)(2,1)S(1)}, bf16[1024,512]{1,0:T(8,128)(2,1)}, u32[]{:S(2)}) copy-start(bf16[1024,512]{1,0:T(8,128)(2,1)} %param.7) | copy-start | bytes 3145732
  2.3 8.9 %collective-permute-start = (bf16[2,32,128]{2,1,0:T(8,128)(2,1)S(1)}, bf16[2,32,128]{2,1,0:T(8,128)(2,1)S(1)}, u32[]{:S(2)}, u32[]{:S(2)}) collective-permute-start(bf16[2,32,128]{2,1,0:T(8,128)(2,1)S(1)} %fusion.2), channel_id=1, source_target_pairs={{0,1},{1,0},{2,3},{3,2},{4,5},{5,4},{6,7},{7,6},{8,9},{9,8},{10,11... | collective-permute-start | bytes 49160 | tf_op jit(solution)/shard_map/ppermute | solution.py:394
  4.4 19.7 %collective-permute-start.2 = (bf16[272,512]{1,0:T(8,128)(2,1)S(1)}, bf16[272,512]{1,0:T(8,128)(2,1)S(1)}, u32[]{:S(2)}, u32[]{:S(2)}) collective-permute-start(bf16[272,512]{1,0:T(8,128)(2,1)S(1)} %maximum_maximum_fusion.refs_0_), channel_id=1, source_target_pairs={{0,4},{4,0},{8,12},{12,8},{16,20},{20,16},{24,28},{28,24},{1,5},{5... | collective-permute-start | bytes 835592 | tf_op jit(solution)/shard_map/ppermute | solution.py:394
  7.0 16.0 %collective-permute-start.4 = (bf16[272,512]{1,0:T(8,128)(2,1)S(1)}, bf16[272,512]{1,0:T(8,128)(2,1)S(1)}, u32[]{:S(2)}, u32[]{:S(2)}) collective-permute-start(bf16[272,512]{1,0:T(8,128)(2,1)S(1)} %maximum_maximum_fusion.refs_0_), channel_id=1, source_target_pairs={{0,16},{4,20},{8,24},{12,28},{16,0},{20,4},{24,8},{28,12},{1,17},{... | collective-permute-start | bytes 835592 | tf_op jit(solution)/shard_map/ppermute | solution.py:394
  9.6 25.1 %collective-permute-start.8 = (bf16[272,512]{1,0:T(8,128)(2,1)S(1)}, bf16[272,512]{1,0:T(8,128)(2,1)S(1)}, u32[]{:S(2)}, u32[]{:S(2)}) collective-permute-start(bf16[272,512]{1,0:T(8,128)(2,1)S(1)} %maximum_maximum_fusion.refs_0_), channel_id=1, source_target_pairs={{0,8},{4,12},{8,0},{12,4},{16,24},{20,28},{24,16},{28,20},{1,9},{5... | collective-permute-start | bytes 835592 | tf_op jit(solution)/shard_map/ppermute | solution.py:394
  11.2 3.8 %collective-permute-start.1 = (bf16[2,32,128]{2,1,0:T(8,128)(2,1)S(1)}, bf16[2,32,128]{2,1,0:T(8,128)(2,1)S(1)}, u32[]{:S(2)}, u32[]{:S(2)}) collective-permute-start(bf16[2,32,128]{2,1,0:T(8,128)(2,1)S(1)} %add.64), channel_id=1, source_target_pairs={{0,2},{1,3},{2,0},{3,1},{4,6},{5,7},{6,4},{7,5},{8,10},{9,11},{10,... | collective-permute-start | bytes 49160 | tf_op jit(solution)/shard_map/ppermute | solution.py:394
  23.1 9.6 %collective-permute-start.5 = (bf16[272,512]{1,0:T(8,128)(2,1)S(1)}, bf16[272,512]{1,0:T(8,128)(2,1)S(1)}, u32[]{:S(2)}, u32[]{:S(2)}) collective-permute-start(bf16[272,512]{1,0:T(8,128)(2,1)S(1)} %collective-permute-done.4.refs_1_), channel_id=1, source_target_pairs={{0,8},{4,12},{8,0},{12,4},{16,24},{20,28},{24,16},{28,20},{1,9},{5... | collective-permute-start | bytes 835592 | tf_op jit(solution)/shard_map/ppermute | solution.py:394
  23.6 14.8 %collective-permute-start.7 = (bf16[272,512]{1,0:T(8,128)(2,1)S(1)}, bf16[272,512]{1,0:T(8,128)(2,1)S(1)}, u32[]{:S(2)}, u32[]{:S(2)}) collective-permute-start(bf16[272,512]{1,0:T(8,128)(2,1)S(1)} %broadcast_add_fusion), channel_id=1, source_target_pairs={{0,4},{4,0},{8,12},{12,8},{16,20},{20,16},{24,28},{28,24},{1,5},{5... | collective-permute-start | bytes 835592 | tf_op jit(solution)/shard_map/ppermute | solution.py:394
  24.2 16.4 %collective-permute-start.3 = (bf16[272,512]{1,0:T(8,128)(2,1)S(1)}, bf16[272,512]{1,0:T(8,128)(2,1)S(1)}, u32[]{:S(2)}, u32[]{:S(2)}) collective-permute-start(bf16[272,512]{1,0:T(8,128)(2,1)S(1)} %collective-permute-done.2.refs_1_), channel_id=1, source_target_pairs={{0,8},{4,12},{8,0},{12,4},{16,24},{20,28},{24,16},{28,20},{1,9},{5... | collective-permute-start | bytes 835592 | tf_op jit(solution)/shard_map/ppermute | solution.py:394
  32.6 7.9 %collective-permute-start.6 = (bf16[272,512]{1,0:T(8,128)(2,1)S(1)}, bf16[272,512]{1,0:T(8,128)(2,1)S(1)}, u32[]{:S(2)}, u32[]{:S(2)}) collective-permute-start(bf16[272,512]{1,0:T(8,128)(2,1)S(1)} %collective-permute-done.5.refs_1_), channel_id=1, source_target_pairs={{0,4},{4,0},{8,12},{12,8},{16,20},{20,16},{24,28},{28,24},{1,5},{5... | collective-permute-start | bytes 835592 | tf_op jit(solution)/shard_map/ppermute | solution.py:394
  52.6 5.9 %collective-permute-start.11 = (bf16[8,16,256]{2,1,0:T(8,128)(2,1)S(1)}, bf16[8,16,256]{2,1,0:T(8,128)(2,1)S(1)}, u32[]{:S(2)}, u32[]{:S(2)}) collective-permute-start(bf16[8,16,256]{2,1,0:T(8,128)(2,1)S(1)} %convert_element_type.68), channel_id=1, source_target_pairs={{0,12},{4,8},{8,4},{12,0},{16,28},{20,24},{24,20},{28,16},{1,13},{... | collective-permute-start | bytes 196616 | tf_op jit(solution)/shard_map/ppermute | solution.py:394
  54.0 5.3 %collective-permute-start.10 = (bf16[8,16,256]{2,1,0:T(8,128)(2,1)S(1)}, bf16[8,16,256]{2,1,0:T(8,128)(2,1)S(1)}, u32[]{:S(2)}, u32[]{:S(2)}) collective-permute-start(bf16[8,16,256]{2,1,0:T(8,128)(2,1)S(1)} %convert_element_type.68), channel_id=1, source_target_pairs={{0,8},{4,12},{8,0},{12,4},{16,24},{20,28},{24,16},{28,20},{1,9},{5... | collective-permute-start | bytes 196616 | tf_op jit(solution)/shard_map/ppermute | solution.py:394
  55.6 4.3 %collective-permute-start.9 = (bf16[8,16,256]{2,1,0:T(8,128)(2,1)S(1)}, bf16[8,16,256]{2,1,0:T(8,128)(2,1)S(1)}, u32[]{:S(2)}, u32[]{:S(2)}) collective-permute-start(bf16[8,16,256]{2,1,0:T(8,128)(2,1)S(1)} %convert_element_type.68), channel_id=1, source_target_pairs={{0,4},{4,0},{8,12},{12,8},{16,20},{20,16},{24,28},{28,24},{1,5},{5... | collective-permute-start | bytes 196616 | tf_op jit(solution)/shard_map/ppermute | solution.py:394
  59.9 5.9 %collective-permute-start.12 = (bf16[8,16,256]{2,1,0:T(8,128)(2,1)S(1)}, bf16[8,16,256]{2,1,0:T(8,128)(2,1)S(1)}, u32[]{:S(2)}, u32[]{:S(2)}) collective-permute-start(bf16[8,16,256]{2,1,0:T(8,128)(2,1)S(1)} %fusion.19), channel_id=1, source_target_pairs={{0,16},{4,20},{8,24},{12,28},{16,0},{20,4},{24,8},{28,12},{1,17},{... | collective-permute-start | bytes 196616 | tf_op jit(solution)/shard_map/ppermute | solution.py:394
  65.9 13.7 %copy-start.1 = (f32[16,4096]{1,0:T(8,128)S(1)}, f32[16,4096]{1,0:T(8,128)}, u32[]{:S(2)}) copy-start(f32[16,4096]{1,0:T(8,128)} %coef_ref.1) | copy-start | bytes 786436
  73.8 18.7 %copy-start.2 = (f32[16,1024]{1,0:T(8,128)S(1)}, f32[16,1024]{1,0:T(8,128)}, u32[]{:S(2)}) copy-start(f32[16,1024]{1,0:T(8,128)} %param.10) | copy-start | bytes 196612
  76.0 5.6 %collective-permute-start.15 = (f32[2,16,256]{2,1,0:T(8,128)S(1)}, f32[2,16,256]{2,1,0:T(8,128)S(1)}, u32[]{:S(2)}, u32[]{:S(2)}) collective-permute-start(f32[2,16,256]{2,1,0:T(8,128)S(1)} %get-tuple-element.74), channel_id=1, source_target_pairs={{0,12},{4,8},{8,4},{12,0},{16,28},{20,24},{24,20},{28,16},{1,13},{... | collective-permute-start | bytes 98312 | tf_op jit(solution)/shard_map/ppermute | solution.py:394
  76.4 5.1 %collective-permute-start.14 = (f32[2,16,256]{2,1,0:T(8,128)S(1)}, f32[2,16,256]{2,1,0:T(8,128)S(1)}, u32[]{:S(2)}, u32[]{:S(2)}) collective-permute-start(f32[2,16,256]{2,1,0:T(8,128)S(1)} %get-tuple-element.73), channel_id=1, source_target_pairs={{0,8},{4,12},{8,0},{12,4},{16,24},{20,28},{24,16},{28,20},{1,9},{5... | collective-permute-start | bytes 98312 | tf_op jit(solution)/shard_map/ppermute | solution.py:394
  78.6 3.9 %collective-permute-start.13 = (f32[2,16,256]{2,1,0:T(8,128)S(1)}, f32[2,16,256]{2,1,0:T(8,128)S(1)}, u32[]{:S(2)}, u32[]{:S(2)}) collective-permute-start(f32[2,16,256]{2,1,0:T(8,128)S(1)} %get-tuple-element.72), channel_id=1, source_target_pairs={{0,4},{4,0},{8,12},{12,8},{16,20},{20,16},{24,28},{28,24},{1,5},{5... | collective-permute-start | bytes 98312 | tf_op jit(solution)/shard_map/ppermute | solution.py:394
  82.6 4.7 %collective-permute-start.16 = (f32[1,16,256]{2,1,0:T(8,128)S(1)}, f32[1,16,256]{2,1,0:T(8,128)S(1)}, u32[]{:S(2)}, u32[]{:S(2)}) collective-permute-start(f32[1,16,256]{2,1,0:T(8,128)S(1)} %slice_bitcast_fusion.4), channel_id=1, source_target_pairs={{0,16},{4,20},{8,24},{12,28},{16,0},{20,4},{24,8},{28,12},{1,17},{... | collective-permute-start | bytes 49160 | tf_op jit(solution)/shard_map/ppermute | solution.py:394

commit v11 on v10

--- a/solution.py
+++ b/solution.py
@@ -159,7 +159,6 @@
     def _():
         walk(POOL_BLOCK + 16, 1)
 
-    ones = jnp.ones((8, features), BF16)
     eye = lax.broadcasted_iota(jnp.int32, (3 * targets, LANES), 0) == lax.broadcasted_iota(
         jnp.int32, (3 * targets, LANES), 1
     )
@@ -167,10 +166,11 @@
     for first in range(0, per_step, tile):
         rows = out_ref[first : first + tile, :].astype(F32)
         square = rows * rows
-        high = square.astype(BF16)
-        low = (square - high.astype(F32)).astype(BF16)
-        norm = lax.dot_general(ones, high, NT, preferred_element_type=F32)
-        norm_ref[:, first : first + tile] = norm + lax.dot_general(ones, low, NT, preferred_element_type=F32)
+        narrow_sum = square[:, :LANES]
+        for lane in range(LANES, features, LANES):
+            narrow_sum = narrow_sum + square[:, lane : lane + LANES]
+        norm = jnp.sum(jnp.transpose(narrow_sum), axis=0, keepdims=True)
+        norm_ref[:, first : first + tile] = jnp.broadcast_to(norm, (8, tile))
         parts = lax.dot_general(eye, side_out[first : first + tile, :], NT, preferred_element_type=F32)
         coef_ref[:, first : first + tile] = (
             parts[:targets] + parts[targets : 2 * targets] + parts[2 * targets :]

time: 93.4 us -> 93.2 us (level)
  Pallas kernels: 33.8 us -> 32.4 us
    pallas_call x2, Pallas kernels: 7.31 us -> 5.92 us  [compact(): pl.pallas_call(functools.partial(compact_kernel, step, per_step, targets)...]
  transfers between devices with their start and end apart: 17 -> 17, of which waited for: 8 -> 9; matrix products, arithmetic and copies ran while one was open for 3% -> 3% of each run, Pallas kernels for 28% -> 27%
where the time goes in v11:
time: 93.2 us; the launch traced here: 92.9 us
  Pallas kernels  32.4 us (35%)
  starting transfers between devices  22.4 us (24%)
  blocking collectives  19.7 us (21%)
  waiting for transfers between devices  12.7 us (14%)
  other arithmetic  3.36 us (4%)
  matrix products  1.15 us (1%)
    ppermute x17, starting transfers between devices, swap(): return lax.ppermute(value, axis, [(i, i ^ bit) for i in range(count)])  22.4 us
    pallas_call x8, Pallas kernels, block_call(): pl.pallas_call(functools.partial(block_kernel, first_step, targets, quart...  14.6 us
    all_gather x2, blocking collectives, local(): lax.all_gather(sums, 'cent')  14.5 us
    ppermute x17, waiting for transfers between devices, swap(): return lax.ppermute(value, axis, [(i, i ^ bit) for i in range(count)])  12.7 us
    pallas_call x2, Pallas kernels, compact(): pl.pallas_call(functools.partial(compact_kernel, step, per_step, targets)...  5.92 us
    all_gather x1, blocking collectives, local(): full = lax.all_gather(own_change, 'cent')  5.22 us
    pallas_call x2, Pallas kernels, scatter_call(): pl.pallas_call(functools.partial(scatter_kernel, targets, step), name='sc...  4.69 us
    pallas_call x2, Pallas kernels, change_call(): pl.pallas_call(functools.partial(change_kernel, targets, before is None,...  4.21 us
  transfers between devices with their start and end apart: 17, of which 9 were waited for; matrix products, arithmetic and copies ran while one was open for 3% of the time, Pallas kernels for 27%

profile of v11, /device:TPU:0, one launch (start us, length us, event | category | flops | bytes accessed | tf_op | source)
XLA Modules:
  0.0 92.9 jit_solution(6624566923550274136)
XLA Ops:
  4.4 2.6 %collective-permute-start.2 = (bf16[272,512]{1,0:T(8,128)(2,1)S(1)}, bf16[272,512]{1,0:T(8,128)(2,1)S(1)}, u32[]{:S(2)}, u32[]{:S(2)}) collective-permute-start(bf16[272,512]{1,0:T(8,128)(2,1)S(1)} %maximum_maximum_fusion.refs_0_), channel_id=1, source_target_pairs={{0,4},{4,0},{8,12},{12,8},{16,20},{20,16},{24,28},{28,24},{1,5},{5... | collective-permute-start | bytes 835592 | tf_op jit(solution)/shard_map/ppermute | solution.py:394
  7.0 2.6 %collective-permute-start.4 = (bf16[272,512]{1,0:T(8,128)(2,1)S(1)}, bf16[272,512]{1,0:T(8,128)(2,1)S(1)}, u32[]{:S(2)}, u32[]{:S(2)}) collective-permute-start(bf16[272,512]{1,0:T(8,128)(2,1)S(1)} %maximum_maximum_fusion.refs_0_), channel_id=1, source_target_pairs={{0,16},{4,20},{8,24},{12,28},{16,0},{20,4},{24,8},{28,12},{1,17},{... | collective-permute-start | bytes 835592 | tf_op jit(solution)/shard_map/ppermute | solution.py:394
  9.6 1.6 %collective-permute-start.8 = (bf16[272,512]{1,0:T(8,128)(2,1)S(1)}, bf16[272,512]{1,0:T(8,128)(2,1)S(1)}, u32[]{:S(2)}, u32[]{:S(2)}) collective-permute-start(bf16[272,512]{1,0:T(8,128)(2,1)S(1)} %maximum_maximum_fusion.refs_0_), channel_id=1, source_target_pairs={{0,8},{4,12},{8,0},{12,4},{16,24},{20,28},{24,16},{28,20},{1,9},{5... | collective-permute-start | bytes 835592 | tf_op jit(solution)/shard_map/ppermute | solution.py:394
  11.2 1.6 %collective-permute-start.1 = (bf16[2,32,128]{2,1,0:T(8,128)(2,1)S(1)}, bf16[2,32,128]{2,1,0:T(8,128)(2,1)S(1)}, u32[]{:S(2)}, u32[]{:S(2)}) collective-permute-start(bf16[2,32,128]{2,1,0:T(8,128)(2,1)S(1)} %add.64), channel_id=1, source_target_pairs={{0,2},{1,3},{2,0},{3,1},{4,6},{5,7},{6,4},{7,5},{8,10},{9,11},{10,... | collective-permute-start | bytes 49160 | tf_op jit(solution)/shard_map/ppermute | solution.py:394
  12.8 1.7 %load.1 = (bf16[2048,512]{1,0:T(8,128)(2,1)S(1)}, bf16[128,4096]{1,0:T(8,128)(2,1)S(1)}) custom-call(bf16[4096,512]{1,0:T(8,128)(2,1)} %refs_2_.1, f32[16,4096]{1,0:T(8,128)} %coef_ref.1), custom_call_target="tpu_custom_call" | custom-call | flops 1000000 | bytes 3000000 | tf_op jit(solution)/shard_map/load/pallas_call | solution.py:88
  15.7 3.0 %compact.2 = (bf16[1808,512]{1,0:T(8,128)(2,1)S(1)}, f32[8,1536]{1,0:T(8,128)S(1)}, f32[16,1536]{1,0:T(8,128)S(1)}, bf16[2048,512]{1,0:T(8,128)(2,1)S(1)}) custom-call(s32[2,17]{1,0:T(2,128)S(1)} %convolution_convert_fusion.off_ref, s32[2,32,128]{2,1,0:T(8,128)S(1)} %select_convert_fusion.dest_ref, bf16[2048,512]{1,0:T(8,128)(2,1)S(1)} %get-tuple-element.36.refs_0_, ...), custom_call_target="tpu_custom_call" | custom-call | flops 2000000000 | bytes 6000000 | tf_op jit(solution)/shard_map/compact/pallas_call | solution.py:197
  18.8 2.9 %compact.3 = (bf16[1808,512]{1,0:T(8,128)(2,1)S(1)}, f32[8,1536]{1,0:T(8,128)S(1)}, f32[16,1536]{1,0:T(8,128)S(1)}) custom-call(s32[2,17]{1,0:T(2,128)S(1)} %convolution_convert_fusion.off_ref, s32[2,32,128]{2,1,0:T(8,128)S(1)} %select_convert_fusion.dest_ref, bf16[2048,512]{1,0:T(8,128)(2,1)S(1)} %get-tuple-element.36.refs_0_, ...), custom_call_target="tpu_custom_call" | custom-call | flops 2000000000 | bytes 6000000 | tf_op jit(solution)/shard_map/compact/pallas_call | solution.py:197
  25.3 2.1 %kernel_block.8 = (bf16[8,256,1536]{2,1,0:T(8,128)(2,1)S(1)}, f32[24,1536]{1,0:T(8,128)S(1)}, f32[8,24,256]{2,1,0:T(8,128)S(1)}) custom-call(s32[1]{0:T(128)} %bitcast.1.me_ref, bf16[1808,512]{1,0:T(8,128)(2,1)S(1)} %get-tuple-element.38.chosen_ref, f32[8,1536]{1,0:T(8,128)S(1)} %get-tuple-element.39.norm_ref, ...), custom_call_target="tpu_custom_call" | custom-call | flops 805306368 | bytes 1572864 | tf_op jit(solution)/shard_map/kernel_block/pallas_call | solution.py:272
  27.5 4.8 %collective-permute-done.5.refs_1_ = bf16[272,512]{1,0:T(8,128)(2,1)S(1)} collective-permute-done((bf16[272,512]{1,0:T(8,128)(2,1)S(1)}, bf16[272,512]{1,0:T(8,128)(2,1)S(1)}, u32[]{:S(2)}, u32[]{:S(2)}) %collective-permute-start.5) | collective-permute-done | bytes 278560 | tf_op jit(solution)/shard_map/ppermute | solution.py:394
  32.8 1.6 %kernel_block.12 = (bf16[8,256,1536]{2,1,0:T(8,128)(2,1)S(1)}, f32[8,1536]{1,0:T(8,128)S(1)}) custom-call(s32[1]{0:T(128)} %bitcast.1.me_ref, bf16[1808,512]{1,0:T(8,128)(2,1)S(1)} %get-tuple-element.55.chosen_ref, f32[8,1536]{1,0:T(8,128)S(1)} %get-tuple-element.56.norm_ref, bf16[272,512]{1,0:T(8,128)(2,1)S(1)} %maximum_maximum_fusion.refs_0_, ...), custom_call_target="tpu_custom_call" | custom-call | flops 805306368 | bytes 1572864 | tf_op jit(solution)/shard_map/kernel_block/pallas_call | solution.py:272
  35.9 2.1 %kernel_block.9 = (bf16[8,256,1536]{2,1,0:T(8,128)(2,1)S(1)}, f32[24,1536]{1,0:T(8,128)S(1)}, f32[8,24,256]{2,1,0:T(8,128)S(1)}) custom-call(s32[1]{0:T(128)} %bitcast.1.me_ref, bf16[1808,512]{1,0:T(8,128)(2,1)S(1)} %get-tuple-element.38.chosen_ref, ...), custom_call_target="tpu_custom_call", output_to_operand_aliasing={{0}: (5, {}), {1}: (6, {}), {2}: (7, {})} | custom-call | flops 805306368 | bytes 1572864 | tf_op jit(solution)/shard_map/kernel_block/pallas_call | solution.py:272
  38.0 2.1 %kernel_block.10 = (bf16[8,256,1536]{2,1,0:T(8,128)(2,1)S(1)}, f32[24,1536]{1,0:T(8,128)S(1)}, f32[8,24,256]{2,1,0:T(8,128)S(1)}) custom-call(s32[1]{0:T(128)} %bitcast.1.me_ref, bf16[1808,512]{1,0:T(8,128)(2,1)S(1)} %get-tuple-element.38.chosen_ref, ...), custom_call_target="tpu_custom_call", output_to_operand_aliasing={{0}: (5, {}), {1}: (6, {}), {2}: (7, {})} | custom-call | flops 805306368 | bytes 1572864 | tf_op jit(solution)/shard_map/kernel_block/pallas_call | solution.py:272
  40.1 2.1 %kernel_block.11 = (bf16[8,256,1536]{2,1,0:T(8,128)(2,1)S(1)}, f32[24,1536]{1,0:T(8,128)S(1)}, f32[8,24,256]{2,1,0:T(8,128)S(1)}) custom-call(s32[1]{0:T(128)} %bitcast.1.me_ref, bf16[1808,512]{1,0:T(8,128)(2,1)S(1)} %get-tuple-element.38.chosen_ref, ...), custom_call_target="tpu_custom_call", output_to_operand_aliasing={{0}: (5, {}), {1}: (6, {}), {2}: (7, {})} | custom-call | flops 805306368 | bytes 1572864 | tf_op jit(solution)/shard_map/kernel_block/pallas_call | solution.py:272
  42.3 7.8 %all-gather = f32[96,1536]{1,0:T(8,128)S(1)} all-gather(f32[24,1536]{1,0:T(8,128)S(1)} %get-tuple-element.49), channel_id=2, replica_groups=mesh['rows'=8,'cent'=4] {'cent'}, dimensions={0}, use_global_device_ids=true | all-gather | bytes 737280 | tf_op jit(solution)/shard_map/all_gather | solution.py:508
  50.1 2.1 %change.2 = (f32[16,1536]{1,0:T(8,128)S(1)}, f32[8,16,256]{2,1,0:T(8,128)S(1)}, f32[8,16,256]{2,1,0:T(8,128)S(1)}) custom-call(s32[1]{0:T(128)} %bitcast.1.me_ref, f32[4,24,1536]{2,1,0:T(8,128)S(1)} %bitcast.44, f32[16,1536]{1,0:T(8,128)S(1)} %get-tuple-element.50.coef_ref, bf16[8,256,1536]{2,1,0:T(8,128)(2,1)S(1)} %get-tuple-element.51.k_ref, ...), custom_call_target="tpu_custom_call" | custom-call | flops 100663296 | bytes 6291456 | tf_op jit(solution)/shard_map/change/pallas_call | solution.py:320
  52.2 1.6 %collective-permute-start.11 = (bf16[8,16,256]{2,1,0:T(8,128)(2,1)S(1)}, bf16[8,16,256]{2,1,0:T(8,128)(2,1)S(1)}, u32[]{:S(2)}, u32[]{:S(2)}) collective-permute-start(bf16[8,16,256]{2,1,0:T(8,128)(2,1)S(1)} %convert_element_type.68), channel_id=1, source_target_pairs={{0,12},{4,8},{8,4},{12,0},{16,28},{20,24},{24,20},{28,16},{1,13},{... | collective-permute-start | bytes 196616 | tf_op jit(solution)/shard_map/ppermute | solution.py:394
  59.6 2.0 %collective-permute-start.12 = (bf16[8,16,256]{2,1,0:T(8,128)(2,1)S(1)}, bf16[8,16,256]{2,1,0:T(8,128)(2,1)S(1)}, u32[]{:S(2)}, u32[]{:S(2)}) collective-permute-start(bf16[8,16,256]{2,1,0:T(8,128)(2,1)S(1)} %fusion.19), channel_id=1, source_target_pairs={{0,16},{4,20},{8,24},{12,28},{16,0},{20,4},{24,8},{28,12},{1,17},{... | collective-permute-start | bytes 196616 | tf_op jit(solution)/shard_map/ppermute | solution.py:394
  63.1 2.4 %collective-permute-done.12 = bf16[8,16,256]{2,1,0:T(8,128)(2,1)S(1)} collective-permute-done((bf16[8,16,256]{2,1,0:T(8,128)(2,1)S(1)}, bf16[8,16,256]{2,1,0:T(8,128)(2,1)S(1)}, u32[]{:S(2)}, u32[]{:S(2)}) %collective-permute-start.12) | collective-permute-done | bytes 65568 | tf_op jit(solution)/shard_map/ppermute | solution.py:394
  66.8 6.7 %all-gather.1 = f32[96,1536]{1,0:T(8,128)S(1)} all-gather(f32[24,1536]{1,0:T(8,128)S(1)} %gradient.1), channel_id=3, replica_groups=mesh['rows'=8,'cent'=4] {'cent'}, dimensions={0}, use_global_device_ids=true | all-gather | bytes 737280 | tf_op jit(solution)/shard_map/all_gather | solution.py:508
  73.5 2.1 %change.3 = (f32[16,1536]{1,0:T(8,128)S(1)}, f32[8,16,256]{2,1,0:T(8,128)S(1)}) custom-call(s32[1]{0:T(128)} %bitcast.1.me_ref, f32[4,24,1536]{2,1,0:T(8,128)S(1)} %bitcast.45, f32[16,1536]{1,0:T(8,128)S(1)} %get-tuple-element.65.coef_ref, bf16[8,256,1536]{2,1,0:T(8,128)(2,1)S(1)} %get-tuple-element.63.k_ref, f32[8,24,256]{2,1,0:T(8,128)S(1)} %get-tuple-element.52.side_ref, ...), custom_call_target="tpu_custom_call" | custom-call | flops 100663296 | bytes 6291456 | tf_op jit(solution)/shard_map/change/pallas_call | solution.py:320
  76.4 1.8 %collective-permute-start.14 = (f32[2,16,256]{2,1,0:T(8,128)S(1)}, f32[2,16,256]{2,1,0:T(8,128)S(1)}, u32[]{:S(2)}, u32[]{:S(2)}) collective-permute-start(f32[2,16,256]{2,1,0:T(8,128)S(1)} %get-tuple-element.73), channel_id=1, source_target_pairs={{0,8},{4,12},{8,0},{12,4},{16,24},{20,28},{24,16},{28,20},{1,9},{5... | collective-permute-start | bytes 98312 | tf_op jit(solution)/shard_map/ppermute | solution.py:394
  79.2 2.0 %scatter.2.coef_ref = f32[16,4096]{1,0:T(8,128)S(1)} custom-call(s32[2,17]{1,0:T(2,128)S(1)} %convolution_convert_fusion.off_ref, s32[2,32,128]{2,1,0:T(8,128)S(1)} %select_convert_fusion.dest_ref, f32[16,4096]{1,0:T(8,128)S(1)} %copy-done.1, f32[16,1536]{1,0:T(8,128)S(1)} %get-tuple-element.67.delta_ref), custom_call_target="tpu_custom_call" | custom-call | flops 1000000000 | bytes 1000000 | tf_op jit(solution)/shard_map/scatter/pallas_call | solution.py:380
  83.6 2.7 %scatter.3 = f32[16,4096]{1,0:T(8,128)} custom-call(s32[2,17]{1,0:T(2,128)S(1)} %convolution_convert_fusion.off_ref, s32[2,32,128]{2,1,0:T(8,128)S(1)} %select_convert_fusion.dest_ref, f32[16,4096]{1,0:T(8,128)S(1)} %scatter.2.coef_ref, f32[16,1536]{1,0:T(8,128)S(1)} %get-tuple-element.68.delta_ref), custom_call_target="tpu_custom_call" | custom-call | flops 1000000000 | bytes 1000000 | tf_op jit(solution)/shard_map/scatter/pallas_call | solution.py:380
  87.0 5.2 %all_gather.19 = f32[4,16,256]{2,1,0:T(8,128)S(1)} all-gather(f32[1,16,256]{2,1,0:T(8,128)S(1)} %fusion.14), channel_id=1, replica_groups=mesh['rows'=8,'cent'=4] {'cent'}, dimensions={0}, use_global_device_ids=true | all-gather | bytes 81920 | tf_op jit(solution)/shard_map/all_gather | solution.py:528
  (63 shorter events, 24.8 us)
Async XLA Ops:
  0.6 3.0 %copy-start = (bf16[1024,512]{1,0:T(8,128)(2,1)S(1)}, bf16[1024,512]{1,0:T(8,128)(2,1)}, u32[]{:S(2)}) copy-start(bf16[1024,512]{1,0:T(8,128)(2,1)} %param.7) | copy-start | bytes 3145732
  2.3 8.9 %collective-permute-start = (bf16[2,32,128]{2,1,0:T(8,128)(2,1)S(1)}, bf16[2,32,128]{2,1,0:T(8,128)(2,1)S(1)}, u32[]{:S(2)}, u32[]{:S(2)}) collective-permute-start(bf16[2,32,128]{2,1,0:T(8,128)(2,1)S(1)} %fusion.2), channel_id=1, source_target_pairs={{0,1},{1,0},{2,3},{3,2},{4,5},{5,4},{6,7},{7,6},{8,9},{9,8},{10,11... | collective-permute-start | bytes 49160 | tf_op jit(solution)/shard_map/ppermute | solution.py:394
  4.4 19.5 %collective-permute-start.2 = (bf16[272,512]{1,0:T(8,128)(2,1)S(1)}, bf16[272,512]{1,0:T(8,128)(2,1)S(1)}, u32[]{:S(2)}, u32[]{:S(2)}) collective-permute-start(bf16[272,512]{1,0:T(8,128)(2,1)S(1)} %maximum_maximum_fusion.refs_0_), channel_id=1, source_target_pairs={{0,4},{4,0},{8,12},{12,8},{16,20},{20,16},{24,28},{28,24},{1,5},{5... | collective-permute-start | bytes 835592 | tf_op jit(solution)/shard_map/ppermute | solution.py:394
  7.0 15.7 %collective-permute-start.4 = (bf16[272,512]{1,0:T(8,128)(2,1)S(1)}, bf16[272,512]{1,0:T(8,128)(2,1)S(1)}, u32[]{:S(2)}, u32[]{:S(2)}) collective-permute-start(bf16[272,512]{1,0:T(8,128)(2,1)S(1)} %maximum_maximum_fusion.refs_0_), channel_id=1, source_target_pairs={{0,16},{4,20},{8,24},{12,28},{16,0},{20,4},{24,8},{28,12},{1,17},{... | collective-permute-start | bytes 835592 | tf_op jit(solution)/shard_map/ppermute | solution.py:394
  9.6 24.7 %collective-permute-start.8 = (bf16[272,512]{1,0:T(8,128)(2,1)S(1)}, bf16[272,512]{1,0:T(8,128)(2,1)S(1)}, u32[]{:S(2)}, u32[]{:S(2)}) collective-permute-start(bf16[272,512]{1,0:T(8,128)(2,1)S(1)} %maximum_maximum_fusion.refs_0_), channel_id=1, source_target_pairs={{0,8},{4,12},{8,0},{12,4},{16,24},{20,28},{24,16},{28,20},{1,9},{5... | collective-permute-start | bytes 835592 | tf_op jit(solution)/shard_map/ppermute | solution.py:394
  11.2 3.8 %collective-permute-start.1 = (bf16[2,32,128]{2,1,0:T(8,128)(2,1)S(1)}, bf16[2,32,128]{2,1,0:T(8,128)(2,1)S(1)}, u32[]{:S(2)}, u32[]{:S(2)}) collective-permute-start(bf16[2,32,128]{2,1,0:T(8,128)(2,1)S(1)} %add.64), channel_id=1, source_target_pairs={{0,2},{1,3},{2,0},{3,1},{4,6},{5,7},{6,4},{7,5},{8,10},{9,11},{10,... | collective-permute-start | bytes 49160 | tf_op jit(solution)/shard_map/ppermute | solution.py:394
  22.8 9.5 %collective-permute-start.5 = (bf16[272,512]{1,0:T(8,128)(2,1)S(1)}, bf16[272,512]{1,0:T(8,128)(2,1)S(1)}, u32[]{:S(2)}, u32[]{:S(2)}) collective-permute-start(bf16[272,512]{1,0:T(8,128)(2,1)S(1)} %collective-permute-done.4.refs_1_), channel_id=1, source_target_pairs={{0,8},{4,12},{8,0},{12,4},{16,24},{20,28},{24,16},{28,20},{1,9},{5... | collective-permute-start | bytes 835592 | tf_op jit(solution)/shard_map/ppermute | solution.py:394
  23.4 14.6 %collective-permute-start.7 = (bf16[272,512]{1,0:T(8,128)(2,1)S(1)}, bf16[272,512]{1,0:T(8,128)(2,1)S(1)}, u32[]{:S(2)}, u32[]{:S(2)}) collective-permute-start(bf16[272,512]{1,0:T(8,128)(2,1)S(1)} %broadcast_add_fusion), channel_id=1, source_target_pairs={{0,4},{4,0},{8,12},{12,8},{16,20},{20,16},{24,28},{28,24},{1,5},{5... | collective-permute-start | bytes 835592 | tf_op jit(solution)/shard_map/ppermute | solution.py:394
  23.9 16.2 %collective-permute-start.3 = (bf16[272,512]{1,0:T(8,128)(2,1)S(1)}, bf16[272,512]{1,0:T(8,128)(2,1)S(1)}, u32[]{:S(2)}, u32[]{:S(2)}) collective-permute-start(bf16[272,512]{1,0:T(8,128)(2,1)S(1)} %collective-permute-done.2.refs_1_), channel_id=1, source_target_pairs={{0,8},{4,12},{8,0},{12,4},{16,24},{20,28},{24,16},{28,20},{1,9},{5... | collective-permute-start | bytes 835592 | tf_op jit(solution)/shard_map/ppermute | solution.py:394
  32.3 7.8 %collective-permute-start.6 = (bf16[272,512]{1,0:T(8,128)(2,1)S(1)}, bf16[272,512]{1,0:T(8,128)(2,1)S(1)}, u32[]{:S(2)}, u32[]{:S(2)}) collective-permute-start(bf16[272,512]{1,0:T(8,128)(2,1)S(1)} %collective-permute-done.5.refs_1_), channel_id=1, source_target_pairs={{0,4},{4,0},{8,12},{12,8},{16,20},{20,16},{24,28},{28,24},{1,5},{5... | collective-permute-start | bytes 835592 | tf_op jit(solution)/shard_map/ppermute | solution.py:394
  52.2 5.9 %collective-permute-start.11 = (bf16[8,16,256]{2,1,0:T(8,128)(2,1)S(1)}, bf16[8,16,256]{2,1,0:T(8,128)(2,1)S(1)}, u32[]{:S(2)}, u32[]{:S(2)}) collective-permute-start(bf16[8,16,256]{2,1,0:T(8,128)(2,1)S(1)} %convert_element_type.68), channel_id=1, source_target_pairs={{0,12},{4,8},{8,4},{12,0},{16,28},{20,24},{24,20},{28,16},{1,13},{... | collective-permute-start | bytes 196616 | tf_op jit(solution)/shard_map/ppermute | solution.py:394
  53.8 5.2 %collective-permute-start.10 = (bf16[8,16,256]{2,1,0:T(8,128)(2,1)S(1)}, bf16[8,16,256]{2,1,0:T(8,128)(2,1)S(1)}, u32[]{:S(2)}, u32[]{:S(2)}) collective-permute-start(bf16[8,16,256]{2,1,0:T(8,128)(2,1)S(1)} %convert_element_type.68), channel_id=1, source_target_pairs={{0,8},{4,12},{8,0},{12,4},{16,24},{20,28},{24,16},{28,20},{1,9},{5... | collective-permute-start | bytes 196616 | tf_op jit(solution)/shard_map/ppermute | solution.py:394
  55.3 4.3 %collective-permute-start.9 = (bf16[8,16,256]{2,1,0:T(8,128)(2,1)S(1)}, bf16[8,16,256]{2,1,0:T(8,128)(2,1)S(1)}, u32[]{:S(2)}, u32[]{:S(2)}) collective-permute-start(bf16[8,16,256]{2,1,0:T(8,128)(2,1)S(1)} %convert_element_type.68), channel_id=1, source_target_pairs={{0,4},{4,0},{8,12},{12,8},{16,20},{20,16},{24,28},{28,24},{1,5},{5... | collective-permute-start | bytes 196616 | tf_op jit(solution)/shard_map/ppermute | solution.py:394
  59.6 5.9 %collective-permute-start.12 = (bf16[8,16,256]{2,1,0:T(8,128)(2,1)S(1)}, bf16[8,16,256]{2,1,0:T(8,128)(2,1)S(1)}, u32[]{:S(2)}, u32[]{:S(2)}) collective-permute-start(bf16[8,16,256]{2,1,0:T(8,128)(2,1)S(1)} %fusion.19), channel_id=1, source_target_pairs={{0,16},{4,20},{8,24},{12,28},{16,0},{20,4},{24,8},{28,12},{1,17},{... | collective-permute-start | bytes 196616 | tf_op jit(solution)/shard_map/ppermute | solution.py:394
  65.5 13.7 %copy-start.1 = (f32[16,4096]{1,0:T(8,128)S(1)}, f32[16,4096]{1,0:T(8,128)}, u32[]{:S(2)}) copy-start(f32[16,4096]{1,0:T(8,128)} %coef_ref.1) | copy-start | bytes 786436
  73.5 18.7 %copy-start.2 = (f32[16,1024]{1,0:T(8,128)S(1)}, f32[16,1024]{1,0:T(8,128)}, u32[]{:S(2)}) copy-start(f32[16,1024]{1,0:T(8,128)} %param.10) | copy-start | bytes 196612
  75.6 5.6 %collective-permute-start.15 = (f32[2,16,256]{2,1,0:T(8,128)S(1)}, f32[2,16,256]{2,1,0:T(8,128)S(1)}, u32[]{:S(2)}, u32[]{:S(2)}) collective-permute-start(f32[2,16,256]{2,1,0:T(8,128)S(1)} %get-tuple-element.74), channel_id=1, source_target_pairs={{0,12},{4,8},{8,4},{12,0},{16,28},{20,24},{24,20},{28,16},{1,13},{... | collective-permute-start | bytes 98312 | tf_op jit(solution)/shard_map/ppermute | solution.py:394
  76.4 4.8 %collective-permute-start.14 = (f32[2,16,256]{2,1,0:T(8,128)S(1)}, f32[2,16,256]{2,1,0:T(8,128)S(1)}, u32[]{:S(2)}, u32[]{:S(2)}) collective-permute-start(f32[2,16,256]{2,1,0:T(8,128)S(1)} %get-tuple-element.73), channel_id=1, source_target_pairs={{0,8},{4,12},{8,0},{12,4},{16,24},{20,28},{24,16},{28,20},{1,9},{5... | collective-permute-start | bytes 98312 | tf_op jit(solution)/shard_map/ppermute | solution.py:394
  78.2 3.9 %collective-permute-start.13 = (f32[2,16,256]{2,1,0:T(8,128)S(1)}, f32[2,16,256]{2,1,0:T(8,128)S(1)}, u32[]{:S(2)}, u32[]{:S(2)}) collective-permute-start(f32[2,16,256]{2,1,0:T(8,128)S(1)} %get-tuple-element.72), channel_id=1, source_target_pairs={{0,4},{4,0},{8,12},{12,8},{16,20},{20,16},{24,28},{28,24},{1,5},{5... | collective-permute-start | bytes 98312 | tf_op jit(solution)/shard_map/ppermute | solution.py:394
  82.2 4.8 %collective-permute-start.16 = (f32[1,16,256]{2,1,0:T(8,128)S(1)}, f32[1,16,256]{2,1,0:T(8,128)S(1)}, u32[]{:S(2)}, u32[]{:S(2)}) collective-permute-start(f32[1,16,256]{2,1,0:T(8,128)S(1)} %slice_bitcast_fusion.4), channel_id=1, source_target_pairs={{0,16},{4,20},{8,24},{12,28},{16,0},{20,4},{24,8},{28,12},{1,17},{... | collective-permute-start | bytes 49160 | tf_op jit(solution)/shard_map/ppermute | solution.py:394

commit v12 on v11

--- a/solution.py
+++ b/solution.py
@@ -525,8 +525,11 @@
             kept = kept + swap(pieces[:, k], "rows", k * pair[0])
         pieces = kept
     own_change = pieces[0]
-    full = lax.all_gather(own_change, "cent")
-    full = full.transpose(1, 0, 2).reshape(target_count, rows_dev)
+    full = own_change
+    for bit in bits_of(cent_devices):
+        other = swap(full, "cent", bit)
+        high = (my_cent & bit) > 0
+        full = jnp.concatenate([jnp.where(high, other, full), jnp.where(high, full, other)], axis=1)
     return (coef_now, predictions + full)
 
 

time: 93.2 us -> 94.1 us (level)
  blocking collectives: 19.7 us -> 14.5 us
  waiting for transfers between devices: 12.7 us -> 17.4 us
  starting transfers between devices: 22.4 us -> 23.8 us
    all_gather x1 -> x0, blocking collectives: 5.22 us -> none  [local(): full = lax.all_gather(own_change, 'cent')]
    ppermute x17 -> x19, waiting for transfers between devices: 12.7 us -> 17.4 us  [swap(): return lax.ppermute(value, axis, [(i, i ^ bit) for i in range(count)])]
    ppermute x17 -> x19, starting transfers between devices: 22.4 us -> 23.8 us  [swap(): return lax.ppermute(value, axis, [(i, i ^ bit) for i in range(count)])]
  transfers between devices with their start and end apart: 17 -> 19, of which waited for: 9 -> 10; matrix products, arithmetic and copies ran while one was open for 3% -> 2% of each run, Pallas kernels for 27% -> 26%
where the time goes in v12:
time: 94.1 us; the launch traced here: 93.8 us
  Pallas kernels  32.4 us (34%)
  starting transfers between devices  23.8 us (25%)
  waiting for transfers between devices  17.4 us (18%)
  blocking collectives  14.5 us (15%)
  other arithmetic  3.39 us (4%)
  matrix products  1.15 us (1%)
    ppermute x19, starting transfers between devices, swap(): return lax.ppermute(value, axis, [(i, i ^ bit) for i in range(count)])  23.8 us
    ppermute x19, waiting for transfers between devices, swap(): return lax.ppermute(value, axis, [(i, i ^ bit) for i in range(count)])  17.4 us
    pallas_call x8, Pallas kernels, block_call(): pl.pallas_call(functools.partial(block_kernel, first_step, targets, quart...  14.6 us
    all_gather x2, blocking collectives, local(): lax.all_gather(sums, 'cent')  14.5 us
    pallas_call x2, Pallas kernels, compact(): pl.pallas_call(functools.partial(compact_kernel, step, per_step, targets)...  5.91 us
    pallas_call x2, Pallas kernels, scatter_call(): pl.pallas_call(functools.partial(scatter_kernel, targets, step), name='sc...  4.69 us
    pallas_call x2, Pallas kernels, change_call(): pl.pallas_call(functools.partial(change_kernel, targets, before is None,...  4.21 us
  transfers between devices with their start and end apart: 19, of which 10 were waited for; matrix products, arithmetic and copies ran while one was open for 2% of the time, Pallas kernels for 26%

profile of v12, /device:TPU:0, one launch (start us, length us, event | category | flops | bytes accessed | tf_op | source)
XLA Modules:
  0.0 93.8 jit_solution(6747707440170053078)
XLA Ops:
  4.4 2.6 %collective-permute-start.2 = (bf16[272,512]{1,0:T(8,128)(2,1)S(1)}, bf16[272,512]{1,0:T(8,128)(2,1)S(1)}, u32[]{:S(2)}, u32[]{:S(2)}) collective-permute-start(bf16[272,512]{1,0:T(8,128)(2,1)S(1)} %maximum_maximum_fusion.refs_0_), channel_id=1, source_target_pairs={{0,4},{4,0},{8,12},{12,8},{16,20},{20,16},{24,28},{28,24},{1,5},{5... | collective-permute-start | bytes 835592 | tf_op jit(solution)/shard_map/ppermute | solution.py:394
  7.0 2.6 %collective-permute-start.4 = (bf16[272,512]{1,0:T(8,128)(2,1)S(1)}, bf16[272,512]{1,0:T(8,128)(2,1)S(1)}, u32[]{:S(2)}, u32[]{:S(2)}) collective-permute-start(bf16[272,512]{1,0:T(8,128)(2,1)S(1)} %maximum_maximum_fusion.refs_0_), channel_id=1, source_target_pairs={{0,16},{4,20},{8,24},{12,28},{16,0},{20,4},{24,8},{28,12},{1,17},{... | collective-permute-start | bytes 835592 | tf_op jit(solution)/shard_map/ppermute | solution.py:394
  9.6 1.6 %collective-permute-start.8 = (bf16[272,512]{1,0:T(8,128)(2,1)S(1)}, bf16[272,512]{1,0:T(8,128)(2,1)S(1)}, u32[]{:S(2)}, u32[]{:S(2)}) collective-permute-start(bf16[272,512]{1,0:T(8,128)(2,1)S(1)} %maximum_maximum_fusion.refs_0_), channel_id=1, source_target_pairs={{0,8},{4,12},{8,0},{12,4},{16,24},{20,28},{24,16},{28,20},{1,9},{5... | collective-permute-start | bytes 835592 | tf_op jit(solution)/shard_map/ppermute | solution.py:394
  11.2 1.6 %collective-permute-start.1 = (bf16[2,32,128]{2,1,0:T(8,128)(2,1)S(1)}, bf16[2,32,128]{2,1,0:T(8,128)(2,1)S(1)}, u32[]{:S(2)}, u32[]{:S(2)}) collective-permute-start(bf16[2,32,128]{2,1,0:T(8,128)(2,1)S(1)} %add.64), channel_id=1, source_target_pairs={{0,2},{1,3},{2,0},{3,1},{4,6},{5,7},{6,4},{7,5},{8,10},{9,11},{10,... | collective-permute-start | bytes 49160 | tf_op jit(solution)/shard_map/ppermute | solution.py:394
  12.8 1.7 %load.1 = (bf16[2048,512]{1,0:T(8,128)(2,1)S(1)}, bf16[128,4096]{1,0:T(8,128)(2,1)S(1)}) custom-call(bf16[4096,512]{1,0:T(8,128)(2,1)} %refs_2_.1, f32[16,4096]{1,0:T(8,128)} %coef_ref.1), custom_call_target="tpu_custom_call" | custom-call | flops 1000000 | bytes 3000000 | tf_op jit(solution)/shard_map/load/pallas_call | solution.py:88
  15.7 3.0 %compact.2 = (bf16[1808,512]{1,0:T(8,128)(2,1)S(1)}, f32[8,1536]{1,0:T(8,128)S(1)}, f32[16,1536]{1,0:T(8,128)S(1)}, bf16[2048,512]{1,0:T(8,128)(2,1)S(1)}) custom-call(s32[2,17]{1,0:T(2,128)S(1)} %convolution_convert_fusion.off_ref, s32[2,32,128]{2,1,0:T(8,128)S(1)} %select_convert_fusion.dest_ref, bf16[2048,512]{1,0:T(8,128)(2,1)S(1)} %get-tuple-element.36.refs_0_, ...), custom_call_target="tpu_custom_call" | custom-call | flops 2000000000 | bytes 6000000 | tf_op jit(solution)/shard_map/compact/pallas_call | solution.py:197
  18.8 2.9 %compact.3 = (bf16[1808,512]{1,0:T(8,128)(2,1)S(1)}, f32[8,1536]{1,0:T(8,128)S(1)}, f32[16,1536]{1,0:T(8,128)S(1)}) custom-call(s32[2,17]{1,0:T(2,128)S(1)} %convolution_convert_fusion.off_ref, s32[2,32,128]{2,1,0:T(8,128)S(1)} %select_convert_fusion.dest_ref, bf16[2048,512]{1,0:T(8,128)(2,1)S(1)} %get-tuple-element.36.refs_0_, ...), custom_call_target="tpu_custom_call" | custom-call | flops 2000000000 | bytes 6000000 | tf_op jit(solution)/shard_map/compact/pallas_call | solution.py:197
  25.3 2.1 %kernel_block.8 = (bf16[8,256,1536]{2,1,0:T(8,128)(2,1)S(1)}, f32[24,1536]{1,0:T(8,128)S(1)}, f32[8,24,256]{2,1,0:T(8,128)S(1)}) custom-call(s32[1]{0:T(128)} %bitcast.1.me_ref, bf16[1808,512]{1,0:T(8,128)(2,1)S(1)} %get-tuple-element.38.chosen_ref, f32[8,1536]{1,0:T(8,128)S(1)} %get-tuple-element.39.norm_ref, ...), custom_call_target="tpu_custom_call" | custom-call | flops 805306368 | bytes 1572864 | tf_op jit(solution)/shard_map/kernel_block/pallas_call | solution.py:272
  27.5 4.8 %collective-permute-done.5.refs_1_ = bf16[272,512]{1,0:T(8,128)(2,1)S(1)} collective-permute-done((bf16[272,512]{1,0:T(8,128)(2,1)S(1)}, bf16[272,512]{1,0:T(8,128)(2,1)S(1)}, u32[]{:S(2)}, u32[]{:S(2)}) %collective-permute-start.5) | collective-permute-done | bytes 278560 | tf_op jit(solution)/shard_map/ppermute | solution.py:394
  32.8 1.6 %kernel_block.12 = (bf16[8,256,1536]{2,1,0:T(8,128)(2,1)S(1)}, f32[8,1536]{1,0:T(8,128)S(1)}) custom-call(s32[1]{0:T(128)} %bitcast.1.me_ref, bf16[1808,512]{1,0:T(8,128)(2,1)S(1)} %get-tuple-element.55.chosen_ref, f32[8,1536]{1,0:T(8,128)S(1)} %get-tuple-element.56.norm_ref, bf16[272,512]{1,0:T(8,128)(2,1)S(1)} %maximum_maximum_fusion.refs_0_, ...), custom_call_target="tpu_custom_call" | custom-call | flops 805306368 | bytes 1572864 | tf_op jit(solution)/shard_map/kernel_block/pallas_call | solution.py:272
  35.9 2.1 %kernel_block.9 = (bf16[8,256,1536]{2,1,0:T(8,128)(2,1)S(1)}, f32[24,1536]{1,0:T(8,128)S(1)}, f32[8,24,256]{2,1,0:T(8,128)S(1)}) custom-call(s32[1]{0:T(128)} %bitcast.1.me_ref, bf16[1808,512]{1,0:T(8,128)(2,1)S(1)} %get-tuple-element.38.chosen_ref, ...), custom_call_target="tpu_custom_call", output_to_operand_aliasing={{0}: (5, {}), {1}: (6, {}), {2}: (7, {})} | custom-call | flops 805306368 | bytes 1572864 | tf_op jit(solution)/shard_map/kernel_block/pallas_call | solution.py:272
  38.0 2.1 %kernel_block.10 = (bf16[8,256,1536]{2,1,0:T(8,128)(2,1)S(1)}, f32[24,1536]{1,0:T(8,128)S(1)}, f32[8,24,256]{2,1,0:T(8,128)S(1)}) custom-call(s32[1]{0:T(128)} %bitcast.1.me_ref, bf16[1808,512]{1,0:T(8,128)(2,1)S(1)} %get-tuple-element.38.chosen_ref, ...), custom_call_target="tpu_custom_call", output_to_operand_aliasing={{0}: (5, {}), {1}: (6, {}), {2}: (7, {})} | custom-call | flops 805306368 | bytes 1572864 | tf_op jit(solution)/shard_map/kernel_block/pallas_call | solution.py:272
  40.1 2.1 %kernel_block.11 = (bf16[8,256,1536]{2,1,0:T(8,128)(2,1)S(1)}, f32[24,1536]{1,0:T(8,128)S(1)}, f32[8,24,256]{2,1,0:T(8,128)S(1)}) custom-call(s32[1]{0:T(128)} %bitcast.1.me_ref, bf16[1808,512]{1,0:T(8,128)(2,1)S(1)} %get-tuple-element.38.chosen_ref, ...), custom_call_target="tpu_custom_call", output_to_operand_aliasing={{0}: (5, {}), {1}: (6, {}), {2}: (7, {})} | custom-call | flops 805306368 | bytes 1572864 | tf_op jit(solution)/shard_map/kernel_block/pallas_call | solution.py:272
  42.3 7.8 %all-gather = f32[96,1536]{1,0:T(8,128)S(1)} all-gather(f32[24,1536]{1,0:T(8,128)S(1)} %get-tuple-element.49), channel_id=2, replica_groups=mesh['rows'=8,'cent'=4] {'cent'}, dimensions={0}, use_global_device_ids=true | all-gather | bytes 737280 | tf_op jit(solution)/shard_map/all_gather | solution.py:508
  50.1 2.1 %change.2 = (f32[16,1536]{1,0:T(8,128)S(1)}, f32[8,16,256]{2,1,0:T(8,128)S(1)}, f32[8,16,256]{2,1,0:T(8,128)S(1)}) custom-call(s32[1]{0:T(128)} %bitcast.1.me_ref, f32[4,24,1536]{2,1,0:T(8,128)S(1)} %bitcast.45, f32[16,1536]{1,0:T(8,128)S(1)} %get-tuple-element.50.coef_ref, bf16[8,256,1536]{2,1,0:T(8,128)(2,1)S(1)} %get-tuple-element.51.k_ref, ...), custom_call_target="tpu_custom_call" | custom-call | flops 100663296 | bytes 6291456 | tf_op jit(solution)/shard_map/change/pallas_call | solution.py:320
  52.2 1.6 %collective-permute-start.11 = (bf16[8,16,256]{2,1,0:T(8,128)(2,1)S(1)}, bf16[8,16,256]{2,1,0:T(8,128)(2,1)S(1)}, u32[]{:S(2)}, u32[]{:S(2)}) collective-permute-start(bf16[8,16,256]{2,1,0:T(8,128)(2,1)S(1)} %convert_element_type.68), channel_id=1, source_target_pairs={{0,12},{4,8},{8,4},{12,0},{16,28},{20,24},{24,20},{28,16},{1,13},{... | collective-permute-start | bytes 196616 | tf_op jit(solution)/shard_map/ppermute | solution.py:394
  59.6 2.0 %collective-permute-start.12 = (bf16[8,16,256]{2,1,0:T(8,128)(2,1)S(1)}, bf16[8,16,256]{2,1,0:T(8,128)(2,1)S(1)}, u32[]{:S(2)}, u32[]{:S(2)}) collective-permute-start(bf16[8,16,256]{2,1,0:T(8,128)(2,1)S(1)} %fusion.20), channel_id=1, source_target_pairs={{0,16},{4,20},{8,24},{12,28},{16,0},{20,4},{24,8},{28,12},{1,17},{... | collective-permute-start | bytes 196616 | tf_op jit(solution)/shard_map/ppermute | solution.py:394
  63.1 2.4 %collective-permute-done.12 = bf16[8,16,256]{2,1,0:T(8,128)(2,1)S(1)} collective-permute-done((bf16[8,16,256]{2,1,0:T(8,128)(2,1)S(1)}, bf16[8,16,256]{2,1,0:T(8,128)(2,1)S(1)}, u32[]{:S(2)}, u32[]{:S(2)}) %collective-permute-start.12) | collective-permute-done | bytes 65568 | tf_op jit(solution)/shard_map/ppermute | solution.py:394
  66.8 6.7 %all-gather.1 = f32[96,1536]{1,0:T(8,128)S(1)} all-gather(f32[24,1536]{1,0:T(8,128)S(1)} %gradient.1), channel_id=3, replica_groups=mesh['rows'=8,'cent'=4] {'cent'}, dimensions={0}, use_global_device_ids=true | all-gather | bytes 737280 | tf_op jit(solution)/shard_map/all_gather | solution.py:508
  73.5 2.1 %change.3 = (f32[16,1536]{1,0:T(8,128)S(1)}, f32[8,16,256]{2,1,0:T(8,128)S(1)}) custom-call(s32[1]{0:T(128)} %bitcast.1.me_ref, f32[4,24,1536]{2,1,0:T(8,128)S(1)} %bitcast.46, f32[16,1536]{1,0:T(8,128)S(1)} %get-tuple-element.65.coef_ref, bf16[8,256,1536]{2,1,0:T(8,128)(2,1)S(1)} %get-tuple-element.63.k_ref, f32[8,24,256]{2,1,0:T(8,128)S(1)} %get-tuple-element.52.side_ref, ...), custom_call_target="tpu_custom_call" | custom-call | flops 100663296 | bytes 6291456 | tf_op jit(solution)/shard_map/change/pallas_call | solution.py:320
  76.4 1.8 %collective-permute-start.14 = (f32[2,16,256]{2,1,0:T(8,128)S(1)}, f32[2,16,256]{2,1,0:T(8,128)S(1)}, u32[]{:S(2)}, u32[]{:S(2)}) collective-permute-start(f32[2,16,256]{2,1,0:T(8,128)S(1)} %get-tuple-element.73), channel_id=1, source_target_pairs={{0,8},{4,12},{8,0},{12,4},{16,24},{20,28},{24,16},{28,20},{1,9},{5... | collective-permute-start | bytes 98312 | tf_op jit(solution)/shard_map/ppermute | solution.py:394
  83.6 3.4 %collective-permute-done.16 = f32[1,16,256]{2,1,0:T(8,128)S(1)} collective-permute-done((f32[1,16,256]{2,1,0:T(8,128)S(1)}, f32[1,16,256]{2,1,0:T(8,128)S(1)}, u32[]{:S(2)}, u32[]{:S(2)}) %collective-permute-start.16) | collective-permute-done | bytes 16416 | tf_op jit(solution)/shard_map/ppermute | solution.py:394
  87.0 2.0 %scatter.2.coef_ref = f32[16,4096]{1,0:T(8,128)S(1)} custom-call(s32[2,17]{1,0:T(2,128)S(1)} %convolution_convert_fusion.off_ref, s32[2,32,128]{2,1,0:T(8,128)S(1)} %select_convert_fusion.dest_ref, f32[16,4096]{1,0:T(8,128)S(1)} %copy-done.1, f32[16,1536]{1,0:T(8,128)S(1)} %get-tuple-element.67.delta_ref), custom_call_target="tpu_custom_call" | custom-call | flops 1000000000 | bytes 1000000 | tf_op jit(solution)/shard_map/scatter/pallas_call | solution.py:380
  90.4 2.7 %scatter.3 = f32[16,4096]{1,0:T(8,128)} custom-call(s32[2,17]{1,0:T(2,128)S(1)} %convolution_convert_fusion.off_ref, s32[2,32,128]{2,1,0:T(8,128)S(1)} %select_convert_fusion.dest_ref, f32[16,4096]{1,0:T(8,128)S(1)} %scatter.2.coef_ref, f32[16,1536]{1,0:T(8,128)S(1)} %get-tuple-element.68.delta_ref), custom_call_target="tpu_custom_call" | custom-call | flops 1000000000 | bytes 1000000 | tf_op jit(solution)/shard_map/scatter/pallas_call | solution.py:380
  (68 shorter events, 27.6 us)
Async XLA Ops:
  0.6 3.0 %copy-start = (bf16[1024,512]{1,0:T(8,128)(2,1)S(1)}, bf16[1024,512]{1,0:T(8,128)(2,1)}, u32[]{:S(2)}) copy-start(bf16[1024,512]{1,0:T(8,128)(2,1)} %param.7) | copy-start | bytes 3145732
  2.3 8.9 %collective-permute-start = (bf16[2,32,128]{2,1,0:T(8,128)(2,1)S(1)}, bf16[2,32,128]{2,1,0:T(8,128)(2,1)S(1)}, u32[]{:S(2)}, u32[]{:S(2)}) collective-permute-start(bf16[2,32,128]{2,1,0:T(8,128)(2,1)S(1)} %fusion.2), channel_id=1, source_target_pairs={{0,1},{1,0},{2,3},{3,2},{4,5},{5,4},{6,7},{7,6},{8,9},{9,8},{10,11... | collective-permute-start | bytes 49160 | tf_op jit(solution)/shard_map/ppermute | solution.py:394
  4.4 19.5 %collective-permute-start.2 = (bf16[272,512]{1,0:T(8,128)(2,1)S(1)}, bf16[272,512]{1,0:T(8,128)(2,1)S(1)}, u32[]{:S(2)}, u32[]{:S(2)}) collective-permute-start(bf16[272,512]{1,0:T(8,128)(2,1)S(1)} %maximum_maximum_fusion.refs_0_), channel_id=1, source_target_pairs={{0,4},{4,0},{8,12},{12,8},{16,20},{20,16},{24,28},{28,24},{1,5},{5... | collective-permute-start | bytes 835592 | tf_op jit(solution)/shard_map/ppermute | solution.py:394
  7.0 15.7 %collective-permute-start.4 = (bf16[272,512]{1,0:T(8,128)(2,1)S(1)}, bf16[272,512]{1,0:T(8,128)(2,1)S(1)}, u32[]{:S(2)}, u32[]{:S(2)}) collective-permute-start(bf16[272,512]{1,0:T(8,128)(2,1)S(1)} %maximum_maximum_fusion.refs_0_), channel_id=1, source_target_pairs={{0,16},{4,20},{8,24},{12,28},{16,0},{20,4},{24,8},{28,12},{1,17},{... | collective-permute-start | bytes 835592 | tf_op jit(solution)/shard_map/ppermute | solution.py:394
  9.6 24.7 %collective-permute-start.8 = (bf16[272,512]{1,0:T(8,128)(2,1)S(1)}, bf16[272,512]{1,0:T(8,128)(2,1)S(1)}, u32[]{:S(2)}, u32[]{:S(2)}) collective-permute-start(bf16[272,512]{1,0:T(8,128)(2,1)S(1)} %maximum_maximum_fusion.refs_0_), channel_id=1, source_target_pairs={{0,8},{4,12},{8,0},{12,4},{16,24},{20,28},{24,16},{28,20},{1,9},{5... | collective-permute-start | bytes 835592 | tf_op jit(solution)/shard_map/ppermute | solution.py:394
  11.2 3.8 %collective-permute-start.1 = (bf16[2,32,128]{2,1,0:T(8,128)(2,1)S(1)}, bf16[2,32,128]{2,1,0:T(8,128)(2,1)S(1)}, u32[]{:S(2)}, u32[]{:S(2)}) collective-permute-start(bf16[2,32,128]{2,1,0:T(8,128)(2,1)S(1)} %add.64), channel_id=1, source_target_pairs={{0,2},{1,3},{2,0},{3,1},{4,6},{5,7},{6,4},{7,5},{8,10},{9,11},{10,... | collective-permute-start | bytes 49160 | tf_op jit(solution)/shard_map/ppermute | solution.py:394
  22.8 9.5 %collective-permute-start.5 = (bf16[272,512]{1,0:T(8,128)(2,1)S(1)}, bf16[272,512]{1,0:T(8,128)(2,1)S(1)}, u32[]{:S(2)}, u32[]{:S(2)}) collective-permute-start(bf16[272,512]{1,0:T(8,128)(2,1)S(1)} %collective-permute-done.4.refs_1_), channel_id=1, source_target_pairs={{0,8},{4,12},{8,0},{12,4},{16,24},{20,28},{24,16},{28,20},{1,9},{5... | collective-permute-start | bytes 835592 | tf_op jit(solution)/shard_map/ppermute | solution.py:394
  23.4 14.6 %collective-permute-start.7 = (bf16[272,512]{1,0:T(8,128)(2,1)S(1)}, bf16[272,512]{1,0:T(8,128)(2,1)S(1)}, u32[]{:S(2)}, u32[]{:S(2)}) collective-permute-start(bf16[272,512]{1,0:T(8,128)(2,1)S(1)} %broadcast_add_fusion), channel_id=1, source_target_pairs={{0,4},{4,0},{8,12},{12,8},{16,20},{20,16},{24,28},{28,24},{1,5},{5... | collective-permute-start | bytes 835592 | tf_op jit(solution)/shard_map/ppermute | solution.py:394
  23.9 16.2 %collective-permute-start.3 = (bf16[272,512]{1,0:T(8,128)(2,1)S(1)}, bf16[272,512]{1,0:T(8,128)(2,1)S(1)}, u32[]{:S(2)}, u32[]{:S(2)}) collective-permute-start(bf16[272,512]{1,0:T(8,128)(2,1)S(1)} %collective-permute-done.2.refs_1_), channel_id=1, source_target_pairs={{0,8},{4,12},{8,0},{12,4},{16,24},{20,28},{24,16},{28,20},{1,9},{5... | collective-permute-start | bytes 835592 | tf_op jit(solution)/shard_map/ppermute | solution.py:394
  32.3 7.8 %collective-permute-start.6 = (bf16[272,512]{1,0:T(8,128)(2,1)S(1)}, bf16[272,512]{1,0:T(8,128)(2,1)S(1)}, u32[]{:S(2)}, u32[]{:S(2)}) collective-permute-start(bf16[272,512]{1,0:T(8,128)(2,1)S(1)} %collective-permute-done.5.refs_1_), channel_id=1, source_target_pairs={{0,4},{4,0},{8,12},{12,8},{16,20},{20,16},{24,28},{28,24},{1,5},{5... | collective-permute-start | bytes 835592 | tf_op jit(solution)/shard_map/ppermute | solution.py:394
  52.2 5.9 %collective-permute-start.11 = (bf16[8,16,256]{2,1,0:T(8,128)(2,1)S(1)}, bf16[8,16,256]{2,1,0:T(8,128)(2,1)S(1)}, u32[]{:S(2)}, u32[]{:S(2)}) collective-permute-start(bf16[8,16,256]{2,1,0:T(8,128)(2,1)S(1)} %convert_element_type.68), channel_id=1, source_target_pairs={{0,12},{4,8},{8,4},{12,0},{16,28},{20,24},{24,20},{28,16},{1,13},{... | collective-permute-start | bytes 196616 | tf_op jit(solution)/shard_map/ppermute | solution.py:394
  53.8 5.2 %collective-permute-start.10 = (bf16[8,16,256]{2,1,0:T(8,128)(2,1)S(1)}, bf16[8,16,256]{2,1,0:T(8,128)(2,1)S(1)}, u32[]{:S(2)}, u32[]{:S(2)}) collective-permute-start(bf16[8,16,256]{2,1,0:T(8,128)(2,1)S(1)} %convert_element_type.68), channel_id=1, source_target_pairs={{0,8},{4,12},{8,0},{12,4},{16,24},{20,28},{24,16},{28,20},{1,9},{5... | collective-permute-start | bytes 196616 | tf_op jit(solution)/shard_map/ppermute | solution.py:394
  55.3 4.3 %collective-permute-start.9 = (bf16[8,16,256]{2,1,0:T(8,128)(2,1)S(1)}, bf16[8,16,256]{2,1,0:T(8,128)(2,1)S(1)}, u32[]{:S(2)}, u32[]{:S(2)}) collective-permute-start(bf16[8,16,256]{2,1,0:T(8,128)(2,1)S(1)} %convert_element_type.68), channel_id=1, source_target_pairs={{0,4},{4,0},{8,12},{12,8},{16,20},{20,16},{24,28},{28,24},{1,5},{5... | collective-permute-start | bytes 196616 | tf_op jit(solution)/shard_map/ppermute | solution.py:394
  59.6 5.9 %collective-permute-start.12 = (bf16[8,16,256]{2,1,0:T(8,128)(2,1)S(1)}, bf16[8,16,256]{2,1,0:T(8,128)(2,1)S(1)}, u32[]{:S(2)}, u32[]{:S(2)}) collective-permute-start(bf16[8,16,256]{2,1,0:T(8,128)(2,1)S(1)} %fusion.20), channel_id=1, source_target_pairs={{0,16},{4,20},{8,24},{12,28},{16,0},{20,4},{24,8},{28,12},{1,17},{... | collective-permute-start | bytes 196616 | tf_op jit(solution)/shard_map/ppermute | solution.py:394
  65.5 21.5 %copy-start.1 = (f32[16,4096]{1,0:T(8,128)S(1)}, f32[16,4096]{1,0:T(8,128)}, u32[]{:S(2)}) copy-start(f32[16,4096]{1,0:T(8,128)} %coef_ref.1) | copy-start | bytes 786436
  73.5 19.7 %copy-start.2 = (f32[16,1024]{1,0:T(8,128)S(1)}, f32[16,1024]{1,0:T(8,128)}, u32[]{:S(2)}) copy-start(f32[16,1024]{1,0:T(8,128)} %param.10) | copy-start | bytes 196612
  75.6 5.0 %collective-permute-start.15 = (f32[2,16,256]{2,1,0:T(8,128)S(1)}, f32[2,16,256]{2,1,0:T(8,128)S(1)}, u32[]{:S(2)}, u32[]{:S(2)}) collective-permute-start(f32[2,16,256]{2,1,0:T(8,128)S(1)} %get-tuple-element.74), channel_id=1, source_target_pairs={{0,12},{4,8},{8,4},{12,0},{16,28},{20,24},{24,20},{28,16},{1,13},{... | collective-permute-start | bytes 98312 | tf_op jit(solution)/shard_map/ppermute | solution.py:394
  76.4 4.2 %collective-permute-start.14 = (f32[2,16,256]{2,1,0:T(8,128)S(1)}, f32[2,16,256]{2,1,0:T(8,128)S(1)}, u32[]{:S(2)}, u32[]{:S(2)}) collective-permute-start(f32[2,16,256]{2,1,0:T(8,128)S(1)} %get-tuple-element.73), channel_id=1, source_target_pairs={{0,8},{4,12},{8,0},{12,4},{16,24},{20,28},{24,16},{28,20},{1,9},{5... | collective-permute-start | bytes 98312 | tf_op jit(solution)/shard_map/ppermute | solution.py:394
  78.2 3.9 %collective-permute-start.13 = (f32[2,16,256]{2,1,0:T(8,128)S(1)}, f32[2,16,256]{2,1,0:T(8,128)S(1)}, u32[]{:S(2)}, u32[]{:S(2)}) collective-permute-start(f32[2,16,256]{2,1,0:T(8,128)S(1)} %get-tuple-element.72), channel_id=1, source_target_pairs={{0,4},{4,0},{8,12},{12,8},{16,20},{20,16},{24,28},{28,24},{1,5},{5... | collective-permute-start | bytes 98312 | tf_op jit(solution)/shard_map/ppermute | solution.py:394
  82.2 4.8 %collective-permute-start.16 = (f32[1,16,256]{2,1,0:T(8,128)S(1)}, f32[1,16,256]{2,1,0:T(8,128)S(1)}, u32[]{:S(2)}, u32[]{:S(2)}) collective-permute-start(f32[1,16,256]{2,1,0:T(8,128)S(1)} %slice_bitcast_fusion.4), channel_id=1, source_target_pairs={{0,16},{4,20},{8,24},{12,28},{16,0},{20,4},{24,8},{28,12},{1,17},{... | collective-permute-start | bytes 49160 | tf_op jit(solution)/shard_map/ppermute | solution.py:394
  87.0 2.0 %collective-permute-start.17 = (f32[16,256]{1,0:T(8,128)S(1)}, f32[16,256]{1,0:T(8,128)S(1)}, u32[]{:S(2)}, u32[]{:S(2)}) collective-permute-start(f32[16,256]{1,0:T(8,128)S(1)} %fusion.15), channel_id=1, source_target_pairs={{0,1},{1,0},{2,3},{3,2},{4,5},{5,4},{6,7},{7,6},{8,9},{9,8},{10,11... | collective-permute-start | bytes 49160 | tf_op jit(solution)/shard_map/ppermute | solution.py:394
  89.0 4.1 %collective-permute-start.18 = (f32[16,512]{1,0:T(8,128)S(1)}, f32[16,512]{1,0:T(8,128)S(1)}, u32[]{:S(2)}, u32[]{:S(2)}) collective-permute-start(f32[16,512]{1,0:T(8,128)S(1)} %pad_maximum_fusion), channel_id=1, source_target_pairs={{0,2},{1,3},{2,0},{3,1},{4,6},{5,7},{6,4},{7,5},{8,10},{9,11},{10,... | collective-permute-start | bytes 98312 | tf_op jit(solution)/shard_map/ppermute | solution.py:394

commit v13 on v12

--- a/solution.py
+++ b/solution.py
@@ -30,14 +30,6 @@
     return first, second, third
 
 
-def split3_outside(x):
-    first = lax.reduce_precision(x, 8, 7)
-    rest = x - first
-    second = lax.reduce_precision(rest, 8, 7)
-    third = rest - second
-    return first.astype(BF16), second.astype(BF16), third.astype(BF16)
-
-
 def round_up(value, multiple):
     return -(-value // multiple) * multiple
 
@@ -61,6 +53,54 @@
 def two_rows(ref, step, block):
     row = 2 * block
     return jnp.concatenate([ref[step, pl.ds(row, 1), :], ref[step, pl.ds(row + 1, 1), :]], axis=1)
+
+
+def own_kernel(quarter, at_ref, rows_hbm, weight_hbm, target_hbm, pred_hbm, out_ref, weight_ref, target_ref, pred_ref, done):
+    targets = target_ref.shape[0]
+    at = pl.ds(pl.multiple_of(at_ref[0] * quarter, quarter), quarter)
+    copies = [
+        pltpu.make_async_copy(rows_hbm.at[at, :], out_ref.at[pl.ds(0, quarter), :], done.at[0]),
+        pltpu.make_async_copy(weight_hbm.at[:, at], weight_ref, done.at[1]),
+        pltpu.make_async_copy(target_hbm.at[:, at], target_ref, done.at[2]),
+        pltpu.make_async_copy(pred_hbm.at[:, at], pred_ref, done.at[3]),
+    ]
+    for copy in copies:
+        copy.start()
+    rows = out_ref.shape[0] - quarter
+    out_ref[quarter:, :] = jnp.zeros((rows, out_ref.shape[1]), BF16)
+    for copy in copies[1:]:
+        copy.wait()
+    weight = weight_ref[...]
+    weighted = (weight * (target_ref[...] - pred_ref[...])).astype(BF16)
+    out_ref[quarter : quarter + targets, :quarter] = weighted
+    row = lax.broadcasted_iota(jnp.int32, (rows, quarter), 0)
+    parts = jnp.zeros((rows, quarter), F32)
+    for i, part in enumerate(split3(weight)):
+        parts = jnp.where(row == i, part.astype(F32), parts)
+    out_ref[quarter:, quarter : 2 * quarter] = parts.astype(BF16)
+    copies[0].wait()
+
+
+def own_call(my_cent, samples, weights, targets, predictions, quarter):
+    target_count = targets.shape[0]
+    return pl.pallas_call(
+        functools.partial(own_kernel, quarter),
+        name="own",
+        in_specs=[pl.BlockSpec(memory_space=pltpu.SMEM)] + [pl.BlockSpec(memory_space=pltpu.HBM)] * 4,
+        out_specs=in_vmem(1)[0],
+        out_shape=jax.ShapeDtypeStruct((quarter + round_up(target_count, 16), samples.shape[1]), BF16),
+        scratch_shapes=[
+            pltpu.VMEM((1, quarter), F32),
+            pltpu.VMEM((target_count, quarter), F32),
+            pltpu.VMEM((target_count, quarter), F32),
+            pltpu.SemaphoreType.DMA((4,)),
+        ],
+        compiler_params=params(),
+        cost_estimate=pl.CostEstimate(flops=10**5, bytes_accessed=10**6, transcendentals=0),
+    )(
+        my_cent.astype(jnp.int32)[None], in_hbm(samples), in_hbm(weights[None, :]),
+        in_hbm(targets), in_hbm(predictions),
+    )
 
 
 def pool_copy(source, target, half, block, done):
@@ -424,22 +464,7 @@
     sharpness = 1.3 / math.sqrt(8.0 * features)
     offset = 2.0 * features * sharpness - 1.5 - 0.5 * math.log(rows_dev * row_devices)
 
-    at = my_cent * quarter
-    own_rows = lax.dynamic_slice_in_dim(samples, at, quarter, 0)
-    own_weight = lax.dynamic_slice_in_dim(weights, at, quarter, 0)[None, :]
-    own_target = lax.dynamic_slice_in_dim(targets, at, quarter, 1)
-    own_pred = lax.dynamic_slice_in_dim(predictions, at, quarter, 1)
-    weighted = (own_weight * (own_target - own_pred)).astype(BF16)
-    side_count = round_up(target_count, 16)
-    weight_parts = jnp.concatenate(split3_outside(own_weight), axis=0)
-    side_block = jnp.concatenate(
-        [
-            jnp.pad(weighted, ((0, side_count - target_count), (0, 0))),
-            jnp.pad(weight_parts, ((0, side_count - 3), (0, features - 2 * quarter))),
-        ],
-        axis=1,
-    )
-    chunks = {0: jnp.concatenate([own_rows, side_block], axis=0)}
+    chunks = {0: own_call(my_cent, samples, weights, targets, predictions, quarter)}
 
     high_count = pool_dev // LANES
     place = block_index - my_row * pool_dev

time: 94.1 us -> 93.4 us (level)
  other arithmetic: 3.39 us -> 1.75 us
  Pallas kernels: 32.4 us -> 33.4 us
    convert_element_type x3 -> x0, other arithmetic: 1.52 us -> none  [the longest x2 0.77 us: split3_outside(): return (first.astype(BF16), second.astype(BF16), third.astype(BF16))]
    pallas_call x0 -> x1, Pallas kernels: none -> 0.98 us  [own_call(): pl.pallas_call(functools.partial(own_kernel, quarter), name='own', in_spe...]
  transfers between devices with their start and end apart: 19 -> 19, of which waited for: 10 -> 10; matrix products, arithmetic and copies ran while one was open for 2% -> 1% of each run, Pallas kernels for 26% -> 28%
where the time goes in v13:
time: 93.4 us; the launch traced here: 93.1 us
  Pallas kernels  33.4 us (36%)
  starting transfers between devices  23.8 us (25%)
  waiting for transfers between devices  17.4 us (19%)
  blocking collectives  14.5 us (16%)
  other arithmetic  1.75 us (2%)
  matrix products  1.15 us (1%)
    ppermute x19, starting transfers between devices, swap(): return lax.ppermute(value, axis, [(i, i ^ bit) for i in range(count)])  23.8 us
    ppermute x19, waiting for transfers between devices, swap(): return lax.ppermute(value, axis, [(i, i ^ bit) for i in range(count)])  17.4 us
    pallas_call x8, Pallas kernels, block_call(): pl.pallas_call(functools.partial(block_kernel, first_step, targets, quart...  14.6 us
    all_gather x2, blocking collectives, local(): lax.all_gather(sums, 'cent')  14.5 us
    pallas_call x2, Pallas kernels, compact(): pl.pallas_call(functools.partial(compact_kernel, step, per_step, targets)...  5.91 us
    pallas_call x2, Pallas kernels, scatter_call(): pl.pallas_call(functools.partial(scatter_kernel, targets, step), name='sc...  4.69 us
    pallas_call x2, Pallas kernels, change_call(): pl.pallas_call(functools.partial(change_kernel, targets, before is None,...  4.21 us
  transfers between devices with their start and end apart: 19, of which 10 were waited for; matrix products, arithmetic and copies ran while one was open for 1% of the time, Pallas kernels for 28%

profile of v13, /device:TPU:0, one launch (start us, length us, event | category | flops | bytes accessed | tf_op | source)
XLA Modules:
  0.0 93.1 jit_solution(3371329280946080945)
XLA Ops:
  3.7 2.6 %collective-permute-start.2 = (bf16[272,512]{1,0:T(8,128)(2,1)S(1)}, bf16[272,512]{1,0:T(8,128)(2,1)S(1)}, u32[]{:S(2)}, u32[]{:S(2)}) collective-permute-start(bf16[272,512]{1,0:T(8,128)(2,1)S(1)} %own.1.refs_0_), channel_id=1, source_target_pairs={{0,4},{4,0},{8,12},{12,8},{16,20},{20,16},{24,28},{28,24},{1,5},{5... | collective-permute-start | bytes 835592 | tf_op jit(solution)/shard_map/ppermute | solution.py:434
  6.3 2.6 %collective-permute-start.4 = (bf16[272,512]{1,0:T(8,128)(2,1)S(1)}, bf16[272,512]{1,0:T(8,128)(2,1)S(1)}, u32[]{:S(2)}, u32[]{:S(2)}) collective-permute-start(bf16[272,512]{1,0:T(8,128)(2,1)S(1)} %own.1.refs_0_), channel_id=1, source_target_pairs={{0,16},{4,20},{8,24},{12,28},{16,0},{20,4},{24,8},{28,12},{1,17},{... | collective-permute-start | bytes 835592 | tf_op jit(solution)/shard_map/ppermute | solution.py:434
  8.9 1.6 %collective-permute-start.8 = (bf16[272,512]{1,0:T(8,128)(2,1)S(1)}, bf16[272,512]{1,0:T(8,128)(2,1)S(1)}, u32[]{:S(2)}, u32[]{:S(2)}) collective-permute-start(bf16[272,512]{1,0:T(8,128)(2,1)S(1)} %own.1.refs_0_), channel_id=1, source_target_pairs={{0,8},{4,12},{8,0},{12,4},{16,24},{20,28},{24,16},{28,20},{1,9},{5... | collective-permute-start | bytes 835592 | tf_op jit(solution)/shard_map/ppermute | solution.py:434
  10.5 1.6 %collective-permute-start.1 = (bf16[2,32,128]{2,1,0:T(8,128)(2,1)S(1)}, bf16[2,32,128]{2,1,0:T(8,128)(2,1)S(1)}, u32[]{:S(2)}, u32[]{:S(2)}) collective-permute-start(bf16[2,32,128]{2,1,0:T(8,128)(2,1)S(1)} %add.56), channel_id=1, source_target_pairs={{0,2},{1,3},{2,0},{3,1},{4,6},{5,7},{6,4},{7,5},{8,10},{9,11},{10,... | collective-permute-start | bytes 49160 | tf_op jit(solution)/shard_map/ppermute | solution.py:434
  12.0 1.7 %load.1 = (bf16[2048,512]{1,0:T(8,128)(2,1)S(1)}, bf16[128,4096]{1,0:T(8,128)(2,1)S(1)}) custom-call(bf16[4096,512]{1,0:T(8,128)(2,1)} %refs_2_.1, f32[16,4096]{1,0:T(8,128)} %coef_ref.1), custom_call_target="tpu_custom_call" | custom-call | flops 1000000 | bytes 3000000 | tf_op jit(solution)/shard_map/load/pallas_call | solution.py:128
  15.0 3.0 %compact.2 = (bf16[1808,512]{1,0:T(8,128)(2,1)S(1)}, f32[8,1536]{1,0:T(8,128)S(1)}, f32[16,1536]{1,0:T(8,128)S(1)}, bf16[2048,512]{1,0:T(8,128)(2,1)S(1)}) custom-call(s32[2,17]{1,0:T(2,128)S(1)} %convolution_convert_fusion.off_ref, s32[2,32,128]{2,1,0:T(8,128)S(1)} %select_convert_fusion.dest_ref, bf16[2048,512]{1,0:T(8,128)(2,1)S(1)} %get-tuple-element.36.refs_0_, ...), custom_call_target="tpu_custom_call" | custom-call | flops 2000000000 | bytes 6000000 | tf_op jit(solution)/shard_map/compact/pallas_call | solution.py:237
  18.0 2.9 %compact.3 = (bf16[1808,512]{1,0:T(8,128)(2,1)S(1)}, f32[8,1536]{1,0:T(8,128)S(1)}, f32[16,1536]{1,0:T(8,128)S(1)}) custom-call(s32[2,17]{1,0:T(2,128)S(1)} %convolution_convert_fusion.off_ref, s32[2,32,128]{2,1,0:T(8,128)S(1)} %select_convert_fusion.dest_ref, bf16[2048,512]{1,0:T(8,128)(2,1)S(1)} %get-tuple-element.36.refs_0_, ...), custom_call_target="tpu_custom_call" | custom-call | flops 2000000000 | bytes 6000000 | tf_op jit(solution)/shard_map/compact/pallas_call | solution.py:237
  24.6 2.1 %kernel_block.8 = (bf16[8,256,1536]{2,1,0:T(8,128)(2,1)S(1)}, f32[24,1536]{1,0:T(8,128)S(1)}, f32[8,24,256]{2,1,0:T(8,128)S(1)}) custom-call(s32[1]{0:T(128)} %bitcast.1.me_ref, bf16[1808,512]{1,0:T(8,128)(2,1)S(1)} %get-tuple-element.38.chosen_ref, f32[8,1536]{1,0:T(8,128)S(1)} %get-tuple-element.39.norm_ref, bf16[272,512]{1,0:T(8,128)(2,1)S(1)} %own.1.refs_0_, ...), custom_call_target="tpu_custom_call" | custom-call | flops 805306368 | bytes 1572864 | tf_op jit(solution)/shard_map/kernel_block/pallas_call | solution.py:312
  26.7 4.9 %collective-permute-done.5.refs_1_ = bf16[272,512]{1,0:T(8,128)(2,1)S(1)} collective-permute-done((bf16[272,512]{1,0:T(8,128)(2,1)S(1)}, bf16[272,512]{1,0:T(8,128)(2,1)S(1)}, u32[]{:S(2)}, u32[]{:S(2)}) %collective-permute-start.5) | collective-permute-done | bytes 278560 | tf_op jit(solution)/shard_map/ppermute | solution.py:434
  32.0 1.5 %kernel_block.12 = (bf16[8,256,1536]{2,1,0:T(8,128)(2,1)S(1)}, f32[8,1536]{1,0:T(8,128)S(1)}) custom-call(s32[1]{0:T(128)} %bitcast.1.me_ref, bf16[1808,512]{1,0:T(8,128)(2,1)S(1)} %get-tuple-element.55.chosen_ref, f32[8,1536]{1,0:T(8,128)S(1)} %get-tuple-element.56.norm_ref, bf16[272,512]{1,0:T(8,128)(2,1)S(1)} %own.1.refs_0_, ...), custom_call_target="tpu_custom_call" | custom-call | flops 805306368 | bytes 1572864 | tf_op jit(solution)/shard_map/kernel_block/pallas_call | solution.py:312
  35.1 2.1 %kernel_block.9 = (bf16[8,256,1536]{2,1,0:T(8,128)(2,1)S(1)}, f32[24,1536]{1,0:T(8,128)S(1)}, f32[8,24,256]{2,1,0:T(8,128)S(1)}) custom-call(s32[1]{0:T(128)} %bitcast.1.me_ref, bf16[1808,512]{1,0:T(8,128)(2,1)S(1)} %get-tuple-element.38.chosen_ref, ...), custom_call_target="tpu_custom_call", output_to_operand_aliasing={{0}: (5, {}), {1}: (6, {}), {2}: (7, {})} | custom-call | flops 805306368 | bytes 1572864 | tf_op jit(solution)/shard_map/kernel_block/pallas_call | solution.py:312
  37.3 2.1 %kernel_block.10 = (bf16[8,256,1536]{2,1,0:T(8,128)(2,1)S(1)}, f32[24,1536]{1,0:T(8,128)S(1)}, f32[8,24,256]{2,1,0:T(8,128)S(1)}) custom-call(s32[1]{0:T(128)} %bitcast.1.me_ref, bf16[1808,512]{1,0:T(8,128)(2,1)S(1)} %get-tuple-element.38.chosen_ref, ...), custom_call_target="tpu_custom_call", output_to_operand_aliasing={{0}: (5, {}), {1}: (6, {}), {2}: (7, {})} | custom-call | flops 805306368 | bytes 1572864 | tf_op jit(solution)/shard_map/kernel_block/pallas_call | solution.py:312
  39.4 2.1 %kernel_block.11 = (bf16[8,256,1536]{2,1,0:T(8,128)(2,1)S(1)}, f32[24,1536]{1,0:T(8,128)S(1)}, f32[8,24,256]{2,1,0:T(8,128)S(1)}) custom-call(s32[1]{0:T(128)} %bitcast.1.me_ref, bf16[1808,512]{1,0:T(8,128)(2,1)S(1)} %get-tuple-element.38.chosen_ref, ...), custom_call_target="tpu_custom_call", output_to_operand_aliasing={{0}: (5, {}), {1}: (6, {}), {2}: (7, {})} | custom-call | flops 805306368 | bytes 1572864 | tf_op jit(solution)/shard_map/kernel_block/pallas_call | solution.py:312
  41.5 7.8 %all-gather = f32[96,1536]{1,0:T(8,128)S(1)} all-gather(f32[24,1536]{1,0:T(8,128)S(1)} %get-tuple-element.49), channel_id=2, replica_groups=mesh['rows'=8,'cent'=4] {'cent'}, dimensions={0}, use_global_device_ids=true | all-gather | bytes 737280 | tf_op jit(solution)/shard_map/all_gather | solution.py:533
  49.3 2.1 %change.2 = (f32[16,1536]{1,0:T(8,128)S(1)}, f32[8,16,256]{2,1,0:T(8,128)S(1)}, f32[8,16,256]{2,1,0:T(8,128)S(1)}) custom-call(s32[1]{0:T(128)} %bitcast.1.me_ref, f32[4,24,1536]{2,1,0:T(8,128)S(1)} %bitcast.47, f32[16,1536]{1,0:T(8,128)S(1)} %get-tuple-element.50.coef_ref, bf16[8,256,1536]{2,1,0:T(8,128)(2,1)S(1)} %get-tuple-element.51.k_ref, ...), custom_call_target="tpu_custom_call" | custom-call | flops 100663296 | bytes 6291456 | tf_op jit(solution)/shard_map/change/pallas_call | solution.py:360
  51.5 1.6 %collective-permute-start.11 = (bf16[8,16,256]{2,1,0:T(8,128)(2,1)S(1)}, bf16[8,16,256]{2,1,0:T(8,128)(2,1)S(1)}, u32[]{:S(2)}, u32[]{:S(2)}) collective-permute-start(bf16[8,16,256]{2,1,0:T(8,128)(2,1)S(1)} %convert_element_type.38), channel_id=1, source_target_pairs={{0,12},{4,8},{8,4},{12,0},{16,28},{20,24},{24,20},{28,16},{1,13},{... | collective-permute-start | bytes 196616 | tf_op jit(solution)/shard_map/ppermute | solution.py:434
  58.8 2.0 %collective-permute-start.12 = (bf16[8,16,256]{2,1,0:T(8,128)(2,1)S(1)}, bf16[8,16,256]{2,1,0:T(8,128)(2,1)S(1)}, u32[]{:S(2)}, u32[]{:S(2)}) collective-permute-start(bf16[8,16,256]{2,1,0:T(8,128)(2,1)S(1)} %fusion.17), channel_id=1, source_target_pairs={{0,16},{4,20},{8,24},{12,28},{16,0},{20,4},{24,8},{28,12},{1,17},{... | collective-permute-start | bytes 196616 | tf_op jit(solution)/shard_map/ppermute | solution.py:434
  62.4 2.4 %collective-permute-done.12 = bf16[8,16,256]{2,1,0:T(8,128)(2,1)S(1)} collective-permute-done((bf16[8,16,256]{2,1,0:T(8,128)(2,1)S(1)}, bf16[8,16,256]{2,1,0:T(8,128)(2,1)S(1)}, u32[]{:S(2)}, u32[]{:S(2)}) %collective-permute-start.12) | collective-permute-done | bytes 65568 | tf_op jit(solution)/shard_map/ppermute | solution.py:434
  66.1 6.7 %all-gather.1 = f32[96,1536]{1,0:T(8,128)S(1)} all-gather(f32[24,1536]{1,0:T(8,128)S(1)} %gradient.1), channel_id=3, replica_groups=mesh['rows'=8,'cent'=4] {'cent'}, dimensions={0}, use_global_device_ids=true | all-gather | bytes 737280 | tf_op jit(solution)/shard_map/all_gather | solution.py:533
  72.8 2.1 %change.3 = (f32[16,1536]{1,0:T(8,128)S(1)}, f32[8,16,256]{2,1,0:T(8,128)S(1)}) custom-call(s32[1]{0:T(128)} %bitcast.1.me_ref, f32[4,24,1536]{2,1,0:T(8,128)S(1)} %bitcast.48, f32[16,1536]{1,0:T(8,128)S(1)} %get-tuple-element.65.coef_ref, bf16[8,256,1536]{2,1,0:T(8,128)(2,1)S(1)} %get-tuple-element.63.k_ref, f32[8,24,256]{2,1,0:T(8,128)S(1)} %get-tuple-element.52.side_ref, ...), custom_call_target="tpu_custom_call" | custom-call | flops 100663296 | bytes 6291456 | tf_op jit(solution)/shard_map/change/pallas_call | solution.py:360
  75.7 1.8 %collective-permute-start.14 = (f32[2,16,256]{2,1,0:T(8,128)S(1)}, f32[2,16,256]{2,1,0:T(8,128)S(1)}, u32[]{:S(2)}, u32[]{:S(2)}) collective-permute-start(f32[2,16,256]{2,1,0:T(8,128)S(1)} %get-tuple-element.71), channel_id=1, source_target_pairs={{0,8},{4,12},{8,0},{12,4},{16,24},{20,28},{24,16},{28,20},{1,9},{5... | collective-permute-start | bytes 98312 | tf_op jit(solution)/shard_map/ppermute | solution.py:434
  82.9 3.4 %collective-permute-done.16 = f32[1,16,256]{2,1,0:T(8,128)S(1)} collective-permute-done((f32[1,16,256]{2,1,0:T(8,128)S(1)}, f32[1,16,256]{2,1,0:T(8,128)S(1)}, u32[]{:S(2)}, u32[]{:S(2)}) %collective-permute-start.16) | collective-permute-done | bytes 16416 | tf_op jit(solution)/shard_map/ppermute | solution.py:434
  86.3 2.0 %scatter.2.coef_ref = f32[16,4096]{1,0:T(8,128)S(1)} custom-call(s32[2,17]{1,0:T(2,128)S(1)} %convolution_convert_fusion.off_ref, s32[2,32,128]{2,1,0:T(8,128)S(1)} %select_convert_fusion.dest_ref, f32[16,4096]{1,0:T(8,128)S(1)} %copy-done, f32[16,1536]{1,0:T(8,128)S(1)} %get-tuple-element.67.delta_ref), custom_call_target="tpu_custom_call" | custom-call | flops 1000000000 | bytes 1000000 | tf_op jit(solution)/shard_map/scatter/pallas_call | solution.py:420
  89.7 2.7 %scatter.3 = f32[16,4096]{1,0:T(8,128)} custom-call(s32[2,17]{1,0:T(2,128)S(1)} %convolution_convert_fusion.off_ref, s32[2,32,128]{2,1,0:T(8,128)S(1)} %select_convert_fusion.dest_ref, f32[16,4096]{1,0:T(8,128)S(1)} %scatter.2.coef_ref, f32[16,1536]{1,0:T(8,128)S(1)} %get-tuple-element.68.delta_ref), custom_call_target="tpu_custom_call" | custom-call | flops 1000000000 | bytes 1000000 | tf_op jit(solution)/shard_map/scatter/pallas_call | solution.py:420
  (58 shorter events, 26.9 us)
Async XLA Ops:
  2.2 8.3 %collective-permute-start = (bf16[2,32,128]{2,1,0:T(8,128)(2,1)S(1)}, bf16[2,32,128]{2,1,0:T(8,128)(2,1)S(1)}, u32[]{:S(2)}, u32[]{:S(2)}) collective-permute-start(bf16[2,32,128]{2,1,0:T(8,128)(2,1)S(1)} %fusion.2), channel_id=1, source_target_pairs={{0,1},{1,0},{2,3},{3,2},{4,5},{5,4},{6,7},{7,6},{8,9},{9,8},{10,11... | collective-permute-start | bytes 49160 | tf_op jit(solution)/shard_map/ppermute | solution.py:434
  3.7 19.5 %collective-permute-start.2 = (bf16[272,512]{1,0:T(8,128)(2,1)S(1)}, bf16[272,512]{1,0:T(8,128)(2,1)S(1)}, u32[]{:S(2)}, u32[]{:S(2)}) collective-permute-start(bf16[272,512]{1,0:T(8,128)(2,1)S(1)} %own.1.refs_0_), channel_id=1, source_target_pairs={{0,4},{4,0},{8,12},{12,8},{16,20},{20,16},{24,28},{28,24},{1,5},{5... | collective-permute-start | bytes 835592 | tf_op jit(solution)/shard_map/ppermute | solution.py:434
  6.3 15.7 %collective-permute-start.4 = (bf16[272,512]{1,0:T(8,128)(2,1)S(1)}, bf16[272,512]{1,0:T(8,128)(2,1)S(1)}, u32[]{:S(2)}, u32[]{:S(2)}) collective-permute-start(bf16[272,512]{1,0:T(8,128)(2,1)S(1)} %own.1.refs_0_), channel_id=1, source_target_pairs={{0,16},{4,20},{8,24},{12,28},{16,0},{20,4},{24,8},{28,12},{1,17},{... | collective-permute-start | bytes 835592 | tf_op jit(solution)/shard_map/ppermute | solution.py:434
  8.9 24.7 %collective-permute-start.8 = (bf16[272,512]{1,0:T(8,128)(2,1)S(1)}, bf16[272,512]{1,0:T(8,128)(2,1)S(1)}, u32[]{:S(2)}, u32[]{:S(2)}) collective-permute-start(bf16[272,512]{1,0:T(8,128)(2,1)S(1)} %own.1.refs_0_), channel_id=1, source_target_pairs={{0,8},{4,12},{8,0},{12,4},{16,24},{20,28},{24,16},{28,20},{1,9},{5... | collective-permute-start | bytes 835592 | tf_op jit(solution)/shard_map/ppermute | solution.py:434
  10.5 3.8 %collective-permute-start.1 = (bf16[2,32,128]{2,1,0:T(8,128)(2,1)S(1)}, bf16[2,32,128]{2,1,0:T(8,128)(2,1)S(1)}, u32[]{:S(2)}, u32[]{:S(2)}) collective-permute-start(bf16[2,32,128]{2,1,0:T(8,128)(2,1)S(1)} %add.56), channel_id=1, source_target_pairs={{0,2},{1,3},{2,0},{3,1},{4,6},{5,7},{6,4},{7,5},{8,10},{9,11},{10,... | collective-permute-start | bytes 49160 | tf_op jit(solution)/shard_map/ppermute | solution.py:434
  22.0 9.5 %collective-permute-start.5 = (bf16[272,512]{1,0:T(8,128)(2,1)S(1)}, bf16[272,512]{1,0:T(8,128)(2,1)S(1)}, u32[]{:S(2)}, u32[]{:S(2)}) collective-permute-start(bf16[272,512]{1,0:T(8,128)(2,1)S(1)} %collective-permute-done.4.refs_1_), channel_id=1, source_target_pairs={{0,8},{4,12},{8,0},{12,4},{16,24},{20,28},{24,16},{28,20},{1,9},{5... | collective-permute-start | bytes 835592 | tf_op jit(solution)/shard_map/ppermute | solution.py:434
  22.6 14.6 %collective-permute-start.7 = (bf16[272,512]{1,0:T(8,128)(2,1)S(1)}, bf16[272,512]{1,0:T(8,128)(2,1)S(1)}, u32[]{:S(2)}, u32[]{:S(2)}) collective-permute-start(bf16[272,512]{1,0:T(8,128)(2,1)S(1)} %broadcast_add_fusion), channel_id=1, source_target_pairs={{0,4},{4,0},{8,12},{12,8},{16,20},{20,16},{24,28},{28,24},{1,5},{5... | collective-permute-start | bytes 835592 | tf_op jit(solution)/shard_map/ppermute | solution.py:434
  23.2 16.2 %collective-permute-start.3 = (bf16[272,512]{1,0:T(8,128)(2,1)S(1)}, bf16[272,512]{1,0:T(8,128)(2,1)S(1)}, u32[]{:S(2)}, u32[]{:S(2)}) collective-permute-start(bf16[272,512]{1,0:T(8,128)(2,1)S(1)} %collective-permute-done.2.refs_1_), channel_id=1, source_target_pairs={{0,8},{4,12},{8,0},{12,4},{16,24},{20,28},{24,16},{28,20},{1,9},{5... | collective-permute-start | bytes 835592 | tf_op jit(solution)/shard_map/ppermute | solution.py:434
  31.6 7.8 %collective-permute-start.6 = (bf16[272,512]{1,0:T(8,128)(2,1)S(1)}, bf16[272,512]{1,0:T(8,128)(2,1)S(1)}, u32[]{:S(2)}, u32[]{:S(2)}) collective-permute-start(bf16[272,512]{1,0:T(8,128)(2,1)S(1)} %collective-permute-done.5.refs_1_), channel_id=1, source_target_pairs={{0,4},{4,0},{8,12},{12,8},{16,20},{20,16},{24,28},{28,24},{1,5},{5... | collective-permute-start | bytes 835592 | tf_op jit(solution)/shard_map/ppermute | solution.py:434
  51.5 5.9 %collective-permute-start.11 = (bf16[8,16,256]{2,1,0:T(8,128)(2,1)S(1)}, bf16[8,16,256]{2,1,0:T(8,128)(2,1)S(1)}, u32[]{:S(2)}, u32[]{:S(2)}) collective-permute-start(bf16[8,16,256]{2,1,0:T(8,128)(2,1)S(1)} %convert_element_type.38), channel_id=1, source_target_pairs={{0,12},{4,8},{8,4},{12,0},{16,28},{20,24},{24,20},{28,16},{1,13},{... | collective-permute-start | bytes 196616 | tf_op jit(solution)/shard_map/ppermute | solution.py:434
  53.1 5.2 %collective-permute-start.10 = (bf16[8,16,256]{2,1,0:T(8,128)(2,1)S(1)}, bf16[8,16,256]{2,1,0:T(8,128)(2,1)S(1)}, u32[]{:S(2)}, u32[]{:S(2)}) collective-permute-start(bf16[8,16,256]{2,1,0:T(8,128)(2,1)S(1)} %convert_element_type.38), channel_id=1, source_target_pairs={{0,8},{4,12},{8,0},{12,4},{16,24},{20,28},{24,16},{28,20},{1,9},{5... | collective-permute-start | bytes 196616 | tf_op jit(solution)/shard_map/ppermute | solution.py:434
  54.5 4.3 %collective-permute-start.9 = (bf16[8,16,256]{2,1,0:T(8,128)(2,1)S(1)}, bf16[8,16,256]{2,1,0:T(8,128)(2,1)S(1)}, u32[]{:S(2)}, u32[]{:S(2)}) collective-permute-start(bf16[8,16,256]{2,1,0:T(8,128)(2,1)S(1)} %convert_element_type.38), channel_id=1, source_target_pairs={{0,4},{4,0},{8,12},{12,8},{16,20},{20,16},{24,28},{28,24},{1,5},{5... | collective-permute-start | bytes 196616 | tf_op jit(solution)/shard_map/ppermute | solution.py:434
  58.8 5.9 %collective-permute-start.12 = (bf16[8,16,256]{2,1,0:T(8,128)(2,1)S(1)}, bf16[8,16,256]{2,1,0:T(8,128)(2,1)S(1)}, u32[]{:S(2)}, u32[]{:S(2)}) collective-permute-start(bf16[8,16,256]{2,1,0:T(8,128)(2,1)S(1)} %fusion.17), channel_id=1, source_target_pairs={{0,16},{4,20},{8,24},{12,28},{16,0},{20,4},{24,8},{28,12},{1,17},{... | collective-permute-start | bytes 196616 | tf_op jit(solution)/shard_map/ppermute | solution.py:434
  64.8 21.5 %copy-start = (f32[16,4096]{1,0:T(8,128)S(1)}, f32[16,4096]{1,0:T(8,128)}, u32[]{:S(2)}) copy-start(f32[16,4096]{1,0:T(8,128)} %coef_ref.1) | copy-start | bytes 786436
  72.8 19.7 %copy-start.1 = (f32[16,1024]{1,0:T(8,128)S(1)}, f32[16,1024]{1,0:T(8,128)}, u32[]{:S(2)}) copy-start(f32[16,1024]{1,0:T(8,128)} %pred_hbm.1) | copy-start | bytes 196612
  74.9 5.0 %collective-permute-start.15 = (f32[2,16,256]{2,1,0:T(8,128)S(1)}, f32[2,16,256]{2,1,0:T(8,128)S(1)}, u32[]{:S(2)}, u32[]{:S(2)}) collective-permute-start(f32[2,16,256]{2,1,0:T(8,128)S(1)} %get-tuple-element.72), channel_id=1, source_target_pairs={{0,12},{4,8},{8,4},{12,0},{16,28},{20,24},{24,20},{28,16},{1,13},{... | collective-permute-start | bytes 98312 | tf_op jit(solution)/shard_map/ppermute | solution.py:434
  75.7 4.2 %collective-permute-start.14 = (f32[2,16,256]{2,1,0:T(8,128)S(1)}, f32[2,16,256]{2,1,0:T(8,128)S(1)}, u32[]{:S(2)}, u32[]{:S(2)}) collective-permute-start(f32[2,16,256]{2,1,0:T(8,128)S(1)} %get-tuple-element.71), channel_id=1, source_target_pairs={{0,8},{4,12},{8,0},{12,4},{16,24},{20,28},{24,16},{28,20},{1,9},{5... | collective-permute-start | bytes 98312 | tf_op jit(solution)/shard_map/ppermute | solution.py:434
  77.5 3.9 %collective-permute-start.13 = (f32[2,16,256]{2,1,0:T(8,128)S(1)}, f32[2,16,256]{2,1,0:T(8,128)S(1)}, u32[]{:S(2)}, u32[]{:S(2)}) collective-permute-start(f32[2,16,256]{2,1,0:T(8,128)S(1)} %get-tuple-element.70), channel_id=1, source_target_pairs={{0,4},{4,0},{8,12},{12,8},{16,20},{20,16},{24,28},{28,24},{1,5},{5... | collective-permute-start | bytes 98312 | tf_op jit(solution)/shard_map/ppermute | solution.py:434
  81.4 4.8 %collective-permute-start.16 = (f32[1,16,256]{2,1,0:T(8,128)S(1)}, f32[1,16,256]{2,1,0:T(8,128)S(1)}, u32[]{:S(2)}, u32[]{:S(2)}) collective-permute-start(f32[1,16,256]{2,1,0:T(8,128)S(1)} %slice_bitcast_fusion.4), channel_id=1, source_target_pairs={{0,16},{4,20},{8,24},{12,28},{16,0},{20,4},{24,8},{28,12},{1,17},{... | collective-permute-start | bytes 49160 | tf_op jit(solution)/shard_map/ppermute | solution.py:434
  86.3 2.0 %collective-permute-start.17 = (f32[16,256]{1,0:T(8,128)S(1)}, f32[16,256]{1,0:T(8,128)S(1)}, u32[]{:S(2)}, u32[]{:S(2)}) collective-permute-start(f32[16,256]{1,0:T(8,128)S(1)} %fusion.15), channel_id=1, source_target_pairs={{0,1},{1,0},{2,3},{3,2},{4,5},{5,4},{6,7},{7,6},{8,9},{9,8},{10,11... | collective-permute-start | bytes 49160 | tf_op jit(solution)/shard_map/ppermute | solution.py:434
  88.3 4.1 %collective-permute-start.18 = (f32[16,512]{1,0:T(8,128)S(1)}, f32[16,512]{1,0:T(8,128)S(1)}, u32[]{:S(2)}, u32[]{:S(2)}) collective-permute-start(f32[16,512]{1,0:T(8,128)S(1)} %pad_maximum_fusion), channel_id=1, source_target_pairs={{0,2},{1,3},{2,0},{3,1},{4,6},{5,7},{6,4},{7,5},{8,10},{9,11},{10,... | collective-permute-start | bytes 98312 | tf_op jit(solution)/shard_map/ppermute | solution.py:434
